TPU v7x, 32 devices: a whole 2x2x4 slice. The times are simulated.
32 devices in a mesh: dp: 8 (over z, x), tensor: 4 (over y, core).
Axes of the slice: x: 2, y: 2, z: 4, core: 2. Of those that a mesh axis runs over, the one named last changes fastest.
Arguments:
- inputs: bfloat16 [32, 577, 1024], P('dp', None, 'tensor'), may hold values from -6 to 6
- cotangent: bfloat16 [32, 577, 1024], P('dp', None, 'tensor'), may hold values from -6 to 6
- slot_mask: int32 [32], P('dp'), may hold values from 0 to 1, as said below
- w_qkv: bfloat16 [3, 1024, 1024], P(None, None, 'tensor'), may hold values from -0.1875 to 0.1875
- bias_qv: bfloat16 [2, 1024], P(None, 'tensor'), may hold values from -3 to 3
- w_out: bfloat16 [1024, 1024], P('tensor'), may hold values from -2 to 2
- bias_out: bfloat16 [1024], replicated, may hold values from -3 to 3
- ln1_gain: bfloat16 [1024], replicated, may hold values from 0.25 to 1.75
- ln1_bias: bfloat16 [1024], replicated, may hold values from -2 to 2
- ln2_gain: bfloat16 [1024], replicated, may hold values from 0.25 to 1.75
- ln2_bias: bfloat16 [1024], replicated, may hold values from -2 to 2
- w_up: bfloat16 [1024, 4096], P(None, 'tensor'), may hold values from -0.1875 to 0.1875
- bias_up: bfloat16 [4096], P('tensor'), may hold values from -3 to 3
- w_down: bfloat16 [4096, 1024], P('tensor'), may hold values from -0.09375 to 0.09375
- bias_down: bfloat16 [1024], replicated, may hold values from -3 to 3
Outputs:
- layer_out: bfloat16 [32, 577, 1024], P('dp', None, 'tensor')
- input_grad: bfloat16 [32, 577, 1024], P('dp', None, 'tensor')
- grad_qkv: float32 [3, 1024, 1024], P(None, None, 'tensor')
- grad_bias_qv: float32 [2, 1024], P(None, 'tensor')
- grad_out: float32 [1024, 1024], P('tensor')
- grad_bias_out: float32 [1024], replicated
- grad_ln1_gain: float32 [1024], replicated
- grad_ln1_bias: float32 [1024], replicated
- grad_ln2_gain: float32 [1024], replicated
- grad_ln2_bias: float32 [1024], replicated
- grad_up: float32 [1024, 4096], P(None, 'tensor')
- grad_bias_up: float32 [4096], P('tensor')
- grad_down: float32 [4096, 1024], P('tensor')
- grad_bias_down: float32 [1024], replicated
Inputs may be any that keep to these rules, and one draw needn't show every extreme that they name: `slot_mask`: exactly 28 of the 32 entries are 1.
All inputs are finite; a program needn't handle non-finite values.
Results may differ from a plain program's by a relative error of at most 0.012.
The roundings to bfloat16 on the way count: a program that leaves them out, or rounds other values in their place, can miss the bound.
Values may be sent and summed in bfloat16 or wider, within the bound.
No kernel may reach another device: no remote copies, remote signals or barrier semaphores. Data moves between devices by JAX's collectives and lax.ppermute only.
A program may use at most 256 MiB of HBM per device.

v0:
```python
import jax
import jax.numpy as jnp
from jax import lax
from jax.sharding import PartitionSpec as P

HEAD = 64
MICRO = 4


EPS = 1e-05
GELU_K = 1.702


def normalize(rows, gain, shift):
    center = rows - jnp.mean(rows, axis=-1, keepdims=True)
    inv_std = lax.rsqrt(jnp.mean(center * center, axis=-1, keepdims=True) + EPS)
    unit = center * inv_std
    return (unit, inv_std, unit * gain + shift)


def feature_sum(partial_value):
    return lax.psum_scatter(partial_value, "tensor", scatter_dimension=2, tiled=True)


def norm_back(grad_norm, unit_full, inv_std, gain_slice, offset, width):
    unit_slice = lax.dynamic_slice_in_dim(unit_full, offset, width, 2)
    scaled = grad_norm * gain_slice
    first, second = lax.psum(
        (jnp.sum(scaled, axis=-1), jnp.sum(scaled * unit_slice, axis=-1)), "tensor"
    )
    full_width = unit_full.shape[2]
    grad_rows = inv_std * (
        scaled - first[..., None] / full_width - unit_slice * second[..., None] / full_width
    )
    return (
        grad_rows,
        jnp.sum(grad_norm * unit_slice, axis=(0, 1)),
        jnp.sum(grad_norm, axis=(0, 1)),
    )


def per_device(
    inputs,
    cotangent,
    slot_mask,
    w_qkv,
    bias_qv,
    w_out,
    bias_out,
    ln1_gain,
    ln1_bias,
    ln2_gain,
    ln2_bias,
    w_up,
    bias_up,
    w_down,
    bias_down,
):
    f32 = jnp.float32
    bf16 = jnp.bfloat16
    width = inputs.shape[2]
    offset = lax.axis_index("tensor") * width
    heads_here = width // HEAD
    per_block = inputs.shape[0] // MICRO
    seq_len = inputs.shape[1]
    shape4 = (per_block, seq_len, heads_here, HEAD)

    def sliced(vector):
        return lax.dynamic_slice_in_dim(vector.astype(f32), offset, width, 0)

    gain_one = ln1_gain.astype(f32)
    shift_one = ln1_bias.astype(f32)
    gain_two = ln2_gain.astype(f32)
    shift_two = ln2_bias.astype(f32)
    gain_one_s = sliced(ln1_gain)
    gain_two_s = sliced(ln2_gain)
    out_bias_s = sliced(bias_out)
    down_bias_s = sliced(bias_down)
    qv_bias = bias_qv.astype(f32)
    up_bias = bias_up.astype(f32)
    groups = lax.axis_size("dp")
    acc_qkv = jnp.zeros((3, w_qkv.shape[1] // groups, width), f32)
    acc_out = jnp.zeros((width, w_out.shape[1] // groups), f32)
    acc_up = jnp.zeros((w_up.shape[0] // groups, w_up.shape[1]), f32)
    acc_down = jnp.zeros((w_down.shape[0], w_down.shape[1] // groups), f32)
    acc_bqv = jnp.zeros((2, width), f32)
    acc_bup = jnp.zeros(bias_up.shape, f32)
    acc_vec = jnp.zeros((6, width), f32)
    out_pieces = []
    grad_pieces = []
    for block in range(MICRO):
        first_row = block * per_block
        in_rows = inputs[first_row : first_row + per_block]
        live = slot_mask[first_row : first_row + per_block].astype(f32)[:, None, None]
        grad_rows = (cotangent[first_row : first_row + per_block].astype(f32) * live).astype(bf16)
        full_in, full_grad = (
            lax.all_gather(in_rows, "tensor", axis=2, tiled=True),
            lax.all_gather(grad_rows, "tensor", axis=2, tiled=True),
        )
        unit_one, inv_one, normed_one = normalize(full_in.astype(f32), gain_one, shift_one)
        normed_one = normed_one.astype(bf16)
        projected = jnp.einsum("bsd,tdc->tbsc", normed_one, w_qkv, preferred_element_type=f32)
        query4 = ((projected[0] + qv_bias[0]) * 0.125).astype(bf16).reshape(shape4)
        keys4 = projected[1].astype(bf16).reshape(shape4)
        values4 = (projected[2] + qv_bias[1]).astype(bf16).reshape(shape4)
        scores = jnp.einsum("bqhe,bkhe->bhqk", query4, keys4, preferred_element_type=f32)
        peak = jnp.max(scores, axis=-1, keepdims=True)
        expo = jnp.exp(scores - peak)
        total = jnp.sum(expo, axis=-1, keepdims=True)
        log_total = peak + jnp.log(total)
        probs = (expo / total).astype(bf16)
        attended = jnp.einsum("bhqk,bkhe->bqhe", probs, values4, preferred_element_type=f32)
        attended = attended.reshape(per_block, seq_len, width).astype(bf16)
        attn_part = jnp.einsum("bsc,cd->bsd", attended, w_out, preferred_element_type=f32)
        resid = in_rows.astype(f32) + (feature_sum(attn_part) + out_bias_s)
        full_resid = lax.all_gather(resid, "tensor", axis=2, tiled=True)
        unit_two, inv_two, normed_two = normalize(full_resid, gain_two, shift_two)
        normed_two = normed_two.astype(bf16)
        hidden = jnp.einsum("bsd,df->bsf", normed_two, w_up, preferred_element_type=f32) + up_bias
        sigma = jax.nn.sigmoid(GELU_K * hidden)
        active = (hidden * sigma).astype(bf16)
        mlp_part = jnp.einsum("bsf,fd->bsd", active, w_down, preferred_element_type=f32)
        out_rows = resid + (feature_sum(mlp_part) + down_bias_s)
        out_pieces.append(out_rows.astype(bf16))
        part_down = jnp.einsum("bsf,bsd->fd", active, full_grad, preferred_element_type=f32)
        grad_act = jnp.einsum("bsd,fd->bsf", full_grad, w_down, preferred_element_type=f32)
        grad_hidden = (grad_act * (sigma + GELU_K * hidden * sigma * (1.0 - sigma))).astype(bf16)
        part_up = jnp.einsum("bsd,bsf->df", normed_two, grad_hidden, preferred_element_type=f32)
        bup_add = jnp.sum(grad_hidden, axis=(0, 1), dtype=f32)
        grad_norm_two = feature_sum(
            jnp.einsum("bsf,df->bsd", grad_hidden, w_up, preferred_element_type=f32)
        )
        back_two, gain_two_add, shift_two_add = norm_back(
            grad_norm_two, unit_two, inv_two, gain_two_s, offset, width
        )
        grad_resid = grad_rows.astype(f32) + back_two
        grad_branch = grad_resid.astype(bf16)
        full_branch = lax.all_gather(grad_branch, "tensor", axis=2, tiled=True)
        part_out = jnp.einsum("bsc,bsd->cd", attended, full_branch, preferred_element_type=f32)
        grad_att = jnp.einsum("bsd,cd->bsc", full_branch, w_out, preferred_element_type=f32)
        grad_att = grad_att.astype(bf16).reshape(shape4)
        scores_again = jnp.einsum("bqhe,bkhe->bhqk", query4, keys4, preferred_element_type=f32)
        probs_again = jnp.exp(scores_again - log_total)
        grad_probs = jnp.einsum("bqhe,bkhe->bhqk", grad_att, values4, preferred_element_type=f32)
        grad_values = jnp.einsum(
            "bhqk,bqhe->bkhe", probs_again.astype(bf16), grad_att, preferred_element_type=f32
        ).astype(bf16)
        inner = jnp.sum(probs_again * grad_probs, axis=-1, keepdims=True)
        grad_scores = (probs_again * (grad_probs - inner)).astype(bf16)
        grad_query = (
            jnp.einsum("bhqk,bkhe->bqhe", grad_scores, keys4, preferred_element_type=f32).astype(
                bf16
            )
            * 0.125
        )
        grad_keys = jnp.einsum(
            "bhqk,bqhe->bkhe", grad_scores, query4, preferred_element_type=f32
        ).astype(bf16)
        grad_proj = jnp.stack([grad_query, grad_keys, grad_values]).reshape(
            3, per_block, seq_len, width
        )
        part_qkv = jnp.einsum("bsd,tbsc->tdc", normed_one, grad_proj, preferred_element_type=f32)
        bqv_add = jnp.stack(
            [
                jnp.sum(grad_proj[0], axis=(0, 1), dtype=f32),
                jnp.sum(grad_proj[2], axis=(0, 1), dtype=f32),
            ]
        )
        grad_norm_one = feature_sum(
            jnp.einsum("tbsc,tdc->bsd", grad_proj, w_qkv, preferred_element_type=f32)
        )
        back_one, gain_one_add, shift_one_add = norm_back(
            grad_norm_one, unit_one, inv_one, gain_one_s, offset, width
        )
        grad_pieces.append((grad_resid + back_one).astype(bf16))
        vec_add = jnp.stack(
            [
                jnp.sum(grad_branch, axis=(0, 1), dtype=f32),
                gain_one_add,
                shift_one_add,
                gain_two_add,
                shift_two_add,
                jnp.sum(grad_rows, axis=(0, 1), dtype=f32),
            ]
        )
        acc_bqv = acc_bqv + bqv_add
        acc_bup = acc_bup + bup_add
        acc_vec = acc_vec + vec_add
        share_qkv, share_out, share_up, share_down = (
            lax.psum_scatter(part_qkv, "dp", scatter_dimension=1, tiled=True),
            lax.psum_scatter(part_out, "dp", scatter_dimension=1, tiled=True),
            lax.psum_scatter(part_up, "dp", scatter_dimension=0, tiled=True),
            lax.psum_scatter(part_down, "dp", scatter_dimension=1, tiled=True),
        )
        acc_qkv = acc_qkv + share_qkv
        acc_out = acc_out + share_out
        acc_up = acc_up + share_up
        acc_down = acc_down + share_down
    acc_qkv, acc_out, acc_up, acc_down = (
        lax.all_gather(acc_qkv, "dp", axis=1, tiled=True),
        lax.all_gather(acc_out, "dp", axis=1, tiled=True),
        lax.all_gather(acc_up, "dp", axis=0, tiled=True),
        lax.all_gather(acc_down, "dp", axis=1, tiled=True),
    )
    acc_bqv, acc_bup, acc_vec = lax.psum((acc_bqv, acc_bup, acc_vec), "dp")
    vec_full = lax.all_gather(acc_vec, "tensor", axis=1, tiled=True)
    layer_out = jnp.concatenate(out_pieces, axis=0)
    input_grad = jnp.concatenate(grad_pieces, axis=0)
    return (
        layer_out,
        input_grad,
        acc_qkv,
        acc_bqv,
        acc_out,
        vec_full[0],
        vec_full[1],
        vec_full[2],
        vec_full[3],
        vec_full[4],
        acc_up,
        acc_bup,
        acc_down,
        vec_full[5],
    )


def solution(mesh):
    return jax.shard_map(
        per_device,
        mesh=mesh,
        in_specs=(
            P("dp", None, "tensor"),
            P("dp", None, "tensor"),
            P("dp"),
            P(None, None, "tensor"),
            P(None, "tensor"),
            P("tensor", None),
            P(),
            P(),
            P(),
            P(),
            P(),
            P(None, "tensor"),
            P("tensor"),
            P("tensor", None),
            P(),
        ),
        out_specs=(
            P("dp", None, "tensor"),
            P("dp", None, "tensor"),
            P(None, None, "tensor"),
            P(None, "tensor"),
            P("tensor", None),
            P(),
            P(),
            P(),
            P(),
            P(),
            P(None, "tensor"),
            P("tensor"),
            P("tensor", None),
            P(),
        ),
        check_vma=False,
    )
```

profile of v0, /device:TPU:0, one launch (start us, length us, event | category | flops | bytes accessed | tf_op | source)
XLA Modules:
  0.0 1545.7 jit_solution(14197826525542874732)
XLA Ops:
  7.2 5.3 fusion.149
  18.1 16.6 %all-gather.21.cloned.1.call-done = bf16[1,577,1024]{2,1,0:T(8,128)(2,1)} async-done(((bf16[1,577,256]{2,1,0:T(8,128)(2,1)}), bf16[1,577,1024]{2,1,0:T(8,128)(2,1)}) %all-gather.21.cloned.1.call-update) | async-done | bytes 1181712 | tf_op jit(solution)/shard_map/all_gather | solution.py:97
  129.4 36.0 %reduce-scatter.25.cloned.1.call-done = f32[1,577,256]{2,1,0:T(8,128)} async-done(((f32[1,577,1024]{2,1,0:T(8,128)}), f32[1,577,256]{2,1,0:T(8,128)}) %reduce-scatter.25.cloned.1.call-update) | async-done | bytes 590864 | tf_op jit(solution)/shard_map/reduce_scatter | solution.py:22
  165.4 36.1 %reduce-scatter.29.cloned.1.call-done = f32[1,577,256]{2,1,0:T(8,128)} async-done(((f32[1,577,1024]{2,1,0:T(8,128)}), f32[1,577,256]{2,1,0:T(8,128)}) %reduce-scatter.29.cloned.1.call-update) | async-done | bytes 590864 | tf_op jit(solution)/shard_map/reduce_scatter | solution.py:22
  201.5 35.5 %reduce-scatter.33.cloned.1.call-done = f32[1,577,256]{2,1,0:T(8,128)} async-done(((f32[1,577,1024]{2,1,0:T(8,128)}), f32[1,577,256]{2,1,0:T(8,128)}) %reduce-scatter.33.cloned.1.call-update) | async-done | bytes 590864 | tf_op jit(solution)/shard_map/reduce_scatter | solution.py:22
  242.0 5.5 fusion.148
  259.6 5.6 all-gather.23.cloned.1.call-done
  274.6 9.6 all-gather.37.cloned.1.call-done
  284.2 4.9 convert_reduce_fusion.7
  293.0 17.0 %all-gather.31.cloned.1.call-done = f32[1,577,1024]{2,1,0:T(8,128)} async-done(((f32[1,577,256]{2,1,0:T(8,128)}), f32[1,577,1024]{2,1,0:T(8,128)}) %all-gather.31.cloned.1.call-update) | async-done | bytes 2363408 | tf_op jit(solution)/shard_map/all_gather | solution.py:116
  319.6 9.5 all-gather.45.cloned.1.call-done
  329.1 4.9 convert_reduce_fusion.5
  338.4 16.5 %all-gather.35.cloned.1.call-done = f32[1,577,1024]{2,1,0:T(8,128)} async-done(((f32[1,577,256]{2,1,0:T(8,128)}), f32[1,577,1024]{2,1,0:T(8,128)}) %all-gather.35.cloned.1.call-update) | async-done | bytes 2363408 | tf_op jit(solution)/shard_map/all_gather | solution.py:116
  364.5 10.1 all-gather.49.cloned.1.call-done
  374.6 4.9 convert_reduce_fusion.4
  383.5 16.8 %all-gather.27.cloned.1.call-done = f32[1,577,1024]{2,1,0:T(8,128)} async-done(((f32[1,577,256]{2,1,0:T(8,128)}), f32[1,577,1024]{2,1,0:T(8,128)}) %all-gather.27.cloned.1.call-update) | async-done | bytes 2363408 | tf_op jit(solution)/shard_map/all_gather | solution.py:116
  409.4 10.0 all-gather.41.cloned.1.call-done
  419.4 4.9 convert_reduce_fusion.6
  428.3 27.1 %reduce-scatter.37.cloned.1.call-done = f32[1,577,256]{2,1,0:T(8,128)} async-done(((f32[1,577,1024]{2,1,0:T(8,128)}), f32[1,577,256]{2,1,0:T(8,128)}) %reduce-scatter.37.cloned.1.call-update) | async-done | bytes 590864 | tf_op jit(solution)/shard_map/reduce_scatter | solution.py:22
  455.4 36.0 %reduce-scatter.45.cloned.1.call-done = f32[1,577,256]{2,1,0:T(8,128)} async-done(((f32[1,577,1024]{2,1,0:T(8,128)}), f32[1,577,256]{2,1,0:T(8,128)}) %reduce-scatter.45.cloned.1.call-update) | async-done | bytes 590864 | tf_op jit(solution)/shard_map/reduce_scatter | solution.py:22
  491.3 35.5 %reduce-scatter.49.cloned.1.call-done = f32[1,577,256]{2,1,0:T(8,128)} async-done(((f32[1,577,1024]{2,1,0:T(8,128)}), f32[1,577,256]{2,1,0:T(8,128)}) %reduce-scatter.49.cloned.1.call-update) | async-done | bytes 590864 | tf_op jit(solution)/shard_map/reduce_scatter | solution.py:22
  526.9 35.4 %reduce-scatter.41.cloned.1.call-done = f32[1,577,256]{2,1,0:T(8,128)} async-done(((f32[1,577,1024]{2,1,0:T(8,128)}), f32[1,577,256]{2,1,0:T(8,128)}) %reduce-scatter.41.cloned.1.call-update) | async-done | bytes 590864 | tf_op jit(solution)/shard_map/reduce_scatter | solution.py:22
  566.2 11.1 all-reduce.2
  577.4 4.0 convert_reduce_fusion.23
  581.5 4.1 convert_reduce_fusion.22
  587.0 12.8 all-gather.39.cloned.1.call-done
  602.7 17.0 %all-gather.43.cloned.1.call-done = bf16[1,577,1024]{2,1,0:T(8,128)(2,1)} async-done(((bf16[1,577,256]{2,1,0:T(8,128)(2,1)}), bf16[1,577,1024]{2,1,0:T(8,128)(2,1)}) %all-gather.43.cloned.1.call-update) | async-done | bytes 1181712 | tf_op jit(solution)/shard_map/all_gather | solution.py:138
  622.8 16.1 %all-gather.47.cloned.1.call-done = bf16[1,577,1024]{2,1,0:T(8,128)(2,1)} async-done(((bf16[1,577,256]{2,1,0:T(8,128)(2,1)}), bf16[1,577,1024]{2,1,0:T(8,128)(2,1)}) %all-gather.47.cloned.1.call-update) | async-done | bytes 1181712 | tf_op jit(solution)/shard_map/all_gather | solution.py:138
  642.0 16.5 %all-gather.51.cloned.1.call-done = bf16[1,577,1024]{2,1,0:T(8,128)(2,1)} async-done(((bf16[1,577,256]{2,1,0:T(8,128)(2,1)}), bf16[1,577,1024]{2,1,0:T(8,128)(2,1)}) %all-gather.51.cloned.1.call-update) | async-done | bytes 1181712 | tf_op jit(solution)/shard_map/all_gather | solution.py:138
  661.8 4.0 fusion.92
  669.9 4.4 add_add_fusion.1
  675.1 4.1 fusion.66
  683.4 4.4 add_add_fusion
  690.3 4.0 convert_reduce_fusion.16
  694.3 4.2 multiply_reduce_fusion.2
  712.6 4.3 multiply_reduce_fusion.3
  734.7 4.3 multiply_reduce_fusion.1
  756.6 4.2 multiply_reduce_fusion
  786.2 4.6 convolution_bitcast_fusion.11
  790.9 4.5 convolution_bitcast_fusion.10
  795.5 4.5 convolution_bitcast_fusion.9
  800.1 4.6 convolution_bitcast_fusion.8
  805.3 4.2 convolution_bitcast_fusion.4
  809.9 4.3 convolution_bitcast_fusion.6
  814.3 4.3 convolution_bitcast_fusion.2
  818.7 4.3 convolution_bitcast_fusion
  823.8 87.2 %reduce-scatter.59.cloned.1.call-done = f32[1024,128]{1,0:T(8,128)} async-done(((f32[1024,1024]{1,0:T(8,128)}), f32[1024,128]{1,0:T(8,128)}) %reduce-scatter.59.cloned.1.call-update) | async-done | bytes 524304 | tf_op jit(solution)/shard_map/reduce_scatter | solution.py:193
  911.1 78.6 %reduce-scatter.53.cloned.1.call-done = f32[3,128,256]{1,2,0:T(8,128)} async-done(((f32[3,1024,256]{1,2,0:T(8,128)}), f32[3,128,256]{1,2,0:T(8,128)}) %reduce-scatter.53.cloned.1.call-update) | async-done | bytes 393232 | tf_op jit(solution)/shard_map/reduce_scatter | solution.py:190
  998.2 26.1 %reduce-scatter.23.cloned.1.call-done = f32[1,577,256]{2,1,0:T(8,128)} async-done(((f32[1,577,1024]{2,1,0:T(8,128)}), f32[1,577,256]{2,1,0:T(8,128)}) %reduce-scatter.23.cloned.1.call-update) | async-done | bytes 590864 | tf_op jit(solution)/shard_map/reduce_scatter | solution.py:22
  1024.4 35.4 %reduce-scatter.27.cloned.1.call-done = f32[1,577,256]{2,1,0:T(8,128)} async-done(((f32[1,577,1024]{2,1,0:T(8,128)}), f32[1,577,256]{2,1,0:T(8,128)}) %reduce-scatter.27.cloned.1.call-update) | async-done | bytes 590864 | tf_op jit(solution)/shard_map/reduce_scatter | solution.py:22
  1059.8 35.5 %reduce-scatter.31.cloned.1.call-done = f32[1,577,256]{2,1,0:T(8,128)} async-done(((f32[1,577,1024]{2,1,0:T(8,128)}), f32[1,577,256]{2,1,0:T(8,128)}) %reduce-scatter.31.cloned.1.call-update) | async-done | bytes 590864 | tf_op jit(solution)/shard_map/reduce_scatter | solution.py:22
  1095.3 35.5 %reduce-scatter.35.cloned.1.call-done = f32[1,577,256]{2,1,0:T(8,128)} async-done(((f32[1,577,1024]{2,1,0:T(8,128)}), f32[1,577,256]{2,1,0:T(8,128)}) %reduce-scatter.35.cloned.1.call-update) | async-done | bytes 590864 | tf_op jit(solution)/shard_map/reduce_scatter | solution.py:22
  1135.8 36.3 %all-gather.55.cloned.1.call-done = f32[256,1024]{1,0:T(8,128)} async-done(((f32[256,128]{1,0:T(8,128)}), f32[256,1024]{1,0:T(8,128)}) %all-gather.55.cloned.1.call-update) | async-done | bytes 1048592 | tf_op jit(solution)/shard_map/all_gather | solution.py:201
  1172.2 34.6 %reduce-scatter.43.cloned.1.call-done = f32[1,577,256]{2,1,0:T(8,128)} async-done(((f32[1,577,1024]{2,1,0:T(8,128)}), f32[1,577,256]{2,1,0:T(8,128)}) %reduce-scatter.43.cloned.1.call-update) | async-done | bytes 590864 | tf_op jit(solution)/shard_map/reduce_scatter | solution.py:22
  1206.8 35.6 %reduce-scatter.39.cloned.1.call-done = f32[1,577,256]{2,1,0:T(8,128)} async-done(((f32[1,577,1024]{2,1,0:T(8,128)}), f32[1,577,256]{2,1,0:T(8,128)}) %reduce-scatter.39.cloned.1.call-update) | async-done | bytes 590864 | tf_op jit(solution)/shard_map/reduce_scatter | solution.py:22
  1242.3 35.4 %reduce-scatter.47.cloned.1.call-done = f32[1,577,256]{2,1,0:T(8,128)} async-done(((f32[1,577,1024]{2,1,0:T(8,128)}), f32[1,577,256]{2,1,0:T(8,128)}) %reduce-scatter.47.cloned.1.call-update) | async-done | bytes 590864 | tf_op jit(solution)/shard_map/reduce_scatter | solution.py:22
  1277.7 35.4 %reduce-scatter.51.cloned.1.call-done = f32[1,577,256]{2,1,0:T(8,128)} async-done(((f32[1,577,1024]{2,1,0:T(8,128)}), f32[1,577,256]{2,1,0:T(8,128)}) %reduce-scatter.51.cloned.1.call-update) | async-done | bytes 590864 | tf_op jit(solution)/shard_map/reduce_scatter | solution.py:22
  1316.4 10.4 all-reduce.1
  1333.5 39.4 %all-reduce = (f32[2,256]{1,0:T(2,128)}, f32[6,256]{1,0:T(8,128)S(1)}, f32[1024]{0:T(1024)}) all-reduce(f32[2,256]{1,0:T(2,128)S(1)} %fusion.119, f32[6,256]{1,0:T(8,128)S(1)} %add_add_fusion.6, f32[1024]{0:T(1024)S(1)} %add_add_fusion.7), channel_id=1, replica_groups=mesh['dp'=8,'tensor'=4] {'dp'}, use_global_device_ids=true, to_apply=%region_88.0 | all-reduce | flops 3072 | bytes 24576 | tf_op jit(solution)/shard_map/psum | solution.py:205
  1372.9 5.2 all_gather.81
  1378.7 10.2 all-gather.57.cloned.1.call-done
  1388.8 75.2 %all-gather.59.cloned.1.call-done = f32[1024,1024]{1,0:T(8,128)} async-done(((f32[1024,128]{1,0:T(8,128)}), f32[1024,1024]{1,0:T(8,128)}) %all-gather.59.cloned.1.call-update) | async-done | bytes 4194320 | tf_op jit(solution)/shard_map/all_gather | solution.py:203
  1464.0 62.9 %all-gather.53.cloned.1.call-done = f32[3,1024,256]{1,2,0:T(8,128)} async-done(((f32[3,128,256]{1,2,0:T(8,128)}), f32[3,1024,256]{1,2,0:T(8,128)}) %all-gather.53.cloned.1.call-update) | async-done | bytes 3145744 | tf_op jit(solution)/shard_map/all_gather | solution.py:200
  1531.4 4.9 copy.187
  (655 shorter events, 302.8 us)
Async XLA Ops:
  7.2 277.0 %copy-start = (bf16[1024,1024]{1,0:T(8,128)(2,1)S(1)}, bf16[1024,1024]{1,0:T(8,128)(2,1)}, u32[]{:S(2)}) copy-start(bf16[1024,1024]{1,0:T(8,128)(2,1)} %param.28) | copy-start | bytes 6291460
  7.2 27.5 %all-gather.21.cloned.1.call-start = ((), (), s32[]{:S(2)}) async-start(), calls=%async_computation.20 | async-start | bytes 1495040 | tf_op jit(solution)/shard_map/all_gather | solution.py:97
  14.1 40.4 %all-gather.25.cloned.1.call-start = ((), (), s32[]{:S(2)}) async-start(), calls=%async_computation.24 | async-start | bytes 1495040 | tf_op jit(solution)/shard_map/all_gather | solution.py:97
  15.0 63.2 %all-gather.29.cloned.1.call-start = ((), (), s32[]{:S(2)}) async-start(), calls=%async_computation.28 | async-start | bytes 1495040 | tf_op jit(solution)/shard_map/all_gather | solution.py:97
  15.8 85.8 %all-gather.33.cloned.1.call-start = ((), (), s32[]{:S(2)}) async-start(), calls=%async_computation.32 | async-start | bytes 1495040 | tf_op jit(solution)/shard_map/all_gather | solution.py:97
  17.7 111.7 %reduce-scatter.21.cloned.1.call-start = ((), (), s32[]{:S(2)}) async-start(), calls=%async_computation.21 | async-start | bytes 2990080 | tf_op jit(solution)/shard_map/reduce_scatter | solution.py:22
  17.8 87.4 %copy-start.123 = (f32[1024]{0:T(1024)}, f32[1024]{0:T(1024)S(1)}, u32[]{:S(2)}) copy-start(f32[1024]{0:T(1024)S(1)} %convert_element_type.629) | copy-start | bytes 12292
  17.8 87.4 %copy-start.125 = (f32[1024]{0:T(1024)}, f32[1024]{0:T(1024)S(1)}, u32[]{:S(2)}) copy-start(f32[1024]{0:T(1024)S(1)} %convert_element_type.628) | copy-start | bytes 12292
  18.0 99.0 %copy-start.85 = (f32[4,64]{1,0:T(4,128)}, f32[4,64]{1,0:T(4,128)S(1)}, u32[]{:S(2)}) copy-start(f32[4,64]{1,0:T(4,128)S(1)} %add.591) | copy-start | bytes 3076
  53.8 111.6 %reduce-scatter.25.cloned.1.call-start = ((), (), s32[]{:S(2)}) async-start(), calls=%async_computation.25 | async-start | bytes 2990080 | tf_op jit(solution)/shard_map/reduce_scatter | solution.py:22
  77.6 123.9 %reduce-scatter.29.cloned.1.call-start = ((), (), s32[]{:S(2)}) async-start(), calls=%async_computation.29 | async-start | bytes 2990080 | tf_op jit(solution)/shard_map/reduce_scatter | solution.py:22
  101.4 135.6 %reduce-scatter.33.cloned.1.call-start = ((), (), s32[]{:S(2)}) async-start(), calls=%async_computation.33 | async-start | bytes 2990080 | tf_op jit(solution)/shard_map/reduce_scatter | solution.py:22
  123.7 113.4 %copy-start.39 = (bf16[1,577,256]{2,0,1:T(2,128)(2,1)S(1)}, bf16[1,577,256]{2,0,1:T(2,128)(2,1)}, u32[]{:S(2)}) copy-start(bf16[1,577,256]{2,0,1:T(2,128)(2,1)} %copy-done.38) | copy-start | bytes 886276
  125.7 139.4 %all-gather.23.cloned.1.call-start = ((), (), s32[]{:S(2)}) async-start(), calls=%async_computation.22 | async-start | bytes 2990080 | tf_op jit(solution)/shard_map/all_gather | solution.py:116
  125.8 114.9 %copy-start.131 = (s32[4]{0:T(128)S(1)}, s32[4]{0:T(128)}, u32[]{:S(2)}) copy-start(s32[4]{0:T(128)} %param.17) | copy-start | bytes 52
  240.7 43.5 %all-gather.37.cloned.1.call-start = ((), (), s32[]{:S(2)}) async-start(), calls=%async_computation.36 | async-start | bytes 1495040 | tf_op jit(solution)/shard_map/all_gather | solution.py:98
  248.8 61.2 %all-gather.31.cloned.1.call-start = ((), (), s32[]{:S(2)}) async-start(), calls=%async_computation.30 | async-start | bytes 2990080 | tf_op jit(solution)/shard_map/all_gather | solution.py:116
  249.6 79.6 %all-gather.45.cloned.1.call-start = ((), (), s32[]{:S(2)}) async-start(), calls=%async_computation.44 | async-start | bytes 1495040 | tf_op jit(solution)/shard_map/all_gather | solution.py:98
  250.3 9.2 copy-start.159
  252.7 102.3 %all-gather.35.cloned.1.call-start = ((), (), s32[]{:S(2)}) async-start(), calls=%async_computation.34 | async-start | bytes 2990080 | tf_op jit(solution)/shard_map/all_gather | solution.py:116
  253.5 121.2 %all-gather.49.cloned.1.call-start = ((), (), s32[]{:S(2)}) async-start(), calls=%async_computation.48 | async-start | bytes 1495040 | tf_op jit(solution)/shard_map/all_gather | solution.py:98
  256.6 143.8 %all-gather.27.cloned.1.call-start = ((), (), s32[]{:S(2)}) async-start(), calls=%async_computation.26 | async-start | bytes 2990080 | tf_op jit(solution)/shard_map/all_gather | solution.py:116
  257.1 162.3 %all-gather.41.cloned.1.call-start = ((), (), s32[]{:S(2)}) async-start(), calls=%async_computation.40 | async-start | bytes 1495040 | tf_op jit(solution)/shard_map/all_gather | solution.py:98
  259.2 196.2 %reduce-scatter.37.cloned.1.call-start = ((), (), s32[]{:S(2)}) async-start(), calls=%async_computation.37 | async-start | bytes 2990080 | tf_op jit(solution)/shard_map/reduce_scatter | solution.py:22
  259.5 145.4 %copy-start.127 = (f32[1024]{0:T(1024)}, f32[1024]{0:T(1024)S(1)}, u32[]{:S(2)}) copy-start(f32[1024]{0:T(1024)S(1)} %convert_element_type.642) | copy-start | bytes 12292
  259.5 145.4 %copy-start.129 = (f32[1024]{0:T(1024)}, f32[1024]{0:T(1024)S(1)}, u32[]{:S(2)}) copy-start(f32[1024]{0:T(1024)S(1)} %convert_element_type.641) | copy-start | bytes 12292
  259.5 159.9 %copy-start.120 = (f32[1024]{0:T(1024)}, f32[1024]{0:T(1024)S(1)}, u32[]{:S(2)}) copy-start(f32[1024]{0:T(1024)S(1)} %convert_element_type.644) | copy-start | bytes 12292
  293.0 198.4 %reduce-scatter.45.cloned.1.call-start = ((), (), s32[]{:S(2)}) async-start(), calls=%async_computation.45 | async-start | bytes 2990080 | tf_op jit(solution)/shard_map/reduce_scatter | solution.py:22
  338.0 188.9 %reduce-scatter.49.cloned.1.call-start = ((), (), s32[]{:S(2)}) async-start(), calls=%async_computation.49 | async-start | bytes 2990080 | tf_op jit(solution)/shard_map/reduce_scatter | solution.py:22
  383.5 178.8 %reduce-scatter.41.cloned.1.call-start = ((), (), s32[]{:S(2)}) async-start(), calls=%async_computation.41 | async-start | bytes 2990080 | tf_op jit(solution)/shard_map/reduce_scatter | solution.py:22
  428.2 171.7 %all-gather.39.cloned.1.call-start = ((), (), s32[]{:S(2)}) async-start(), calls=%async_computation.38 | async-start | bytes 1495040 | tf_op jit(solution)/shard_map/all_gather | solution.py:138
  428.3 137.8 %copy-start.122 = (f32[256]{0:T(256)}, f32[256]{0:T(256)S(1)}, u32[]{:S(2)}) copy-start(f32[256]{0:T(256)S(1)} %dynamic_slice.38) | copy-start | bytes 3076
  428.3 149.0 %copy-start.47 = (bf16[1,577,256]{2,1,0:T(8,128)(2,1)S(1)}, bf16[1,577,256]{2,1,0:T(8,128)(2,1)}, u32[]{:S(2)}) copy-start(bf16[1,577,256]{2,1,0:T(8,128)(2,1)} %get-tuple-element.101) | copy-start | bytes 886276
  428.3 149.0 %copy-start.49 = (bf16[1,577,256]{2,1,0:T(8,128)(2,1)S(1)}, bf16[1,577,256]{2,1,0:T(8,128)(2,1)}, u32[]{:S(2)}) copy-start(bf16[1,577,256]{2,1,0:T(8,128)(2,1)} %get-tuple-element.106) | copy-start | bytes 886276
  581.4 38.2 %all-gather.43.cloned.1.call-start = ((), (), s32[]{:S(2)}) async-start(), calls=%async_computation.42 | async-start | bytes 1495040 | tf_op jit(solution)/shard_map/all_gather | solution.py:138
  581.5 18.3 %copy-start.62 = (bf16[4,64,577]{2,1,0:T(8,128)(2,1)S(1)}, bf16[4,64,577]{2,1,0:T(8,128)(2,1)}, u32[]{:S(2)}) copy-start(bf16[4,64,577]{2,1,0:T(8,128)(2,1)} %copy-done.61) | copy-start | bytes 886276
  585.6 34.0 %copy-start.64 = (bf16[4,64,577]{2,1,0:T(8,128)(2,1)S(1)}, bf16[4,64,577]{2,1,0:T(8,128)(2,1)}, u32[]{:S(2)}) copy-start(bf16[4,64,577]{2,1,0:T(8,128)(2,1)} %copy-done.63) | copy-start | bytes 886276
  585.7 53.2 %all-gather.47.cloned.1.call-start = ((), (), s32[]{:S(2)}) async-start(), calls=%async_computation.46 | async-start | bytes 1495040 | tf_op jit(solution)/shard_map/all_gather | solution.py:138
  586.4 72.2 %all-gather.51.cloned.1.call-start = ((), (), s32[]{:S(2)}) async-start(), calls=%async_computation.50 | async-start | bytes 1495040 | tf_op jit(solution)/shard_map/all_gather | solution.py:138
  587.0 217.8 %reduce-scatter.55.cloned.1.call-start = ((), (), s32[]{:S(2)}) async-start(), calls=%async_computation.57 | async-start | bytes 1179648 | tf_op jit(solution)/shard_map/reduce_scatter | solution.py:191
  602.7 36.2 %copy-start.66 = (bf16[4,64,577]{2,1,0:T(8,128)(2,1)S(1)}, bf16[4,64,577]{2,1,0:T(8,128)(2,1)}, u32[]{:S(2)}) copy-start(bf16[4,64,577]{2,1,0:T(8,128)(2,1)} %copy-done.65) | copy-start | bytes 886276
  622.8 35.8 %copy-start.68 = (bf16[4,64,577]{2,1,0:T(8,128)(2,1)S(1)}, bf16[4,64,577]{2,1,0:T(8,128)(2,1)}, u32[]{:S(2)}) copy-start(bf16[4,64,577]{2,1,0:T(8,128)(2,1)} %copy-done.67) | copy-start | bytes 886276
  642.0 19.8 %copy-start.128 = (f32[1024]{0:T(1024)S(1)}, f32[1024]{0:T(1024)}, u32[]{:S(2)}) copy-start(f32[1024]{0:T(1024)} %copy-done.127) | copy-start | bytes 12292
  642.0 19.8 %copy-start.130 = (f32[1024]{0:T(1024)S(1)}, f32[1024]{0:T(1024)}, u32[]{:S(2)}) copy-start(f32[1024]{0:T(1024)} %copy-done.129) | copy-start | bytes 12292
  661.7 161.3 %reduce-scatter.57.cloned.1.call-start = ((), (), s32[]{:S(2)}) async-start(), calls=%async_computation.58 | async-start | bytes 4718592 | tf_op jit(solution)/shard_map/reduce_scatter | solution.py:192
  674.4 236.7 %reduce-scatter.59.cloned.1.call-start = ((), (), s32[]{:S(2)}) async-start(), calls=%async_computation.59 | async-start | bytes 4718592 | tf_op jit(solution)/shard_map/reduce_scatter | solution.py:193
  687.8 301.9 %reduce-scatter.53.cloned.1.call-start = ((), (), s32[]{:S(2)}) async-start(), calls=%async_computation.56 | async-start | bytes 3538944 | tf_op jit(solution)/shard_map/reduce_scatter | solution.py:190
  786.1 238.3 %reduce-scatter.23.cloned.1.call-start = ((), (), s32[]{:S(2)}) async-start(), calls=%async_computation.23 | async-start | bytes 2990080 | tf_op jit(solution)/shard_map/reduce_scatter | solution.py:22
  790.8 268.9 %reduce-scatter.27.cloned.1.call-start = ((), (), s32[]{:S(2)}) async-start(), calls=%async_computation.27 | async-start | bytes 2990080 | tf_op jit(solution)/shard_map/reduce_scatter | solution.py:22
  795.4 299.9 %reduce-scatter.31.cloned.1.call-start = ((), (), s32[]{:S(2)}) async-start(), calls=%async_computation.31 | async-start | bytes 2990080 | tf_op jit(solution)/shard_map/reduce_scatter | solution.py:22
  800.0 330.8 %reduce-scatter.35.cloned.1.call-start = ((), (), s32[]{:S(2)}) async-start(), calls=%async_computation.35 | async-start | bytes 2990080 | tf_op jit(solution)/shard_map/reduce_scatter | solution.py:22
  804.7 367.5 %all-gather.55.cloned.1.call-start = ((), (), s32[]{:S(2)}) async-start(), calls=%async_computation.53 | async-start | bytes 1179648 | tf_op jit(solution)/shard_map/all_gather | solution.py:201
  805.3 401.5 %reduce-scatter.43.cloned.1.call-start = ((), (), s32[]{:S(2)}) async-start(), calls=%async_computation.43 | async-start | bytes 2990080 | tf_op jit(solution)/shard_map/reduce_scatter | solution.py:22
  809.6 432.7 %reduce-scatter.39.cloned.1.call-start = ((), (), s32[]{:S(2)}) async-start(), calls=%async_computation.39 | async-start | bytes 2990080 | tf_op jit(solution)/shard_map/reduce_scatter | solution.py:22
  814.2 463.5 %reduce-scatter.47.cloned.1.call-start = ((), (), s32[]{:S(2)}) async-start(), calls=%async_computation.47 | async-start | bytes 2990080 | tf_op jit(solution)/shard_map/reduce_scatter | solution.py:22
  818.6 494.5 %reduce-scatter.51.cloned.1.call-start = ((), (), s32[]{:S(2)}) async-start(), calls=%async_computation.51 | async-start | bytes 2990080 | tf_op jit(solution)/shard_map/reduce_scatter | solution.py:22
  823.0 166.8 %copy-start.134 = (bf16[1024]{0:T(1024)(128)(2,1)S(1)}, bf16[1024]{0:T(1024)(128)(2,1)}, u32[]{:S(2)}) copy-start(bf16[1024]{0:T(1024)(128)(2,1)} %param.22) | copy-start | bytes 6148
  823.0 166.9 %copy-start.162 = (bf16[1024]{0:T(1024)(128)(2,1)S(1)}, bf16[1024]{0:T(1024)(128)(2,1)}, u32[]{:S(2)}) copy-start(bf16[1024]{0:T(1024)(128)(2,1)} %param.29) | copy-start | bytes 6148
  823.0 565.8 %all-gather.57.cloned.1.call-start = ((), (), s32[]{:S(2)}) async-start(), calls=%async_computation.54 | async-start | bytes 4718592 | tf_op jit(solution)/shard_map/all_gather | solution.py:202
  823.7 640.2 %all-gather.59.cloned.1.call-start = ((), (), s32[]{:S(2)}) async-start(), calls=%async_computation.55 | async-start | bytes 4718592 | tf_op jit(solution)/shard_map/all_gather | solution.py:203
  911.0 615.9 %all-gather.53.cloned.1.call-start = ((), (), s32[]{:S(2)}) async-start(), calls=%async_computation.52 | async-start | bytes 3538944 | tf_op jit(solution)/shard_map/all_gather | solution.py:200
  1316.4 13.2 copy-start.57
  1316.4 13.2 copy-start.58
  1378.7 151.8 %copy-start.78 = (f32[256,1024]{1,0:T(8,128)S(1)}, f32[256,1024]{1,0:T(8,128)}, u32[]{:S(2)}) copy-start(f32[256,1024]{1,0:T(8,128)} %all-gather.55.cloned.1.call-done) | copy-start | bytes 3145732
  (158 other events, 442.7 us)
Sparse Core Ops, SparseCore 0:
  14.3 20.3 all-gather.20
  36.8 17.6 all-gather.24
  56.6 17.6 all-gather.28
  75.7 17.6 all-gather.32
  96.4 32.9 reduce-scatter.20
  132.4 32.9 reduce-scatter.24
  168.5 32.9 reduce-scatter.28
  204.0 32.9 reduce-scatter.32
  240.8 24.2 all-gather.22
  266.5 17.6 all-gather.36
  285.8 24.2 all-gather.30
  311.4 17.6 all-gather.44
  330.7 24.2 all-gather.34
  356.9 17.6 all-gather.48
  376.1 24.2 all-gather.26
  401.7 17.6 all-gather.40
  422.4 32.9 reduce-scatter.36
  458.3 32.9 reduce-scatter.44
  493.9 32.9 reduce-scatter.48
  529.3 32.9 reduce-scatter.40
  581.5 18.2 all-gather.38
  602.0 17.6 all-gather.42
  621.2 17.6 all-gather.46
  640.9 17.6 all-gather.50
  662.6 64.7 reduce-scatter.54
  731.4 87.1 reduce-scatter.56
  822.6 88.3 reduce-scatter.58
  915.2 74.4 reduce-scatter.52
  992.3 32.0 reduce-scatter.22
  1026.8 32.9 reduce-scatter.26
  1062.3 32.9 reduce-scatter.30
  1097.9 32.9 reduce-scatter.34
  1132.7 39.3 all-gather.54
  1174.7 31.9 reduce-scatter.42
  1209.3 32.9 reduce-scatter.38
  1244.7 32.9 reduce-scatter.46
  1280.1 32.9 reduce-scatter.50
  1315.3 73.4 all-gather.56
  1390.7 73.2 all-gather.58
  1466.0 60.8 all-gather.52
where the time goes:
time: 1550 us
  waiting for transfers between devices  1050 us (68%)
  matrix products  211 us (14%)
  local copies, waits for them, and re-layouts  106 us (7%)
  other arithmetic  89.6 us (6%)
  blocking collectives  66.1 us (4%)
  between operations  20.3 us (1%)
    reduce_scatter x16, waiting for transfers between devices, feature_sum(): lax.psum_scatter(partial_value, 'tensor', scatter_dimension=2, tiled=True)  519 us
    reduce_scatter x1, waiting for transfers between devices, per_device(): lax.psum_scatter(part_down, 'dp', scatter_dimension=1, tiled=True)  87.2 us
    reduce_scatter x1, waiting for transfers between devices, per_device(): lax.psum_scatter(part_qkv, 'dp', scatter_dimension=1, tiled=True)  78.6 us
    all_gather x1, waiting for transfers between devices, per_device(): lax.all_gather(acc_down, 'dp', axis=1, tiled=True)  75.2 us
    all_gather x1, waiting for transfers between devices, per_device(): lax.all_gather(acc_qkv, 'dp', axis=1, tiled=True)  62.9 us
    all_gather x4, waiting for transfers between devices, per_device(): full_branch = lax.all_gather(grad_branch, 'tensor', axis=2, tiled=True)  62.4 us
    all_gather x4, waiting for transfers between devices, per_device(): full_resid = lax.all_gather(resid, 'tensor', axis=2, tiled=True)  55.9 us
    unnamed x374, local copies, waits for them, and re-layouts  52.1 us
  transfers between devices with their start and end apart: 40, of which 36 were waited for; matrix products, arithmetic and copies ran while one was open for 22% of the time, Pallas kernels for 0%

commit v1 on v0

v1 whole, which is shorter than its diff:
```python
import functools

import jax
import jax.numpy as jnp
from jax import lax
from jax.experimental import pallas as pl
from jax.experimental.pallas import tpu as pltpu
from jax.sharding import PartitionSpec as P

HEAD = 64
LANES = 128
ROW_TILE = 16
EPS = 1e-05
GELU_K = 1.702
FAR = -1e30

F32 = jnp.float32
BF16 = jnp.bfloat16

NT = (((1,), (1,)), ((), ()))
NN = (((1,), (0,)), ((), ()))
TN = (((0,), (0,)), ((), ()))


def mm(left, right, dims):
    return lax.dot_general(left, right, dims, preferred_element_type=F32)


def head_views(half, seq, q, k):
    lane = lax.broadcasted_iota(jnp.int32, q.shape, 1)
    row = lax.broadcasted_iota(jnp.int32, q.shape, 0)
    mine = (lane >= HEAD) if half else (lane < HEAD)
    spare = lane == (0 if half else HEAD)
    zero = jnp.zeros_like(q)
    q_only = jnp.where(mine, q, zero)
    k_only = jnp.where(mine, k, zero)
    q_mask = jnp.where(spare, jnp.ones_like(q), q_only)
    far = jnp.full_like(k, FAR)
    k_mask = jnp.where(spare & (row >= seq), far, k_only)
    return mine, q_only, k_only, q_mask, k_mask


def attn_fwd_kernel(seq, q_ref, k_ref, v_ref, o_ref, lse_ref):
    q, k, v = q_ref[...], k_ref[...], v_ref[...]
    v_t = v.T
    pieces = []
    for half in range(2):
        _, _, _, q_mask, k_mask = head_views(half, seq, q, k)
        s_t = mm(k_mask, q_mask, NT)
        peak = jnp.max(s_t, axis=0, keepdims=True)
        expo = jnp.exp(s_t - peak)
        total = jnp.sum(expo, axis=0, keepdims=True)
        p_t = (expo * (1.0 / total)).astype(BF16)
        pieces.append(mm(v_t[half * HEAD : (half + 1) * HEAD], p_t, NN))
        lse_ref[0, 0, half : half + 1, :] = peak + jnp.log(total)
    o_ref[...] = jnp.concatenate(pieces, axis=0).T.astype(BF16)


def attn_bwd_kernel(seq, q_ref, k_ref, v_ref, do_ref, lse_ref, dq_ref, dk_ref, dv_ref):
    q, k, v, do = q_ref[...], k_ref[...], v_ref[...], do_ref[...]
    k_t = k.T
    dq_t, dk, dv = [], None, None
    for half in range(2):
        mine, q_only, _, q_mask, k_mask = head_views(half, seq, q, k)
        do_only = jnp.where(mine, do, jnp.zeros_like(do))
        s_t = mm(k_mask, q_mask, NT)
        p_t = jnp.exp(s_t - lse_ref[0, 0, half : half + 1, :])
        dp_t = mm(v, do_only, NT)
        inner = jnp.sum(p_t * dp_t, axis=0, keepdims=True)
        ds_t = (p_t * (dp_t - inner)).astype(BF16)
        dv_half = mm(p_t.astype(BF16), do_only, NN)
        dk_half = mm(ds_t, q_only, NN)
        dq_t.append(mm(k_t[half * HEAD : (half + 1) * HEAD], ds_t, NN))
        dv = dv_half if dv is None else dv + dv_half
        dk = dk_half if dk is None else dk + dk_half
    dq_ref[...] = jnp.concatenate(dq_t, axis=0).T.astype(BF16) * 0.125
    dk_ref[...] = dk.astype(BF16)
    dv_ref[...] = dv.astype(BF16)


def attention_forward(q, k, v, images, seq):
    rows, width = q.shape
    s = rows // images
    pairs = width // LANES
    block = pl.BlockSpec((s, LANES), lambda i, j: (i, j))
    lse_block = pl.BlockSpec((1, 1, 2, s), lambda i, j: (i, j, 0, 0))
    n = images * pairs * 2
    return pl.pallas_call(
        functools.partial(attn_fwd_kernel, seq),
        grid=(images, pairs),
        in_specs=[block] * 3,
        out_specs=[block, lse_block],
        out_shape=[
            jax.ShapeDtypeStruct((rows, width), BF16),
            jax.ShapeDtypeStruct((images, pairs, 2, s), F32),
        ],
        cost_estimate=pl.CostEstimate(
            flops=n * 4 * s * s * 256, bytes_accessed=rows * width * 8, transcendentals=n * s * s
        ),
        name="attn_fwd",
    )(q, k, v)


def attention_backward(q, k, v, do, lse, images, seq):
    rows, width = q.shape
    s = rows // images
    pairs = width // LANES
    block = pl.BlockSpec((s, LANES), lambda i, j: (i, j))
    lse_block = pl.BlockSpec((1, 1, 2, s), lambda i, j: (i, j, 0, 0))
    n = images * pairs * 2
    return pl.pallas_call(
        functools.partial(attn_bwd_kernel, seq),
        grid=(images, pairs),
        in_specs=[block] * 4 + [lse_block],
        out_specs=[block] * 3,
        out_shape=[jax.ShapeDtypeStruct((rows, width), BF16)] * 3,
        cost_estimate=pl.CostEstimate(
            flops=n * 10 * s * s * 256, bytes_accessed=rows * width * 14, transcendentals=n * s * s
        ),
        name="attn_bwd",
    )(q, k, v, do, lse)


def norm_stats(rows):
    mean = jnp.mean(rows, axis=-1, keepdims=True)
    center = rows - mean
    inv = lax.rsqrt(jnp.mean(center * center, axis=-1, keepdims=True) + EPS)
    return mean, inv


def norm_back(grad, unit, inv, gain):
    scaled = grad * gain
    first = jnp.mean(scaled, axis=-1, keepdims=True)
    second = jnp.mean(scaled * unit, axis=-1, keepdims=True)
    return (
        inv * (scaled - first - unit * second),
        jnp.sum(grad * unit, axis=0),
        jnp.sum(grad, axis=0),
    )


def pick(pieces, index):
    out = pieces[0]
    for n in range(1, len(pieces)):
        out = jnp.where(index == n, pieces[n], out)
    return out


def per_device(
    inputs,
    cotangent,
    slot_mask,
    w_qkv,
    bias_qv,
    w_out,
    bias_out,
    ln1_gain,
    ln1_bias,
    ln2_gain,
    ln2_bias,
    w_up,
    bias_up,
    w_down,
    bias_down,
):
    n_img, seq, width = inputs.shape
    n_tensor = lax.axis_size("tensor")
    n_dp = lax.axis_size("dp")
    chips = n_tensor // 2
    images = n_img // chips
    full = width * n_tensor
    padded = -(-seq // ROW_TILE) * ROW_TILE
    rows = images * padded
    t_idx = lax.axis_index("tensor")
    d_idx = lax.axis_index("dp")
    chip, core = t_idx // 2, t_idx % 2
    bits = n_dp.bit_length() - 1

    def chip_shift(value, step):
        perm = [
            (2 * a + b, 2 * ((a + step) % chips) + b) for a in range(chips) for b in range(2)
        ]
        return lax.ppermute(value, "tensor", perm)

    def core_swap(value):
        return lax.ppermute(value, "tensor", [(a, a ^ 1) for a in range(n_tensor)])

    def dp_swap(value, bit):
        return lax.ppermute(value, "dp", [(a, a ^ (1 << bit)) for a in range(n_dp)])

    def my_images(value, step):
        return lax.dynamic_slice_in_dim(value, ((chip + step) % chips) * images, images, 0)

    def gather_rows(value):
        mine = [my_images(value, 0)] + [
            chip_shift(my_images(value, step), step) for step in range(1, chips)
        ]
        theirs = [core_swap(piece) for piece in mine]
        parts = []
        for a in range(chips):
            which = (chip - a) % chips
            own, other = pick(mine, which), pick(theirs, which)
            parts += [jnp.where(core == 0, own, other), jnp.where(core == 0, other, own)]
        out = jnp.concatenate(parts, axis=2)
        out = jnp.pad(out, ((0, 0), (0, padded - seq), (0, 0)))
        return out.reshape(rows, full)

    def scatter_rows(value):
        value = value.reshape(images, padded, full)[:, :seq]
        pieces = []
        for step in range(chips):
            block = 2 * ((chip + step) % chips) + core
            piece = pick(
                [value[:, :, n * width : (n + 1) * width] for n in range(n_tensor)], block
            )
            pieces.append(piece if step == 0 else chip_shift(piece, step))
        return jnp.concatenate([pick(pieces, (chip - a) % chips) for a in range(chips)], axis=0)

    side = d_idx & 1

    def gather_weight(weight, axis):
        half = weight.shape[axis] // 2
        blocks = [weight]
        send = lax.dynamic_slice_in_dim(weight, side * half, half, axis)
        for step in range(1, chips):
            got = chip_shift(send, step)
            other = dp_swap(got, 0)
            blocks.append(
                jnp.where(
                    side == 0,
                    jnp.concatenate([got, other], axis),
                    jnp.concatenate([other, got], axis),
                )
            )
        return blocks

    def reduce_blocks(blocks):
        total = blocks[0].astype(F32)
        for step in range(1, chips):
            total = total + chip_shift(blocks[step].astype(BF16), chips - step).astype(F32)
        total = total.astype(BF16)
        for bit in range(bits):
            half = total.shape[0] // 2
            at = (d_idx >> bit) & 1
            keep = lax.dynamic_slice_in_dim(total, at * half, half, 0)
            send = lax.dynamic_slice_in_dim(total, (1 - at) * half, half, 0)
            total = (keep.astype(F32) + dp_swap(send, bit).astype(F32)).astype(BF16)
        for bit in reversed(range(bits)):
            at = (d_idx >> bit) & 1
            other = dp_swap(total, bit)
            total = jnp.where(
                at == 0,
                jnp.concatenate([total, other], 0),
                jnp.concatenate([other, total], 0),
            )
        return total.astype(F32)

    def exchange(part):
        part = part.astype(BF16)
        return part.astype(F32) + core_swap(part).astype(F32)

    gain_one, shift_one = ln1_gain.astype(F32), ln1_bias.astype(F32)
    gain_two, shift_two = ln2_gain.astype(F32), ln2_bias.astype(F32)

    x = gather_rows(inputs)
    wq = gather_weight(w_qkv, 1)
    small = jnp.concatenate([bias_up, bias_qv.reshape(-1)])
    smalls = [small] + [chip_shift(small, step) for step in range(1, chips)]
    n_up = bias_up.shape[0]
    up_bias = [v[:n_up].astype(F32) for v in smalls]
    qv_bias = [v[n_up:].reshape(2, width).astype(F32) for v in smalls]
    wo = gather_weight(w_out, 0)
    wu = gather_weight(w_up, 0)
    live = my_images(slot_mask, 0).astype(BF16)[:, None, None]
    dy = gather_rows(cotangent)
    dy = (dy.reshape(images, padded, full) * live).reshape(rows, full)
    wd = gather_weight(w_down, 0)

    x32 = x.astype(F32)
    mean_one, inv_one = norm_stats(x32)
    unit_one = (x32 - mean_one) * inv_one
    normed_one = (unit_one * gain_one + shift_one).astype(BF16)
    saved = []
    attn_part = None
    for r in range(chips):
        q = ((mm(normed_one, wq[r][0], NN) + qv_bias[r][0]) * 0.125).astype(BF16)
        k = mm(normed_one, wq[r][1], NN).astype(BF16)
        v = (mm(normed_one, wq[r][2], NN) + qv_bias[r][1]).astype(BF16)
        o, lse = attention_forward(q, k, v, images, seq)
        saved.append((q, k, v, o, lse))
        part = mm(o, wo[r], NN)
        attn_part = part if attn_part is None else attn_part + part
    resid = x32 + (exchange(attn_part) + bias_out.astype(F32))
    mean_two, inv_two = norm_stats(resid)
    unit_two = (resid - mean_two) * inv_two
    normed_two = (unit_two * gain_two + shift_two).astype(BF16)
    mlp_part = None
    acts, slopes = [], []
    for r in range(chips):
        hidden = mm(normed_two, wu[r], NN) + up_bias[r]
        sigma = jax.nn.sigmoid(GELU_K * hidden)
        acts.append((hidden * sigma).astype(BF16))
        slopes.append(sigma + GELU_K * hidden * sigma * (1.0 - sigma))
        part = mm(acts[r], wd[r], NN)
        mlp_part = part if mlp_part is None else mlp_part + part
    out = (resid + (exchange(mlp_part) + bias_down.astype(F32))).astype(BF16)
    layer_out = scatter_rows(out)

    grad_down = reduce_blocks([mm(acts[r], dy, TN) for r in range(chips)])
    d_hidden = []
    part_two = None
    for r in range(chips):
        d_hidden.append((mm(dy, wd[r], NT) * slopes[r]).astype(BF16))
        part = mm(d_hidden[r], wu[r], NT)
        part_two = part if part_two is None else part_two + part
    grad_up = reduce_blocks([mm(normed_two, d_hidden[r], TN) for r in range(chips)])
    back_two, g_gain_two, g_shift_two = norm_back(exchange(part_two), unit_two, inv_two, gain_two)
    d_resid = dy.astype(F32) + back_two
    d_attn = d_resid.astype(BF16)
    part_one = None
    attn_blocks = []
    bqv_blocks = []
    for r in range(chips):
        q, k, v, o, lse = saved[r]
        do = mm(d_attn, wo[r], NT).astype(BF16)
        grads = attention_backward(q, k, v, do, lse, images, seq)
        for n in range(3):
            part = mm(grads[n], wq[r][n], NT)
            part_one = part if part_one is None else part_one + part
        attn_blocks.append(
            jnp.concatenate(
                [mm(normed_one, g, TN) for g in grads] + [mm(d_attn, o, TN)], axis=0
            )
        )
        bqv_blocks.append(
            jnp.concatenate([jnp.sum(grads[n], axis=0, dtype=F32) for n in (0, 2)])
        )
    grad_attn = reduce_blocks(attn_blocks)
    back_one, g_gain_one, g_shift_one = norm_back(exchange(part_one), unit_one, inv_one, gain_one)
    input_grad = scatter_rows((d_resid + back_one).astype(BF16))
    grad_qkv = grad_attn[: 3 * full].reshape(3, full, width)
    grad_out = grad_attn[3 * full :].T

    shared = jnp.concatenate(
        [
            jnp.sum(d_attn, axis=0, dtype=F32),
            g_gain_one,
            g_shift_one,
            g_gain_two,
            g_shift_two,
            jnp.sum(dy, axis=0, dtype=F32),
        ]
    )
    shared = jnp.where(core == 0, shared, 0.0)
    own = [
        jnp.concatenate([jnp.sum(d_hidden[r], axis=0, dtype=F32), bqv_blocks[r]])
        for r in range(chips)
    ]
    placed = []
    for n in range(n_tensor):
        here = pick(own, (chip - n // 2) % chips)
        placed.append(jnp.where(core == n % 2, here, 0.0))
    vector = lax.psum(jnp.concatenate([shared] + placed), ("dp", "tensor"))
    vecs = [vector[n * full : (n + 1) * full] for n in range(6)]
    size = n_up + 2 * width
    mine = pick(
        [vector[6 * full + n * size : 6 * full + (n + 1) * size] for n in range(n_tensor)], t_idx
    )
    return (
        layer_out,
        input_grad,
        grad_qkv,
        mine[n_up:].reshape(2, width),
        grad_out,
        vecs[0],
        vecs[1],
        vecs[2],
        vecs[3],
        vecs[4],
        grad_up,
        mine[:n_up],
        grad_down,
        vecs[5],
    )


def solution(mesh):
    return jax.shard_map(
        per_device,
        mesh=mesh,
        in_specs=(
            P("dp", None, "tensor"),
            P("dp", None, "tensor"),
            P("dp"),
            P(None, None, "tensor"),
            P(None, "tensor"),
            P("tensor", None),
            P(),
            P(),
            P(),
            P(),
            P(),
            P(None, "tensor"),
            P("tensor"),
            P("tensor", None),
            P(),
        ),
        out_specs=(
            P("dp", None, "tensor"),
            P("dp", None, "tensor"),
            P(None, None, "tensor"),
            P(None, "tensor"),
            P("tensor", None),
            P(),
            P(),
            P(),
            P(),
            P(),
            P(None, "tensor"),
            P("tensor"),
            P("tensor", None),
            P(),
        ),
        check_vma=False,
    )
```

time: 1550 us -> 587 us (0.38)
  waiting for transfers between devices: 1050 us -> 248 us
  matrix products: 211 us -> 111 us
  local copies, waits for them, and re-layouts: 106 us -> 30.7 us
  Pallas kernels: 0 us -> 42.8 us
  starting transfers between devices: 4.11 us -> 42.7 us
  other arithmetic: 89.6 us -> 63.7 us
  blocking collectives: 66.1 us -> 41.4 us
  between operations: 20.3 us -> 2.32 us
    reduce_scatter x20 -> x0, waiting for transfers between devices: 685 us -> none  [the longest x16 519 us: feature_sum(): lax.psum_scatter(partial_value, 'tensor', scatter_dimension=2, tiled=True)]
    all_gather x20 -> x0, waiting for transfers between devices: 359 us -> none  [the longest x1 75.2 us: per_device(): lax.all_gather(acc_down, 'dp', axis=1, tiled=True)]
    ppermute x0 -> x42, waiting for transfers between devices: none -> 248 us  [the longest x12 145 us: chip_shift(): return lax.ppermute(value, 'tensor', perm)]
    dot_general x72 -> x36, matrix products: 211 us -> 111 us  [mm(): return lax.dot_general(left, right, dims, preferred_element_type=F32)]
    pallas_call x0 -> x4, Pallas kernels: none -> 42.8 us  [the longest x2 25.9 us: attention_backward(): pl.pallas_call(functools.partial(attn_bwd_kernel, seq), grid=(images, pai...]
    ppermute x0 -> x42, starting transfers between devices: none -> 42.7 us  [the longest x22 25.2 us: dp_swap(): return lax.ppermute(value, 'dp', [(a, a ^ 1 << bit) for a in range(n_dp)])]
    unnamed x374 -> x137, local copies, waits for them, and re-layouts: 52.1 us -> 13.2 us
    slice x25 -> x7, local copies, waits for them, and re-layouts: 38.1 us -> 3.68 us  [the longest x1 1.87 us: per_device(): grad_qkv = grad_attn[:3 * full].reshape(3, full, width)]
  transfers between devices with their start and end apart: 40 -> 42, of which waited for: 36 -> 18; matrix products, arithmetic and copies ran while one was open for 22% -> 32% of each run, Pallas kernels for 0% -> 7%
where the time goes in v1:
time: 587 us; the launch traced here: 583 us
  waiting for transfers between devices  248 us (42%)
  matrix products  111 us (19%)
  other arithmetic  63.7 us (11%)
  Pallas kernels  42.8 us (7%)
  starting transfers between devices  42.7 us (7%)
  blocking collectives  41.4 us (7%)
  local copies, waits for them, and re-layouts  30.7 us (5%)
    ppermute x12, waiting for transfers between devices, chip_shift(): return lax.ppermute(value, 'tensor', perm)  145 us
    dot_general x36, matrix products, mm(): return lax.dot_general(left, right, dims, preferred_element_type=F32)  111 us
    ppermute x22, waiting for transfers between devices, dp_swap(): return lax.ppermute(value, 'dp', [(a, a ^ 1 << bit) for a in range(n_dp)])  103 us
    psum x1, blocking collectives, per_device(): vector = lax.psum(jnp.concatenate([shared] + placed), ('dp', 'tensor'))  41.4 us
    pallas_call x2, Pallas kernels, attention_backward(): pl.pallas_call(functools.partial(attn_bwd_kernel, seq), grid=(images, pai...  25.9 us
    ppermute x22, starting transfers between devices, dp_swap(): return lax.ppermute(value, 'dp', [(a, a ^ 1 << bit) for a in range(n_dp)])  25.2 us
    ppermute x12, starting transfers between devices, chip_shift(): return lax.ppermute(value, 'tensor', perm)  16.9 us
    pallas_call x2, Pallas kernels, attention_forward(): pl.pallas_call(functools.partial(attn_fwd_kernel, seq), grid=(images, pai...  16.8 us
  transfers between devices with their start and end apart: 42, of which 18 were waited for; matrix products, arithmetic and copies ran while one was open for 32% of the time, Pallas kernels for 7%

profile of v1, /device:TPU:0, one launch (start us, length us, event | category | flops | bytes accessed | tf_op | source)
XLA Modules:
  0.0 583.3 jit_solution(6919944488249147238)
XLA Ops:
  0.8 3.8 constant_dynamic-slice_fusion.16
  4.6 3.0 collective-permute-start
  7.7 2.1 constant_dynamic-slice_fusion.14
  9.8 2.0 collective-permute-start.3
  12.5 9.6 %collective-permute-done = bf16[2,577,256]{2,0,1:T(2,128)(2,1)} collective-permute-done((bf16[2,577,256]{2,0,1:T(2,128)(2,1)}, bf16[2,577,256]{2,0,1:T(2,128)(2,1)}, u32[]{:S(2)}, u32[]{:S(2)}) %collective-permute-start) | collective-permute-done | bytes 590880 | tf_op jit(solution)/shard_map/ppermute | solution.py:183
  22.2 21.5 %collective-permute-done.6 = bf16[128,1024]{1,0:T(8,128)(2,1)S(1)} collective-permute-done((bf16[128,1024]{1,0:T(8,128)(2,1)}, bf16[128,1024]{1,0:T(8,128)(2,1)S(1)}, u32[]{:S(2)}, u32[]{:S(2)}) %collective-permute-start.6) | collective-permute-done | bytes 262176 | tf_op jit(solution)/shard_map/ppermute | solution.py:183
  55.5 8.3 %attn_fwd.2 = (bf16[1184,256]{1,0:T(8,128)(2,1)}, f32[2,2,2,592]{3,2,1,0:T(2,128)}) custom-call(bf16[1184,256]{1,0:T(8,128)(2,1)} %fusion.16.q_ref, bf16[1184,256]{1,0:T(8,128)(2,1)} %convolution_convert_fusion.3.k_ref, bf16[1184,256]{1,0:T(8,128)(2,1)} %fusion.17.v_ref), custom_call_target="tpu_custom_call" | custom-call | flops 2871001088 | bytes 2424832 | tf_op jit(solution)/shard_map/attn_fwd/pallas_call | solution.py:88
  63.8 4.1 fusion.63
  68.1 2.3 maximum_select_fusion.5
  75.4 8.5 %attn_fwd.3 = (bf16[1184,256]{1,0:T(8,128)(2,1)}, f32[2,2,2,592]{3,2,1,0:T(2,128)}) custom-call(bf16[1184,256]{1,0:T(8,128)(2,1)} %multiply_convert_fusion.4.q_ref, bf16[1184,256]{1,0:T(8,128)(2,1)} %convolution_convert_fusion.2.k_ref, bf16[1184,256]{1,0:T(8,128)(2,1)} %add_convert_fusion.14.v_ref), custom_call_target="tpu_custom_call" | custom-call | flops 2871001088 | bytes 2424832 | tf_op jit(solution)/shard_map/attn_fwd/pallas_call | solution.py:88
  84.0 5.1 add_convert_fusion.7
  96.3 32.9 %collective-permute-done.15 = bf16[2,577,256]{2,0,1:T(2,128)(2,1)} collective-permute-done((bf16[2,577,256]{2,0,1:T(2,128)(2,1)S(1)}, bf16[2,577,256]{2,0,1:T(2,128)(2,1)}, u32[]{:S(2)}, u32[]{:S(2)}) %collective-permute-start.15) | collective-permute-done | bytes 590880 | tf_op jit(solution)/shard_map/ppermute | solution.py:183
  131.2 20.1 %collective-permute-done.9 = bf16[512,1024]{1,0:T(8,128)(2,1)} collective-permute-done((bf16[512,1024]{1,0:T(8,128)(2,1)}, bf16[512,1024]{1,0:T(8,128)(2,1)}, u32[]{:S(2)}, u32[]{:S(2)}) %collective-permute-start.9) | collective-permute-done | bytes 1048608 | tf_op jit(solution)/shard_map/ppermute | solution.py:183
  156.2 2.6 convert_reduce_fusion.2
  158.7 6.3 %add_add_fusion = f32[1184,1024]{1,0:T(8,128)} fusion(bf16[1184,1024]{1,0:T(8,128)(2,1)} %collective-permute-done.8, bf16[1184,1024]{1,0:T(8,128)(2,1)} %add_convert_fusion.7, f32[1024]{0:T(1024)S(1)} %convert_element_type.311, bf16[2,592,1024]{2,1,0:T(8,128)(2,1)S(1)} %copy-done.4), kind=kLoop, calls=%fused_computation.35 | loop fusion | flops 7274496 | bytes 12128256 | tf_op jit(solution)/shard_map/add | solution.py:293
  165.0 2.7 reduce_sum.182
  167.7 3.1 multiply_reduce_fusion.4
  172.4 5.4 collective-permute-done.10
  177.8 5.0 fusion.47
  182.8 4.7 convolution_convert_fusion.4
  189.4 7.2 %convert_reduce_fusion.1 = (f32[1024]{0:T(1024)}, bf16[1184,1024]{1,0:T(8,128)(2,1)S(1)}) fusion(f32[1184,1024]{1,0:T(8,128)S(1)} %fusion.47, f32[1024]{0:T(1024)S(1)} %slice_convert_fusion, bf16[1184,1024]{1,0:T(8,128)(2,1)S(1)} %bitcast.114, bf16[512,1024]{1,0:T(8,128)(2,1)} %collective-permute-done.12, bf16[512,1024]{1,0:T(8,128)(2,1)} %collective-permute-done.11, ...), kind=kOutput, calls=%fused_computation.10 | convolution fusion | flops 2508225536 | bytes 11804673 | tf_op jit(solution)/shard_map/dot_general | solution.py:26
  198.0 3.1 convolution_convert_fusion.5
  201.5 3.3 multiply_convert_fusion.3
  204.8 4.6 convert_reduce_fusion
  210.9 4.6 fusion.65
  215.6 6.5 %add_convert_fusion.3 = bf16[1184,1024]{1,0:T(8,128)(2,1)S(1)} fusion(f32[1184,1024]{1,0:T(8,128)} %fusion.65, bf16[1184,1024]{1,0:T(8,128)(2,1)S(1)} %copy-done.55, bf16[512,1024]{1,0:T(8,128)(2,1)} %collective-permute-done.10, bf16[512,1024]{1,0:T(8,128)(2,1)} %collective-permute-done.9, pred[]{:T(512)S(6)} %eq.118), kind=kOutput, calls=%fused_computation.24 | convolution fusion | flops 2494889984 | bytes 11796481 | tf_op jit(solution)/shard_map/dot_general | solution.py:26
  222.2 4.4 fusion.64
  226.6 8.2 %add_convert_fusion.5 = bf16[1184,1024]{1,0:T(8,128)(2,1)S(1)} fusion(f32[1184,1024]{1,0:T(8,128)} %fusion.64, bf16[512,1024]{1,0:T(8,128)(2,1)} %collective-permute-done.12, bf16[512,1024]{1,0:T(8,128)(2,1)} %collective-permute-done.11, pred[]{:T(512)S(6)} %eq.118, f32[1184,1024]{1,0:T(8,128)} %copy-done.52, f32[1024]{0:T(1024)S(1)} %slice_convert_fusion), kind=kOutput, calls=%fused_computation.28 | convolution fusion | flops 2503376896 | bytes 14225409 | tf_op jit(solution)/shard_map/dot_general | solution.py:26
  235.3 6.4 %fusion.70 = f32[1024,1024]{1,0:T(8,128)} fusion(bf16[1184,1024]{1,0:T(8,128)(2,1)} %copy-done.53, bf16[1184,1024]{1,0:T(8,128)(2,1)S(1)} %bitcast.116), kind=kOutput, calls=%fused_computation.218 | convolution fusion | flops 2483027968 | bytes 9043968 | tf_op jit(solution)/shard_map/dot_general | solution.py:26
  241.7 38.3 %collective-permute-done.28 = bf16[1024,1024]{1,0:T(8,128)(2,1)S(1)} collective-permute-done((bf16[1024,1024]{1,0:T(8,128)(2,1)S(1)}, bf16[1024,1024]{1,0:T(8,128)(2,1)S(1)}, u32[]{:S(2)}, u32[]{:S(2)}) %collective-permute-start.28) | collective-permute-done | bytes 2097184 | tf_op jit(solution)/shard_map/ppermute | solution.py:183
  280.0 3.2 add_convert_fusion.10
  286.0 3.3 multiply_reduce_fusion
  289.3 5.3 convert_reduce_fusion.3
  296.3 12.9 %attn_bwd.2 = (bf16[1184,256]{1,0:T(8,128)(2,1)}, bf16[1184,256]{1,0:T(8,128)(2,1)}, bf16[1184,256]{1,0:T(8,128)(2,1)}) custom-call(bf16[1184,256]{1,0:T(8,128)(2,1)} %fusion.16.q_ref, bf16[1184,256]{1,0:T(8,128)(2,1)} %convolution_convert_fusion.3.k_ref, bf16[1184,256]{1,0:T(8,128)(2,1)} %fusion.17.v_ref, ...), custom_call_target="tpu_custom_call" | custom-call | flops 7177502720 | bytes 4243456 | tf_op jit(solution)/shard_map/attn_bwd/pallas_call | solution.py:111
  309.2 4.2 fusion.31
  313.4 3.1 fusion.34
  316.5 2.7 convolution_convert_fusion.do_ref
  319.2 13.1 %attn_bwd.3 = (bf16[1184,256]{1,0:T(8,128)(2,1)}, bf16[1184,256]{1,0:T(8,128)(2,1)}, bf16[1184,256]{1,0:T(8,128)(2,1)}) custom-call(bf16[1184,256]{1,0:T(8,128)(2,1)} %multiply_convert_fusion.4.q_ref, bf16[1184,256]{1,0:T(8,128)(2,1)} %convolution_convert_fusion.2.k_ref, bf16[1184,256]{1,0:T(8,128)(2,1)} %add_convert_fusion.14.v_ref, ...), custom_call_target="tpu_custom_call" | custom-call | flops 7177502720 | bytes 4243456 | tf_op jit(solution)/shard_map/attn_bwd/pallas_call | solution.py:111
  332.3 2.2 fusion.28
  335.6 3.3 fusion.37
  340.4 5.9 %add_convert_fusion.2 = bf16[1184,1024]{1,0:T(8,128)(2,1)} fusion(f32[1184,1024]{1,0:T(8,128)S(1)} %fusion.39, f32[1184,1024]{1,0:T(8,128)} %fusion.37, f32[1184,1024]{1,0:T(8,128)S(1)} %fusion.28, f32[1184,1024]{1,0:T(8,128)S(1)} %bitcast.106, f32[1184,1024]{1,0:T(8,128)S(1)} %bitcast.104, bf16[1184,256]{1,0:T(8,128)(2,1)} %get-tuple-element.33, ...), kind=kOutput, calls=%fused_computation.20 | convolution fusion | flops 628031488 | bytes 27803648 | tf_op jit(solution)/shard_map/dot_general | solution.py:26
  346.3 3.7 add_convert_fusion.9
  359.0 16.8 %collective-permute-done.36 = bf16[512,1024]{1,0:T(8,128)(2,1)S(1)} collective-permute-done((bf16[512,1024]{1,0:T(8,128)(2,1)S(1)}, bf16[512,1024]{1,0:T(8,128)(2,1)S(1)}, u32[]{:S(2)}, u32[]{:S(2)}) %collective-permute-start.36) | collective-permute-done | bytes 1048608 | tf_op jit(solution)/shard_map/ppermute | solution.py:189
  377.9 3.1 multiply_reduce_fusion.1
  381.1 2.8 add_convert_fusion
  389.2 2.7 collective-permute-start.31
  393.2 2.6 collective-permute-start.14
  395.8 13.0 %collective-permute-done.31 = bf16[128,1024]{1,0:T(8,128)(2,1)S(1)} collective-permute-done((bf16[128,1024]{1,0:T(8,128)(2,1)S(1)}, bf16[128,1024]{1,0:T(8,128)(2,1)S(1)}, u32[]{:S(2)}, u32[]{:S(2)}) %collective-permute-start.31) | collective-permute-done | bytes 262176 | tf_op jit(solution)/shard_map/ppermute | solution.py:189
  408.9 11.1 %collective-permute-done.38 = bf16[128,1024]{1,0:T(8,128)(2,1)S(1)} collective-permute-done((bf16[128,1024]{1,0:T(8,128)(2,1)S(1)}, bf16[128,1024]{1,0:T(8,128)(2,1)S(1)}, u32[]{:S(2)}, u32[]{:S(2)}) %collective-permute-start.38) | collective-permute-done | bytes 262176 | tf_op jit(solution)/shard_map/ppermute | solution.py:189
  422.9 13.0 %collective-permute-done.21 = bf16[4096,256]{1,0:T(8,128)(2,1)S(1)} collective-permute-done((bf16[4096,256]{1,0:T(8,128)(2,1)S(1)}, bf16[4096,256]{1,0:T(8,128)(2,1)S(1)}, u32[]{:S(2)}, u32[]{:S(2)}) %collective-permute-start.21) | collective-permute-done | bytes 2097184 | tf_op jit(solution)/shard_map/ppermute | solution.py:183
  437.2 9.8 %collective-permute-done.14 = bf16[2,577,256]{2,0,1:T(2,128)(2,1)S(1)} collective-permute-done((bf16[2,577,256]{2,0,1:T(2,128)(2,1)S(1)}, bf16[2,577,256]{2,0,1:T(2,128)(2,1)S(1)}, u32[]{:S(2)}, u32[]{:S(2)}) %collective-permute-start.14) | collective-permute-done | bytes 590880 | tf_op jit(solution)/shard_map/ppermute | solution.py:183
  451.3 10.9 %collective-permute-done.33 = bf16[256,1024]{1,0:T(8,128)(2,1)S(1)} collective-permute-done((bf16[256,1024]{1,0:T(8,128)(2,1)S(1)}, bf16[256,1024]{1,0:T(8,128)(2,1)S(1)}, u32[]{:S(2)}, u32[]{:S(2)}) %collective-permute-start.33) | collective-permute-done | bytes 524320 | tf_op jit(solution)/shard_map/ppermute | solution.py:189
  463.3 7.7 %collective-permute-done.40 = bf16[256,1024]{1,0:T(8,128)(2,1)S(1)} collective-permute-done((bf16[256,1024]{1,0:T(8,128)(2,1)S(1)}, bf16[256,1024]{1,0:T(8,128)(2,1)S(1)}, u32[]{:S(2)}, u32[]{:S(2)}) %collective-permute-start.40) | collective-permute-done | bytes 524320 | tf_op jit(solution)/shard_map/ppermute | solution.py:189
  476.0 8.7 %collective-permute-done.23 = bf16[1024,256]{1,0:T(8,128)(2,1)S(1)} collective-permute-done((bf16[1024,256]{1,0:T(8,128)(2,1)S(1)}, bf16[1024,256]{1,0:T(8,128)(2,1)S(1)}, u32[]{:S(2)}, u32[]{:S(2)}) %collective-permute-start.23) | collective-permute-done | bytes 524320 | tf_op jit(solution)/shard_map/ppermute | solution.py:189
  484.8 4.1 collective-permute-start.24
  489.0 10.9 %collective-permute-done.24 = bf16[512,256]{1,0:T(8,128)(2,1)S(1)} collective-permute-done((bf16[512,256]{1,0:T(8,128)(2,1)S(1)}, bf16[512,256]{1,0:T(8,128)(2,1)S(1)}, u32[]{:S(2)}, u32[]{:S(2)}) %collective-permute-start.24) | collective-permute-done | bytes 262176 | tf_op jit(solution)/shard_map/ppermute | solution.py:189
  500.1 10.0 %collective-permute-done.25 = bf16[512,256]{1,0:T(8,128)(2,1)S(1)} collective-permute-done((bf16[512,256]{1,0:T(8,128)(2,1)S(1)}, bf16[512,256]{1,0:T(8,128)(2,1)S(1)}, u32[]{:S(2)}, u32[]{:S(2)}) %collective-permute-start.25) | collective-permute-done | bytes 262176 | tf_op jit(solution)/shard_map/ppermute | solution.py:189
  510.5 41.4 %psum.7 = f32[12288]{0:T(1024)S(1)} all-reduce(f32[12288]{0:T(1024)S(1)} %select_dynamic-update-slice_fusion.1), channel_id=1, replica_groups=mesh['dp'=8,'tensor'=4] {'dp','tensor'}, use_global_device_ids=true, to_apply=%region_20.21 | all-reduce | flops 12288 | bytes 98304 | tf_op jit(solution)/shard_map/psum | solution.py:363
  555.1 2.3 collective-permute-start.27
  557.4 1.9 broadcast_select_fusion.14
  561.0 4.4 fusion.26
  565.5 5.3 fusion.27
  570.7 8.6 %collective-permute-done.27 = bf16[2048,256]{1,0:T(8,128)(2,1)S(1)} collective-permute-done((bf16[2048,256]{1,0:T(8,128)(2,1)S(1)}, bf16[2048,256]{1,0:T(8,128)(2,1)S(1)}, u32[]{:S(2)}, u32[]{:S(2)}) %collective-permute-start.27) | collective-permute-done | bytes 1048608 | tf_op jit(solution)/shard_map/ppermute | solution.py:189
  579.9 1.9 slice.222
  (301 shorter events, 85.6 us)
Async XLA Ops:
  0.6 93.1 %copy-start = (bf16[1024,1024]{1,0:T(8,128)(2,1)S(1)}, bf16[1024,1024]{1,0:T(8,128)(2,1)}, u32[]{:S(2)}) copy-start(bf16[1024,1024]{1,0:T(8,128)(2,1)} %param.26) | copy-start | bytes 6291460
  0.7 11.1 %copy-start.31 = (bf16[256,1024]{1,0:T(8,128)(2,1)S(1)}, bf16[256,1024]{1,0:T(8,128)(2,1)}, u32[]{:S(2)}) copy-start(bf16[256,1024]{1,0:T(8,128)(2,1)} %param.20) | copy-start | bytes 1572868
  0.7 21.4 %copy-start.45 = (bf16[1024]{0:T(1024)(128)(2,1)S(1)}, bf16[1024]{0:T(1024)(128)(2,1)}, u32[]{:S(2)}) copy-start(bf16[1024]{0:T(1024)(128)(2,1)} %param.22) | copy-start | bytes 6148
  0.7 21.4 %copy-start.46 = (bf16[1024]{0:T(1024)(128)(2,1)S(1)}, bf16[1024]{0:T(1024)(128)(2,1)}, u32[]{:S(2)}) copy-start(bf16[1024]{0:T(1024)(128)(2,1)} %param.23) | copy-start | bytes 6148
  4.6 17.5 %collective-permute-start = (bf16[2,577,256]{2,0,1:T(2,128)(2,1)}, bf16[2,577,256]{2,0,1:T(2,128)(2,1)}, u32[]{:S(2)}, u32[]{:S(2)}) collective-permute-start(bf16[2,577,256]{2,0,1:T(2,128)(2,1)} %get-tuple-element.108), channel_id=1, source_target_pairs={{0,2},{1,3},{2,0},{3,1},{4,6},{5,7},{6,4},{7,5},{8,10},{9,11},{10,... | collective-permute-start | bytes 1772552 | tf_op jit(solution)/shard_map/ppermute | solution.py:183
  7.6 14.6 %collective-permute-start.5 = (bf16[1536]{0:T(1024)(128)(2,1)S(1)}, bf16[1536]{0:T(1024)(128)(2,1)S(1)}, u32[]{:S(2)}, u32[]{:S(2)}) collective-permute-start(bf16[1536]{0:T(1024)(128)(2,1)S(1)} %pad_maximum_fusion.5), channel_id=1, source_target_pairs={{0,2},{1,3},{2,0},{3,1},{4,6},{5,7},{6,4},{7,5},{8,10},{9,11},{10,... | collective-permute-start | bytes 9224 | tf_op jit(solution)/shard_map/ppermute | solution.py:183
  9.8 35.6 %collective-permute-start.3 = (bf16[3,512,256]{2,1,0:T(8,128)(2,1)}, bf16[3,512,256]{2,1,0:T(8,128)(2,1)}, u32[]{:S(2)}, u32[]{:S(2)}) collective-permute-start(bf16[3,512,256]{2,1,0:T(8,128)(2,1)} %constant_dynamic-slice_fusion.14), channel_id=1, source_target_pairs={{0,2},{1,3},{2,0},{3,1},{4,6},{5,7},{6,4},{7,5},{8,10},{9,11},{10,... | collective-permute-start | bytes 2359304 | tf_op jit(solution)/shard_map/ppermute | solution.py:183
  12.5 31.2 %collective-permute-start.6 = (bf16[128,1024]{1,0:T(8,128)(2,1)}, bf16[128,1024]{1,0:T(8,128)(2,1)S(1)}, u32[]{:S(2)}, u32[]{:S(2)}) collective-permute-start(bf16[128,1024]{1,0:T(8,128)(2,1)} %constant_dynamic-slice_fusion.13), channel_id=1, source_target_pairs={{0,2},{1,3},{2,0},{3,1},{4,6},{5,7},{6,4},{7,5},{8,10},{9,11},{10,... | collective-permute-start | bytes 786440 | tf_op jit(solution)/shard_map/ppermute | solution.py:183
  12.5 33.2 %collective-permute-start.2 = (bf16[2,577,256]{2,0,1:T(2,128)(2,1)S(1)}, bf16[2,577,256]{2,0,1:T(2,128)(2,1)}, u32[]{:S(2)}, u32[]{:S(2)}) collective-permute-start(bf16[2,577,256]{2,0,1:T(2,128)(2,1)S(1)} %get-tuple-element.109), channel_id=1, source_target_pairs={{0,1},{1,0},{2,3},{3,2},{4,5},{5,4},{6,7},{7,6},{8,9},{9,8},{10,11... | collective-permute-start | bytes 1772552 | tf_op jit(solution)/shard_map/ppermute | solution.py:186
  22.1 23.6 %collective-permute-start.1 = (bf16[2,577,256]{2,0,1:T(2,128)(2,1)}, bf16[2,577,256]{2,0,1:T(2,128)(2,1)}, u32[]{:S(2)}, u32[]{:S(2)}) collective-permute-start(bf16[2,577,256]{2,0,1:T(2,128)(2,1)} %collective-permute-done), channel_id=1, source_target_pairs={{0,1},{1,0},{2,3},{3,2},{4,5},{5,4},{6,7},{7,6},{8,9},{9,8},{10,11... | collective-permute-start | bytes 1772552 | tf_op jit(solution)/shard_map/ppermute | solution.py:186
  22.1 27.0 %copy-start.38 = (f32[1024]{0:T(1024)}, f32[1024]{0:T(1024)S(1)}, u32[]{:S(2)}) copy-start(f32[1024]{0:T(1024)S(1)} %convert_element_type.296) | copy-start | bytes 12292
  22.2 27.0 %copy-start.40 = (f32[1024]{0:T(1024)}, f32[1024]{0:T(1024)S(1)}, u32[]{:S(2)}) copy-start(f32[1024]{0:T(1024)S(1)} %convert_element_type.297) | copy-start | bytes 12292
  43.7 40.3 %collective-permute-start.7 = (bf16[128,1024]{1,0:T(8,128)(2,1)S(1)}, bf16[128,1024]{1,0:T(8,128)(2,1)}, u32[]{:S(2)}, u32[]{:S(2)}) collective-permute-start(bf16[128,1024]{1,0:T(8,128)(2,1)S(1)} %collective-permute-done.6), channel_id=1, source_target_pairs={{0,4},{4,0},{8,12},{12,8},{16,20},{20,16},{24,28},{28,24},{1,5},{5... | collective-permute-start | bytes 786440 | tf_op jit(solution)/shard_map/ppermute | solution.py:189
  45.4 22.7 %collective-permute-start.4 = (bf16[3,512,256]{2,1,0:T(8,128)(2,1)}, bf16[3,512,256]{2,1,0:T(8,128)(2,1)}, u32[]{:S(2)}, u32[]{:S(2)}) collective-permute-start(bf16[3,512,256]{2,1,0:T(8,128)(2,1)} %collective-permute-done.3), channel_id=1, source_target_pairs={{0,4},{4,0},{8,12},{12,8},{16,20},{20,16},{24,28},{28,24},{1,5},{5... | collective-permute-start | bytes 2359304 | tf_op jit(solution)/shard_map/ppermute | solution.py:189
  89.1 69.6 %collective-permute-start.8 = (bf16[1184,1024]{1,0:T(8,128)(2,1)}, bf16[1184,1024]{1,0:T(8,128)(2,1)}, u32[]{:S(2)}, u32[]{:S(2)}) collective-permute-start(bf16[1184,1024]{1,0:T(8,128)(2,1)} %add_convert_fusion.7), channel_id=1, source_target_pairs={{0,1},{1,0},{2,3},{3,2},{4,5},{5,4},{6,7},{7,6},{8,9},{9,8},{10,11... | collective-permute-start | bytes 7274504 | tf_op jit(solution)/shard_map/ppermute | solution.py:186
  90.2 39.1 %copy-start.47 = (bf16[1024]{0:T(1024)(128)(2,1)S(1)}, bf16[1024]{0:T(1024)(128)(2,1)}, u32[]{:S(2)}) copy-start(bf16[1024]{0:T(1024)(128)(2,1)} %param.24) | copy-start | bytes 6148
  90.2 39.1 %copy-start.48 = (bf16[1024]{0:T(1024)(128)(2,1)S(1)}, bf16[1024]{0:T(1024)(128)(2,1)}, u32[]{:S(2)}) copy-start(bf16[1024]{0:T(1024)(128)(2,1)} %param.21) | copy-start | bytes 6148
  90.2 39.1 %copy-start.49 = (bf16[1024]{0:T(1024)(128)(2,1)S(1)}, bf16[1024]{0:T(1024)(128)(2,1)}, u32[]{:S(2)}) copy-start(bf16[1024]{0:T(1024)(128)(2,1)} %param.25) | copy-start | bytes 6148
  90.2 39.2 %copy-start.50 = (bf16[1024]{0:T(1024)(128)(2,1)S(1)}, bf16[1024]{0:T(1024)(128)(2,1)}, u32[]{:S(2)}) copy-start(bf16[1024]{0:T(1024)(128)(2,1)} %param.29) | copy-start | bytes 6148
  90.2 39.2 %copy-start.51 = (s32[4]{0:T(128)S(1)}, s32[4]{0:T(128)}, u32[]{:S(2)}) copy-start(s32[4]{0:T(128)} %param.17) | copy-start | bytes 52
  90.2 39.3 %collective-permute-start.11 = (bf16[512,1024]{1,0:T(8,128)(2,1)}, bf16[512,1024]{1,0:T(8,128)(2,1)}, u32[]{:S(2)}, u32[]{:S(2)}) collective-permute-start(bf16[512,1024]{1,0:T(8,128)(2,1)} %constant_dynamic-slice_fusion.11), channel_id=1, source_target_pairs={{0,2},{1,3},{2,0},{3,1},{4,6},{5,7},{6,4},{7,5},{8,10},{9,11},{10,... | collective-permute-start | bytes 3145736 | tf_op jit(solution)/shard_map/ppermute | solution.py:183
  93.2 36.1 %collective-permute-start.15 = (bf16[2,577,256]{2,0,1:T(2,128)(2,1)S(1)}, bf16[2,577,256]{2,0,1:T(2,128)(2,1)}, u32[]{:S(2)}, u32[]{:S(2)}) collective-permute-start(bf16[2,577,256]{2,0,1:T(2,128)(2,1)S(1)} %get-tuple-element.106), channel_id=1, source_target_pairs={{0,2},{1,3},{2,0},{3,1},{4,6},{5,7},{6,4},{7,5},{8,10},{9,11},{10,... | collective-permute-start | bytes 1772552 | tf_op jit(solution)/shard_map/ppermute | solution.py:183
  94.8 56.4 %collective-permute-start.9 = (bf16[512,1024]{1,0:T(8,128)(2,1)}, bf16[512,1024]{1,0:T(8,128)(2,1)}, u32[]{:S(2)}, u32[]{:S(2)}) collective-permute-start(bf16[512,1024]{1,0:T(8,128)(2,1)} %constant_dynamic-slice_fusion.12), channel_id=1, source_target_pairs={{0,2},{1,3},{2,0},{3,1},{4,6},{5,7},{6,4},{7,5},{8,10},{9,11},{10,... | collective-permute-start | bytes 3145736 | tf_op jit(solution)/shard_map/ppermute | solution.py:183
  96.3 58.0 %collective-permute-start.17 = (bf16[2,577,256]{2,0,1:T(2,128)(2,1)S(1)}, bf16[2,577,256]{2,0,1:T(2,128)(2,1)}, u32[]{:S(2)}, u32[]{:S(2)}) collective-permute-start(bf16[2,577,256]{2,0,1:T(2,128)(2,1)S(1)} %get-tuple-element.107), channel_id=1, source_target_pairs={{0,1},{1,0},{2,3},{3,2},{4,5},{5,4},{6,7},{7,6},{8,9},{9,8},{10,11... | collective-permute-start | bytes 1772552 | tf_op jit(solution)/shard_map/ppermute | solution.py:186
  129.3 25.1 %collective-permute-start.16 = (bf16[2,577,256]{2,0,1:T(2,128)(2,1)}, bf16[2,577,256]{2,0,1:T(2,128)(2,1)}, u32[]{:S(2)}, u32[]{:S(2)}) collective-permute-start(bf16[2,577,256]{2,0,1:T(2,128)(2,1)} %collective-permute-done.15), channel_id=1, source_target_pairs={{0,1},{1,0},{2,3},{3,2},{4,5},{5,4},{6,7},{7,6},{8,9},{9,8},{10,11... | collective-permute-start | bytes 1772552 | tf_op jit(solution)/shard_map/ppermute | solution.py:186
  129.4 59.9 %collective-permute-start.12 = (bf16[512,1024]{1,0:T(8,128)(2,1)}, bf16[512,1024]{1,0:T(8,128)(2,1)}, u32[]{:S(2)}, u32[]{:S(2)}) collective-permute-start(bf16[512,1024]{1,0:T(8,128)(2,1)} %collective-permute-done.11), channel_id=1, source_target_pairs={{0,4},{4,0},{8,12},{12,8},{16,20},{20,16},{24,28},{28,24},{1,5},{5... | collective-permute-start | bytes 3145736 | tf_op jit(solution)/shard_map/ppermute | solution.py:189
  151.3 26.6 %collective-permute-start.10 = (bf16[512,1024]{1,0:T(8,128)(2,1)}, bf16[512,1024]{1,0:T(8,128)(2,1)}, u32[]{:S(2)}, u32[]{:S(2)}) collective-permute-start(bf16[512,1024]{1,0:T(8,128)(2,1)} %collective-permute-done.9), channel_id=1, source_target_pairs={{0,4},{4,0},{8,12},{12,8},{16,20},{20,16},{24,28},{28,24},{1,5},{5... | collective-permute-start | bytes 3145736 | tf_op jit(solution)/shard_map/ppermute | solution.py:189
  187.6 158.7 %collective-permute-start.35 = (bf16[1024,1024]{1,0:T(8,128)(2,1)}, bf16[1024,1024]{1,0:T(8,128)(2,1)}, u32[]{:S(2)}, u32[]{:S(2)}) collective-permute-start(bf16[1024,1024]{1,0:T(8,128)(2,1)} %convolution_convert_fusion.4), channel_id=1, source_target_pairs={{0,2},{1,3},{2,0},{3,1},{4,6},{5,7},{6,4},{7,5},{8,10},{9,11},{10,... | collective-permute-start | bytes 6291464 | tf_op jit(solution)/shard_map/ppermute | solution.py:183
  201.1 78.8 %collective-permute-start.28 = (bf16[1024,1024]{1,0:T(8,128)(2,1)S(1)}, bf16[1024,1024]{1,0:T(8,128)(2,1)S(1)}, u32[]{:S(2)}, u32[]{:S(2)}) collective-permute-start(bf16[1024,1024]{1,0:T(8,128)(2,1)S(1)} %convolution_convert_fusion.5), channel_id=1, source_target_pairs={{0,2},{1,3},{2,0},{3,1},{4,6},{5,7},{6,4},{7,5},{8,10},{9,11},{10,... | collective-permute-start | bytes 6291464 | tf_op jit(solution)/shard_map/ppermute | solution.py:183
  204.8 17.3 %copy-start.53 = (bf16[1184,1024]{1,0:T(8,128)(2,1)}, bf16[1184,1024]{1,0:T(8,128)(2,1)S(1)}, u32[]{:S(2)}) copy-start(bf16[1184,1024]{1,0:T(8,128)(2,1)S(1)} %get-tuple-element.120) | copy-start | bytes 7274500
  222.1 63.9 %collective-permute-start.18 = (bf16[1184,1024]{1,0:T(8,128)(2,1)S(1)}, bf16[1184,1024]{1,0:T(8,128)(2,1)S(1)}, u32[]{:S(2)}, u32[]{:S(2)}) collective-permute-start(bf16[1184,1024]{1,0:T(8,128)(2,1)S(1)} %add_convert_fusion.3), channel_id=1, source_target_pairs={{0,1},{1,0},{2,3},{3,2},{4,5},{5,4},{6,7},{7,6},{8,9},{9,8},{10,11... | collective-permute-start | bytes 7274504 | tf_op jit(solution)/shard_map/ppermute | solution.py:186
  234.7 45.2 %copy-start.57 = (bf16[1184,1024]{1,0:T(8,128)(2,1)S(1)}, bf16[1184,1024]{1,0:T(8,128)(2,1)}, u32[]{:S(2)}) copy-start(bf16[1184,1024]{1,0:T(8,128)(2,1)} %copy-done.56) | copy-start | bytes 7274500
  234.8 54.5 %collective-permute-start.13 = (bf16[1184,1024]{1,0:T(8,128)(2,1)S(1)}, bf16[1184,1024]{1,0:T(8,128)(2,1)S(1)}, u32[]{:S(2)}, u32[]{:S(2)}) collective-permute-start(bf16[1184,1024]{1,0:T(8,128)(2,1)S(1)} %add_convert_fusion.5), channel_id=1, source_target_pairs={{0,1},{1,0},{2,3},{3,2},{4,5},{5,4},{6,7},{7,6},{8,9},{9,8},{10,11... | collective-permute-start | bytes 7274504 | tf_op jit(solution)/shard_map/ppermute | solution.py:186
  284.3 70.6 %collective-permute-start.29 = (bf16[512,1024]{1,0:T(8,128)(2,1)}, bf16[512,1024]{1,0:T(8,128)(2,1)}, u32[]{:S(2)}, u32[]{:S(2)}) collective-permute-start(bf16[512,1024]{1,0:T(8,128)(2,1)} %constant_dynamic-slice_fusion.5), channel_id=1, source_target_pairs={{0,4},{4,0},{8,12},{12,8},{16,20},{20,16},{24,28},{28,24},{1,5},{5... | collective-permute-start | bytes 3145736 | tf_op jit(solution)/shard_map/ppermute | solution.py:189
  296.3 12.9 %copy-start.17 = (bf16[3,1024,256]{2,1,0:T(8,128)(2,1)S(1)}, bf16[3,1024,256]{2,1,0:T(8,128)(2,1)}, u32[]{:S(2)}) copy-start(bf16[3,1024,256]{2,1,0:T(8,128)(2,1)} %param.18) | copy-start | bytes 4718596
  346.3 31.6 %collective-permute-start.19 = (bf16[1184,1024]{1,0:T(8,128)(2,1)}, bf16[1184,1024]{1,0:T(8,128)(2,1)S(1)}, u32[]{:S(2)}, u32[]{:S(2)}) collective-permute-start(bf16[1184,1024]{1,0:T(8,128)(2,1)} %add_convert_fusion.2), channel_id=1, source_target_pairs={{0,1},{1,0},{2,3},{3,2},{4,5},{5,4},{6,7},{7,6},{8,9},{9,8},{10,11... | collective-permute-start | bytes 7274504 | tf_op jit(solution)/shard_map/ppermute | solution.py:186
  350.1 25.6 %collective-permute-start.36 = (bf16[512,1024]{1,0:T(8,128)(2,1)S(1)}, bf16[512,1024]{1,0:T(8,128)(2,1)S(1)}, u32[]{:S(2)}, u32[]{:S(2)}) collective-permute-start(bf16[512,1024]{1,0:T(8,128)(2,1)S(1)} %constant_dynamic-slice_fusion.2), channel_id=1, source_target_pairs={{0,4},{4,0},{8,12},{12,8},{16,20},{20,16},{24,28},{28,24},{1,5},{5... | collective-permute-start | bytes 3145736 | tf_op jit(solution)/shard_map/ppermute | solution.py:189
  357.2 20.7 %copy-start.5 = (bf16[2,592,1024]{2,1,0:T(8,128)(2,1)S(1)}, bf16[2,592,1024]{2,1,0:T(8,128)(2,1)}, u32[]{:S(2)}) copy-start(bf16[2,592,1024]{2,1,0:T(8,128)(2,1)} %copy-done.3) | copy-start | bytes 7274500
  357.2 20.7 %copy-start.6 = (bf16[1184,1024]{1,0:T(8,128)(2,1)S(1)}, bf16[1184,1024]{1,0:T(8,128)(2,1)}, u32[]{:S(2)}) copy-start(bf16[1184,1024]{1,0:T(8,128)(2,1)} %add_convert_fusion.2) | copy-start | bytes 7274500
  357.2 20.7 %copy-start.35 = (f32[1184]{0:T(1024)S(1)}, f32[1184]{0:T(1024)}, u32[]{:S(2)}) copy-start(f32[1184]{0:T(1024)} %rsqrt.22) | copy-start | bytes 14212
  357.2 20.7 %copy-start.36 = (f32[1184]{0:T(1024)S(1)}, f32[1184]{0:T(1024)}, u32[]{:S(2)}) copy-start(f32[1184]{0:T(1024)} %div.52) | copy-start | bytes 14212
  357.2 20.7 %copy-start.39 = (f32[1024]{0:T(1024)S(1)}, f32[1024]{0:T(1024)}, u32[]{:S(2)}) copy-start(f32[1024]{0:T(1024)} %copy-done.38) | copy-start | bytes 12292
  357.3 31.7 %collective-permute-start.30 = (bf16[256,1024]{1,0:T(8,128)(2,1)S(1)}, bf16[256,1024]{1,0:T(8,128)(2,1)S(1)}, u32[]{:S(2)}, u32[]{:S(2)}) collective-permute-start(bf16[256,1024]{1,0:T(8,128)(2,1)S(1)} %constant_dynamic-slice_fusion.4), channel_id=1, source_target_pairs={{0,8},{4,12},{8,0},{12,4},{16,24},{20,28},{24,16},{28,20},{1,9},{5... | collective-permute-start | bytes 1572872 | tf_op jit(solution)/shard_map/ppermute | solution.py:189
  376.2 15.6 %collective-permute-start.37 = (bf16[256,1024]{1,0:T(8,128)(2,1)S(1)}, bf16[256,1024]{1,0:T(8,128)(2,1)S(1)}, u32[]{:S(2)}, u32[]{:S(2)}) collective-permute-start(bf16[256,1024]{1,0:T(8,128)(2,1)S(1)} %constant_dynamic-slice_fusion.1), channel_id=1, source_target_pairs={{0,8},{4,12},{8,0},{12,4},{16,24},{20,28},{24,16},{28,20},{1,9},{5... | collective-permute-start | bytes 1572872 | tf_op jit(solution)/shard_map/ppermute | solution.py:189
  383.9 89.9 %copy-start.7 = (bf16[1184,1024]{1,0:T(8,128)(2,1)}, bf16[1184,1024]{1,0:T(8,128)(2,1)S(1)}, u32[]{:S(2)}) copy-start(bf16[1184,1024]{1,0:T(8,128)(2,1)S(1)} %get-tuple-element.97) | copy-start | bytes 7274500
  387.4 48.6 %collective-permute-start.21 = (bf16[4096,256]{1,0:T(8,128)(2,1)S(1)}, bf16[4096,256]{1,0:T(8,128)(2,1)S(1)}, u32[]{:S(2)}, u32[]{:S(2)}) collective-permute-start(bf16[4096,256]{1,0:T(8,128)(2,1)S(1)} %pad_maximum_fusion), channel_id=1, source_target_pairs={{0,2},{1,3},{2,0},{3,1},{4,6},{5,7},{6,4},{7,5},{8,10},{9,11},{10,... | collective-permute-start | bytes 6291464 | tf_op jit(solution)/shard_map/ppermute | solution.py:183
  389.2 19.5 %collective-permute-start.31 = (bf16[128,1024]{1,0:T(8,128)(2,1)S(1)}, bf16[128,1024]{1,0:T(8,128)(2,1)S(1)}, u32[]{:S(2)}, u32[]{:S(2)}) collective-permute-start(bf16[128,1024]{1,0:T(8,128)(2,1)S(1)} %constant_dynamic-slice_fusion.3), channel_id=1, source_target_pairs={{0,16},{4,20},{8,24},{12,28},{16,0},{20,4},{24,8},{28,12},{1,17},{... | collective-permute-start | bytes 786440 | tf_op jit(solution)/shard_map/ppermute | solution.py:189
  392.1 27.9 %collective-permute-start.38 = (bf16[128,1024]{1,0:T(8,128)(2,1)S(1)}, bf16[128,1024]{1,0:T(8,128)(2,1)S(1)}, u32[]{:S(2)}, u32[]{:S(2)}) collective-permute-start(bf16[128,1024]{1,0:T(8,128)(2,1)S(1)} %constant_dynamic-slice_fusion), channel_id=1, source_target_pairs={{0,16},{4,20},{8,24},{12,28},{16,0},{20,4},{24,8},{28,12},{1,17},{... | collective-permute-start | bytes 786440 | tf_op jit(solution)/shard_map/ppermute | solution.py:189
  393.2 53.8 %collective-permute-start.14 = (bf16[2,577,256]{2,0,1:T(2,128)(2,1)S(1)}, bf16[2,577,256]{2,0,1:T(2,128)(2,1)S(1)}, u32[]{:S(2)}, u32[]{:S(2)}) collective-permute-start(bf16[2,577,256]{2,0,1:T(2,128)(2,1)S(1)} %copy.55), channel_id=1, source_target_pairs={{0,2},{1,3},{2,0},{3,1},{4,6},{5,7},{6,4},{7,5},{8,10},{9,11},{10,... | collective-permute-start | bytes 1772552 | tf_op jit(solution)/shard_map/ppermute | solution.py:183
  408.8 38.4 %collective-permute-start.32 = (bf16[128,1024]{1,0:T(8,128)(2,1)S(1)}, bf16[128,1024]{1,0:T(8,128)(2,1)S(1)}, u32[]{:S(2)}, u32[]{:S(2)}) collective-permute-start(bf16[128,1024]{1,0:T(8,128)(2,1)S(1)} %add_convert_fusion.19), channel_id=1, source_target_pairs={{0,16},{4,20},{8,24},{12,28},{16,0},{20,4},{24,8},{28,12},{1,17},{... | collective-permute-start | bytes 786440 | tf_op jit(solution)/shard_map/ppermute | solution.py:189
  420.1 27.8 %collective-permute-start.39 = (bf16[128,1024]{1,0:T(8,128)(2,1)S(1)}, bf16[128,1024]{1,0:T(8,128)(2,1)S(1)}, u32[]{:S(2)}, u32[]{:S(2)}) collective-permute-start(bf16[128,1024]{1,0:T(8,128)(2,1)S(1)} %add_convert_fusion.18), channel_id=1, source_target_pairs={{0,16},{4,20},{8,24},{12,28},{16,0},{20,4},{24,8},{28,12},{1,17},{... | collective-permute-start | bytes 786440 | tf_op jit(solution)/shard_map/ppermute | solution.py:189
  436.6 36.3 %collective-permute-start.22 = (bf16[2048,256]{1,0:T(8,128)(2,1)S(1)}, bf16[2048,256]{1,0:T(8,128)(2,1)S(1)}, u32[]{:S(2)}, u32[]{:S(2)}) collective-permute-start(bf16[2048,256]{1,0:T(8,128)(2,1)S(1)} %constant_dynamic-slice_fusion.8), channel_id=1, source_target_pairs={{0,4},{4,0},{8,12},{12,8},{16,20},{20,16},{24,28},{28,24},{1,5},{5... | collective-permute-start | bytes 3145736 | tf_op jit(solution)/shard_map/ppermute | solution.py:189
  447.3 14.9 %collective-permute-start.33 = (bf16[256,1024]{1,0:T(8,128)(2,1)S(1)}, bf16[256,1024]{1,0:T(8,128)(2,1)S(1)}, u32[]{:S(2)}, u32[]{:S(2)}) collective-permute-start(bf16[256,1024]{1,0:T(8,128)(2,1)S(1)} %maximum_select_fusion.11), channel_id=1, source_target_pairs={{0,8},{4,12},{8,0},{12,4},{16,24},{20,28},{24,16},{28,20},{1,9},{5... | collective-permute-start | bytes 1572872 | tf_op jit(solution)/shard_map/ppermute | solution.py:189
  448.0 23.0 %collective-permute-start.40 = (bf16[256,1024]{1,0:T(8,128)(2,1)S(1)}, bf16[256,1024]{1,0:T(8,128)(2,1)S(1)}, u32[]{:S(2)}, u32[]{:S(2)}) collective-permute-start(bf16[256,1024]{1,0:T(8,128)(2,1)S(1)} %maximum_select_fusion.12), channel_id=1, source_target_pairs={{0,8},{4,12},{8,0},{12,4},{16,24},{20,28},{24,16},{28,20},{1,9},{5... | collective-permute-start | bytes 1572872 | tf_op jit(solution)/shard_map/ppermute | solution.py:189
  462.7 98.4 %collective-permute-start.34 = (bf16[512,1024]{1,0:T(8,128)(2,1)S(1)}, bf16[512,1024]{1,0:T(8,128)(2,1)}, u32[]{:S(2)}, u32[]{:S(2)}) collective-permute-start(bf16[512,1024]{1,0:T(8,128)(2,1)S(1)} %maximum_select_fusion.7), channel_id=1, source_target_pairs={{0,4},{4,0},{8,12},{12,8},{16,20},{20,16},{24,28},{28,24},{1,5},{5... | collective-permute-start | bytes 3145736 | tf_op jit(solution)/shard_map/ppermute | solution.py:189
  472.4 93.1 %collective-permute-start.41 = (bf16[512,1024]{1,0:T(8,128)(2,1)}, bf16[512,1024]{1,0:T(8,128)(2,1)}, u32[]{:S(2)}, u32[]{:S(2)}) collective-permute-start(bf16[512,1024]{1,0:T(8,128)(2,1)} %maximum_select_fusion.8), channel_id=1, source_target_pairs={{0,4},{4,0},{8,12},{12,8},{16,20},{20,16},{24,28},{28,24},{1,5},{5... | collective-permute-start | bytes 3145736 | tf_op jit(solution)/shard_map/ppermute | solution.py:189
  473.3 11.4 %collective-permute-start.23 = (bf16[1024,256]{1,0:T(8,128)(2,1)S(1)}, bf16[1024,256]{1,0:T(8,128)(2,1)S(1)}, u32[]{:S(2)}, u32[]{:S(2)}) collective-permute-start(bf16[1024,256]{1,0:T(8,128)(2,1)S(1)} %constant_dynamic-slice_fusion.7), channel_id=1, source_target_pairs={{0,8},{4,12},{8,0},{12,4},{16,24},{20,28},{24,16},{28,20},{1,9},{5... | collective-permute-start | bytes 1572872 | tf_op jit(solution)/shard_map/ppermute | solution.py:189
  473.8 15.2 %copy-start.42 = (f32[1024]{0:T(1024)S(1)}, f32[1024]{0:T(1024)}, u32[]{:S(2)}) copy-start(f32[1024]{0:T(1024)} %get-tuple-element.84) | copy-start | bytes 12292
  473.9 26.1 %copy-start.37 = (f32[1024]{0:T(1024)S(1)}, f32[1024]{0:T(1024)}, u32[]{:S(2)}) copy-start(f32[1024]{0:T(1024)} %get-tuple-element.124) | copy-start | bytes 12292
  474.4 83.0 %collective-permute-start.20 = (bf16[2,577,256]{2,0,1:T(2,128)(2,1)S(1)}, bf16[2,577,256]{2,0,1:T(2,128)(2,1)S(1)}, u32[]{:S(2)}, u32[]{:S(2)}) collective-permute-start(bf16[2,577,256]{2,0,1:T(2,128)(2,1)S(1)} %copy.66), channel_id=1, source_target_pairs={{0,2},{1,3},{2,0},{3,1},{4,6},{5,7},{6,4},{7,5},{8,10},{9,11},{10,... | collective-permute-start | bytes 1772552 | tf_op jit(solution)/shard_map/ppermute | solution.py:183
  484.8 15.0 %collective-permute-start.24 = (bf16[512,256]{1,0:T(8,128)(2,1)S(1)}, bf16[512,256]{1,0:T(8,128)(2,1)S(1)}, u32[]{:S(2)}, u32[]{:S(2)}) collective-permute-start(bf16[512,256]{1,0:T(8,128)(2,1)S(1)} %constant_dynamic-slice_fusion.6), channel_id=1, source_target_pairs={{0,16},{4,20},{8,24},{12,28},{16,0},{20,4},{24,8},{28,12},{1,17},{... | collective-permute-start | bytes 786440 | tf_op jit(solution)/shard_map/ppermute | solution.py:189
  499.9 10.2 %collective-permute-start.25 = (bf16[512,256]{1,0:T(8,128)(2,1)S(1)}, bf16[512,256]{1,0:T(8,128)(2,1)S(1)}, u32[]{:S(2)}, u32[]{:S(2)}) collective-permute-start(bf16[512,256]{1,0:T(8,128)(2,1)S(1)} %add_convert_fusion.20), channel_id=1, source_target_pairs={{0,16},{4,20},{8,24},{12,28},{16,0},{20,4},{24,8},{28,12},{1,17},{... | collective-permute-start | bytes 786440 | tf_op jit(solution)/shard_map/ppermute | solution.py:189
  510.4 43.3 %collective-permute-start.26 = (bf16[1024,256]{1,0:T(8,128)(2,1)S(1)}, bf16[1024,256]{1,0:T(8,128)(2,1)}, u32[]{:S(2)}, u32[]{:S(2)}) collective-permute-start(bf16[1024,256]{1,0:T(8,128)(2,1)S(1)} %maximum_select_fusion.10), channel_id=1, source_target_pairs={{0,8},{4,12},{8,0},{12,4},{16,24},{20,28},{24,16},{28,20},{1,9},{5... | collective-permute-start | bytes 1572872 | tf_op jit(solution)/shard_map/ppermute | solution.py:189
  555.1 24.2 %collective-permute-start.27 = (bf16[2048,256]{1,0:T(8,128)(2,1)S(1)}, bf16[2048,256]{1,0:T(8,128)(2,1)S(1)}, u32[]{:S(2)}, u32[]{:S(2)}) collective-permute-start(bf16[2048,256]{1,0:T(8,128)(2,1)S(1)} %maximum_select_fusion.6), channel_id=1, source_target_pairs={{0,4},{4,0},{8,12},{12,8},{16,20},{20,16},{24,28},{28,24},{1,5},{5... | collective-permute-start | bytes 3145736 | tf_op jit(solution)/shard_map/ppermute | solution.py:189
  (42 other events, 143.0 us)

commit v2 on v1

v2 whole, which is shorter than its diff:
```python
import functools

import jax
import jax.numpy as jnp
from jax import lax
from jax.experimental import pallas as pl
from jax.experimental.pallas import tpu as pltpu
from jax.sharding import PartitionSpec as P

HEAD = 64
LANES = 128
ROW_TILE = 16
EPS = 1e-05
GELU_K = 1.702
FAR = -1e30

F32 = jnp.float32
BF16 = jnp.bfloat16

NT = (((1,), (1,)), ((), ()))
NN = (((1,), (0,)), ((), ()))
TN = (((0,), (0,)), ((), ()))


def mm(left, right, dims):
    return lax.dot_general(left, right, dims, preferred_element_type=F32)


def head_views(half, seq, q, k):
    lane = lax.broadcasted_iota(jnp.int32, q.shape, 1)
    row = lax.broadcasted_iota(jnp.int32, q.shape, 0)
    mine = (lane >= HEAD) if half else (lane < HEAD)
    spare = lane == (0 if half else HEAD)
    zero = jnp.zeros_like(q)
    q_only = jnp.where(mine, q, zero)
    k_only = jnp.where(mine, k, zero)
    q_mask = jnp.where(spare, jnp.ones_like(q), q_only)
    far = jnp.full_like(k, FAR)
    k_mask = jnp.where(spare & (row >= seq), far, k_only)
    return mine, q_only, k_only, q_mask, k_mask


def attn_fwd_kernel(seq, q_ref, k_ref, v_ref, o_ref, lse_ref):
    q, k, v = q_ref[...], k_ref[...], v_ref[...]
    v_t = v.T
    pieces = []
    for half in range(2):
        _, _, _, q_mask, k_mask = head_views(half, seq, q, k)
        s_t = mm(k_mask, q_mask, NT)
        peak = jnp.max(s_t, axis=0, keepdims=True)
        expo = jnp.exp(s_t - peak)
        total = jnp.sum(expo, axis=0, keepdims=True)
        p_t = (expo * (1.0 / total)).astype(BF16)
        pieces.append(mm(v_t[half * HEAD : (half + 1) * HEAD], p_t, NN))
        lse_ref[0, 0, half : half + 1, :] = peak + jnp.log(total)
    o_ref[...] = jnp.concatenate(pieces, axis=0).T.astype(BF16)


def attn_bwd_kernel(seq, width, q_ref, k_ref, v_ref, do_ref, lse_ref, grads_ref):
    q, k, v, do = q_ref[...], k_ref[...], v_ref[...], do_ref[...]
    k_t = k.T
    dq_t, dk, dv = [], None, None
    for half in range(2):
        mine, q_only, _, q_mask, k_mask = head_views(half, seq, q, k)
        do_only = jnp.where(mine, do, jnp.zeros_like(do))
        s_t = mm(k_mask, q_mask, NT)
        p_t = jnp.exp(s_t - lse_ref[0, 0, half : half + 1, :])
        dp_t = mm(v, do_only, NT)
        inner = jnp.sum(p_t * dp_t, axis=0, keepdims=True)
        ds_t = (p_t * (dp_t - inner)).astype(BF16)
        dv_half = mm(p_t.astype(BF16), do_only, NN)
        dk_half = mm(ds_t, q_only, NN)
        dq_t.append(mm(k_t[half * HEAD : (half + 1) * HEAD], ds_t, NN))
        dv = dv_half if dv is None else dv + dv_half
        dk = dk_half if dk is None else dk + dk_half
    dq = jnp.concatenate(dq_t, axis=0).T.astype(BF16) * 0.125
    for n, grad in enumerate((dq, dk.astype(BF16), dv.astype(BF16))):
        at = pl.multiple_of(n * width + pl.program_id(1) * LANES, LANES)
        grads_ref[:, pl.ds(at, LANES)] = grad


def column_blocks(s, pairs, parts):
    def at(part):
        return pl.BlockSpec((s, LANES), lambda i, j: (i, part * pairs + j))

    return [at(part) for part in range(parts)]


def attention_forward(qkv, images, seq):
    rows, width = qkv.shape[0], qkv.shape[1] // 3
    s = rows // images
    pairs = width // LANES
    block = pl.BlockSpec((s, LANES), lambda i, j: (i, j))
    lse_block = pl.BlockSpec((1, 1, 2, s), lambda i, j: (i, j, 0, 0))
    n = images * pairs * 2
    return pl.pallas_call(
        functools.partial(attn_fwd_kernel, seq),
        grid=(images, pairs),
        in_specs=column_blocks(s, pairs, 3),
        out_specs=[block, lse_block],
        out_shape=[
            jax.ShapeDtypeStruct((rows, width), BF16),
            jax.ShapeDtypeStruct((images, pairs, 2, s), F32),
        ],
        cost_estimate=pl.CostEstimate(
            flops=n * 4 * s * s * 256, bytes_accessed=rows * width * 8, transcendentals=n * s * s
        ),
        name="attn_fwd",
    )(qkv, qkv, qkv)


def attention_backward(qkv, do, lse, images, seq):
    rows, width = do.shape
    s = rows // images
    pairs = width // LANES
    block = pl.BlockSpec((s, LANES), lambda i, j: (i, j))
    lse_block = pl.BlockSpec((1, 1, 2, s), lambda i, j: (i, j, 0, 0))
    n = images * pairs * 2
    return pl.pallas_call(
        functools.partial(attn_bwd_kernel, seq, width),
        grid=(images, pairs),
        in_specs=column_blocks(s, pairs, 3) + [block, lse_block],
        out_specs=pl.BlockSpec((s, 3 * width), lambda i, j: (i, 0)),
        out_shape=jax.ShapeDtypeStruct((rows, 3 * width), BF16),
        cost_estimate=pl.CostEstimate(
            flops=n * 10 * s * s * 256, bytes_accessed=rows * width * 14, transcendentals=n * s * s
        ),
        name="attn_bwd",
    )(qkv, qkv, qkv, do, lse)


def norm_stats(rows):
    mean = jnp.mean(rows, axis=-1, keepdims=True)
    center = rows - mean
    inv = lax.rsqrt(jnp.mean(center * center, axis=-1, keepdims=True) + EPS)
    return mean, inv


def norm_back(grad, unit, inv, gain):
    scaled = grad * gain
    first = jnp.mean(scaled, axis=-1, keepdims=True)
    second = jnp.mean(scaled * unit, axis=-1, keepdims=True)
    return (
        inv * (scaled - first - unit * second),
        jnp.sum(grad * unit, axis=0),
        jnp.sum(grad, axis=0),
    )


def pick(pieces, index):
    out = pieces[0]
    for n in range(1, len(pieces)):
        out = jnp.where(index == n, pieces[n], out)
    return out


def per_device(
    inputs,
    cotangent,
    slot_mask,
    w_qkv,
    bias_qv,
    w_out,
    bias_out,
    ln1_gain,
    ln1_bias,
    ln2_gain,
    ln2_bias,
    w_up,
    bias_up,
    w_down,
    bias_down,
):
    n_img, seq, width = inputs.shape
    n_tensor = lax.axis_size("tensor")
    n_dp = lax.axis_size("dp")
    chips = n_tensor // 2
    images = n_img // chips
    full = width * n_tensor
    padded = -(-seq // ROW_TILE) * ROW_TILE
    split = images % 2 == 0
    near = images // 2 if split else images
    local = near * padded
    t_idx = lax.axis_index("tensor")
    d_idx = lax.axis_index("dp")
    chip, core = t_idx // 2, t_idx % 2
    bits = n_dp.bit_length() - 1
    side = d_idx & 1
    steps = range(1, chips)

    def chip_shift(value, step):
        perm = [
            (2 * a + b, 2 * ((a + step) % chips) + b) for a in range(chips) for b in range(2)
        ]
        return lax.ppermute(value, "tensor", perm)

    def core_swap(value):
        return lax.ppermute(value, "tensor", [(a, a ^ 1) for a in range(n_tensor)])

    def dp_swap(value, bit):
        return lax.ppermute(value, "dp", [(a, a ^ (1 << bit)) for a in range(n_dp)])

    def my_images(value, step):
        return lax.dynamic_slice_in_dim(value, ((chip + step) % chips) * images, images, 0)

    def by_core(first, second):
        return jnp.where(core == 0, first, second)

    def fetch_rows(value):
        return [chip_shift(my_images(value, step), step) for step in steps]

    def core_rows(value, arrived):
        mine = [my_images(value, 0)] + arrived
        theirs = []
        for n, piece in enumerate(mine):
            if split:
                theirs.append(core_swap(by_core(piece[near:], piece[:near])))
                mine[n] = by_core(piece[:near], piece[near:])
            else:
                theirs.append(core_swap(piece))
        parts = []
        for a in range(chips):
            which = (chip - a) % chips
            own, other = pick(mine, which), pick(theirs, which)
            parts += [by_core(own, other), by_core(other, own)]
        out = jnp.concatenate(parts, axis=2)
        out = jnp.pad(out, ((0, 0), (0, padded - seq), (0, 0)))
        return out.reshape(local, full)

    def complete(rows):
        return jnp.concatenate([rows, core_swap(rows)], axis=0) if split else rows

    def exchange(part):
        part = part.astype(BF16)
        return part[:local].astype(F32) + core_swap(part[-local:]).astype(F32)

    def scatter_rows(value):
        value = value.reshape(near, padded, full)[:, :seq]
        cols = [value[:, :, n * width : (n + 1) * width] for n in range(n_tensor)]
        keep = [by_core(cols[2 * a], cols[2 * a + 1]) for a in range(chips)]
        if split:
            give = [by_core(cols[2 * a + 1], cols[2 * a]) for a in range(chips)]
            got = core_swap(jnp.concatenate(give, axis=2))
            got = [got[:, :, a * width : (a + 1) * width] for a in range(chips)]
            keep = [
                jnp.concatenate([by_core(m, g), by_core(g, m)], axis=0)
                for m, g in zip(keep, got)
            ]
        pieces = [pick(keep, chip)]
        for step in steps:
            pieces.append(chip_shift(pick(keep, (chip + step) % chips), step))
        return jnp.concatenate([pick(pieces, (chip - a) % chips) for a in range(chips)], axis=0)

    def fetch_weight(weight):
        half = weight.shape[0] // 2
        send = lax.dynamic_slice_in_dim(weight, side * half, half, 0)
        return [chip_shift(send, step) for step in steps]

    def whole_weight(weight, arrived):
        blocks = [weight]
        for got in arrived:
            other = dp_swap(got, 0)
            blocks.append(
                jnp.where(
                    side == 0,
                    jnp.concatenate([got, other], 0),
                    jnp.concatenate([other, got], 0),
                )
            )
        return blocks

    def halves(value, bit):
        half = value.shape[0] // 2
        at = (d_idx >> bit) & 1
        keep = lax.dynamic_slice_in_dim(value, at * half, half, 0)
        send = lax.dynamic_slice_in_dim(value, (1 - at) * half, half, 0)
        return keep, send

    def reduce_blocks(blocks, dp_first):
        first = 0
        if dp_first:
            cut = [halves(block, 0) for block in blocks]
            got = yield [dp_swap(jnp.concatenate([c[1] for c in cut], 0), 0)]
            size = cut[0][0].shape[0]
            blocks = [
                (c[0].astype(F32) + got[0][n * size : (n + 1) * size].astype(F32)).astype(BF16)
                for n, c in enumerate(cut)
            ]
            first = 1
        got = yield [chip_shift(blocks[step], chips - step) for step in steps]
        total = blocks[0].astype(F32)
        for piece in got:
            total = total + piece.astype(F32)
        total = total.astype(BF16)
        for bit in range(first, bits):
            keep, send = halves(total, bit)
            got = yield [dp_swap(send, bit)]
            total = (keep.astype(F32) + got[0].astype(F32)).astype(BF16)
        for bit in reversed(range(bits)):
            at = (d_idx >> bit) & 1
            got = yield [dp_swap(total, bit)]
            total = jnp.where(
                at == 0,
                jnp.concatenate([total, got[0]], 0),
                jnp.concatenate([got[0], total], 0),
            )
        return total.astype(F32)

    def begin(blocks, dp_first=False):
        flow = reduce_blocks(blocks, dp_first)
        return [flow, next(flow)]

    def advance(flow, got):
        flow[1] = flow[0].send(got)

    def finish(flow):
        try:
            while True:
                advance(flow, flow[1])
        except StopIteration as end:
            return end.value

    def tie(value, *flows):
        value, arrived = lax.optimization_barrier((value, [flow[1] for flow in flows]))
        for flow, got in zip(flows, arrived):
            advance(flow, got)
        return value

    def after(value, *earlier):
        return lax.optimization_barrier((value, earlier))[0]

    gain_one, shift_one = ln1_gain.astype(F32), ln1_bias.astype(F32)
    gain_two, shift_two = ln2_gain.astype(F32), ln2_bias.astype(F32)

    x_got = fetch_rows(inputs)
    cat_qkv = jnp.concatenate([w_qkv[n] for n in range(3)], axis=1)
    q_got = fetch_weight(cat_qkv)
    small = jnp.concatenate([bias_up, bias_qv.reshape(-1)])
    small_got = [chip_shift(small, step) for step in steps]
    o_got = fetch_weight(w_out)
    u_got = fetch_weight(w_up)
    dy_got = fetch_rows(cotangent)
    d_got = fetch_weight(w_down)

    n_up = bias_up.shape[0]
    scale = jnp.concatenate([jnp.full((width,), 0.125, F32), jnp.ones((2 * width,), F32)])

    def qkv_bias(vector):
        vector = vector[n_up:].astype(F32)
        return jnp.concatenate([vector[:width], jnp.zeros((width,), F32), vector[width:]])

    def project(block, vector):
        return ((mm(normed_one, block, NN) + qkv_bias(vector)) * scale).astype(BF16)

    x32 = core_rows(inputs, x_got).astype(F32)
    mean_one, inv_one = norm_stats(x32)
    unit_one = (x32 - mean_one) * inv_one
    normed_one = complete((unit_one * gain_one + shift_one).astype(BF16))
    qkv = [project(cat_qkv, small)]
    qkv[0], q_got = lax.optimization_barrier((qkv[0], q_got))
    wq = whole_weight(cat_qkv, q_got)
    o, lse = attention_forward(qkv[0], images, seq)
    o, o_got, small_got = lax.optimization_barrier((o, o_got, small_got))
    heads, norms = [o], [lse]
    wo = whole_weight(w_out, o_got)
    smalls = [small] + small_got
    for r in steps:
        qkv.append(project(wq[r], smalls[r]))
        o, lse = attention_forward(qkv[r], images, seq)
        heads.append(o)
        norms.append(lse)
    heads[-1], u_got = lax.optimization_barrier((heads[-1], u_got))
    wu = whole_weight(w_up, u_got)
    attn_part = mm(heads[0], wo[0], NN)
    for r in steps:
        attn_part = attn_part + mm(heads[r], wo[r], NN)
    resid = x32 + (exchange(attn_part) + bias_out.astype(F32))
    mean_two, inv_two = norm_stats(resid)
    unit_two = (resid - mean_two) * inv_two
    normed_two = complete((unit_two * gain_two + shift_two).astype(BF16))
    normed_two, dy_got = lax.optimization_barrier((normed_two, dy_got))

    acts, slopes = [], []
    for r in range(chips):
        hidden = mm(normed_two, wu[r], NN) + smalls[r][:n_up].astype(F32)
        sigma = jax.nn.sigmoid(GELU_K * hidden)
        acts.append((hidden * sigma).astype(BF16))
        slopes.append(sigma + GELU_K * hidden * sigma * (1.0 - sigma))
    acts[-1], d_got = lax.optimization_barrier((acts[-1], d_got))
    wd = whole_weight(w_down, d_got)

    live = my_images(slot_mask, 0).astype(BF16)
    if split:
        live = by_core(live[:near], live[near:])
    dy_local = core_rows(cotangent, dy_got).reshape(near, padded, full)
    dy_local = (dy_local * live[:, None, None]).reshape(local, full)
    dy = complete(dy_local)
    down_blocks = [None] + [mm(acts[r], dy, TN).astype(BF16) for r in steps]
    down_blocks[0] = mm(after(acts[0], *down_blocks[1:]), dy, TN).astype(BF16)
    flow_down = begin(down_blocks)
    d_hidden = [(mm(dy, wd[r], NT) * slopes[r]).astype(BF16) for r in range(chips)]
    up_blocks = [None] + [mm(normed_two, d_hidden[r], TN).astype(BF16) for r in steps]
    up_blocks[0] = mm(normed_two, after(d_hidden[0], *up_blocks[1:]), TN).astype(BF16)
    flow_up = begin(up_blocks)
    part_two = mm(d_hidden[0], wu[0], NT)
    for r in steps:
        part_two = part_two + mm(d_hidden[r], wu[r], NT)
    back_two, g_gain_two, g_shift_two = norm_back(exchange(part_two), unit_two, inv_two, gain_two)
    d_resid = dy_local.astype(F32) + back_two
    da_local = d_resid.astype(BF16)
    da = tie(complete(da_local), flow_down)

    grads = [None] * chips
    last = da
    for r in list(steps) + [0]:
        do = mm(last, wo[r], NT).astype(BF16)
        grads[r] = attention_backward(qkv[r], do, norms[r], images, seq)
        if r:
            grads[r] = tie(grads[r], flow_down)
            last = after(da, grads[r])
    grads[0] = tie(grads[0], flow_down, flow_up)
    out_blocks = [mm(heads[r], da, TN).astype(BF16) for r in range(chips)]
    flow_out = begin(out_blocks)
    qkv_blocks = [None] + [mm(normed_one, grads[r], TN).astype(BF16) for r in steps]
    qkv_blocks[0] = mm(normed_one, grads[0], TN).astype(BF16)
    middle = full // 2
    flow_low = begin([block[:middle] for block in qkv_blocks])
    flow_high = begin([block[middle:] for block in qkv_blocks], True)
    part_one = mm(grads[0], wq[0], NT)
    for r in steps:
        part_one = part_one + mm(grads[r], wq[r], NT)
    back_one, g_gain_one, g_shift_one = norm_back(exchange(part_one), unit_one, inv_one, gain_one)
    input_grad = scatter_rows((d_resid + back_one).astype(BF16))

    mlp_part = mm(after(acts[0], grads[0]), wd[0], NN)
    for r in steps:
        mlp_part = mlp_part + mm(acts[r], wd[r], NN)
    out = (resid + (exchange(mlp_part) + bias_down.astype(F32))).astype(BF16)
    layer_out = scatter_rows(out)

    shared = jnp.concatenate(
        [
            jnp.sum(da_local, axis=0, dtype=F32),
            g_gain_one,
            g_shift_one,
            g_gain_two,
            g_shift_two,
            jnp.sum(dy_local, axis=0, dtype=F32),
        ]
    )
    if split:
        shared = shared + core_swap(shared)
    own = []
    for r in range(chips):
        rows_sum = jnp.sum(grads[r], axis=0, dtype=F32)
        own.append(
            jnp.concatenate(
                [
                    shared,
                    jnp.sum(d_hidden[r], axis=0, dtype=F32),
                    rows_sum[:width],
                    rows_sum[2 * width :],
                ]
            )
        )
    vector = own[0]
    for step in steps:
        vector = vector + chip_shift(own[step], chips - step)
    for bit in range(bits):
        vector = vector + dp_swap(vector, bit)
    vecs = [vector[n * full : (n + 1) * full] for n in range(6)]
    mine = vector[6 * full :]

    grad_down = finish(flow_down)
    grad_up = finish(flow_up)
    grad_out = finish(flow_out)
    grad_cat = jnp.concatenate([finish(flow_low), finish(flow_high)], axis=0)
    grad_qkv = jnp.stack([grad_cat[:, n * width : (n + 1) * width] for n in range(3)])
    return (
        layer_out,
        input_grad,
        grad_qkv,
        mine[n_up:].reshape(2, width),
        grad_out,
        vecs[0],
        vecs[1],
        vecs[2],
        vecs[3],
        vecs[4],
        grad_up,
        mine[:n_up],
        grad_down,
        vecs[5],
    )


def solution(mesh):
    return jax.shard_map(
        per_device,
        mesh=mesh,
        in_specs=(
            P("dp", None, "tensor"),
            P("dp", None, "tensor"),
            P("dp"),
            P(None, None, "tensor"),
            P(None, "tensor"),
            P("tensor", None),
            P(),
            P(),
            P(),
            P(),
            P(),
            P(None, "tensor"),
            P("tensor"),
            P("tensor", None),
            P(),
        ),
        out_specs=(
            P("dp", None, "tensor"),
            P("dp", None, "tensor"),
            P(None, None, "tensor"),
            P(None, "tensor"),
            P("tensor", None),
            P(),
            P(),
            P(),
            P(),
            P(),
            P(None, "tensor"),
            P("tensor"),
            P("tensor", None),
            P(),
        ),
        check_vma=False,
    )
```

time: 587 us -> 633 us (1.078)
  waiting for transfers between devices: 248 us -> 340 us
  blocking collectives: 41.4 us -> 0 us
  starting transfers between devices: 42.7 us -> 55.8 us
  other arithmetic: 63.7 us -> 51.5 us
  matrix products: 111 us -> 101 us
    ppermute x22 -> x37, waiting for transfers between devices: 103 us -> 217 us  [dp_swap(): return lax.ppermute(value, 'dp', [(a, a ^ 1 << bit) for a in range(n_dp)])]
    psum x1 -> x0, blocking collectives: 41.4 us -> none  [per_device(): vector = lax.psum(jnp.concatenate([shared] + placed), ('dp', 'tensor'))]
    ppermute x12 -> x15, waiting for transfers between devices: 145 us -> 120 us  [chip_shift(): return lax.ppermute(value, 'tensor', perm)]
    ppermute x22 -> x37, starting transfers between devices: 25.2 us -> 37.8 us  [dp_swap(): return lax.ppermute(value, 'dp', [(a, a ^ 1 << bit) for a in range(n_dp)])]
    dot_general x36 -> x24, matrix products: 111 us -> 101 us  [mm(): return lax.dot_general(left, right, dims, preferred_element_type=F32)]
    slice x4 -> x14, local copies, waits for them, and re-layouts: 2.47 us -> 9.77 us  [the longest x3 6.42 us: core_rows(): mine[n] = by_core(piece[:near], piece[near:])]
    unnamed x137 -> x158, local copies, waits for them, and re-layouts: 13.2 us -> 8.46 us
    ppermute x12 -> x15, starting transfers between devices: 16.9 us -> 16.4 us  [chip_shift(): return lax.ppermute(value, 'tensor', perm)]
  transfers between devices with their start and end apart: 42 -> 67, of which waited for: 18 -> 31; matrix products, arithmetic and copies ran while one was open for 32% -> 24% of each run, Pallas kernels for 7% -> 7%
where the time goes in v2:
time: 633 us; the launch traced here: 626 us
  waiting for transfers between devices  340 us (54%)
  matrix products  101 us (16%)
  starting transfers between devices  55.8 us (9%)
  other arithmetic  51.5 us (8%)
  Pallas kernels  43.1 us (7%)
  local copies, waits for them, and re-layouts  30.6 us (5%)
    ppermute x37, waiting for transfers between devices, dp_swap(): return lax.ppermute(value, 'dp', [(a, a ^ 1 << bit) for a in range(n_dp)])  217 us
    ppermute x15, waiting for transfers between devices, chip_shift(): return lax.ppermute(value, 'tensor', perm)  120 us
    dot_general x24, matrix products, mm(): return lax.dot_general(left, right, dims, preferred_element_type=F32)  101 us
    ppermute x37, starting transfers between devices, dp_swap(): return lax.ppermute(value, 'dp', [(a, a ^ 1 << bit) for a in range(n_dp)])  37.8 us
    pallas_call x2, Pallas kernels, attention_backward(): pl.pallas_call(functools.partial(attn_bwd_kernel, seq, width), grid=(imag...  26.1 us
    pallas_call x2, Pallas kernels, attention_forward(): pl.pallas_call(functools.partial(attn_fwd_kernel, seq), grid=(images, pai...  17 us
    ppermute x15, starting transfers between devices, chip_shift(): return lax.ppermute(value, 'tensor', perm)  16.4 us
  transfers between devices with their start and end apart: 67, of which 31 were waited for; matrix products, arithmetic and copies ran while one was open for 24% of the time, Pallas kernels for 7%

profile of v2, /device:TPU:0, one launch (start us, length us, event | category | flops | bytes accessed | tf_op | source)
XLA Modules:
  0.0 626.1 jit_solution(1157416232063034091)
XLA Ops:
  2.7 3.1 collective-permute-start
  5.8 2.9 constant_dynamic-slice_fusion.1
  9.6 9.6 %collective-permute-done = bf16[2,577,256]{2,0,1:T(2,128)(2,1)} collective-permute-done((bf16[2,577,256]{2,0,1:T(2,128)(2,1)S(1)}, bf16[2,577,256]{2,0,1:T(2,128)(2,1)}, u32[]{:S(2)}, u32[]{:S(2)}) %collective-permute-start) | collective-permute-done | bytes 590880 | tf_op jit(solution)/shard_map/ppermute | solution.py:195
  19.2 2.3 fusion.75
  37.9 5.4 fusion.2.q_ref.k_ref.v_ref
  43.3 8.4 %collective-permute-done.4 = bf16[512,768]{1,0:T(8,128)(2,1)} collective-permute-done((bf16[512,768]{1,0:T(8,128)(2,1)}, bf16[512,768]{1,0:T(8,128)(2,1)}, u32[]{:S(2)}, u32[]{:S(2)}) %collective-permute-start.4) | collective-permute-done | bytes 786464 | tf_op jit(solution)/shard_map/ppermute | solution.py:195
  53.4 8.6 %attn_fwd.2 = (bf16[1184,256]{1,0:T(8,128)(2,1)}, f32[2,2,2,592]{3,2,1,0:T(2,128)}) custom-call(bf16[1184,768]{1,0:T(8,128)(2,1)} %fusion.2.q_ref.k_ref.v_ref, bf16[1184,768]{1,0:T(8,128)(2,1)} %fusion.2.q_ref.k_ref.v_ref, bf16[1184,768]{1,0:T(8,128)(2,1)} %fusion.2.q_ref.k_ref.v_ref), custom_call_target="tpu_custom_call" | custom-call | flops 2871001088 | bytes 2424832 | tf_op jit(solution)/shard_map/attn_fwd/pallas_call | solution.py:96
  62.5 10.0 %collective-permute-done.7 = bf16[512,768]{1,0:T(8,128)(2,1)} collective-permute-done((bf16[512,768]{1,0:T(8,128)(2,1)}, bf16[512,768]{1,0:T(8,128)(2,1)}, u32[]{:S(2)}, u32[]{:S(2)}) %collective-permute-start.7) | collective-permute-done | bytes 786464 | tf_op jit(solution)/shard_map/ppermute | solution.py:201
  72.4 6.1 fusion.3.q_ref.k_ref.v_ref
  78.6 8.4 %attn_fwd.3 = (bf16[1184,256]{1,0:T(8,128)(2,1)}, f32[2,2,2,592]{3,2,1,0:T(2,128)}) custom-call(bf16[1184,768]{1,0:T(8,128)(2,1)} %fusion.3.q_ref.k_ref.v_ref, bf16[1184,768]{1,0:T(8,128)(2,1)} %fusion.3.q_ref.k_ref.v_ref, bf16[1184,768]{1,0:T(8,128)(2,1)} %fusion.3.q_ref.k_ref.v_ref), custom_call_target="tpu_custom_call" | custom-call | flops 2871001088 | bytes 2424832 | tf_op jit(solution)/shard_map/attn_fwd/pallas_call | solution.py:96
  87.0 2.3 fusion.53
  90.8 2.4 collective-permute-done.10
  100.6 12.3 %collective-permute-done.12 = bf16[2,577,256]{2,0,1:T(2,128)(2,1)S(1)} collective-permute-done((bf16[2,577,256]{2,0,1:T(2,128)(2,1)S(1)}, bf16[2,577,256]{2,0,1:T(2,128)(2,1)S(1)}, u32[]{:S(2)}, u32[]{:S(2)}) %collective-permute-start.12) | collective-permute-done | bytes 590880 | tf_op jit(solution)/shard_map/ppermute | solution.py:195
  118.2 22.6 %collective-permute-done.16 = bf16[512,1024]{1,0:T(8,128)(2,1)S(1)} collective-permute-done((bf16[512,1024]{1,0:T(8,128)(2,1)}, bf16[512,1024]{1,0:T(8,128)(2,1)S(1)}, u32[]{:S(2)}, u32[]{:S(2)}) %collective-permute-start.16) | collective-permute-done | bytes 1048608 | tf_op jit(solution)/shard_map/ppermute | solution.py:201
  140.8 6.4 %multiply_convert_fusion.1 = (bf16[1184,1024]{1,0:T(8,128)(2,1)}, f32[1184,1024]{1,0:T(8,128)S(1)}) fusion(f32[1024]{0:T(1024)S(1)} %slice_convert_fusion, bf16[1184,1024]{1,0:T(8,128)(2,1)S(1)} %pad_maximum_fusion.2, bf16[512,1024]{1,0:T(8,128)(2,1)S(1)} %collective-permute-done.16, bf16[512,1024]{1,0:T(8,128)(2,1)} %collective-permute-done.8, pred[]{:T(512)S(6)} %eq.39), kind=kOutput, calls=%fused_computation.6 | convolution fusion | flops 2500952064 | bytes 11800577 | tf_op jit(solution)/shard_map/dot_general | solution.py:26
  148.9 15.5 %multiply_convert_fusion.3 = (bf16[1184,1024]{1,0:T(8,128)(2,1)}, f32[1184,1024]{1,0:T(8,128)S(1)}) fusion(f32[1024]{0:T(1024)S(1)} %convert_element_type.376, bf16[1184,1024]{1,0:T(8,128)(2,1)S(1)} %pad_maximum_fusion.2, bf16[1024,1024]{1,0:T(8,128)(2,1)S(1)} %copy-done), kind=kOutput, calls=%fused_computation.9 | convolution fusion | flops 2491514880 | bytes 11800576 | tf_op jit(solution)/shard_map/dot_general | solution.py:26
  164.4 5.6 convert_reduce_fusion.1
  170.0 2.7 fusion.82
  172.8 4.9 convert_reduce_fusion
  177.7 5.1 add_convert_fusion.2
  185.5 5.5 convolution_convert_fusion.3
  192.5 2.9 multiply_reduce_fusion
  195.5 3.6 convert_reduce_fusion.6
  199.3 4.2 convolution_convert_fusion.2
  204.0 4.2 fusion.84
  208.5 31.0 %collective-permute-done.21 = bf16[1024,1024]{1,0:T(8,128)(2,1)S(1)} collective-permute-done((bf16[1024,1024]{1,0:T(8,128)(2,1)S(1)}, bf16[1024,1024]{1,0:T(8,128)(2,1)S(1)}, u32[]{:S(2)}, u32[]{:S(2)}) %collective-permute-start.21) | collective-permute-done | bytes 2097184 | tf_op jit(solution)/shard_map/ppermute | solution.py:195
  242.0 3.1 fusion.69
  245.7 49.5 %collective-permute-done.50 = bf16[256,1024]{1,0:T(8,128)(2,1)S(1)} collective-permute-done((bf16[256,1024]{1,0:T(8,128)(2,1)S(1)}, bf16[256,1024]{1,0:T(8,128)(2,1)S(1)}, u32[]{:S(2)}, u32[]{:S(2)}) %collective-permute-start.50) | collective-permute-done | bytes 524320 | tf_op jit(solution)/shard_map/ppermute | solution.py:195
  300.3 5.0 collective-permute-done.51
  307.1 2.9 convolution_convert_fusion.1.do_ref
  310.6 3.4 collective-permute-start.53
  313.9 13.2 %attn_bwd.2 = bf16[1184,768]{1,0:T(8,128)(2,1)} custom-call(bf16[1184,768]{1,0:T(8,128)(2,1)} %fusion.3.q_ref.k_ref.v_ref, bf16[1184,768]{1,0:T(8,128)(2,1)} %fusion.3.q_ref.k_ref.v_ref, bf16[1184,768]{1,0:T(8,128)(2,1)} %fusion.3.q_ref.k_ref.v_ref, bf16[1184,256]{1,0:T(8,128)(2,1)} %convolution_convert_fusion.1.do_ref, ...), custom_call_target="tpu_custom_call" | custom-call | flops 7177502720 | bytes 4243456 | tf_op jit(solution)/shard_map/attn_bwd/pallas_call | solution.py:119
  327.2 3.5 convolution_convert_fusion.do_ref
  334.6 4.0 convolution_convert_fusion.4
  341.3 13.0 %attn_bwd.3 = bf16[1184,768]{1,0:T(8,128)(2,1)} custom-call(bf16[1184,768]{1,0:T(8,128)(2,1)} %fusion.2.q_ref.k_ref.v_ref, bf16[1184,768]{1,0:T(8,128)(2,1)} %fusion.2.q_ref.k_ref.v_ref, bf16[1184,768]{1,0:T(8,128)(2,1)} %fusion.2.q_ref.k_ref.v_ref, bf16[1184,256]{1,0:T(8,128)(2,1)} %convolution_convert_fusion.do_ref, f32[2,2,2,592]{3,2,1,0:T(2,128)} %get-tuple-element.59.lse_ref), custom_call_target="tpu_custom_call" | custom-call | flops 7177502720 | bytes 4243456 | tf_op jit(solution)/shard_map/attn_bwd/pallas_call | solution.py:119
  354.3 4.6 fusion.52
  361.2 3.9 collective-permute-done.55
  366.0 5.5 collective-permute-done.56
  372.7 2.7 fusion.83
  375.5 3.2 add_convert_fusion.1
  379.0 2.1 add_convert_fusion
  381.7 4.0 convolution_convert_fusion.5
  387.3 2.5 add_convert_fusion.4
  395.1 41.2 %collective-permute-done.32 = bf16[256,768]{1,0:T(8,128)(2,1)S(1)} collective-permute-done((bf16[256,768]{1,0:T(8,128)(2,1)S(1)}, bf16[256,768]{1,0:T(8,128)(2,1)S(1)}, u32[]{:S(2)}, u32[]{:S(2)}) %collective-permute-start.32) | collective-permute-done | bytes 393248 | tf_op jit(solution)/shard_map/ppermute | solution.py:201
  436.3 2.4 collective-permute-start.63
  438.9 11.4 %collective-permute-done.63 = bf16[128,1024]{1,0:T(8,128)(2,1)S(1)} collective-permute-done((bf16[128,1024]{1,0:T(8,128)(2,1)S(1)}, bf16[128,1024]{1,0:T(8,128)(2,1)S(1)}, u32[]{:S(2)}, u32[]{:S(2)}) %collective-permute-start.63) | collective-permute-done | bytes 262176 | tf_op jit(solution)/shard_map/ppermute | solution.py:201
  450.5 6.3 %collective-permute-done.33 = bf16[128,768]{1,0:T(8,128)(2,1)S(1)} collective-permute-done((bf16[128,768]{1,0:T(8,128)(2,1)S(1)}, bf16[128,768]{1,0:T(8,128)(2,1)S(1)}, u32[]{:S(2)}, u32[]{:S(2)}) %collective-permute-start.33) | collective-permute-done | bytes 196640 | tf_op jit(solution)/shard_map/ppermute | solution.py:201
  458.6 11.7 %collective-permute-done.64 = bf16[128,1024]{1,0:T(8,128)(2,1)S(1)} collective-permute-done((bf16[128,1024]{1,0:T(8,128)(2,1)S(1)}, bf16[128,1024]{1,0:T(8,128)(2,1)S(1)}, u32[]{:S(2)}, u32[]{:S(2)}) %collective-permute-start.64) | collective-permute-done | bytes 262176 | tf_op jit(solution)/shard_map/ppermute | solution.py:201
  470.4 7.2 %collective-permute-done.34 = bf16[64,768]{1,0:T(8,128)(2,1)S(1)} collective-permute-done((bf16[64,768]{1,0:T(8,128)(2,1)S(1)}, bf16[64,768]{1,0:T(8,128)(2,1)S(1)}, u32[]{:S(2)}, u32[]{:S(2)}) %collective-permute-start.34) | collective-permute-done | bytes 98336 | tf_op jit(solution)/shard_map/ppermute | solution.py:201
  479.7 11.1 %collective-permute-done.35 = bf16[64,768]{1,0:T(8,128)(2,1)S(1)} collective-permute-done((bf16[64,768]{1,0:T(8,128)(2,1)S(1)}, bf16[64,768]{1,0:T(8,128)(2,1)S(1)}, u32[]{:S(2)}, u32[]{:S(2)}) %collective-permute-start.35) | collective-permute-done | bytes 98336 | tf_op jit(solution)/shard_map/ppermute | solution.py:201
  491.1 2.3 collective-permute-start.36
  495.3 5.3 collective-permute-done.39
  508.6 3.3 collective-permute-done.46
  514.1 10.1 %collective-permute-done.47 = f32[7680]{0:T(1024)S(1)} collective-permute-done((f32[7680]{0:T(1024)S(1)}, f32[7680]{0:T(1024)S(1)}, u32[]{:S(2)}, u32[]{:S(2)}) %collective-permute-start.47) | collective-permute-done | bytes 30752 | tf_op jit(solution)/shard_map/ppermute | solution.py:201
  528.2 2.9 collective-permute-start.49
  533.8 4.8 collective-permute-done.41
  539.9 5.5 collective-permute-done.42
  548.6 8.1 %collective-permute-done.37 = bf16[256,768]{1,0:T(8,128)(2,1)S(1)} collective-permute-done((bf16[256,768]{1,0:T(8,128)(2,1)}, bf16[256,768]{1,0:T(8,128)(2,1)S(1)}, u32[]{:S(2)}, u32[]{:S(2)}) %collective-permute-start.37) | collective-permute-done | bytes 393248 | tf_op jit(solution)/shard_map/ppermute | solution.py:201
  560.2 9.9 %collective-permute-done.59 = bf16[128,1024]{1,0:T(8,128)(2,1)S(1)} collective-permute-done((bf16[128,1024]{1,0:T(8,128)(2,1)S(1)}, bf16[128,1024]{1,0:T(8,128)(2,1)S(1)}, u32[]{:S(2)}, u32[]{:S(2)}) %collective-permute-start.59) | collective-permute-done | bytes 262176 | tf_op jit(solution)/shard_map/ppermute | solution.py:201
  572.4 11.6 %collective-permute-done.60 = bf16[128,1024]{1,0:T(8,128)(2,1)S(1)} collective-permute-done((bf16[128,1024]{1,0:T(8,128)(2,1)S(1)}, bf16[128,1024]{1,0:T(8,128)(2,1)S(1)}, u32[]{:S(2)}, u32[]{:S(2)}) %collective-permute-start.60) | collective-permute-done | bytes 262176 | tf_op jit(solution)/shard_map/ppermute | solution.py:201
  584.2 4.4 fusion.34
  589.1 8.9 %collective-permute-done.61 = bf16[256,1024]{1,0:T(8,128)(2,1)S(1)} collective-permute-done((bf16[256,1024]{1,0:T(8,128)(2,1)S(1)}, bf16[256,1024]{1,0:T(8,128)(2,1)S(1)}, u32[]{:S(2)}, u32[]{:S(2)}) %collective-permute-start.61) | collective-permute-done | bytes 524320 | tf_op jit(solution)/shard_map/ppermute | solution.py:201
  605.1 17.7 %collective-permute-done.62 = bf16[512,1024]{1,0:T(8,128)(2,1)S(1)} collective-permute-done((bf16[512,1024]{1,0:T(8,128)(2,1)S(1)}, bf16[512,1024]{1,0:T(8,128)(2,1)S(1)}, u32[]{:S(2)}, u32[]{:S(2)}) %collective-permute-start.62) | collective-permute-done | bytes 1048608 | tf_op jit(solution)/shard_map/ppermute | solution.py:201
  622.8 2.9 fusion.33
  (402 shorter events, 111.1 us)
Async XLA Ops:
  2.7 16.5 %collective-permute-start = (bf16[2,577,256]{2,0,1:T(2,128)(2,1)S(1)}, bf16[2,577,256]{2,0,1:T(2,128)(2,1)}, u32[]{:S(2)}, u32[]{:S(2)}) collective-permute-start(bf16[2,577,256]{2,0,1:T(2,128)(2,1)S(1)} %constant_dynamic-slice_fusion.25), channel_id=1, source_target_pairs={{0,2},{1,3},{2,0},{3,1},{4,6},{5,7},{6,4},{7,5},{8,10},{9,11},{10,... | collective-permute-start | bytes 1772552 | tf_op jit(solution)/shard_map/ppermute | solution.py:195
  9.6 12.8 %collective-permute-start.2 = (bf16[1,577,256]{2,1,0:T(8,128)(2,1)}, bf16[1,577,256]{2,1,0:T(8,128)(2,1)}, u32[]{:S(2)}, u32[]{:S(2)}) collective-permute-start(bf16[1,577,256]{2,1,0:T(8,128)(2,1)} %broadcast_select_fusion.44), channel_id=1, source_target_pairs={{0,1},{1,0},{2,3},{3,2},{4,5},{5,4},{6,7},{7,6},{8,9},{9,8},{10,11... | collective-permute-start | bytes 886280 | tf_op jit(solution)/shard_map/ppermute | solution.py:198
  29.3 8.6 %collective-permute-start.3 = (bf16[592,1024]{1,0:T(8,128)(2,1)}, bf16[592,1024]{1,0:T(8,128)(2,1)}, u32[]{:S(2)}, u32[]{:S(2)}) collective-permute-start(bf16[592,1024]{1,0:T(8,128)(2,1)} %fusion.13), channel_id=1, source_target_pairs={{0,1},{1,0},{2,3},{3,2},{4,5},{5,4},{6,7},{7,6},{8,9},{9,8},{10,11... | collective-permute-start | bytes 3637256 | tf_op jit(solution)/shard_map/ppermute | solution.py:198
  31.0 20.7 %collective-permute-start.4 = (bf16[512,768]{1,0:T(8,128)(2,1)}, bf16[512,768]{1,0:T(8,128)(2,1)}, u32[]{:S(2)}, u32[]{:S(2)}) collective-permute-start(bf16[512,768]{1,0:T(8,128)(2,1)} %constant_dynamic-slice_fusion.23), channel_id=1, source_target_pairs={{0,2},{1,3},{2,0},{3,1},{4,6},{5,7},{6,4},{7,5},{8,10},{9,11},{10,... | collective-permute-start | bytes 2359304 | tf_op jit(solution)/shard_map/ppermute | solution.py:195
  34.4 27.7 %collective-permute-start.5 = (bf16[128,1024]{1,0:T(8,128)(2,1)}, bf16[128,1024]{1,0:T(8,128)(2,1)}, u32[]{:S(2)}, u32[]{:S(2)}) collective-permute-start(bf16[128,1024]{1,0:T(8,128)(2,1)} %constant_dynamic-slice_fusion.22), channel_id=1, source_target_pairs={{0,2},{1,3},{2,0},{3,1},{4,6},{5,7},{6,4},{7,5},{8,10},{9,11},{10,... | collective-permute-start | bytes 786440 | tf_op jit(solution)/shard_map/ppermute | solution.py:195
  34.7 27.4 %collective-permute-start.6 = (bf16[1536]{0:T(1024)(128)(2,1)S(1)}, bf16[1536]{0:T(1024)(128)(2,1)S(1)}, u32[]{:S(2)}, u32[]{:S(2)}) collective-permute-start(bf16[1536]{0:T(1024)(128)(2,1)S(1)} %pad_maximum_fusion.19), channel_id=1, source_target_pairs={{0,2},{1,3},{2,0},{3,1},{4,6},{5,7},{6,4},{7,5},{8,10},{9,11},{10,... | collective-permute-start | bytes 9224 | tf_op jit(solution)/shard_map/ppermute | solution.py:195
  37.5 49.4 %collective-permute-start.8 = (bf16[512,1024]{1,0:T(8,128)(2,1)}, bf16[512,1024]{1,0:T(8,128)(2,1)}, u32[]{:S(2)}, u32[]{:S(2)}) collective-permute-start(bf16[512,1024]{1,0:T(8,128)(2,1)} %constant_dynamic-slice_fusion.21), channel_id=1, source_target_pairs={{0,2},{1,3},{2,0},{3,1},{4,6},{5,7},{6,4},{7,5},{8,10},{9,11},{10,... | collective-permute-start | bytes 3145736 | tf_op jit(solution)/shard_map/ppermute | solution.py:195
  51.7 20.7 %collective-permute-start.7 = (bf16[512,768]{1,0:T(8,128)(2,1)}, bf16[512,768]{1,0:T(8,128)(2,1)}, u32[]{:S(2)}, u32[]{:S(2)}) collective-permute-start(bf16[512,768]{1,0:T(8,128)(2,1)} %collective-permute-done.4), channel_id=1, source_target_pairs={{0,4},{4,0},{8,12},{12,8},{16,20},{20,16},{24,28},{28,24},{1,5},{5... | collective-permute-start | bytes 2359304 | tf_op jit(solution)/shard_map/ppermute | solution.py:201
  62.1 24.9 %collective-permute-start.9 = (bf16[128,1024]{1,0:T(8,128)(2,1)}, bf16[128,1024]{1,0:T(8,128)(2,1)}, u32[]{:S(2)}, u32[]{:S(2)}) collective-permute-start(bf16[128,1024]{1,0:T(8,128)(2,1)} %collective-permute-done.5), channel_id=1, source_target_pairs={{0,4},{4,0},{8,12},{12,8},{16,20},{20,16},{24,28},{28,24},{1,5},{5... | collective-permute-start | bytes 786440 | tf_op jit(solution)/shard_map/ppermute | solution.py:201
  95.3 5.1 collective-permute-start.11
  96.6 16.3 %collective-permute-start.12 = (bf16[2,577,256]{2,0,1:T(2,128)(2,1)S(1)}, bf16[2,577,256]{2,0,1:T(2,128)(2,1)S(1)}, u32[]{:S(2)}, u32[]{:S(2)}) collective-permute-start(bf16[2,577,256]{2,0,1:T(2,128)(2,1)S(1)} %constant_dynamic-slice_fusion.20), channel_id=1, source_target_pairs={{0,2},{1,3},{2,0},{3,1},{4,6},{5,7},{6,4},{7,5},{8,10},{9,11},{10,... | collective-permute-start | bytes 1772552 | tf_op jit(solution)/shard_map/ppermute | solution.py:195
  99.7 17.0 %collective-permute-start.14 = (bf16[1,577,256]{2,1,0:T(8,128)(2,1)S(1)}, bf16[1,577,256]{2,1,0:T(8,128)(2,1)S(1)}, u32[]{:S(2)}, u32[]{:S(2)}) collective-permute-start(bf16[1,577,256]{2,1,0:T(8,128)(2,1)S(1)} %broadcast_select_fusion.36), channel_id=1, source_target_pairs={{0,1},{1,0},{2,3},{3,2},{4,5},{5,4},{6,7},{7,6},{8,9},{9,8},{10,11... | collective-permute-start | bytes 886280 | tf_op jit(solution)/shard_map/ppermute | solution.py:198
  99.9 47.3 %collective-permute-start.17 = (bf16[512,1024]{1,0:T(8,128)(2,1)S(1)}, bf16[512,1024]{1,0:T(8,128)(2,1)S(1)}, u32[]{:S(2)}, u32[]{:S(2)}) collective-permute-start(bf16[512,1024]{1,0:T(8,128)(2,1)S(1)} %constant_dynamic-slice_fusion.18), channel_id=1, source_target_pairs={{0,2},{1,3},{2,0},{3,1},{4,6},{5,7},{6,4},{7,5},{8,10},{9,11},{10,... | collective-permute-start | bytes 3145736 | tf_op jit(solution)/shard_map/ppermute | solution.py:195
  113.0 3.8 collective-permute-start.13
  115.0 25.8 %collective-permute-start.16 = (bf16[512,1024]{1,0:T(8,128)(2,1)}, bf16[512,1024]{1,0:T(8,128)(2,1)S(1)}, u32[]{:S(2)}, u32[]{:S(2)}) collective-permute-start(bf16[512,1024]{1,0:T(8,128)(2,1)} %collective-permute-done.8), channel_id=1, source_target_pairs={{0,4},{4,0},{8,12},{12,8},{16,20},{20,16},{24,28},{28,24},{1,5},{5... | collective-permute-start | bytes 3145736 | tf_op jit(solution)/shard_map/ppermute | solution.py:201
  118.0 46.4 %collective-permute-start.15 = (bf16[592,1024]{1,0:T(8,128)(2,1)S(1)}, bf16[592,1024]{1,0:T(8,128)(2,1)S(1)}, u32[]{:S(2)}, u32[]{:S(2)}) collective-permute-start(bf16[592,1024]{1,0:T(8,128)(2,1)S(1)} %get-tuple-element.103), channel_id=1, source_target_pairs={{0,1},{1,0},{2,3},{3,2},{4,5},{5,4},{6,7},{7,6},{8,9},{9,8},{10,11... | collective-permute-start | bytes 3637256 | tf_op jit(solution)/shard_map/ppermute | solution.py:198
  147.2 25.6 %collective-permute-start.18 = (bf16[512,1024]{1,0:T(8,128)(2,1)S(1)}, bf16[512,1024]{1,0:T(8,128)(2,1)S(1)}, u32[]{:S(2)}, u32[]{:S(2)}) collective-permute-start(bf16[512,1024]{1,0:T(8,128)(2,1)S(1)} %collective-permute-done.17), channel_id=1, source_target_pairs={{0,4},{4,0},{8,12},{12,8},{16,20},{20,16},{24,28},{28,24},{1,5},{5... | collective-permute-start | bytes 3145736 | tf_op jit(solution)/shard_map/ppermute | solution.py:201
  185.4 7.1 %collective-permute-start.19 = (bf16[592,1024]{1,0:T(8,128)(2,1)}, bf16[592,1024]{1,0:T(8,128)(2,1)}, u32[]{:S(2)}, u32[]{:S(2)}) collective-permute-start(bf16[592,1024]{1,0:T(8,128)(2,1)} %slice.279), channel_id=1, source_target_pairs={{0,1},{1,0},{2,3},{3,2},{4,5},{5,4},{6,7},{7,6},{8,9},{9,8},{10,11... | collective-permute-start | bytes 3637256 | tf_op jit(solution)/shard_map/ppermute | solution.py:198
  190.9 48.6 %collective-permute-start.21 = (bf16[1024,1024]{1,0:T(8,128)(2,1)S(1)}, bf16[1024,1024]{1,0:T(8,128)(2,1)S(1)}, u32[]{:S(2)}, u32[]{:S(2)}) collective-permute-start(bf16[1024,1024]{1,0:T(8,128)(2,1)S(1)} %convolution_convert_fusion.3), channel_id=1, source_target_pairs={{0,2},{1,3},{2,0},{3,1},{4,6},{5,7},{6,4},{7,5},{8,10},{9,11},{10,... | collective-permute-start | bytes 6291464 | tf_op jit(solution)/shard_map/ppermute | solution.py:195
  199.1 9.2 %collective-permute-start.20 = (bf16[592,1024]{1,0:T(8,128)(2,1)S(1)}, bf16[592,1024]{1,0:T(8,128)(2,1)S(1)}, u32[]{:S(2)}, u32[]{:S(2)}) collective-permute-start(bf16[592,1024]{1,0:T(8,128)(2,1)S(1)} %get-tuple-element.105), channel_id=1, source_target_pairs={{0,1},{1,0},{2,3},{3,2},{4,5},{5,4},{6,7},{7,6},{8,9},{9,8},{10,11... | collective-permute-start | bytes 3637256 | tf_op jit(solution)/shard_map/ppermute | solution.py:198
  203.5 169.2 %collective-permute-start.24 = (bf16[1024,1024]{1,0:T(8,128)(2,1)}, bf16[1024,1024]{1,0:T(8,128)(2,1)}, u32[]{:S(2)}, u32[]{:S(2)}) collective-permute-start(bf16[1024,1024]{1,0:T(8,128)(2,1)} %convolution_convert_fusion.2), channel_id=1, source_target_pairs={{0,2},{1,3},{2,0},{3,1},{4,6},{5,7},{6,4},{7,5},{8,10},{9,11},{10,... | collective-permute-start | bytes 6291464 | tf_op jit(solution)/shard_map/ppermute | solution.py:195
  240.4 54.8 %collective-permute-start.50 = (bf16[256,1024]{1,0:T(8,128)(2,1)S(1)}, bf16[256,1024]{1,0:T(8,128)(2,1)S(1)}, u32[]{:S(2)}, u32[]{:S(2)}) collective-permute-start(bf16[256,1024]{1,0:T(8,128)(2,1)S(1)} %convolution_convert_fusion.6), channel_id=1, source_target_pairs={{0,2},{1,3},{2,0},{3,1},{4,6},{5,7},{6,4},{7,5},{8,10},{9,11},{10,... | collective-permute-start | bytes 1572872 | tf_op jit(solution)/shard_map/ppermute | solution.py:195
  296.1 9.2 %collective-permute-start.51 = (bf16[128,1024]{1,0:T(8,128)(2,1)S(1)}, bf16[128,1024]{1,0:T(8,128)(2,1)S(1)}, u32[]{:S(2)}, u32[]{:S(2)}) collective-permute-start(bf16[128,1024]{1,0:T(8,128)(2,1)S(1)} %constant_dynamic-slice_fusion.8), channel_id=1, source_target_pairs={{0,4},{4,0},{8,12},{12,8},{16,20},{20,16},{24,28},{28,24},{1,5},{5... | collective-permute-start | bytes 786440 | tf_op jit(solution)/shard_map/ppermute | solution.py:201
  299.1 28.1 %collective-permute-start.22 = (bf16[512,1024]{1,0:T(8,128)(2,1)}, bf16[512,1024]{1,0:T(8,128)(2,1)}, u32[]{:S(2)}, u32[]{:S(2)}) collective-permute-start(bf16[512,1024]{1,0:T(8,128)(2,1)} %constant_dynamic-slice_fusion.17), channel_id=1, source_target_pairs={{0,4},{4,0},{8,12},{12,8},{16,20},{20,16},{24,28},{28,24},{1,5},{5... | collective-permute-start | bytes 3145736 | tf_op jit(solution)/shard_map/ppermute | solution.py:201
  305.5 5.0 collective-permute-start.52
  310.6 16.5 %collective-permute-start.53 = (bf16[32,1024]{1,0:T(8,128)(2,1)S(1)}, bf16[32,1024]{1,0:T(8,128)(2,1)S(1)}, u32[]{:S(2)}, u32[]{:S(2)}) collective-permute-start(bf16[32,1024]{1,0:T(8,128)(2,1)S(1)} %constant_dynamic-slice_fusion.6), channel_id=1, source_target_pairs={{0,16},{4,20},{8,24},{12,28},{16,0},{20,4},{24,8},{28,12},{1,17},{... | collective-permute-start | bytes 196616 | tf_op jit(solution)/shard_map/ppermute | solution.py:201
  327.1 31.9 %collective-permute-start.54 = (bf16[32,1024]{1,0:T(8,128)(2,1)S(1)}, bf16[32,1024]{1,0:T(8,128)(2,1)}, u32[]{:S(2)}, u32[]{:S(2)}) collective-permute-start(bf16[32,1024]{1,0:T(8,128)(2,1)S(1)} %add_convert_fusion.25), channel_id=1, source_target_pairs={{0,16},{4,20},{8,24},{12,28},{16,0},{20,4},{24,8},{28,12},{1,17},{... | collective-permute-start | bytes 196616 | tf_op jit(solution)/shard_map/ppermute | solution.py:201
  333.3 39.3 %collective-permute-start.23 = (bf16[256,1024]{1,0:T(8,128)(2,1)}, bf16[256,1024]{1,0:T(8,128)(2,1)}, u32[]{:S(2)}, u32[]{:S(2)}) collective-permute-start(bf16[256,1024]{1,0:T(8,128)(2,1)} %constant_dynamic-slice_fusion.16), channel_id=1, source_target_pairs={{0,8},{4,12},{8,0},{12,4},{16,24},{20,28},{24,16},{28,20},{1,9},{5... | collective-permute-start | bytes 1572872 | tf_op jit(solution)/shard_map/ppermute | solution.py:201
  339.8 52.3 %collective-permute-start.31 = (bf16[512,768]{1,0:T(8,128)(2,1)}, bf16[512,768]{1,0:T(8,128)(2,1)}, u32[]{:S(2)}, u32[]{:S(2)}) collective-permute-start(bf16[512,768]{1,0:T(8,128)(2,1)} %get-tuple-element.132), channel_id=1, source_target_pairs={{0,2},{1,3},{2,0},{3,1},{4,6},{5,7},{6,4},{7,5},{8,10},{9,11},{10,... | collective-permute-start | bytes 2359304 | tf_op jit(solution)/shard_map/ppermute | solution.py:195
  360.0 5.0 collective-permute-start.55
  365.1 6.4 %collective-permute-start.56 = (bf16[128,1024]{1,0:T(8,128)(2,1)S(1)}, bf16[128,1024]{1,0:T(8,128)(2,1)S(1)}, u32[]{:S(2)}, u32[]{:S(2)}) collective-permute-start(bf16[128,1024]{1,0:T(8,128)(2,1)S(1)} %maximum_select_fusion.21), channel_id=1, source_target_pairs={{0,4},{4,0},{8,12},{12,8},{16,20},{20,16},{24,28},{28,24},{1,5},{5... | collective-permute-start | bytes 786440 | tf_op jit(solution)/shard_map/ppermute | solution.py:201
  378.8 125.8 %collective-permute-start.25 = (bf16[592,1024]{1,0:T(8,128)(2,1)S(1)}, bf16[592,1024]{1,0:T(8,128)(2,1)S(1)}, u32[]{:S(2)}, u32[]{:S(2)}) collective-permute-start(bf16[592,1024]{1,0:T(8,128)(2,1)S(1)} %slice.281), channel_id=1, source_target_pairs={{0,1},{1,0},{2,3},{3,2},{4,5},{5,4},{6,7},{7,6},{8,9},{9,8},{10,11... | collective-permute-start | bytes 3637256 | tf_op jit(solution)/shard_map/ppermute | solution.py:198
  381.2 120.4 %collective-permute-start.28 = (bf16[592,1024]{1,0:T(8,128)(2,1)S(1)}, bf16[592,1024]{1,0:T(8,128)(2,1)S(1)}, u32[]{:S(2)}, u32[]{:S(2)}) collective-permute-start(bf16[592,1024]{1,0:T(8,128)(2,1)S(1)} %slice.289), channel_id=1, source_target_pairs={{0,1},{1,0},{2,3},{3,2},{4,5},{5,4},{6,7},{7,6},{8,9},{9,8},{10,11... | collective-permute-start | bytes 3637256 | tf_op jit(solution)/shard_map/ppermute | solution.py:198
  385.9 91.8 %collective-permute-start.38 = (bf16[512,768]{1,0:T(8,128)(2,1)S(1)}, bf16[512,768]{1,0:T(8,128)(2,1)S(1)}, u32[]{:S(2)}, u32[]{:S(2)}) collective-permute-start(bf16[512,768]{1,0:T(8,128)(2,1)S(1)} %pad_maximum_fusion.8), channel_id=1, source_target_pairs={{0,4},{4,0},{8,12},{12,8},{16,20},{20,16},{24,28},{28,24},{1,5},{5... | collective-permute-start | bytes 2359304 | tf_op jit(solution)/shard_map/ppermute | solution.py:201
  389.9 101.2 %collective-permute-start.57 = (bf16[512,1024]{1,0:T(8,128)(2,1)S(1)}, bf16[512,1024]{1,0:T(8,128)(2,1)S(1)}, u32[]{:S(2)}, u32[]{:S(2)}) collective-permute-start(bf16[512,1024]{1,0:T(8,128)(2,1)S(1)} %constant_dynamic-slice_fusion.5), channel_id=1, source_target_pairs={{0,4},{4,0},{8,12},{12,8},{16,20},{20,16},{24,28},{28,24},{1,5},{5... | collective-permute-start | bytes 3145736 | tf_op jit(solution)/shard_map/ppermute | solution.py:201
  393.5 42.8 %collective-permute-start.32 = (bf16[256,768]{1,0:T(8,128)(2,1)S(1)}, bf16[256,768]{1,0:T(8,128)(2,1)S(1)}, u32[]{:S(2)}, u32[]{:S(2)}) collective-permute-start(bf16[256,768]{1,0:T(8,128)(2,1)S(1)} %constant_dynamic-slice_fusion.15), channel_id=1, source_target_pairs={{0,4},{4,0},{8,12},{12,8},{16,20},{20,16},{24,28},{28,24},{1,5},{5... | collective-permute-start | bytes 1179656 | tf_op jit(solution)/shard_map/ppermute | solution.py:201
  436.3 13.9 %collective-permute-start.63 = (bf16[128,1024]{1,0:T(8,128)(2,1)S(1)}, bf16[128,1024]{1,0:T(8,128)(2,1)S(1)}, u32[]{:S(2)}, u32[]{:S(2)}) collective-permute-start(bf16[128,1024]{1,0:T(8,128)(2,1)S(1)} %constant_dynamic-slice_fusion.2), channel_id=1, source_target_pairs={{0,16},{4,20},{8,24},{12,28},{16,0},{20,4},{24,8},{28,12},{1,17},{... | collective-permute-start | bytes 786440 | tf_op jit(solution)/shard_map/ppermute | solution.py:201
  450.2 6.5 %collective-permute-start.33 = (bf16[128,768]{1,0:T(8,128)(2,1)S(1)}, bf16[128,768]{1,0:T(8,128)(2,1)S(1)}, u32[]{:S(2)}, u32[]{:S(2)}) collective-permute-start(bf16[128,768]{1,0:T(8,128)(2,1)S(1)} %constant_dynamic-slice_fusion.14), channel_id=1, source_target_pairs={{0,8},{4,12},{8,0},{12,4},{16,24},{20,28},{24,16},{28,20},{1,9},{5... | collective-permute-start | bytes 589832 | tf_op jit(solution)/shard_map/ppermute | solution.py:201
  456.7 13.6 %collective-permute-start.64 = (bf16[128,1024]{1,0:T(8,128)(2,1)S(1)}, bf16[128,1024]{1,0:T(8,128)(2,1)S(1)}, u32[]{:S(2)}, u32[]{:S(2)}) collective-permute-start(bf16[128,1024]{1,0:T(8,128)(2,1)S(1)} %add_convert_fusion.17), channel_id=1, source_target_pairs={{0,16},{4,20},{8,24},{12,28},{16,0},{20,4},{24,8},{28,12},{1,17},{... | collective-permute-start | bytes 786440 | tf_op jit(solution)/shard_map/ppermute | solution.py:201
  470.3 7.4 %collective-permute-start.34 = (bf16[64,768]{1,0:T(8,128)(2,1)S(1)}, bf16[64,768]{1,0:T(8,128)(2,1)S(1)}, u32[]{:S(2)}, u32[]{:S(2)}) collective-permute-start(bf16[64,768]{1,0:T(8,128)(2,1)S(1)} %constant_dynamic-slice_fusion.13), channel_id=1, source_target_pairs={{0,16},{4,20},{8,24},{12,28},{16,0},{20,4},{24,8},{28,12},{1,17},{... | collective-permute-start | bytes 294920 | tf_op jit(solution)/shard_map/ppermute | solution.py:201
  477.7 17.1 %collective-permute-start.65 = (bf16[256,1024]{1,0:T(8,128)(2,1)S(1)}, bf16[256,1024]{1,0:T(8,128)(2,1)S(1)}, u32[]{:S(2)}, u32[]{:S(2)}) collective-permute-start(bf16[256,1024]{1,0:T(8,128)(2,1)S(1)} %maximum_select_fusion.12), channel_id=1, source_target_pairs={{0,8},{4,12},{8,0},{12,4},{16,24},{20,28},{24,16},{28,20},{1,9},{5... | collective-permute-start | bytes 1572872 | tf_op jit(solution)/shard_map/ppermute | solution.py:201
  477.7 13.0 %collective-permute-start.35 = (bf16[64,768]{1,0:T(8,128)(2,1)S(1)}, bf16[64,768]{1,0:T(8,128)(2,1)S(1)}, u32[]{:S(2)}, u32[]{:S(2)}) collective-permute-start(bf16[64,768]{1,0:T(8,128)(2,1)S(1)} %add_convert_fusion.24), channel_id=1, source_target_pairs={{0,16},{4,20},{8,24},{12,28},{16,0},{20,4},{24,8},{28,12},{1,17},{... | collective-permute-start | bytes 294920 | tf_op jit(solution)/shard_map/ppermute | solution.py:201
  490.8 9.8 %collective-permute-start.39 = (bf16[256,768]{1,0:T(8,128)(2,1)S(1)}, bf16[256,768]{1,0:T(8,128)(2,1)S(1)}, u32[]{:S(2)}, u32[]{:S(2)}) collective-permute-start(bf16[256,768]{1,0:T(8,128)(2,1)S(1)} %add_convert_fusion.14), channel_id=1, source_target_pairs={{0,2},{1,3},{2,0},{3,1},{4,6},{5,7},{6,4},{7,5},{8,10},{9,11},{10,... | collective-permute-start | bytes 1179656 | tf_op jit(solution)/shard_map/ppermute | solution.py:195
  491.1 40.0 %collective-permute-start.36 = (bf16[128,768]{1,0:T(8,128)(2,1)S(1)}, bf16[128,768]{1,0:T(8,128)(2,1)S(1)}, u32[]{:S(2)}, u32[]{:S(2)}) collective-permute-start(bf16[128,768]{1,0:T(8,128)(2,1)S(1)} %maximum_select_fusion.22), channel_id=1, source_target_pairs={{0,8},{4,12},{8,0},{12,4},{16,24},{20,28},{24,16},{28,20},{1,9},{5... | collective-permute-start | bytes 589832 | tf_op jit(solution)/shard_map/ppermute | solution.py:201
  494.8 52.4 %collective-permute-start.58 = (bf16[256,1024]{1,0:T(8,128)(2,1)}, bf16[256,1024]{1,0:T(8,128)(2,1)}, u32[]{:S(2)}, u32[]{:S(2)}) collective-permute-start(bf16[256,1024]{1,0:T(8,128)(2,1)} %constant_dynamic-slice_fusion.4), channel_id=1, source_target_pairs={{0,8},{4,12},{8,0},{12,4},{16,24},{20,28},{24,16},{28,20},{1,9},{5... | collective-permute-start | bytes 1572872 | tf_op jit(solution)/shard_map/ppermute | solution.py:201
  500.6 83.6 %collective-permute-start.66 = (bf16[512,1024]{1,0:T(8,128)(2,1)S(1)}, bf16[512,1024]{1,0:T(8,128)(2,1)}, u32[]{:S(2)}, u32[]{:S(2)}) collective-permute-start(bf16[512,1024]{1,0:T(8,128)(2,1)S(1)} %maximum_select_fusion.6), channel_id=1, source_target_pairs={{0,4},{4,0},{8,12},{12,8},{16,20},{20,16},{24,28},{28,24},{1,5},{5... | collective-permute-start | bytes 3145736 | tf_op jit(solution)/shard_map/ppermute | solution.py:201
  501.6 26.5 %collective-permute-start.40 = (bf16[128,768]{1,0:T(8,128)(2,1)S(1)}, bf16[128,768]{1,0:T(8,128)(2,1)S(1)}, u32[]{:S(2)}, u32[]{:S(2)}) collective-permute-start(bf16[128,768]{1,0:T(8,128)(2,1)S(1)} %constant_dynamic-slice_fusion.10), channel_id=1, source_target_pairs={{0,8},{4,12},{8,0},{12,4},{16,24},{20,28},{24,16},{28,20},{1,9},{5... | collective-permute-start | bytes 589832 | tf_op jit(solution)/shard_map/ppermute | solution.py:201
  507.9 4.0 collective-permute-start.46
  511.9 12.3 %collective-permute-start.47 = (f32[7680]{0:T(1024)S(1)}, f32[7680]{0:T(1024)S(1)}, u32[]{:S(2)}, u32[]{:S(2)}) collective-permute-start(f32[7680]{0:T(1024)S(1)} %fusion.56), channel_id=1, source_target_pairs={{0,4},{4,0},{8,12},{12,8},{16,20},{20,16},{24,28},{28,24},{1,5},{5... | collective-permute-start | bytes 92168 | tf_op jit(solution)/shard_map/ppermute | solution.py:201
  524.2 3.9 collective-permute-start.48
  528.2 29.7 %collective-permute-start.26 = (bf16[1,577,512]{2,1,0:T(8,128)(2,1)}, bf16[1,577,512]{2,1,0:T(8,128)(2,1)}, u32[]{:S(2)}, u32[]{:S(2)}) collective-permute-start(bf16[1,577,512]{2,1,0:T(8,128)(2,1)} %pad_maximum_fusion.9), channel_id=1, source_target_pairs={{0,1},{1,0},{2,3},{3,2},{4,5},{5,4},{6,7},{7,6},{8,9},{9,8},{10,11... | collective-permute-start | bytes 1772552 | tf_op jit(solution)/shard_map/ppermute | solution.py:198
  528.2 5.6 collective-permute-start.49
  531.1 7.4 %collective-permute-start.41 = (bf16[64,768]{1,0:T(8,128)(2,1)S(1)}, bf16[64,768]{1,0:T(8,128)(2,1)S(1)}, u32[]{:S(2)}, u32[]{:S(2)}) collective-permute-start(bf16[64,768]{1,0:T(8,128)(2,1)S(1)} %constant_dynamic-slice_fusion.9), channel_id=1, source_target_pairs={{0,16},{4,20},{8,24},{12,28},{16,0},{20,4},{24,8},{28,12},{1,17},{... | collective-permute-start | bytes 294920 | tf_op jit(solution)/shard_map/ppermute | solution.py:201
  533.8 36.5 %collective-permute-start.29 = (bf16[1,577,512]{2,1,0:T(8,128)(2,1)}, bf16[1,577,512]{2,1,0:T(8,128)(2,1)}, u32[]{:S(2)}, u32[]{:S(2)}) collective-permute-start(bf16[1,577,512]{2,1,0:T(8,128)(2,1)} %pad_maximum_fusion.12), channel_id=1, source_target_pairs={{0,1},{1,0},{2,3},{3,2},{4,5},{5,4},{6,7},{7,6},{8,9},{9,8},{10,11... | collective-permute-start | bytes 1772552 | tf_op jit(solution)/shard_map/ppermute | solution.py:198
  538.6 6.8 %collective-permute-start.42 = (bf16[64,768]{1,0:T(8,128)(2,1)S(1)}, bf16[64,768]{1,0:T(8,128)(2,1)}, u32[]{:S(2)}, u32[]{:S(2)}) collective-permute-start(bf16[64,768]{1,0:T(8,128)(2,1)S(1)} %add_convert_fusion.23), channel_id=1, source_target_pairs={{0,16},{4,20},{8,24},{12,28},{16,0},{20,4},{24,8},{28,12},{1,17},{... | collective-permute-start | bytes 294920 | tf_op jit(solution)/shard_map/ppermute | solution.py:201
  545.4 11.3 %collective-permute-start.37 = (bf16[256,768]{1,0:T(8,128)(2,1)}, bf16[256,768]{1,0:T(8,128)(2,1)S(1)}, u32[]{:S(2)}, u32[]{:S(2)}) collective-permute-start(bf16[256,768]{1,0:T(8,128)(2,1)} %maximum_select_fusion.13), channel_id=1, source_target_pairs={{0,4},{4,0},{8,12},{12,8},{16,20},{20,16},{24,28},{28,24},{1,5},{5... | collective-permute-start | bytes 1179656 | tf_op jit(solution)/shard_map/ppermute | solution.py:201
  547.2 9.8 %collective-permute-start.43 = (bf16[128,768]{1,0:T(8,128)(2,1)S(1)}, bf16[128,768]{1,0:T(8,128)(2,1)S(1)}, u32[]{:S(2)}, u32[]{:S(2)}) collective-permute-start(bf16[128,768]{1,0:T(8,128)(2,1)S(1)} %maximum_select_fusion.23), channel_id=1, source_target_pairs={{0,8},{4,12},{8,0},{12,4},{16,24},{20,28},{24,16},{28,20},{1,9},{5... | collective-permute-start | bytes 589832 | tf_op jit(solution)/shard_map/ppermute | solution.py:201
  556.6 13.6 %collective-permute-start.59 = (bf16[128,1024]{1,0:T(8,128)(2,1)S(1)}, bf16[128,1024]{1,0:T(8,128)(2,1)S(1)}, u32[]{:S(2)}, u32[]{:S(2)}) collective-permute-start(bf16[128,1024]{1,0:T(8,128)(2,1)S(1)} %constant_dynamic-slice_fusion.3), channel_id=1, source_target_pairs={{0,16},{4,20},{8,24},{12,28},{16,0},{20,4},{24,8},{28,12},{1,17},{... | collective-permute-start | bytes 786440 | tf_op jit(solution)/shard_map/ppermute | solution.py:201
  557.0 31.5 %collective-permute-start.44 = (bf16[256,768]{1,0:T(8,128)(2,1)S(1)}, bf16[256,768]{1,0:T(8,128)(2,1)S(1)}, u32[]{:S(2)}, u32[]{:S(2)}) collective-permute-start(bf16[256,768]{1,0:T(8,128)(2,1)S(1)} %maximum_select_fusion.14), channel_id=1, source_target_pairs={{0,4},{4,0},{8,12},{12,8},{16,20},{20,16},{24,28},{28,24},{1,5},{5... | collective-permute-start | bytes 1179656 | tf_op jit(solution)/shard_map/ppermute | solution.py:201
  559.7 41.9 %collective-permute-start.27 = (bf16[2,577,256]{2,0,1:T(2,128)(2,1)S(1)}, bf16[2,577,256]{2,0,1:T(2,128)(2,1)S(1)}, u32[]{:S(2)}, u32[]{:S(2)}) collective-permute-start(bf16[2,577,256]{2,0,1:T(2,128)(2,1)S(1)} %copy.41), channel_id=1, source_target_pairs={{0,2},{1,3},{2,0},{3,1},{4,6},{5,7},{6,4},{7,5},{8,10},{9,11},{10,... | collective-permute-start | bytes 1772552 | tf_op jit(solution)/shard_map/ppermute | solution.py:195
  570.3 13.7 %collective-permute-start.60 = (bf16[128,1024]{1,0:T(8,128)(2,1)S(1)}, bf16[128,1024]{1,0:T(8,128)(2,1)S(1)}, u32[]{:S(2)}, u32[]{:S(2)}) collective-permute-start(bf16[128,1024]{1,0:T(8,128)(2,1)S(1)} %add_convert_fusion.18), channel_id=1, source_target_pairs={{0,16},{4,20},{8,24},{12,28},{16,0},{20,4},{24,8},{28,12},{1,17},{... | collective-permute-start | bytes 786440 | tf_op jit(solution)/shard_map/ppermute | solution.py:201
  572.1 31.2 %collective-permute-start.30 = (bf16[2,577,256]{2,0,1:T(2,128)(2,1)S(1)}, bf16[2,577,256]{2,0,1:T(2,128)(2,1)S(1)}, u32[]{:S(2)}, u32[]{:S(2)}) collective-permute-start(bf16[2,577,256]{2,0,1:T(2,128)(2,1)S(1)} %copy.44), channel_id=1, source_target_pairs={{0,2},{1,3},{2,0},{3,1},{4,6},{5,7},{6,4},{7,5},{8,10},{9,11},{10,... | collective-permute-start | bytes 1772552 | tf_op jit(solution)/shard_map/ppermute | solution.py:195
  584.1 13.9 %collective-permute-start.61 = (bf16[256,1024]{1,0:T(8,128)(2,1)S(1)}, bf16[256,1024]{1,0:T(8,128)(2,1)S(1)}, u32[]{:S(2)}, u32[]{:S(2)}) collective-permute-start(bf16[256,1024]{1,0:T(8,128)(2,1)S(1)} %maximum_select_fusion.11), channel_id=1, source_target_pairs={{0,8},{4,12},{8,0},{12,4},{16,24},{20,28},{24,16},{28,20},{1,9},{5... | collective-permute-start | bytes 1572872 | tf_op jit(solution)/shard_map/ppermute | solution.py:201
  598.5 24.3 %collective-permute-start.62 = (bf16[512,1024]{1,0:T(8,128)(2,1)S(1)}, bf16[512,1024]{1,0:T(8,128)(2,1)S(1)}, u32[]{:S(2)}, u32[]{:S(2)}) collective-permute-start(bf16[512,1024]{1,0:T(8,128)(2,1)S(1)} %maximum_select_fusion.5), channel_id=1, source_target_pairs={{0,4},{4,0},{8,12},{12,8},{16,20},{20,16},{24,28},{28,24},{1,5},{5... | collective-permute-start | bytes 3145736 | tf_op jit(solution)/shard_map/ppermute | solution.py:201
  (78 other events, 892.3 us)

commit v3 on v2

--- a/solution.py
+++ b/solution.py
@@ -197,6 +197,10 @@
     def core_swap(value):
         return lax.ppermute(value, "tensor", [(a, a ^ 1) for a in range(n_tensor)])
 
+    def core_trade(value):
+        pairs = [[2 * a, 2 * a + 1] for a in range(chips)]
+        return lax.all_to_all(value, "tensor", 0, 0, axis_index_groups=pairs)
+
     def dp_swap(value, bit):
         return lax.ppermute(value, "dp", [(a, a ^ (1 << bit)) for a in range(n_dp)])
 
@@ -209,64 +213,69 @@
     def fetch_rows(value):
         return [chip_shift(my_images(value, step), step) for step in steps]
 
-    def core_rows(value, arrived):
-        mine = [my_images(value, 0)] + arrived
-        theirs = []
-        for n, piece in enumerate(mine):
-            if split:
-                theirs.append(core_swap(by_core(piece[near:], piece[:near])))
-                mine[n] = by_core(piece[:near], piece[near:])
-            else:
-                theirs.append(core_swap(piece))
+    def core_rows(value, arrived, whole):
+        mine = jnp.concatenate([my_images(value, 0)] + arrived, axis=2)
+        if split and not whole:
+            both = core_trade(mine.reshape(2, near, seq, chips * width))
+            both = [both[0], both[1]]
+        else:
+            got = core_swap(mine)
+            both = [by_core(mine, got), by_core(got, mine)]
+        both = [[b[:, :, a * width : (a + 1) * width] for a in range(chips)] for b in both]
         parts = []
         for a in range(chips):
-            which = (chip - a) % chips
-            own, other = pick(mine, which), pick(theirs, which)
-            parts += [by_core(own, other), by_core(other, own)]
+            parts += [pick(b, (chip - a) % chips) for b in both]
         out = jnp.concatenate(parts, axis=2)
         out = jnp.pad(out, ((0, 0), (0, padded - seq), (0, 0)))
-        return out.reshape(local, full)
+        return out.reshape(-1, full)
 
     def complete(rows):
-        return jnp.concatenate([rows, core_swap(rows)], axis=0) if split else rows
+        if split:
+            rows = core_trade(jnp.broadcast_to(rows, (2,) + rows.shape)).reshape(-1, full)
+        return rows
 
     def exchange(part):
         part = part.astype(BF16)
-        return part[:local].astype(F32) + core_swap(part[-local:]).astype(F32)
-
-    def scatter_rows(value):
+        if split:
+            both = core_trade(part.reshape(2, local, full)).astype(F32)
+            return both[0] + both[1]
+        return part.astype(F32) + core_swap(part).astype(F32)
+
+    def own_columns(value):
         value = value.reshape(near, padded, full)[:, :seq]
         cols = [value[:, :, n * width : (n + 1) * width] for n in range(n_tensor)]
-        keep = [by_core(cols[2 * a], cols[2 * a + 1]) for a in range(chips)]
+        cols = [jnp.concatenate(cols[core_of::2], axis=2) for core_of in range(2)]
         if split:
-            give = [by_core(cols[2 * a + 1], cols[2 * a]) for a in range(chips)]
-            got = core_swap(jnp.concatenate(give, axis=2))
-            got = [got[:, :, a * width : (a + 1) * width] for a in range(chips)]
-            keep = [
-                jnp.concatenate([by_core(m, g), by_core(g, m)], axis=0)
-                for m, g in zip(keep, got)
-            ]
+            keep = core_trade(jnp.stack(cols)).reshape(images, seq, chips * width)
+        else:
+            keep = by_core(*cols)
+        return [keep[:, :, a * width : (a + 1) * width] for a in range(chips)]
+
+    def scatter_rows(keep):
         pieces = [pick(keep, chip)]
         for step in steps:
             pieces.append(chip_shift(pick(keep, (chip + step) % chips), step))
         return jnp.concatenate([pick(pieces, (chip - a) % chips) for a in range(chips)], axis=0)
 
-    def fetch_weight(weight):
+    def my_half(weight):
         half = weight.shape[0] // 2
-        send = lax.dynamic_slice_in_dim(weight, side * half, half, 0)
+        return lax.dynamic_slice_in_dim(weight, side * half, half, 0)
+
+    def fetch(send):
         return [chip_shift(send, step) for step in steps]
 
-    def whole_weight(weight, arrived):
+    def other_halves(arrived):
+        return [dp_swap(got, 0) for got in arrived]
+
+    def whole_weight(weight, arrived, others):
         blocks = [weight]
-        for got in arrived:
-            other = dp_swap(got, 0)
-            blocks.append(
-                jnp.where(
-                    side == 0,
-                    jnp.concatenate([got, other], 0),
-                    jnp.concatenate([other, got], 0),
-                )
+        for got, other in zip(arrived, others):
+            block = jnp.where(
+                side == 0,
+                jnp.concatenate([got, other], 0),
+                jnp.concatenate([other, got], 0),
             )
+            blocks.append(lax.optimization_barrier(block))
         return blocks
 
     def halves(value, bit):
@@ -276,55 +285,64 @@
         send = lax.dynamic_slice_in_dim(value, (1 - at) * half, half, 0)
         return keep, send
 
+    def add(left, right):
+        return (left.astype(F32) + right.astype(F32)).astype(BF16)
+
     def reduce_blocks(blocks, dp_first):
         first = 0
         if dp_first:
             cut = [halves(block, 0) for block in blocks]
-            got = yield [dp_swap(jnp.concatenate([c[1] for c in cut], 0), 0)]
+            send = yield [jnp.concatenate([c[1] for c in cut], 0)]
+            got = dp_swap(send[0], 0)
             size = cut[0][0].shape[0]
-            blocks = [
-                (c[0].astype(F32) + got[0][n * size : (n + 1) * size].astype(F32)).astype(BF16)
-                for n, c in enumerate(cut)
-            ]
+            blocks = [add(c[0], got[n * size : (n + 1) * size]) for n, c in enumerate(cut)]
             first = 1
-        got = yield [chip_shift(blocks[step], chips - step) for step in steps]
+        send = yield blocks[1:]
         total = blocks[0].astype(F32)
-        for piece in got:
-            total = total + piece.astype(F32)
+        for step in steps:
+            total = total + chip_shift(send[step - 1], chips - step).astype(F32)
         total = total.astype(BF16)
-        for bit in range(first, bits):
+        for bit in range(first, bits - 1):
             keep, send = halves(total, bit)
-            got = yield [dp_swap(send, bit)]
-            total = (keep.astype(F32) + got[0].astype(F32)).astype(BF16)
-        for bit in reversed(range(bits)):
+            send = yield [send]
+            total = add(keep, dp_swap(send[0], bit))
+        send = yield [total]
+        total = add(total, dp_swap(send[0], bits - 1))
+        for bit in reversed(range(bits - 1)):
             at = (d_idx >> bit) & 1
-            got = yield [dp_swap(total, bit)]
+            send = yield [total]
+            got = dp_swap(send[0], bit)
             total = jnp.where(
                 at == 0,
-                jnp.concatenate([total, got[0]], 0),
-                jnp.concatenate([got[0], total], 0),
+                jnp.concatenate([total, got], 0),
+                jnp.concatenate([got, total], 0),
             )
         return total.astype(F32)
 
     def begin(blocks, dp_first=False):
         flow = reduce_blocks(blocks, dp_first)
-        return [flow, next(flow)]
-
-    def advance(flow, got):
-        flow[1] = flow[0].send(got)
+        return [flow, next(flow), None]
+
+    def tie(value, *flows):
+        flows = [flow for flow in flows if flow[2] is None]
+        value, sends = lax.optimization_barrier((value, [flow[1] for flow in flows]))
+        for flow, send in zip(flows, sends):
+            advance(flow, send)
+        return value
+
+    def advance(flow, send):
+        try:
+            flow[1] = flow[0].send(send)
+        except StopIteration as end:
+            flow[1:] = [], end.value
 
     def finish(flow):
-        try:
-            while True:
-                advance(flow, flow[1])
-        except StopIteration as end:
-            return end.value
-
-    def tie(value, *flows):
-        value, arrived = lax.optimization_barrier((value, [flow[1] for flow in flows]))
-        for flow, got in zip(flows, arrived):
-            advance(flow, got)
-        return value
+        while flow[2] is None:
+            advance(flow, flow[1])
+        return flow[2]
+
+    def hold(*values):
+        return lax.optimization_barrier(values)
 
     def after(value, *earlier):
         return lax.optimization_barrier((value, earlier))[0]
@@ -332,17 +350,17 @@
     gain_one, shift_one = ln1_gain.astype(F32), ln1_bias.astype(F32)
     gain_two, shift_two = ln2_gain.astype(F32), ln2_bias.astype(F32)
 
+    n_up = bias_up.shape[0]
+    small = jnp.concatenate([bias_up, bias_qv.reshape(-1)])
+    spare = -small.shape[0] % (ROW_TILE * full)
+    small_rows = jnp.pad(small, (0, spare)).reshape(-1, full)
     x_got = fetch_rows(inputs)
     cat_qkv = jnp.concatenate([w_qkv[n] for n in range(3)], axis=1)
-    q_got = fetch_weight(cat_qkv)
-    small = jnp.concatenate([bias_up, bias_qv.reshape(-1)])
-    small_got = [chip_shift(small, step) for step in steps]
-    o_got = fetch_weight(w_out)
-    u_got = fetch_weight(w_up)
-    dy_got = fetch_rows(cotangent)
-    d_got = fetch_weight(w_down)
-
-    n_up = bias_up.shape[0]
+    out_rows = jnp.concatenate([my_half(w_out), small_rows], axis=0)
+    sends = [my_half(cat_qkv), out_rows, my_half(w_up), my_half(w_down)]
+    dy_sends = [my_images(cotangent, step) for step in steps]
+    x_got, sends, dy_sends = hold(x_got, sends, dy_sends)
+    q_got, o_got, u_got = [fetch(send) for send in sends[:3]]
     scale = jnp.concatenate([jnp.full((width,), 0.125, F32), jnp.ones((2 * width,), F32)])
 
     def qkv_bias(vector):
@@ -352,25 +370,33 @@
     def project(block, vector):
         return ((mm(normed_one, block, NN) + qkv_bias(vector)) * scale).astype(BF16)
 
-    x32 = core_rows(inputs, x_got).astype(F32)
+    x32 = core_rows(inputs, x_got, False).astype(F32)
     mean_one, inv_one = norm_stats(x32)
     unit_one = (x32 - mean_one) * inv_one
     normed_one = complete((unit_one * gain_one + shift_one).astype(BF16))
     qkv = [project(cat_qkv, small)]
-    qkv[0], q_got = lax.optimization_barrier((qkv[0], q_got))
-    wq = whole_weight(cat_qkv, q_got)
+    qkv[0], q_got = hold(qkv[0], q_got)
+    q_more = other_halves(q_got)
     o, lse = attention_forward(qkv[0], images, seq)
-    o, o_got, small_got = lax.optimization_barrier((o, o_got, small_got))
     heads, norms = [o], [lse]
-    wo = whole_weight(w_out, o_got)
-    smalls = [small] + small_got
+    q_more, o_got = hold(q_more, o_got)
+    half_out = w_out.shape[0] // 2
+    smalls = [small] + [got[half_out:].reshape(-1)[: small.shape[0]] for got in o_got]
+    o_got = [got[:half_out] for got in o_got]
+    o_more = other_halves(o_got)
+    wq = whole_weight(cat_qkv, q_got, q_more)
     for r in steps:
         qkv.append(project(wq[r], smalls[r]))
+    qkv[-1], dy_sends, d_send = hold(qkv[-1], dy_sends, sends[3])
+    dy_got = [chip_shift(send, step) for step, send in zip(steps, dy_sends)]
+    d_got = fetch(d_send)
+    for r in steps:
         o, lse = attention_forward(qkv[r], images, seq)
         heads.append(o)
         norms.append(lse)
-    heads[-1], u_got = lax.optimization_barrier((heads[-1], u_got))
-    wu = whole_weight(w_up, u_got)
+    heads[-1], u_got, o_more = hold(heads[-1], u_got, o_more)
+    u_more = other_halves(u_got)
+    wo = whole_weight(w_out, o_got, o_more)
     attn_part = mm(heads[0], wo[0], NN)
     for r in steps:
         attn_part = attn_part + mm(heads[r], wo[r], NN)
@@ -378,30 +404,42 @@
     mean_two, inv_two = norm_stats(resid)
     unit_two = (resid - mean_two) * inv_two
     normed_two = complete((unit_two * gain_two + shift_two).astype(BF16))
-    normed_two, dy_got = lax.optimization_barrier((normed_two, dy_got))
-
+    normed_two, dy_got, u_more = hold(normed_two, dy_got, u_more)
+
+    live = my_images(slot_mask, 0).astype(BF16)
+    dy = core_rows(cotangent, dy_got, True).reshape(images, padded, full)
+    dy = (dy * live[:, None, None]).reshape(-1, full)
+    dy_local = lax.dynamic_slice_in_dim(dy, core * local, local, 0) if split else dy
     acts, slopes = [], []
-    for r in range(chips):
-        hidden = mm(normed_two, wu[r], NN) + smalls[r][:n_up].astype(F32)
+
+    def hidden_units(rows, block, vector):
+        hidden = mm(rows, block, NN) + vector[:n_up].astype(F32)
         sigma = jax.nn.sigmoid(GELU_K * hidden)
         acts.append((hidden * sigma).astype(BF16))
         slopes.append(sigma + GELU_K * hidden * sigma * (1.0 - sigma))
-    acts[-1], d_got = lax.optimization_barrier((acts[-1], d_got))
-    wd = whole_weight(w_down, d_got)
-
-    live = my_images(slot_mask, 0).astype(BF16)
-    if split:
-        live = by_core(live[:near], live[near:])
-    dy_local = core_rows(cotangent, dy_got).reshape(near, padded, full)
-    dy_local = (dy_local * live[:, None, None]).reshape(local, full)
-    dy = complete(dy_local)
-    down_blocks = [None] + [mm(acts[r], dy, TN).astype(BF16) for r in steps]
-    down_blocks[0] = mm(after(acts[0], *down_blocks[1:]), dy, TN).astype(BF16)
+
+    hidden_units(normed_two, w_up, small)
+    acts[0], dy, d_got = hold(acts[0], dy, d_got)
+    d_more = other_halves(d_got)
+    wu = whole_weight(w_up, u_got, u_more)
+    for r in steps:
+        hidden_units(normed_two, wu[r], smalls[r])
+
+    down_sent = [mm(acts[r], dy, TN).astype(BF16) for r in steps]
+    first_act, dy, down_sent = lax.optimization_barrier((acts[0], dy, down_sent))
+    down_blocks = [mm(first_act, dy, TN).astype(BF16)] + down_sent
+    d_hidden = [(mm(dy, w_down, NT) * slopes[0]).astype(BF16)]
+    up_blocks = [mm(normed_two, d_hidden[0], TN).astype(BF16)]
+    up_blocks[0], d_more = lax.optimization_barrier((up_blocks[0], d_more))
+    wd = whole_weight(w_down, d_got, d_more)
+    for r in steps:
+        d_hidden.append((mm(dy, wd[r], NT) * slopes[r]).astype(BF16))
+        up_blocks.append(mm(normed_two, d_hidden[r], TN).astype(BF16))
+    d_hidden, up_blocks = lax.optimization_barrier((d_hidden, up_blocks))
     flow_down = begin(down_blocks)
-    d_hidden = [(mm(dy, wd[r], NT) * slopes[r]).astype(BF16) for r in range(chips)]
-    up_blocks = [None] + [mm(normed_two, d_hidden[r], TN).astype(BF16) for r in steps]
-    up_blocks[0] = mm(normed_two, after(d_hidden[0], *up_blocks[1:]), TN).astype(BF16)
     flow_up = begin(up_blocks)
+    flow_down[1] = flow_down[0].send(flow_down[1])
+    flow_up[1] = flow_up[0].send(flow_up[1])
     part_two = mm(d_hidden[0], wu[0], NT)
     for r in steps:
         part_two = part_two + mm(d_hidden[r], wu[r], NT)
@@ -410,72 +448,104 @@
     da_local = d_resid.astype(BF16)
     da = tie(complete(da_local), flow_down)
 
-    grads = [None] * chips
+    middle = full // 2
+    grads, lows, highs = [None] * chips, [None] * chips, [None] * chips
+    part_one = None
     last = da
     for r in list(steps) + [0]:
         do = mm(last, wo[r], NT).astype(BF16)
         grads[r] = attention_backward(qkv[r], do, norms[r], images, seq)
+        if r == chips - 1:
+            grads[r] = tie(grads[r], flow_down)
+        if r == 0:
+            grads[r] = tie(grads[r], flow_down, flow_up)
+        of_qkv = mm(normed_one, grads[r], TN).astype(BF16)
+        of_out = mm(da, heads[r], TN).astype(BF16)
+        lows[r] = jnp.concatenate([of_qkv[:middle], of_out[:middle]], axis=1)
+        highs[r] = jnp.concatenate([of_qkv[middle:], of_out[middle:]], axis=1)
+        part = mm(grads[r], wq[r], NT)
+        part_one = part if part_one is None else part_one + part
         if r:
-            grads[r] = tie(grads[r], flow_down)
-            last = after(da, grads[r])
-    grads[0] = tie(grads[0], flow_down, flow_up)
-    out_blocks = [mm(heads[r], da, TN).astype(BF16) for r in range(chips)]
-    flow_out = begin(out_blocks)
-    qkv_blocks = [None] + [mm(normed_one, grads[r], TN).astype(BF16) for r in steps]
-    qkv_blocks[0] = mm(normed_one, grads[0], TN).astype(BF16)
-    middle = full // 2
-    flow_low = begin([block[:middle] for block in qkv_blocks])
-    flow_high = begin([block[middle:] for block in qkv_blocks], True)
-    part_one = mm(grads[0], wq[0], NT)
-    for r in steps:
-        part_one = part_one + mm(grads[r], wq[r], NT)
+            last, lows[r], highs[r] = lax.optimization_barrier((last, lows[r], highs[r]))
+            if r == chips - 1:
+                last = tie(last, flow_down)
+    flow_low = begin(lows)
+    flow_low[1] = flow_low[0].send(flow_low[1])
+    flow_high = begin(highs)
+    flow_high[1] = flow_high[0].send(flow_high[1])
     back_one, g_gain_one, g_shift_one = norm_back(exchange(part_one), unit_one, inv_one, gain_one)
-    input_grad = scatter_rows((d_resid + back_one).astype(BF16))
-
-    mlp_part = mm(after(acts[0], grads[0]), wd[0], NN)
+    input_rows = tie((d_resid + back_one).astype(BF16), flow_up, flow_low)
+
+    def reduce_small():
+        shared = jnp.concatenate(
+            [
+                jnp.sum(da_local, axis=0, dtype=F32),
+                g_gain_one,
+                g_shift_one,
+                g_gain_two,
+                g_shift_two,
+                jnp.sum(dy_local, axis=0, dtype=F32),
+            ]
+        )
+        if split:
+            send = yield shared
+            shared = shared + core_swap(send)
+        own = []
+        for r in range(chips):
+            rows_sum = jnp.sum(grads[r], axis=0, dtype=F32)
+            hidden_sum = jnp.sum(d_hidden[r], axis=0, dtype=F32)
+            own.append(
+                jnp.concatenate([shared, hidden_sum, rows_sum[:width], rows_sum[2 * width :]])
+            )
+        send = yield own[1:]
+        vector = own[0]
+        for step in steps:
+            vector = vector + chip_shift(send[step - 1], chips - step)
+        for bit in list(range(1, bits)) + [0]:
+            send = yield vector
+            vector = vector + dp_swap(send, bit)
+        return vector
+
+    flow_small = reduce_small()
+    flow_small = [flow_small, next(flow_small), None]
+
+    mlp_part = mm(after(acts[0], input_rows), w_down, NN)
     for r in steps:
         mlp_part = mlp_part + mm(acts[r], wd[r], NN)
+    mlp_part = tie(mlp_part, flow_small, flow_high, flow_down, flow_up)
     out = (resid + (exchange(mlp_part) + bias_down.astype(F32))).astype(BF16)
-    layer_out = scatter_rows(out)
-
-    shared = jnp.concatenate(
-        [
-            jnp.sum(da_local, axis=0, dtype=F32),
-            g_gain_one,
-            g_shift_one,
-            g_gain_two,
-            g_shift_two,
-            jnp.sum(dy_local, axis=0, dtype=F32),
-        ]
-    )
-    if split:
-        shared = shared + core_swap(shared)
-    own = []
-    for r in range(chips):
-        rows_sum = jnp.sum(grads[r], axis=0, dtype=F32)
-        own.append(
-            jnp.concatenate(
-                [
-                    shared,
-                    jnp.sum(d_hidden[r], axis=0, dtype=F32),
-                    rows_sum[:width],
-                    rows_sum[2 * width :],
-                ]
-            )
-        )
-    vector = own[0]
-    for step in steps:
-        vector = vector + chip_shift(own[step], chips - step)
-    for bit in range(bits):
-        vector = vector + dp_swap(vector, bit)
+    out = tie(out, flow_small, flow_low)
+    keep = [
+        jnp.concatenate(pair, axis=2) for pair in zip(own_columns(out), own_columns(input_rows))
+    ]
+    both = scatter_rows(keep)
+    layer_out, input_grad = both[:, :, :width], both[:, :, width:]
+
+    token = after(slot_mask, keep)
+    for flow in (
+        flow_high,
+        flow_low,
+        flow_small,
+        flow_up,
+        flow_high,
+        flow_small,
+        flow_up,
+        flow_low,
+        flow_high,
+        flow_low,
+        flow_small,
+        flow_high,
+    ):
+        token = tie(token, flow)
+    vector = finish(flow_small)
     vecs = [vector[n * full : (n + 1) * full] for n in range(6)]
     mine = vector[6 * full :]
 
     grad_down = finish(flow_down)
     grad_up = finish(flow_up)
-    grad_out = finish(flow_out)
     grad_cat = jnp.concatenate([finish(flow_low), finish(flow_high)], axis=0)
     grad_qkv = jnp.stack([grad_cat[:, n * width : (n + 1) * width] for n in range(3)])
+    grad_out = grad_cat[:, 3 * width :].T
     return (
         layer_out,
         input_grad,

time: 633 us -> 469 us (0.74)
  waiting for transfers between devices: 340 us -> 98.8 us
  blocking collectives: 0 us -> 33.8 us
  other arithmetic: 51.5 us -> 71.7 us
  local copies, waits for them, and re-layouts: 30.6 us -> 50 us
  starting transfers between devices: 55.8 us -> 68.9 us
  matrix products: 101 us -> 93.6 us
    ppermute x37 -> x27, waiting for transfers between devices: 217 us -> 85.6 us  [dp_swap(): return lax.ppermute(value, 'dp', [(a, a ^ 1 << bit) for a in range(n_dp)])]
    ppermute x15 -> x12, waiting for transfers between devices: 120 us -> 13.1 us  [chip_shift(): return lax.ppermute(value, 'tensor', perm)]
    all_to_all x0 -> x6, blocking collectives: none -> 33.8 us  [core_trade(): return lax.all_to_all(value, 'tensor', 0, 0, axis_index_groups=pairs)]
    all_to_all x0 -> x4, starting transfers between devices: none -> 18.7 us  [core_trade(): return lax.all_to_all(value, 'tensor', 0, 0, axis_index_groups=pairs)]
    convert_element_type x17 -> x19, other arithmetic: 5.27 us -> 17 us  [the longest x12 11.5 us: add(): return (left.astype(F32) + right.astype(F32)).astype(BF16)]
    select_n x12 -> x10, other arithmetic: 4.92 us -> 12.7 us  [the longest x4 8.87 us: whole_weight(): jnp.where(side == 0, jnp.concatenate([got, other], 0), jnp.concatenate([o...]
    select_n x12 -> x1, other arithmetic: 7.19 us -> 0.16 us  [by_core(): return jnp.where(core == 0, first, second)]
    dot_general x24, matrix products: 101 us -> 93.6 us  [mm(): return lax.dot_general(left, right, dims, preferred_element_type=F32)]
  transfers between devices with their start and end apart: 67 -> 45, of which waited for: 31 -> 19; matrix products, arithmetic and copies ran while one was open for 24% -> 43% of each run, Pallas kernels for 7% -> 9%
where the time goes in v3:
time: 469 us; the launch traced here: 462 us
  waiting for transfers between devices  98.8 us (21%)
  matrix products  93.6 us (20%)
  other arithmetic  71.7 us (15%)
  starting transfers between devices  68.9 us (15%)
  local copies, waits for them, and re-layouts  50 us (11%)
  Pallas kernels  42.8 us (9%)
  blocking collectives  33.8 us (7%)
    dot_general x24, matrix products, mm(): return lax.dot_general(left, right, dims, preferred_element_type=F32)  93.6 us
    ppermute x27, waiting for transfers between devices, dp_swap(): return lax.ppermute(value, 'dp', [(a, a ^ 1 << bit) for a in range(n_dp)])  85.6 us
    all_to_all x6, blocking collectives, core_trade(): return lax.all_to_all(value, 'tensor', 0, 0, axis_index_groups=pairs)  33.8 us
    ppermute x27, starting transfers between devices, dp_swap(): return lax.ppermute(value, 'dp', [(a, a ^ 1 << bit) for a in range(n_dp)])  33.4 us
    pallas_call x2, Pallas kernels, attention_backward(): pl.pallas_call(functools.partial(attn_bwd_kernel, seq, width), grid=(imag...  26.1 us
    all_to_all x4, starting transfers between devices, core_trade(): return lax.all_to_all(value, 'tensor', 0, 0, axis_index_groups=pairs)  18.7 us
    pallas_call x2, Pallas kernels, attention_forward(): pl.pallas_call(functools.partial(attn_fwd_kernel, seq), grid=(images, pai...  16.7 us
    ppermute x12, starting transfers between devices, chip_shift(): return lax.ppermute(value, 'tensor', perm)  16.2 us
  transfers between devices with their start and end apart: 45, of which 19 were waited for; matrix products, arithmetic and copies ran while one was open for 43% of the time, Pallas kernels for 9%

profile of v3, /device:TPU:0, one launch (start us, length us, event | category | flops | bytes accessed | tf_op | source)
XLA Modules:
  0.0 462.2 jit_solution(4717261204189585939)
XLA Ops:
  0.7 3.8 constant_dynamic-slice_fusion.15
  4.5 3.0 collective-permute-start
  7.6 4.0 constant_dynamic-slice_fusion.8
  22.4 4.7 %all_to_all.50 = bf16[2,1,577,512]{3,2,1,0:T(8,128)(2,1)S(1)} all-to-all(bf16[2,1,577,512]{3,2,1,0:T(8,128)(2,1)S(1)} %maximum_bitcast_fusion), channel_id=1, replica_groups={{0,1},{2,3},{4,5},{6,7},{8,9},{10,11},{12,13},{14,15},{16,17},{18,19},{..., dimensions={0} | all-to-all | bytes 2363392 | tf_op jit(solution)/shard_map/all_to_all | solution.py:202
  30.8 6.3 %all_to_all.51 = bf16[2,592,1024]{2,1,0:T(8,128)(2,1)S(1)} all-to-all(bf16[2,592,1024]{2,1,0:T(8,128)(2,1)S(1)} %broadcast_in_dim.6), channel_id=1, replica_groups={{0,1},{2,3},{4,5},{6,7},{8,9},{10,11},{12,13},{14,15},{16,17},{18,19},{..., dimensions={0} | all-to-all | bytes 4849664 | tf_op jit(solution)/shard_map/all_to_all | solution.py:202
  37.2 3.3 fusion.6.q_ref.k_ref.v_ref
  40.5 7.4 %collective-permute-done.1 = bf16[512,768]{1,0:T(8,128)(2,1)} collective-permute-done((bf16[512,768]{1,0:T(8,128)(2,1)S(1)}, bf16[512,768]{1,0:T(8,128)(2,1)}, u32[]{:S(2)}, u32[]{:S(2)}) %collective-permute-start.1) | collective-permute-done | bytes 786464 | tf_op jit(solution)/shard_map/ppermute | solution.py:195
  53.2 8.3 %attn_fwd.2 = (bf16[1184,256]{1,0:T(8,128)(2,1)}, f32[2,2,2,592]{3,2,1,0:T(2,128)}) custom-call(bf16[1184,768]{1,0:T(8,128)(2,1)} %fusion.6.q_ref.k_ref.v_ref, bf16[1184,768]{1,0:T(8,128)(2,1)} %fusion.6.q_ref.k_ref.v_ref, bf16[1184,768]{1,0:T(8,128)(2,1)} %fusion.6.q_ref.k_ref.v_ref), custom_call_target="tpu_custom_call" | custom-call | flops 2871001088 | bytes 2424832 | tf_op jit(solution)/shard_map/attn_fwd/pallas_call | solution.py:96
  61.5 4.2 fusion.76
  69.3 2.2 maximum_select_fusion.4
  73.4 3.3 fusion.7.q_ref.k_ref.v_ref
  79.4 8.4 %attn_fwd.3 = (bf16[1184,256]{1,0:T(8,128)(2,1)}, f32[2,2,2,592]{3,2,1,0:T(2,128)}) custom-call(bf16[1184,768]{1,0:T(8,128)(2,1)} %fusion.7.q_ref.k_ref.v_ref, bf16[1184,768]{1,0:T(8,128)(2,1)} %fusion.7.q_ref.k_ref.v_ref, bf16[1184,768]{1,0:T(8,128)(2,1)} %fusion.7.q_ref.k_ref.v_ref), custom_call_target="tpu_custom_call" | custom-call | flops 2871001088 | bytes 2424832 | tf_op jit(solution)/shard_map/attn_fwd/pallas_call | solution.py:96
  89.6 3.4 add_convert_fusion.2
  93.0 5.7 %all_to_all.52 = bf16[2,592,1024]{2,1,0:T(8,128)(2,1)S(1)} all-to-all(bf16[2,592,1024]{2,1,0:T(8,128)(2,1)S(1)} %bitcast.163), channel_id=1, replica_groups={{0,1},{2,3},{4,5},{6,7},{8,9},{10,11},{12,13},{14,15},{16,17},{18,19},{..., dimensions={0} | all-to-all | bytes 4849664 | tf_op jit(solution)/shard_map/all_to_all | solution.py:202
  101.0 5.8 %all_to_all.53 = bf16[2,592,1024]{2,1,0:T(8,128)(2,1)S(1)} all-to-all(bf16[2,592,1024]{2,1,0:T(8,128)(2,1)S(1)} %broadcast_in_dim.7), channel_id=1, replica_groups={{0,1},{2,3},{4,5},{6,7},{8,9},{10,11},{12,13},{14,15},{16,17},{18,19},{..., dimensions={0} | all-to-all | bytes 4849664 | tf_op jit(solution)/shard_map/all_to_all | solution.py:202
  106.8 5.3 %collective-permute-done.7 = bf16[512,1024]{1,0:T(8,128)(2,1)S(1)} collective-permute-done((bf16[512,1024]{1,0:T(8,128)(2,1)}, bf16[512,1024]{1,0:T(8,128)(2,1)S(1)}, u32[]{:S(2)}, u32[]{:S(2)}) %collective-permute-start.7) | collective-permute-done | bytes 1048608 | tf_op jit(solution)/shard_map/ppermute | solution.py:205
  112.1 2.7 maximum_select_fusion
  116.0 2.7 fusion.77
  118.8 4.7 %multiply_convert_fusion.3 = (bf16[1184,1024]{1,0:T(8,128)(2,1)}, f32[1184,1024]{1,0:T(8,128)S(1)}) fusion(f32[1024]{0:T(1024)S(1)} %convert_element_type.321, bf16[1184,1024]{1,0:T(8,128)(2,1)S(1)} %bitcast.177, bf16[1024,1024]{1,0:T(8,128)(2,1)S(1)} %copy-done), kind=kOutput, calls=%fused_computation.13 | convolution fusion | flops 2491514880 | bytes 11800576 | tf_op jit(solution)/shard_map/dot_general | solution.py:26
  124.9 4.3 convolution_convert_fusion.4
  131.0 4.3 multiply_convert_fusion.1
  135.3 4.6 convolution_convert_fusion.3
  139.9 10.5 %collective-permute-done.10 = bf16[512,1024]{1,0:T(8,128)(2,1)S(1)} collective-permute-done((bf16[512,1024]{1,0:T(8,128)(2,1)}, bf16[512,1024]{1,0:T(8,128)(2,1)S(1)}, u32[]{:S(2)}, u32[]{:S(2)}) %collective-permute-start.10) | collective-permute-done | bytes 1048608 | tf_op jit(solution)/shard_map/ppermute | solution.py:205
  150.4 2.6 maximum_select_fusion.1
  153.0 4.3 multiply_convert_fusion
  157.3 4.2 convolution_convert_fusion.2
  163.1 2.7 fusion.78
  165.8 3.0 add_convert_fusion.1
  168.8 5.7 %all_to_all.54 = bf16[2,592,1024]{2,1,0:T(8,128)(2,1)S(1)} all-to-all(bf16[2,592,1024]{2,1,0:T(8,128)(2,1)S(1)} %bitcast.182), channel_id=1, replica_groups={{0,1},{2,3},{4,5},{6,7},{8,9},{10,11},{12,13},{14,15},{16,17},{18,19},{..., dimensions={0} | all-to-all | bytes 4849664 | tf_op jit(solution)/shard_map/all_to_all | solution.py:202
  180.0 4.9 %all-to-all-start.5 = ((bf16[2,592,1024]{2,1,0:T(8,128)(2,1)}), bf16[2,592,1024]{2,1,0:T(8,128)(2,1)}, u32[]{:S(2)}, u32[]{:S(2)}) async-start(bf16[2,592,1024]{2,1,0:T(8,128)(2,1)} %broadcast_in_dim.8), calls=%async_computation.5 | async-start | bytes 4849664 | tf_op jit(solution)/shard_map/all_to_all | solution.py:202
  184.9 2.2 convert_reduce_fusion
  188.1 5.4 %add_convert_fusion.4 = bf16[1024,1024]{1,0:T(8,128)(2,1)S(1)} fusion(bf16[1024,1024]{1,0:T(8,128)(2,1)} %collective-permute-done.11, bf16[1184,1024]{1,0:T(8,128)(2,1)} %get-tuple-element.119, bf16[1184,1024]{1,0:T(8,128)(2,1)S(1)} %bitcast.168), kind=kOutput, calls=%fused_computation.18 | convolution fusion | flops 2488270848 | bytes 9043968 | tf_op jit(solution)/shard_map/dot_general | solution.py:26
  195.8 2.6 convolution_convert_fusion.7
  198.5 2.7 convolution_convert_fusion.8
  203.4 3.3 convolution_convert_fusion.1.do_ref
  206.7 12.9 %attn_bwd.2 = bf16[1184,768]{1,0:T(8,128)(2,1)} custom-call(bf16[1184,768]{1,0:T(8,128)(2,1)} %fusion.7.q_ref.k_ref.v_ref, bf16[1184,768]{1,0:T(8,128)(2,1)} %fusion.7.q_ref.k_ref.v_ref, bf16[1184,768]{1,0:T(8,128)(2,1)} %fusion.7.q_ref.k_ref.v_ref, bf16[1184,256]{1,0:T(8,128)(2,1)} %convolution_convert_fusion.1.do_ref, ...), custom_call_target="tpu_custom_call" | custom-call | flops 7177502720 | bytes 4243456 | tf_op jit(solution)/shard_map/attn_bwd/pallas_call | solution.py:119
  219.6 8.0 %collective-permute-done.12 = bf16[512,1024]{1,0:T(8,128)(2,1)} collective-permute-done((bf16[512,1024]{1,0:T(8,128)(2,1)S(1)}, bf16[512,1024]{1,0:T(8,128)(2,1)}, u32[]{:S(2)}, u32[]{:S(2)}) %collective-permute-start.12) | collective-permute-done | bytes 1048608 | tf_op jit(solution)/shard_map/ppermute | solution.py:205
  231.3 3.8 convolution_convert_fusion.6
  238.0 4.4 fusion.79
  245.4 2.5 add_convert_fusion.3
  249.4 3.4 convolution_convert_fusion.do_ref
  252.8 2.6 collective-permute-start.14
  255.4 13.2 %attn_bwd.3 = bf16[1184,768]{1,0:T(8,128)(2,1)} custom-call(bf16[1184,768]{1,0:T(8,128)(2,1)} %fusion.6.q_ref.k_ref.v_ref, bf16[1184,768]{1,0:T(8,128)(2,1)} %fusion.6.q_ref.k_ref.v_ref, bf16[1184,768]{1,0:T(8,128)(2,1)} %fusion.6.q_ref.k_ref.v_ref, bf16[1184,256]{1,0:T(8,128)(2,1)} %convolution_convert_fusion.do_ref, ...), custom_call_target="tpu_custom_call" | custom-call | flops 7177502720 | bytes 4243456 | tf_op jit(solution)/shard_map/attn_bwd/pallas_call | solution.py:119
  268.5 8.9 %collective-permute-done.14 = bf16[256,1024]{1,0:T(8,128)(2,1)S(1)} collective-permute-done((bf16[256,1024]{1,0:T(8,128)(2,1)S(1)}, bf16[256,1024]{1,0:T(8,128)(2,1)S(1)}, u32[]{:S(2)}, u32[]{:S(2)}) %collective-permute-start.14) | collective-permute-done | bytes 524320 | tf_op jit(solution)/shard_map/ppermute | solution.py:205
  278.3 4.9 %convolution_convert_fusion.5 = bf16[1024,768]{0,1:T(8,128)(2,1)S(1)} fusion(bf16[1184,1024]{1,0:T(8,128)(2,1)} %bitcast.173, bf16[1184,768]{1,0:T(8,128)(2,1)} %attn_bwd.3), kind=kOutput, calls=%fused_computation.97 | convolution fusion | flops 1863057408 | bytes 5816320 | tf_op jit(solution)/shard_map/dot_general | solution.py:26
  287.6 3.0 collective-permute-done.18
  296.1 5.7 %all_to_all.55 = bf16[2,592,1024]{2,1,0:T(8,128)(2,1)S(1)} all-to-all(bf16[2,592,1024]{2,1,0:T(8,128)(2,1)S(1)} %bitcast.181), channel_id=1, replica_groups={{0,1},{2,3},{4,5},{6,7},{8,9},{10,11},{12,13},{14,15},{16,17},{18,19},{..., dimensions={0} | all-to-all | bytes 4849664 | tf_op jit(solution)/shard_map/all_to_all | solution.py:202
  310.2 4.0 all-to-all-start.9
  314.3 5.2 %fusion.80 = f32[1184,1024]{1,0:T(8,128)S(1)} fusion(bf16[1184,1024]{1,0:T(8,128)(2,1)} %get-tuple-element.119, bf16[1024,1024]{1,0:T(8,128)(2,1)} %param.28), kind=kOutput, calls=%fused_computation.231 | convolution fusion | flops 2483027968 | bytes 9371648 | tf_op jit(solution)/shard_map/dot_general | solution.py:26
  319.5 6.8 %convolution_add_fusion = bf16[1184,1024]{1,0:T(8,128)(2,1)} fusion(f32[1184,1024]{1,0:T(8,128)S(1)} %fusion.80, bf16[1024,1024]{1,0:T(8,128)(2,1)S(1)} %copy-done.29, f32[1184,1024]{1,0:T(8,128)} %copy-done.77, f32[1024]{0:T(1024)S(1)} %bitcast.188), kind=kOutput, calls=%fused_computation.16 | convolution fusion | flops 2493939712 | bytes 14225408 | tf_op jit(solution)/shard_map/dot_general | solution.py:26
  328.4 4.9 %all-to-all-start.7 = ((bf16[2,592,1024]{2,1,0:T(8,128)(2,1)}), bf16[2,592,1024]{2,1,0:T(8,128)(2,1)}, u32[]{:S(2)}, u32[]{:S(2)}) async-start(bf16[2,592,1024]{2,1,0:T(8,128)(2,1)} %bitcast.180), calls=%async_computation.7 | async-start | bytes 4849664 | tf_op jit(solution)/shard_map/all_to_all | solution.py:202
  335.4 2.6 collective-permute-start.37
  338.5 2.2 convert_element_type.375
  351.6 4.8 %all-to-all-start.8 = ((bf16[2,1,577,512]{3,2,1,0:T(8,128)(2,1)}), bf16[2,1,577,512]{3,2,1,0:T(8,128)(2,1)}, u32[]{:S(2)}, u32[]{:S(2)}) async-start(bf16[2,1,577,512]{3,2,1,0:T(8,128)(2,1)} %pad_maximum_fusion.3), calls=%async_computation.8 | async-start | bytes 2392064 | tf_op jit(solution)/shard_map/all_to_all | solution.py:202
  356.4 7.2 %collective-permute-done.34 = f32[7680]{0:T(1024)S(1)} collective-permute-done((f32[7680]{0:T(1024)S(1)}, f32[7680]{0:T(1024)S(1)}, u32[]{:S(2)}, u32[]{:S(2)}) %collective-permute-start.34) | collective-permute-done | bytes 30752 | tf_op jit(solution)/shard_map/ppermute | solution.py:205
  380.0 2.5 collective-permute-start.29
  383.7 4.6 %collective-permute-done.25 = bf16[128,1024]{0,1:T(8,128)(2,1)} collective-permute-done((bf16[128,1024]{0,1:T(8,128)(2,1)}, bf16[128,1024]{0,1:T(8,128)(2,1)}, u32[]{:S(2)}, u32[]{:S(2)}) %collective-permute-start.25) | collective-permute-done | bytes 262176 | tf_op jit(solution)/shard_map/ppermute | solution.py:205
  391.9 2.3 collective-permute-start.30
  396.3 6.6 %collective-permute-done.26 = bf16[128,1024]{0,1:T(8,128)(2,1)S(1)} collective-permute-done((bf16[128,1024]{0,1:T(8,128)(2,1)S(1)}, bf16[128,1024]{0,1:T(8,128)(2,1)S(1)}, u32[]{:S(2)}, u32[]{:S(2)}) %collective-permute-start.26) | collective-permute-done | bytes 262176 | tf_op jit(solution)/shard_map/ppermute | solution.py:205
  406.1 4.4 fusion.43
  410.4 4.5 collective-permute-done.38
  425.0 23.8 %collective-permute-done.32 = bf16[256,1024]{0,1:T(8,128)(2,1)S(1)} collective-permute-done((bf16[256,1024]{0,1:T(8,128)(2,1)S(1)}, bf16[256,1024]{0,1:T(8,128)(2,1)S(1)}, u32[]{:S(2)}, u32[]{:S(2)}) %collective-permute-start.32) | collective-permute-done | bytes 524320 | tf_op jit(solution)/shard_map/ppermute | solution.py:205
  453.0 3.7 copy.51
  456.7 5.3 %fusion.42 = f32[1024,1024]{1,0:T(8,128)} fusion(bf16[512,1024]{1,0:T(8,128)(2,1)} %collective-permute-done.39, bf16[512,1024]{1,0:T(8,128)(2,1)} %maximum_select_fusion.8, pred[]{:T(512)S(6)} %eq.67), kind=kLoop, calls=%fused_computation.87 | loop fusion | flops 10485760 | bytes 6291457 | tf_op jit(solution)/shard_map/convert_element_type | solution.py:320
  (373 shorter events, 134.5 us)
Async XLA Ops:
  0.6 16.6 %copy-start = (bf16[1024,1024]{1,0:T(8,128)(2,1)S(1)}, bf16[1024,1024]{1,0:T(8,128)(2,1)}, u32[]{:S(2)}) copy-start(bf16[1024,1024]{1,0:T(8,128)(2,1)} %param.26) | copy-start | bytes 6291460
  4.5 16.7 %collective-permute-start = (bf16[2,577,256]{2,0,1:T(2,128)(2,1)}, bf16[2,577,256]{2,0,1:T(2,128)(2,1)}, u32[]{:S(2)}, u32[]{:S(2)}) collective-permute-start(bf16[2,577,256]{2,0,1:T(2,128)(2,1)} %get-tuple-element.230), channel_id=1, source_target_pairs={{0,2},{1,3},{2,0},{3,1},{4,6},{5,7},{6,4},{7,5},{8,10},{9,11},{10,... | collective-permute-start | bytes 1772552 | tf_op jit(solution)/shard_map/ppermute | solution.py:195
  13.6 16.2 %copy-start.54 = (f32[1024]{0:T(1024)}, f32[1024]{0:T(1024)S(1)}, u32[]{:S(2)}) copy-start(f32[1024]{0:T(1024)S(1)} %convert_element_type.308) | copy-start | bytes 12292
  27.6 71.6 %copy-start.4 = (bf16[1,592,1024]{2,1,0:T(8,128)(2,1)}, bf16[1,592,1024]{2,1,0:T(8,128)(2,1)S(1)}, u32[]{:S(2)}) copy-start(bf16[1,592,1024]{2,1,0:T(8,128)(2,1)S(1)} %get-tuple-element.190) | copy-start | bytes 3637252
  28.1 19.8 %collective-permute-start.1 = (bf16[512,768]{1,0:T(8,128)(2,1)S(1)}, bf16[512,768]{1,0:T(8,128)(2,1)}, u32[]{:S(2)}, u32[]{:S(2)}) collective-permute-start(bf16[512,768]{1,0:T(8,128)(2,1)S(1)} %constant_dynamic-slice_fusion.13), channel_id=1, source_target_pairs={{0,2},{1,3},{2,0},{3,1},{4,6},{5,7},{6,4},{7,5},{8,10},{9,11},{10,... | collective-permute-start | bytes 2359304 | tf_op jit(solution)/shard_map/ppermute | solution.py:195
  37.1 12.5 %copy-start.23 = (bf16[2,577,256]{2,0,1:T(2,128)(2,1)S(1)}, bf16[2,577,256]{2,0,1:T(2,128)(2,1)}, u32[]{:S(2)}) copy-start(bf16[2,577,256]{2,0,1:T(2,128)(2,1)} %get-tuple-element.227) | copy-start | bytes 1772548
  37.1 13.4 %copy-start.70 = (bf16[1024]{0:T(1024)(128)(2,1)S(1)}, bf16[1024]{0:T(1024)(128)(2,1)}, u32[]{:S(2)}) copy-start(bf16[1024]{0:T(1024)(128)(2,1)} %param.24) | copy-start | bytes 6148
  37.1 13.3 %copy-start.71 = (bf16[1024]{0:T(1024)(128)(2,1)S(1)}, bf16[1024]{0:T(1024)(128)(2,1)}, u32[]{:S(2)}) copy-start(bf16[1024]{0:T(1024)(128)(2,1)} %param.21) | copy-start | bytes 6148
  37.1 13.4 %copy-start.72 = (bf16[1024]{0:T(1024)(128)(2,1)S(1)}, bf16[1024]{0:T(1024)(128)(2,1)}, u32[]{:S(2)}) copy-start(bf16[1024]{0:T(1024)(128)(2,1)} %param.25) | copy-start | bytes 6148
  37.1 13.4 %copy-start.73 = (bf16[1024]{0:T(1024)(128)(2,1)S(1)}, bf16[1024]{0:T(1024)(128)(2,1)}, u32[]{:S(2)}) copy-start(bf16[1024]{0:T(1024)(128)(2,1)} %param.29) | copy-start | bytes 6148
  37.1 14.0 %copy-start.75 = (s32[4]{0:T(128)S(1)}, s32[4]{0:T(128)}, u32[]{:S(2)}) copy-start(s32[4]{0:T(128)} %param.17) | copy-start | bytes 52
  47.8 19.0 %collective-permute-start.2 = (bf16[512,768]{1,0:T(8,128)(2,1)}, bf16[512,768]{1,0:T(8,128)(2,1)}, u32[]{:S(2)}, u32[]{:S(2)}) collective-permute-start(bf16[512,768]{1,0:T(8,128)(2,1)} %collective-permute-done.1), channel_id=1, source_target_pairs={{0,4},{4,0},{8,12},{12,8},{16,20},{20,16},{24,28},{28,24},{1,5},{5... | collective-permute-start | bytes 2359304 | tf_op jit(solution)/shard_map/ppermute | solution.py:205
  51.2 14.6 %collective-permute-start.3 = (bf16[144,1024]{1,0:T(8,128)(2,1)}, bf16[144,1024]{1,0:T(8,128)(2,1)}, u32[]{:S(2)}, u32[]{:S(2)}) collective-permute-start(bf16[144,1024]{1,0:T(8,128)(2,1)} %pad_maximum_fusion.9), channel_id=1, source_target_pairs={{0,2},{1,3},{2,0},{3,1},{4,6},{5,7},{6,4},{7,5},{8,10},{9,11},{10,... | collective-permute-start | bytes 884744 | tf_op jit(solution)/shard_map/ppermute | solution.py:195
  52.7 35.1 %collective-permute-start.4 = (bf16[512,1024]{1,0:T(8,128)(2,1)}, bf16[512,1024]{1,0:T(8,128)(2,1)}, u32[]{:S(2)}, u32[]{:S(2)}) collective-permute-start(bf16[512,1024]{1,0:T(8,128)(2,1)} %constant_dynamic-slice_fusion.11), channel_id=1, source_target_pairs={{0,2},{1,3},{2,0},{3,1},{4,6},{5,7},{6,4},{7,5},{8,10},{9,11},{10,... | collective-permute-start | bytes 3145736 | tf_op jit(solution)/shard_map/ppermute | solution.py:195
  71.6 16.2 %collective-permute-start.5 = (bf16[128,1024]{1,0:T(8,128)(2,1)}, bf16[128,1024]{1,0:T(8,128)(2,1)}, u32[]{:S(2)}, u32[]{:S(2)}) collective-permute-start(bf16[128,1024]{1,0:T(8,128)(2,1)} %slice.244), channel_id=1, source_target_pairs={{0,4},{4,0},{8,12},{12,8},{16,20},{20,16},{24,28},{28,24},{1,5},{5... | collective-permute-start | bytes 786440 | tf_op jit(solution)/shard_map/ppermute | solution.py:205
  76.7 30.2 %collective-permute-start.6 = (bf16[2,577,256]{2,1,0:T(8,128)(2,1)}, bf16[2,577,256]{2,1,0:T(8,128)(2,1)}, u32[]{:S(2)}, u32[]{:S(2)}) collective-permute-start(bf16[2,577,256]{2,1,0:T(8,128)(2,1)} %copy.53), channel_id=1, source_target_pairs={{0,2},{1,3},{2,0},{3,1},{4,6},{5,7},{6,4},{7,5},{8,10},{9,11},{10,... | collective-permute-start | bytes 1772552 | tf_op jit(solution)/shard_map/ppermute | solution.py:195
  78.2 46.4 %collective-permute-start.9 = (bf16[512,1024]{1,0:T(8,128)(2,1)}, bf16[512,1024]{1,0:T(8,128)(2,1)}, u32[]{:S(2)}, u32[]{:S(2)}) collective-permute-start(bf16[512,1024]{1,0:T(8,128)(2,1)} %constant_dynamic-slice_fusion.10), channel_id=1, source_target_pairs={{0,2},{1,3},{2,0},{3,1},{4,6},{5,7},{6,4},{7,5},{8,10},{9,11},{10,... | collective-permute-start | bytes 3145736 | tf_op jit(solution)/shard_map/ppermute | solution.py:195
  79.4 73.6 %copy-start.66 = (f32[1,1024]{1,0:T(1,128)}, f32[1,1024]{1,0:T(1,128)S(1)}, u32[]{:S(2)}) copy-start(f32[1,1024]{1,0:T(1,128)S(1)} %slice_convert_fusion) | copy-start | bytes 12292
  89.2 22.9 %collective-permute-start.7 = (bf16[512,1024]{1,0:T(8,128)(2,1)}, bf16[512,1024]{1,0:T(8,128)(2,1)S(1)}, u32[]{:S(2)}, u32[]{:S(2)}) collective-permute-start(bf16[512,1024]{1,0:T(8,128)(2,1)} %collective-permute-done.4), channel_id=1, source_target_pairs={{0,4},{4,0},{8,12},{12,8},{16,20},{20,16},{24,28},{28,24},{1,5},{5... | collective-permute-start | bytes 3145736 | tf_op jit(solution)/shard_map/ppermute | solution.py:205
  99.8 77.1 %copy-start.2 = (f32[592,1024]{1,0:T(8,128)}, f32[592,1024]{1,0:T(8,128)S(1)}, u32[]{:S(2)}) copy-start(f32[592,1024]{1,0:T(8,128)S(1)} %get-tuple-element.188) | copy-start | bytes 7274500
  116.0 7.5 %collective-permute-start.8 = (bf16[2,577,512]{2,1,0:T(8,128)(2,1)S(1)}, bf16[2,577,512]{2,1,0:T(8,128)(2,1)S(1)}, u32[]{:S(2)}, u32[]{:S(2)}) collective-permute-start(bf16[2,577,512]{2,1,0:T(8,128)(2,1)S(1)} %constant_dynamic-update-slice_fusion), channel_id=1, source_target_pairs={{0,1},{1,0},{2,3},{3,2},{4,5},{5,4},{6,7},{7,6},{8,9},{9,8},{10,11... | collective-permute-start | bytes 3545096 | tf_op jit(solution)/shard_map/ppermute | solution.py:198
  118.7 34.2 %copy-start.77 = (f32[1184,1024]{1,0:T(8,128)}, f32[1184,1024]{1,0:T(8,128)S(1)}, u32[]{:S(2)}) copy-start(f32[1184,1024]{1,0:T(8,128)S(1)} %fusion.77) | copy-start | bytes 14548996
  124.5 52.3 %copy-start.8 = (bf16[2,592,1024]{2,1,0:T(8,128)(2,1)}, bf16[2,592,1024]{2,1,0:T(8,128)(2,1)S(1)}, u32[]{:S(2)}) copy-start(bf16[2,592,1024]{2,1,0:T(8,128)(2,1)S(1)} %fusion.28) | copy-start | bytes 7274500
  124.5 25.8 %collective-permute-start.10 = (bf16[512,1024]{1,0:T(8,128)(2,1)}, bf16[512,1024]{1,0:T(8,128)(2,1)S(1)}, u32[]{:S(2)}, u32[]{:S(2)}) collective-permute-start(bf16[512,1024]{1,0:T(8,128)(2,1)} %collective-permute-done.9), channel_id=1, source_target_pairs={{0,4},{4,0},{8,12},{12,8},{16,20},{20,16},{24,28},{28,24},{1,5},{5... | collective-permute-start | bytes 3145736 | tf_op jit(solution)/shard_map/ppermute | solution.py:205
  129.2 58.5 %collective-permute-start.11 = (bf16[1024,1024]{1,0:T(8,128)(2,1)}, bf16[1024,1024]{1,0:T(8,128)(2,1)}, u32[]{:S(2)}, u32[]{:S(2)}) collective-permute-start(bf16[1024,1024]{1,0:T(8,128)(2,1)} %convolution_convert_fusion.4), channel_id=1, source_target_pairs={{0,2},{1,3},{2,0},{3,1},{4,6},{5,7},{6,4},{7,5},{8,10},{9,11},{10,... | collective-permute-start | bytes 6291464 | tf_op jit(solution)/shard_map/ppermute | solution.py:195
  135.3 27.8 %copy-start.20 = (bf16[1184,1024]{1,0:T(8,128)(2,1)}, bf16[1184,1024]{1,0:T(8,128)(2,1)S(1)}, u32[]{:S(2)}) copy-start(bf16[1184,1024]{1,0:T(8,128)(2,1)S(1)} %multiply_convert_fusion.1) | copy-start | bytes 7274500
  161.6 83.9 %collective-permute-start.15 = (bf16[1024,1024]{1,0:T(8,128)(2,1)}, bf16[1024,1024]{1,0:T(8,128)(2,1)}, u32[]{:S(2)}, u32[]{:S(2)}) collective-permute-start(bf16[1024,1024]{1,0:T(8,128)(2,1)} %convolution_convert_fusion.2), channel_id=1, source_target_pairs={{0,2},{1,3},{2,0},{3,1},{4,6},{5,7},{6,4},{7,5},{8,10},{9,11},{10,... | collective-permute-start | bytes 6291464 | tf_op jit(solution)/shard_map/ppermute | solution.py:195
  180.0 15.8 %all-to-all-start.5 = ((bf16[2,592,1024]{2,1,0:T(8,128)(2,1)}), bf16[2,592,1024]{2,1,0:T(8,128)(2,1)}, u32[]{:S(2)}, u32[]{:S(2)}) async-start(bf16[2,592,1024]{2,1,0:T(8,128)(2,1)} %broadcast_in_dim.8), calls=%async_computation.5 | async-start | bytes 4849664 | tf_op jit(solution)/shard_map/all_to_all | solution.py:202
  202.0 25.7 %collective-permute-start.12 = (bf16[512,1024]{1,0:T(8,128)(2,1)S(1)}, bf16[512,1024]{1,0:T(8,128)(2,1)}, u32[]{:S(2)}, u32[]{:S(2)}) collective-permute-start(bf16[512,1024]{1,0:T(8,128)(2,1)S(1)} %copy-done.44), channel_id=1, source_target_pairs={{0,4},{4,0},{8,12},{12,8},{16,20},{20,16},{24,28},{28,24},{1,5},{5... | collective-permute-start | bytes 3145736 | tf_op jit(solution)/shard_map/ppermute | solution.py:205
  219.6 11.7 %copy-start.19 = (bf16[2,592,1024]{2,1,0:T(8,128)(2,1)S(1)}, bf16[2,592,1024]{2,1,0:T(8,128)(2,1)}, u32[]{:S(2)}) copy-start(bf16[2,592,1024]{2,1,0:T(8,128)(2,1)} %copy-done.17) | copy-start | bytes 7274500
  229.7 19.4 %collective-permute-start.13 = (bf16[256,1024]{1,0:T(8,128)(2,1)S(1)}, bf16[256,1024]{1,0:T(8,128)(2,1)S(1)}, u32[]{:S(2)}, u32[]{:S(2)}) collective-permute-start(bf16[256,1024]{1,0:T(8,128)(2,1)S(1)} %constant_dynamic-slice_fusion.6), channel_id=1, source_target_pairs={{0,8},{4,12},{8,0},{12,4},{16,24},{20,28},{24,16},{28,20},{1,9},{5... | collective-permute-start | bytes 1572872 | tf_op jit(solution)/shard_map/ppermute | solution.py:205
  243.4 40.0 %collective-permute-start.17 = (bf16[512,1024]{0,1:T(8,128)(2,1)}, bf16[512,1024]{0,1:T(8,128)(2,1)}, u32[]{:S(2)}, u32[]{:S(2)}) collective-permute-start(bf16[512,1024]{0,1:T(8,128)(2,1)} %pad_maximum_fusion.7), channel_id=1, source_target_pairs={{0,2},{1,3},{2,0},{3,1},{4,6},{5,7},{6,4},{7,5},{8,10},{9,11},{10,... | collective-permute-start | bytes 3145736 | tf_op jit(solution)/shard_map/ppermute | solution.py:195
  243.9 46.7 %collective-permute-start.18 = (bf16[512,1024]{0,1:T(8,128)(2,1)}, bf16[512,1024]{0,1:T(8,128)(2,1)}, u32[]{:S(2)}, u32[]{:S(2)}) collective-permute-start(bf16[512,1024]{0,1:T(8,128)(2,1)} %pad_maximum_fusion.8), channel_id=1, source_target_pairs={{0,2},{1,3},{2,0},{3,1},{4,6},{5,7},{6,4},{7,5},{8,10},{9,11},{10,... | collective-permute-start | bytes 3145736 | tf_op jit(solution)/shard_map/ppermute | solution.py:195
  252.8 24.6 %collective-permute-start.14 = (bf16[256,1024]{1,0:T(8,128)(2,1)S(1)}, bf16[256,1024]{1,0:T(8,128)(2,1)S(1)}, u32[]{:S(2)}, u32[]{:S(2)}) collective-permute-start(bf16[256,1024]{1,0:T(8,128)(2,1)S(1)} %add_convert_fusion.15), channel_id=1, source_target_pairs={{0,16},{4,20},{8,24},{12,28},{16,0},{20,4},{24,8},{28,12},{1,17},{... | collective-permute-start | bytes 1572872 | tf_op jit(solution)/shard_map/ppermute | solution.py:205
  277.4 16.5 %slice-start = ((s8[4849664]{0:T(1024)(128)(4,1)}), s8[4194304]{0:T(1024)(128)(4,1)S(1)}, s32[]{:S(2)}) async-start(s8[4849664]{0:T(1024)(128)(4,1)} %bitcast.190), calls=%async_computation.10 | async-start | bytes 8388608
  277.6 16.3 %slice-start.1 = ((s8[4849664]{0:T(1024)(128)(4,1)}), s8[655360]{0:T(1024)(128)(4,1)S(1)}, s32[]{:S(2)}) async-start(s8[4849664]{0:T(1024)(128)(4,1)} %bitcast.190), calls=%async_computation.11 | async-start | bytes 1310720
  277.6 28.0 %collective-permute-start.19 = (bf16[256,1024]{1,0:T(8,128)(2,1)S(1)}, bf16[256,1024]{1,0:T(8,128)(2,1)S(1)}, u32[]{:S(2)}, u32[]{:S(2)}) collective-permute-start(bf16[256,1024]{1,0:T(8,128)(2,1)S(1)} %add_convert_fusion.14), channel_id=1, source_target_pairs={{0,8},{4,12},{8,0},{12,4},{16,24},{20,28},{24,16},{28,20},{1,9},{5... | collective-permute-start | bytes 1572872 | tf_op jit(solution)/shard_map/ppermute | solution.py:205
  277.7 29.4 %collective-permute-start.16 = (bf16[512,1024]{1,0:T(8,128)(2,1)}, bf16[512,1024]{1,0:T(8,128)(2,1)S(1)}, u32[]{:S(2)}, u32[]{:S(2)}) collective-permute-start(bf16[512,1024]{1,0:T(8,128)(2,1)} %constant_dynamic-slice_fusion.5), channel_id=1, source_target_pairs={{0,4},{4,0},{8,12},{12,8},{16,20},{20,16},{24,28},{28,24},{1,5},{5... | collective-permute-start | bytes 3145736 | tf_op jit(solution)/shard_map/ppermute | solution.py:205
  307.9 19.3 %collective-permute-start.20 = (bf16[256,1024]{1,0:T(8,128)(2,1)S(1)}, bf16[256,1024]{1,0:T(8,128)(2,1)}, u32[]{:S(2)}, u32[]{:S(2)}) collective-permute-start(bf16[256,1024]{1,0:T(8,128)(2,1)S(1)} %constant_dynamic-slice_fusion.4), channel_id=1, source_target_pairs={{0,8},{4,12},{8,0},{12,4},{16,24},{20,28},{24,16},{28,20},{1,9},{5... | collective-permute-start | bytes 1572872 | tf_op jit(solution)/shard_map/ppermute | solution.py:205
  308.4 33.4 %collective-permute-start.22 = (bf16[256,1024]{0,1:T(8,128)(2,1)}, bf16[256,1024]{0,1:T(8,128)(2,1)}, u32[]{:S(2)}, u32[]{:S(2)}) collective-permute-start(bf16[256,1024]{0,1:T(8,128)(2,1)} %constant_dynamic-slice_fusion.3), channel_id=1, source_target_pairs={{0,4},{4,0},{8,12},{12,8},{16,20},{20,16},{24,28},{28,24},{1,5},{5... | collective-permute-start | bytes 1572872 | tf_op jit(solution)/shard_map/ppermute | solution.py:205
  310.2 16.0 %all-to-all-start.9 = ((bf16[2,1,577,512]{3,2,1,0:T(8,128)(2,1)}), bf16[2,1,577,512]{3,2,1,0:T(8,128)(2,1)S(1)}, u32[]{:S(2)}, u32[]{:S(2)}) async-start(bf16[2,1,577,512]{3,2,1,0:T(8,128)(2,1)} %pad_maximum_fusion.4), calls=%async_computation.9 | async-start | bytes 2392064 | tf_op jit(solution)/shard_map/all_to_all | solution.py:202
  328.4 10.1 %all-to-all-start.7 = ((bf16[2,592,1024]{2,1,0:T(8,128)(2,1)}), bf16[2,592,1024]{2,1,0:T(8,128)(2,1)}, u32[]{:S(2)}, u32[]{:S(2)}) async-start(bf16[2,592,1024]{2,1,0:T(8,128)(2,1)} %bitcast.180), calls=%async_computation.7 | async-start | bytes 4849664 | tf_op jit(solution)/shard_map/all_to_all | solution.py:202
  333.4 10.6 %collective-permute-start.21 = (f32[6144]{0:T(1024)}, f32[6144]{0:T(1024)}, u32[]{:S(2)}, u32[]{:S(2)}) collective-permute-start(f32[6144]{0:T(1024)} %copy-done.58), channel_id=1, source_target_pairs={{0,1},{1,0},{2,3},{3,2},{4,5},{5,4},{6,7},{7,6},{8,9},{9,8},{10,11... | collective-permute-start | bytes 73736 | tf_op jit(solution)/shard_map/ppermute | solution.py:198
  333.9 44.2 %collective-permute-start.28 = (bf16[256,1024]{0,1:T(8,128)(2,1)}, bf16[256,1024]{0,1:T(8,128)(2,1)}, u32[]{:S(2)}, u32[]{:S(2)}) collective-permute-start(bf16[256,1024]{0,1:T(8,128)(2,1)} %constant_dynamic-slice_fusion.2), channel_id=1, source_target_pairs={{0,4},{4,0},{8,12},{12,8},{16,20},{20,16},{24,28},{28,24},{1,5},{5... | collective-permute-start | bytes 1572872 | tf_op jit(solution)/shard_map/ppermute | solution.py:205
  335.4 58.8 %collective-permute-start.37 = (bf16[256,1024]{1,0:T(8,128)(2,1)S(1)}, bf16[256,1024]{1,0:T(8,128)(2,1)}, u32[]{:S(2)}, u32[]{:S(2)}) collective-permute-start(bf16[256,1024]{1,0:T(8,128)(2,1)S(1)} %add_convert_fusion.13), channel_id=1, source_target_pairs={{0,16},{4,20},{8,24},{12,28},{16,0},{20,4},{24,8},{28,12},{1,17},{... | collective-permute-start | bytes 1572872 | tf_op jit(solution)/shard_map/ppermute | solution.py:205
  338.0 68.1 %collective-permute-start.40 = (bf16[512,1024]{1,0:T(8,128)(2,1)}, bf16[512,1024]{1,0:T(8,128)(2,1)}, u32[]{:S(2)}, u32[]{:S(2)}) collective-permute-start(bf16[512,1024]{1,0:T(8,128)(2,1)} %maximum_select_fusion.5), channel_id=1, source_target_pairs={{0,4},{4,0},{8,12},{12,8},{16,20},{20,16},{24,28},{28,24},{1,5},{5... | collective-permute-start | bytes 3145736 | tf_op jit(solution)/shard_map/ppermute | solution.py:205
  344.8 4.0 collective-permute-start.33
  345.4 29.3 %collective-permute-start.24 = (bf16[128,1024]{0,1:T(8,128)(2,1)}, bf16[128,1024]{0,1:T(8,128)(2,1)}, u32[]{:S(2)}, u32[]{:S(2)}) collective-permute-start(bf16[128,1024]{0,1:T(8,128)(2,1)} %constant_dynamic-slice_fusion.1), channel_id=1, source_target_pairs={{0,8},{4,12},{8,0},{12,4},{16,24},{20,28},{24,16},{28,20},{1,9},{5... | collective-permute-start | bytes 786440 | tf_op jit(solution)/shard_map/ppermute | solution.py:205
  348.8 14.8 %collective-permute-start.34 = (f32[7680]{0:T(1024)S(1)}, f32[7680]{0:T(1024)S(1)}, u32[]{:S(2)}, u32[]{:S(2)}) collective-permute-start(f32[7680]{0:T(1024)S(1)} %fusion.54), channel_id=1, source_target_pairs={{0,8},{4,12},{8,0},{12,4},{16,24},{20,28},{24,16},{28,20},{1,9},{5... | collective-permute-start | bytes 92168 | tf_op jit(solution)/shard_map/ppermute | solution.py:205
  351.6 19.2 %copy-start.10 = (bf16[2,577,256]{2,1,0:T(8,128)(2,1)S(1)}, bf16[2,577,256]{2,1,0:T(8,128)(2,1)}, u32[]{:S(2)}) copy-start(bf16[2,577,256]{2,1,0:T(8,128)(2,1)} %get-tuple-element.220) | copy-start | bytes 1772548
  351.6 13.7 %all-to-all-start.8 = ((bf16[2,1,577,512]{3,2,1,0:T(8,128)(2,1)}), bf16[2,1,577,512]{3,2,1,0:T(8,128)(2,1)}, u32[]{:S(2)}, u32[]{:S(2)}) async-start(bf16[2,1,577,512]{3,2,1,0:T(8,128)(2,1)} %pad_maximum_fusion.3), calls=%async_computation.8 | async-start | bytes 2392064 | tf_op jit(solution)/shard_map/all_to_all | solution.py:202
  363.6 4.9 %collective-permute-start.35 = (f32[7680]{0:T(1024)S(1)}, f32[7680]{0:T(1024)}, u32[]{:S(2)}, u32[]{:S(2)}) collective-permute-start(f32[7680]{0:T(1024)S(1)} %add.367), channel_id=1, source_target_pairs={{0,16},{4,20},{8,24},{12,28},{16,0},{20,4},{24,8},{28,12},{1,17},{... | collective-permute-start | bytes 92168 | tf_op jit(solution)/shard_map/ppermute | solution.py:205
  369.3 3.9 collective-permute-start.36
  373.2 46.5 %collective-permute-start.23 = (bf16[2,577,512]{2,0,1:T(2,128)(2,1)}, bf16[2,577,512]{2,0,1:T(2,128)(2,1)}, u32[]{:S(2)}, u32[]{:S(2)}) collective-permute-start(bf16[2,577,512]{2,0,1:T(2,128)(2,1)} %copy.46), channel_id=1, source_target_pairs={{0,2},{1,3},{2,0},{3,1},{4,6},{5,7},{6,4},{7,5},{8,10},{9,11},{10,... | collective-permute-start | bytes 3545096 | tf_op jit(solution)/shard_map/ppermute | solution.py:195
  376.5 11.9 %collective-permute-start.25 = (bf16[128,1024]{0,1:T(8,128)(2,1)}, bf16[128,1024]{0,1:T(8,128)(2,1)}, u32[]{:S(2)}, u32[]{:S(2)}) collective-permute-start(bf16[128,1024]{0,1:T(8,128)(2,1)} %add_convert_fusion.19), channel_id=1, source_target_pairs={{0,16},{4,20},{8,24},{12,28},{16,0},{20,4},{24,8},{28,12},{1,17},{... | collective-permute-start | bytes 786440 | tf_op jit(solution)/shard_map/ppermute | solution.py:205
  380.0 10.8 %collective-permute-start.29 = (bf16[128,1024]{0,1:T(8,128)(2,1)}, bf16[128,1024]{0,1:T(8,128)(2,1)}, u32[]{:S(2)}, u32[]{:S(2)}) collective-permute-start(bf16[128,1024]{0,1:T(8,128)(2,1)} %constant_dynamic-slice_fusion), channel_id=1, source_target_pairs={{0,8},{4,12},{8,0},{12,4},{16,24},{20,28},{24,16},{28,20},{1,9},{5... | collective-permute-start | bytes 786440 | tf_op jit(solution)/shard_map/ppermute | solution.py:205
  383.7 22.3 %copy-start.11 = (bf16[512,1024]{1,0:T(8,128)(2,1)S(1)}, bf16[512,1024]{1,0:T(8,128)(2,1)}, u32[]{:S(2)}) copy-start(bf16[512,1024]{1,0:T(8,128)(2,1)} %maximum_select_fusion.5) | copy-start | bytes 3145732
  389.5 13.4 %collective-permute-start.26 = (bf16[128,1024]{0,1:T(8,128)(2,1)S(1)}, bf16[128,1024]{0,1:T(8,128)(2,1)S(1)}, u32[]{:S(2)}, u32[]{:S(2)}) collective-permute-start(bf16[128,1024]{0,1:T(8,128)(2,1)S(1)} %add_convert_fusion.18), channel_id=1, source_target_pairs={{0,8},{4,12},{8,0},{12,4},{16,24},{20,28},{24,16},{28,20},{1,9},{5... | collective-permute-start | bytes 786440 | tf_op jit(solution)/shard_map/ppermute | solution.py:205
  391.9 12.4 %collective-permute-start.30 = (bf16[128,1024]{0,1:T(8,128)(2,1)S(1)}, bf16[128,1024]{0,1:T(8,128)(2,1)S(1)}, u32[]{:S(2)}, u32[]{:S(2)}) collective-permute-start(bf16[128,1024]{0,1:T(8,128)(2,1)S(1)} %add_convert_fusion.17), channel_id=1, source_target_pairs={{0,16},{4,20},{8,24},{12,28},{16,0},{20,4},{24,8},{28,12},{1,17},{... | collective-permute-start | bytes 786440 | tf_op jit(solution)/shard_map/ppermute | solution.py:205
  395.4 19.4 %collective-permute-start.38 = (bf16[256,1024]{1,0:T(8,128)(2,1)S(1)}, bf16[256,1024]{1,0:T(8,128)(2,1)S(1)}, u32[]{:S(2)}, u32[]{:S(2)}) collective-permute-start(bf16[256,1024]{1,0:T(8,128)(2,1)S(1)} %add_convert_fusion.10), channel_id=1, source_target_pairs={{0,8},{4,12},{8,0},{12,4},{16,24},{20,28},{24,16},{28,20},{1,9},{5... | collective-permute-start | bytes 1572872 | tf_op jit(solution)/shard_map/ppermute | solution.py:205
  403.1 21.6 %collective-permute-start.27 = (bf16[256,1024]{0,1:T(8,128)(2,1)S(1)}, bf16[256,1024]{0,1:T(8,128)(2,1)S(1)}, u32[]{:S(2)}, u32[]{:S(2)}) collective-permute-start(bf16[256,1024]{0,1:T(8,128)(2,1)S(1)} %maximum_select_fusion.10), channel_id=1, source_target_pairs={{0,4},{4,0},{8,12},{12,8},{16,20},{20,16},{24,28},{28,24},{1,5},{5... | collective-permute-start | bytes 1572872 | tf_op jit(solution)/shard_map/ppermute | solution.py:205
  404.4 14.0 %collective-permute-start.31 = (bf16[128,1024]{0,1:T(8,128)(2,1)S(1)}, bf16[128,1024]{0,1:T(8,128)(2,1)S(1)}, u32[]{:S(2)}, u32[]{:S(2)}) collective-permute-start(bf16[128,1024]{0,1:T(8,128)(2,1)S(1)} %add_convert_fusion.16), channel_id=1, source_target_pairs={{0,8},{4,12},{8,0},{12,4},{16,24},{20,28},{24,16},{28,20},{1,9},{5... | collective-permute-start | bytes 786440 | tf_op jit(solution)/shard_map/ppermute | solution.py:205
  416.4 40.3 %collective-permute-start.39 = (bf16[512,1024]{1,0:T(8,128)(2,1)}, bf16[512,1024]{1,0:T(8,128)(2,1)}, u32[]{:S(2)}, u32[]{:S(2)}) collective-permute-start(bf16[512,1024]{1,0:T(8,128)(2,1)} %maximum_select_fusion.8), channel_id=1, source_target_pairs={{0,4},{4,0},{8,12},{12,8},{16,20},{20,16},{24,28},{28,24},{1,5},{5... | collective-permute-start | bytes 3145736 | tf_op jit(solution)/shard_map/ppermute | solution.py:205
  418.6 30.2 %collective-permute-start.32 = (bf16[256,1024]{0,1:T(8,128)(2,1)S(1)}, bf16[256,1024]{0,1:T(8,128)(2,1)S(1)}, u32[]{:S(2)}, u32[]{:S(2)}) collective-permute-start(bf16[256,1024]{0,1:T(8,128)(2,1)S(1)} %maximum_select_fusion.11), channel_id=1, source_target_pairs={{0,4},{4,0},{8,12},{12,8},{16,20},{20,16},{24,28},{28,24},{1,5},{5... | collective-permute-start | bytes 1572872 | tf_op jit(solution)/shard_map/ppermute | solution.py:205
  (61 other events, 253.1 us)

commit v4 on v3

--- a/solution.py
+++ b/solution.py
@@ -216,11 +216,11 @@
     def core_rows(value, arrived, whole):
         mine = jnp.concatenate([my_images(value, 0)] + arrived, axis=2)
         if split and not whole:
-            both = core_trade(mine.reshape(2, near, seq, chips * width))
-            both = [both[0], both[1]]
+            got = core_swap(by_core(mine[near:], mine[:near]))
+            mine = by_core(mine[:near], mine[near:])
         else:
             got = core_swap(mine)
-            both = [by_core(mine, got), by_core(got, mine)]
+        both = [by_core(mine, got), by_core(got, mine)]
         both = [[b[:, :, a * width : (a + 1) * width] for a in range(chips)] for b in both]
         parts = []
         for a in range(chips):
@@ -317,7 +317,7 @@
                 jnp.concatenate([total, got], 0),
                 jnp.concatenate([got, total], 0),
             )
-        return total.astype(F32)
+        return total
 
     def begin(blocks, dp_first=False):
         flow = reduce_blocks(blocks, dp_first)
@@ -373,7 +373,8 @@
     x32 = core_rows(inputs, x_got, False).astype(F32)
     mean_one, inv_one = norm_stats(x32)
     unit_one = (x32 - mean_one) * inv_one
-    normed_one = complete((unit_one * gain_one + shift_one).astype(BF16))
+    normed_one = (unit_one * gain_one + shift_one).astype(BF16)
+    normed_one = complete(normed_one)
     qkv = [project(cat_qkv, small)]
     qkv[0], q_got = hold(qkv[0], q_got)
     q_more = other_halves(q_got)
@@ -430,7 +431,10 @@
     down_blocks = [mm(first_act, dy, TN).astype(BF16)] + down_sent
     d_hidden = [(mm(dy, w_down, NT) * slopes[0]).astype(BF16)]
     up_blocks = [mm(normed_two, d_hidden[0], TN).astype(BF16)]
-    up_blocks[0], d_more = lax.optimization_barrier((up_blocks[0], d_more))
+    part_two = mm(d_hidden[0], w_up, NT)
+    up_blocks[0], down_blocks[0], part_two, d_more = hold(
+        up_blocks[0], down_blocks[0], part_two, d_more
+    )
     wd = whole_weight(w_down, d_got, d_more)
     for r in steps:
         d_hidden.append((mm(dy, wd[r], NT) * slopes[r]).astype(BF16))
@@ -440,7 +444,6 @@
     flow_up = begin(up_blocks)
     flow_down[1] = flow_down[0].send(flow_down[1])
     flow_up[1] = flow_up[0].send(flow_up[1])
-    part_two = mm(d_hidden[0], wu[0], NT)
     for r in steps:
         part_two = part_two + mm(d_hidden[r], wu[r], NT)
     back_two, g_gain_two, g_shift_two = norm_back(exchange(part_two), unit_two, inv_two, gain_two)
@@ -448,8 +451,7 @@
     da_local = d_resid.astype(BF16)
     da = tie(complete(da_local), flow_down)
 
-    middle = full // 2
-    grads, lows, highs = [None] * chips, [None] * chips, [None] * chips
+    grads, attn_blocks = [None] * chips, [None] * chips
     part_one = None
     last = da
     for r in list(steps) + [0]:
@@ -458,23 +460,23 @@
         if r == chips - 1:
             grads[r] = tie(grads[r], flow_down)
         if r == 0:
-            grads[r] = tie(grads[r], flow_down, flow_up)
+            grads[r] = tie(grads[r], flow_up, flow_down)
         of_qkv = mm(normed_one, grads[r], TN).astype(BF16)
-        of_out = mm(da, heads[r], TN).astype(BF16)
-        lows[r] = jnp.concatenate([of_qkv[:middle], of_out[:middle]], axis=1)
-        highs[r] = jnp.concatenate([of_qkv[middle:], of_out[middle:]], axis=1)
+        of_out = mm(da, after(heads[r], grads[r]), TN).astype(BF16)
+        attn_blocks[r] = jnp.concatenate([of_qkv, of_out], axis=1)
         part = mm(grads[r], wq[r], NT)
         part_one = part if part_one is None else part_one + part
         if r:
-            last, lows[r], highs[r] = lax.optimization_barrier((last, lows[r], highs[r]))
+            last, attn_blocks[r] = hold(last, attn_blocks[r])
             if r == chips - 1:
-                last = tie(last, flow_down)
-    flow_low = begin(lows)
-    flow_low[1] = flow_low[0].send(flow_low[1])
-    flow_high = begin(highs)
-    flow_high[1] = flow_high[0].send(flow_high[1])
-    back_one, g_gain_one, g_shift_one = norm_back(exchange(part_one), unit_one, inv_one, gain_one)
-    input_rows = tie((d_resid + back_one).astype(BF16), flow_up, flow_low)
+                last = tie(last, flow_down, flow_up)
+    flow_attn = begin(attn_blocks)
+    flow_attn[1] = flow_attn[0].send(flow_attn[1])
+    part_one = tie(part_one, flow_up, flow_attn)
+    back_one, g_gain_one, g_shift_one = norm_back(
+        tie(exchange(part_one), flow_down), unit_one, inv_one, gain_one
+    )
+    input_rows = (d_resid + back_one).astype(BF16)
 
     def reduce_small():
         shared = jnp.concatenate(
@@ -501,7 +503,7 @@
         vector = own[0]
         for step in steps:
             vector = vector + chip_shift(send[step - 1], chips - step)
-        for bit in list(range(1, bits)) + [0]:
+        for bit in range(bits):
             send = yield vector
             vector = vector + dp_swap(send, bit)
         return vector
@@ -512,40 +514,27 @@
     mlp_part = mm(after(acts[0], input_rows), w_down, NN)
     for r in steps:
         mlp_part = mlp_part + mm(acts[r], wd[r], NN)
-    mlp_part = tie(mlp_part, flow_small, flow_high, flow_down, flow_up)
+    keep = own_columns(after(input_rows, mlp_part))
+    mlp_part = tie(after(mlp_part, keep), flow_up, flow_attn, flow_small)
     out = (resid + (exchange(mlp_part) + bias_down.astype(F32))).astype(BF16)
-    out = tie(out, flow_small, flow_low)
-    keep = [
-        jnp.concatenate(pair, axis=2) for pair in zip(own_columns(out), own_columns(input_rows))
-    ]
+    out = tie(out, flow_attn, flow_small)
+    keep = [jnp.concatenate(pair, axis=2) for pair in zip(own_columns(out), keep)]
     both = scatter_rows(keep)
     layer_out, input_grad = both[:, :, :width], both[:, :, width:]
 
-    token = after(slot_mask, keep)
-    for flow in (
-        flow_high,
-        flow_low,
-        flow_small,
-        flow_up,
-        flow_high,
-        flow_small,
-        flow_up,
-        flow_low,
-        flow_high,
-        flow_low,
-        flow_small,
-        flow_high,
-    ):
-        token = tie(token, flow)
+    token = tie(after(slot_mask, keep), flow_up, flow_small)
+    token = tie(token, flow_attn, flow_small)
+    grad_up = finish(flow_up).astype(F32)
+    token, grad_up = hold(token, grad_up)
+    token = tie(token, flow_attn, flow_small)
     vector = finish(flow_small)
     vecs = [vector[n * full : (n + 1) * full] for n in range(6)]
     mine = vector[6 * full :]
 
-    grad_down = finish(flow_down)
-    grad_up = finish(flow_up)
-    grad_cat = jnp.concatenate([finish(flow_low), finish(flow_high)], axis=0)
-    grad_qkv = jnp.stack([grad_cat[:, n * width : (n + 1) * width] for n in range(3)])
-    grad_out = grad_cat[:, 3 * width :].T
+    grad_down = finish(flow_down).astype(F32)
+    grad_cat = hold(finish(flow_attn))[0]
+    grad_qkv = jnp.stack([grad_cat[:, n * width : (n + 1) * width] for n in range(3)]).astype(F32)
+    grad_out = grad_cat[:, 3 * width :].T.astype(F32)
     return (
         layer_out,
         input_grad,

time: 469 us -> 424 us (0.904)
  waiting for transfers between devices: 98.8 us -> 68.5 us
  other arithmetic: 71.7 us -> 87.7 us
  blocking collectives: 33.8 us -> 22.3 us
  matrix products: 93.6 us -> 83.3 us
  starting transfers between devices: 68.9 us -> 63.5 us
    ppermute x27 -> x22, waiting for transfers between devices: 85.6 us -> 54.7 us  [dp_swap(): return lax.ppermute(value, 'dp', [(a, a ^ 1 << bit) for a in range(n_dp)])]
    all_to_all x6 -> x4, blocking collectives: 33.8 us -> 22.3 us  [core_trade(): return lax.all_to_all(value, 'tensor', 0, 0, axis_index_groups=pairs)]
    dot_general x24, matrix products: 93.6 us -> 83.3 us  [mm(): return lax.dot_general(left, right, dims, preferred_element_type=F32)]
    ppermute x27 -> x22, starting transfers between devices: 33.4 us -> 24.3 us  [dp_swap(): return lax.ppermute(value, 'dp', [(a, a ^ 1 << bit) for a in range(n_dp)])]
    convert_element_type x4 -> x7, other arithmetic: 11.1 us -> 17.7 us  [the longest x1 5.18 us: per_device(): grad_down = finish(flow_down).astype(F32)]
    select_n x6 -> x4, other arithmetic: 3.84 us -> 10.2 us  [reduce_blocks(): jnp.where(at == 0, jnp.concatenate([total, got], 0), jnp.concatenate([got...]
    all_to_all x4 -> x5, starting transfers between devices: 18.7 us -> 22.8 us  [core_trade(): return lax.all_to_all(value, 'tensor', 0, 0, axis_index_groups=pairs)]
    ppermute x12 -> x11, waiting for transfers between devices: 13.1 us -> 10.6 us  [chip_shift(): return lax.ppermute(value, 'tensor', perm)]
  transfers between devices with their start and end apart: 45 -> 41, of which waited for: 19 -> 22; matrix products, arithmetic and copies ran while one was open for 43% -> 46% of each run, Pallas kernels for 9% -> 10%
where the time goes in v4:
time: 424 us; the launch traced here: 417 us
  other arithmetic  87.7 us (21%)
  matrix products  83.3 us (20%)
  waiting for transfers between devices  68.5 us (16%)
  starting transfers between devices  63.5 us (15%)
  local copies, waits for them, and re-layouts  46.2 us (11%)
  Pallas kernels  43 us (10%)
  blocking collectives  22.3 us (5%)
    dot_general x24, matrix products, mm(): return lax.dot_general(left, right, dims, preferred_element_type=F32)  83.3 us
    ppermute x22, waiting for transfers between devices, dp_swap(): return lax.ppermute(value, 'dp', [(a, a ^ 1 << bit) for a in range(n_dp)])  54.7 us
    pallas_call x2, Pallas kernels, attention_backward(): pl.pallas_call(functools.partial(attn_bwd_kernel, seq, width), grid=(imag...  26.3 us
    ppermute x22, starting transfers between devices, dp_swap(): return lax.ppermute(value, 'dp', [(a, a ^ 1 << bit) for a in range(n_dp)])  24.3 us
    all_to_all x5, starting transfers between devices, core_trade(): return lax.all_to_all(value, 'tensor', 0, 0, axis_index_groups=pairs)  22.8 us
    all_to_all x4, blocking collectives, core_trade(): return lax.all_to_all(value, 'tensor', 0, 0, axis_index_groups=pairs)  22.3 us
    pallas_call x2, Pallas kernels, attention_forward(): pl.pallas_call(functools.partial(attn_fwd_kernel, seq), grid=(images, pai...  16.7 us
    ppermute x11, starting transfers between devices, chip_shift(): return lax.ppermute(value, 'tensor', perm)  15.8 us
  transfers between devices with their start and end apart: 41, of which 22 were waited for; matrix products, arithmetic and copies ran while one was open for 46% of the time, Pallas kernels for 10%

profile of v4, /device:TPU:0, one launch (start us, length us, event | category | flops | bytes accessed | tf_op | source)
XLA Modules:
  0.0 417.1 jit_solution(15633212887611461544)
XLA Ops:
  0.7 4.0 constant_dynamic-slice_fusion.12
  4.7 3.0 collective-permute-start
  7.8 3.8 constant_dynamic-slice_fusion.6
  29.6 6.0 %all_to_all.45 = bf16[2,592,1024]{2,1,0:T(8,128)(2,1)S(1)} all-to-all(bf16[2,592,1024]{2,1,0:T(8,128)(2,1)S(1)} %broadcast_in_dim.6), channel_id=1, replica_groups={{0,1},{2,3},{4,5},{6,7},{8,9},{10,11},{12,13},{14,15},{16,17},{18,19},{..., dimensions={0} | all-to-all | bytes 4849664 | tf_op jit(solution)/shard_map/all_to_all | solution.py:202
  35.7 3.3 fusion.6.q_ref.k_ref.v_ref
  39.0 4.8 %collective-permute-done.2 = bf16[512,768]{1,0:T(8,128)(2,1)} collective-permute-done((bf16[512,768]{1,0:T(8,128)(2,1)}, bf16[512,768]{1,0:T(8,128)(2,1)}, u32[]{:S(2)}, u32[]{:S(2)}) %collective-permute-start.2) | collective-permute-done | bytes 786464 | tf_op jit(solution)/shard_map/ppermute | solution.py:195
  49.2 8.3 %attn_fwd.2 = (bf16[1184,256]{1,0:T(8,128)(2,1)}, f32[2,2,2,592]{3,2,1,0:T(2,128)}) custom-call(bf16[1184,768]{1,0:T(8,128)(2,1)} %fusion.6.q_ref.k_ref.v_ref, bf16[1184,768]{1,0:T(8,128)(2,1)} %fusion.6.q_ref.k_ref.v_ref, bf16[1184,768]{1,0:T(8,128)(2,1)} %fusion.6.q_ref.k_ref.v_ref), custom_call_target="tpu_custom_call" | custom-call | flops 2871001088 | bytes 2424832 | tf_op jit(solution)/shard_map/attn_fwd/pallas_call | solution.py:96
  57.5 4.2 %fusion.71 = f32[1184,1024]{1,0:T(8,128)} fusion(bf16[1184,256]{1,0:T(8,128)(2,1)} %get-tuple-element.133, bf16[256,1024]{1,0:T(8,128)(2,1)} %param.20), kind=kOutput, calls=%fused_computation.216 | convolution fusion | flops 620756992 | bytes 5980160 | tf_op jit(solution)/shard_map/dot_general | solution.py:26
  69.7 3.3 fusion.7.q_ref.k_ref.v_ref
  75.8 8.4 %attn_fwd.3 = (bf16[1184,256]{1,0:T(8,128)(2,1)}, f32[2,2,2,592]{3,2,1,0:T(2,128)}) custom-call(bf16[1184,768]{1,0:T(8,128)(2,1)} %fusion.7.q_ref.k_ref.v_ref, bf16[1184,768]{1,0:T(8,128)(2,1)} %fusion.7.q_ref.k_ref.v_ref, bf16[1184,768]{1,0:T(8,128)(2,1)} %fusion.7.q_ref.k_ref.v_ref), custom_call_target="tpu_custom_call" | custom-call | flops 2871001088 | bytes 2424832 | tf_op jit(solution)/shard_map/attn_fwd/pallas_call | solution.py:96
  86.0 3.4 add_convert_fusion.1
  89.4 5.7 %all_to_all.46 = bf16[2,592,1024]{2,1,0:T(8,128)(2,1)S(1)} all-to-all(bf16[2,592,1024]{2,1,0:T(8,128)(2,1)S(1)} %bitcast.151), channel_id=1, replica_groups={{0,1},{2,3},{4,5},{6,7},{8,9},{10,11},{12,13},{14,15},{16,17},{18,19},{..., dimensions={0} | all-to-all | bytes 4849664 | tf_op jit(solution)/shard_map/all_to_all | solution.py:202
  97.9 5.9 %all_to_all.47 = bf16[2,592,1024]{2,1,0:T(8,128)(2,1)S(1)} all-to-all(bf16[2,592,1024]{2,1,0:T(8,128)(2,1)S(1)} %broadcast_in_dim.7), channel_id=1, replica_groups={{0,1},{2,3},{4,5},{6,7},{8,9},{10,11},{12,13},{14,15},{16,17},{18,19},{..., dimensions={0} | all-to-all | bytes 4849664 | tf_op jit(solution)/shard_map/all_to_all | solution.py:202
  103.8 5.1 %collective-permute-done.8 = bf16[512,1024]{1,0:T(8,128)(2,1)S(1)} collective-permute-done((bf16[512,1024]{1,0:T(8,128)(2,1)}, bf16[512,1024]{1,0:T(8,128)(2,1)S(1)}, u32[]{:S(2)}, u32[]{:S(2)}) %collective-permute-start.8) | collective-permute-done | bytes 1048608 | tf_op jit(solution)/shard_map/ppermute | solution.py:205
  108.9 2.5 maximum_select_fusion
  112.7 2.7 fusion.72
  115.4 3.3 multiply_convert_fusion.3
  120.2 4.4 %convolution_convert_fusion.5 = bf16[1024,1024]{1,0:T(8,128)(2,1)} fusion(bf16[1184,1024]{1,0:T(8,128)(2,1)S(1)} %bitcast.152, f32[1184,1024]{1,0:T(8,128)S(1)} %fusion.72, f32[1024]{0:T(1024)S(1)} %bitcast.174), kind=kOutput, calls=%fused_computation.97 | convolution fusion | flops 2492563456 | bytes 9375744 | tf_op jit(solution)/shard_map/dot_general | solution.py:26
  124.6 4.3 %multiply_convert_fusion.1 = bf16[1184,1024]{1,0:T(8,128)(2,1)S(1)} fusion(bf16[1184,1024]{1,0:T(8,128)(2,1)S(1)} %bitcast.153, bf16[1024,1024]{1,0:T(8,128)(2,1)S(1)} %copy-done.54, f32[1184,1024]{1,0:T(8,128)S(1)} %get-tuple-element.272, f32[1024]{0:T(1024)S(1)} %convert_element_type.292), kind=kOutput, calls=%fused_computation.9 | convolution fusion | flops 2496364544 | bytes 11800576 | tf_op jit(solution)/shard_map/dot_general | solution.py:26
  128.9 4.6 %convolution_convert_fusion.4 = bf16[1024,1024]{1,0:T(8,128)(2,1)} fusion(bf16[1184,1024]{1,0:T(8,128)(2,1)S(1)} %bitcast.168, bf16[1184,1024]{1,0:T(8,128)(2,1)S(1)} %multiply_convert_fusion.1), kind=kOutput, calls=%fused_computation.96 | convolution fusion | flops 2484076544 | bytes 6946816 | tf_op jit(solution)/shard_map/dot_general | solution.py:26
  135.4 2.7 fusion.73
  138.1 4.2 %convolution_convert_fusion.3 = bf16[1024,1024]{1,0:T(8,128)(2,1)} fusion(bf16[1184,1024]{1,0:T(8,128)(2,1)S(1)} %get-tuple-element.138, bf16[1184,1024]{1,0:T(8,128)(2,1)S(1)} %bitcast.154), kind=kOutput, calls=%fused_computation.95 | convolution fusion | flops 2484076544 | bytes 6946816 | tf_op jit(solution)/shard_map/dot_general | solution.py:26
  142.3 3.3 collective-permute-done.11
  145.6 2.5 maximum_select_fusion.1
  148.2 4.3 %multiply_convert_fusion = bf16[1184,1024]{1,0:T(8,128)(2,1)S(1)} fusion(bf16[1184,1024]{1,0:T(8,128)(2,1)S(1)} %bitcast.155, bf16[1024,1024]{1,0:T(8,128)(2,1)S(1)} %maximum_select_fusion.1, f32[1184,1024]{1,0:T(8,128)S(1)} %fusion.72, f32[1024]{0:T(1024)S(1)} %bitcast.175), kind=kOutput, calls=%fused_computation.8 | convolution fusion | flops 2496364544 | bytes 11800576 | tf_op jit(solution)/shard_map/dot_general | solution.py:26
  152.6 4.2 convolution_convert_fusion.2
  156.7 2.7 fusion.74
  159.5 2.3 add_convert_fusion
  161.7 4.0 all-to-all-start.3
  172.7 2.9 convert_reduce_fusion.6
  177.3 5.0 %all-to-all-start.4 = ((bf16[2,592,1024]{2,1,0:T(8,128)(2,1)}), bf16[2,592,1024]{2,1,0:T(8,128)(2,1)}, u32[]{:S(2)}, u32[]{:S(2)}) async-start(bf16[2,592,1024]{2,1,0:T(8,128)(2,1)} %broadcast_in_dim.8), calls=%async_computation.4 | async-start | bytes 4849664 | tf_op jit(solution)/shard_map/all_to_all | solution.py:202
  185.3 2.5 add_convert_fusion.4
  191.3 3.3 convolution_convert_fusion.1.do_ref
  194.6 12.9 %attn_bwd.2 = bf16[1184,768]{1,0:T(8,128)(2,1)} custom-call(bf16[1184,768]{1,0:T(8,128)(2,1)} %fusion.7.q_ref.k_ref.v_ref, bf16[1184,768]{1,0:T(8,128)(2,1)} %fusion.7.q_ref.k_ref.v_ref, bf16[1184,768]{1,0:T(8,128)(2,1)} %fusion.7.q_ref.k_ref.v_ref, bf16[1184,256]{1,0:T(8,128)(2,1)} %convolution_convert_fusion.1.do_ref, ...), custom_call_target="tpu_custom_call" | custom-call | flops 7177502720 | bytes 4243456 | tf_op jit(solution)/shard_map/attn_bwd/pallas_call | solution.py:119
  207.6 8.7 %collective-permute-done.13 = bf16[512,1024]{1,0:T(8,128)(2,1)} collective-permute-done((bf16[512,1024]{1,0:T(8,128)(2,1)}, bf16[512,1024]{1,0:T(8,128)(2,1)}, u32[]{:S(2)}, u32[]{:S(2)}) %collective-permute-start.13) | collective-permute-done | bytes 1048608 | tf_op jit(solution)/shard_map/ppermute | solution.py:205
  220.8 2.7 convolution_convert_fusion.9
  223.5 4.3 %fusion.75 = f32[1184,1024]{1,0:T(8,128)} fusion(bf16[1184,768]{1,0:T(8,128)(2,1)S(1)} %copy-done.46, bf16[1024,768]{1,0:T(8,128)(2,1)S(1)} %copy-done.49), kind=kOutput, calls=%fused_computation.220 | convolution fusion | flops 1862270976 | bytes 8241152 | tf_op jit(solution)/shard_map/dot_general | solution.py:26
  227.8 2.4 convolution_convert_fusion.7
  233.3 2.5 add_convert_fusion.3
  238.5 2.7 collective-permute-start.17
  241.7 3.3 convolution_convert_fusion.do_ref
  245.0 13.4 %attn_bwd.3 = bf16[1184,768]{1,0:T(8,128)(2,1)} custom-call(bf16[1184,768]{1,0:T(8,128)(2,1)} %fusion.6.q_ref.k_ref.v_ref, bf16[1184,768]{1,0:T(8,128)(2,1)} %fusion.6.q_ref.k_ref.v_ref, bf16[1184,768]{1,0:T(8,128)(2,1)} %fusion.6.q_ref.k_ref.v_ref, bf16[1184,256]{1,0:T(8,128)(2,1)} %convolution_convert_fusion.do_ref, ...), custom_call_target="tpu_custom_call" | custom-call | flops 7177502720 | bytes 4243456 | tf_op jit(solution)/shard_map/attn_bwd/pallas_call | solution.py:119
  258.4 5.2 %collective-permute-done.17 = bf16[256,1024]{1,0:T(8,128)(2,1)} collective-permute-done((bf16[256,1024]{1,0:T(8,128)(2,1)S(1)}, bf16[256,1024]{1,0:T(8,128)(2,1)}, u32[]{:S(2)}, u32[]{:S(2)}) %collective-permute-start.17) | collective-permute-done | bytes 524320 | tf_op jit(solution)/shard_map/ppermute | solution.py:205
  269.4 2.7 convolution_convert_fusion.8
  272.2 2.3 convolution_convert_fusion.6
  274.7 3.6 convolution_add_fusion
  279.1 2.3 add_convert_fusion.2
  283.9 5.1 %all-to-all-start.5 = ((bf16[2,592,1024]{2,1,0:T(8,128)(2,1)}), bf16[2,592,1024]{2,1,0:T(8,128)(2,1)}, u32[]{:S(2)}, u32[]{:S(2)}) async-start(bf16[2,592,1024]{2,1,0:T(8,128)(2,1)} %bitcast.170), calls=%async_computation.5 | async-start | bytes 4849664 | tf_op jit(solution)/shard_map/all_to_all | solution.py:202
  289.1 2.5 collective-permute-start.21
  295.3 2.8 maximum_select_fusion.6
  300.9 2.7 fusion.76
  303.6 4.2 convolution_add_fusion.1
  308.2 4.8 %all_to_all.48 = bf16[2,1,577,512]{3,2,1,0:T(8,128)(2,1)S(1)} all-to-all(bf16[2,1,577,512]{3,2,1,0:T(8,128)(2,1)S(1)} %pad_maximum_fusion.3), channel_id=1, replica_groups={{0,1},{2,3},{4,5},{6,7},{8,9},{10,11},{12,13},{14,15},{16,17},{18,19},{..., dimensions={0} | all-to-all | bytes 2363392 | tf_op jit(solution)/shard_map/all_to_all | solution.py:202
  322.1 4.9 %all-to-all-start.7 = ((bf16[2,592,1024]{2,1,0:T(8,128)(2,1)}), bf16[2,592,1024]{2,1,0:T(8,128)(2,1)}, u32[]{:S(2)}, u32[]{:S(2)}) async-start(bf16[2,592,1024]{2,1,0:T(8,128)(2,1)} %bitcast.165), calls=%async_computation.7 | async-start | bytes 4849664 | tf_op jit(solution)/shard_map/all_to_all | solution.py:202
  339.5 11.7 %collective-permute-done.28 = bf16[256,1024]{1,0:T(8,128)(2,1)} collective-permute-done((bf16[256,1024]{1,0:T(8,128)(2,1)S(1)}, bf16[256,1024]{1,0:T(8,128)(2,1)}, u32[]{:S(2)}, u32[]{:S(2)}) %collective-permute-start.28) | collective-permute-done | bytes 524320 | tf_op jit(solution)/shard_map/ppermute | solution.py:205
  351.2 2.6 maximum_select_fusion.7
  355.2 3.8 all-to-all-start.8
  371.6 5.6 %collective-permute-done.31 = f32[7680]{0:T(1024)S(1)} collective-permute-done((f32[7680]{0:T(1024)S(1)}, f32[7680]{0:T(1024)S(1)}, u32[]{:S(2)}, u32[]{:S(2)}) %collective-permute-start.31) | collective-permute-done | bytes 30752 | tf_op jit(solution)/shard_map/ppermute | solution.py:205
  380.6 5.2 %fusion.43 = f32[1024,1024]{1,0:T(8,128)} fusion(bf16[512,1024]{1,0:T(8,128)(2,1)} %collective-permute-done.35, bf16[512,1024]{1,0:T(8,128)(2,1)} %maximum_select_fusion.6, pred[]{:T(512)S(6)} %eq.69), kind=kLoop, calls=%fused_computation.90 | loop fusion | flops 10485760 | bytes 6291457 | tf_op jit(solution)/shard_map/convert_element_type | solution.py:534
  385.9 4.4 %fusion.42 = f32[1024,1024]{1,0:T(8,128)} fusion(bf16[512,1024]{1,0:T(8,128)(2,1)} %collective-permute-done.34, bf16[512,1024]{1,0:T(8,128)(2,1)S(1)} %copy-done.15, pred[]{:T(512)S(6)} %eq.69), kind=kLoop, calls=%fused_computation.88 | loop fusion | flops 10485760 | bytes 6291457 | tf_op jit(solution)/shard_map/convert_element_type | solution.py:527
  391.9 4.2 %collective-permute-done.25 = bf16[2,577,512]{2,0,1:T(2,128)(2,1)} collective-permute-done((bf16[2,577,512]{2,0,1:T(2,128)(2,1)}, bf16[2,577,512]{2,0,1:T(2,128)(2,1)}, u32[]{:S(2)}, u32[]{:S(2)}) %collective-permute-start.25) | collective-permute-done | bytes 1181728 | tf_op jit(solution)/shard_map/ppermute | solution.py:195
  401.1 6.6 %collective-permute-done.32 = bf16[512,1024]{1,0:T(8,128)(2,1)} collective-permute-done((bf16[512,1024]{1,0:T(8,128)(2,1)}, bf16[512,1024]{1,0:T(8,128)(2,1)}, u32[]{:S(2)}, u32[]{:S(2)}) %collective-permute-start.32) | collective-permute-done | bytes 1048608 | tf_op jit(solution)/shard_map/ppermute | solution.py:205
  407.7 3.4 maximum_select_fusion.2
  413.6 3.3 maximum_convert_fusion
  (378 shorter events, 132.7 us)
Async XLA Ops:
  0.6 17.1 %copy-start = (bf16[1024,1024]{1,0:T(8,128)(2,1)S(1)}, bf16[1024,1024]{1,0:T(8,128)(2,1)}, u32[]{:S(2)}) copy-start(bf16[1024,1024]{1,0:T(8,128)(2,1)} %param.26) | copy-start | bytes 6291460
  4.7 16.7 %collective-permute-start = (bf16[2,577,256]{2,0,1:T(2,128)(2,1)}, bf16[2,577,256]{2,0,1:T(2,128)(2,1)}, u32[]{:S(2)}, u32[]{:S(2)}) collective-permute-start(bf16[2,577,256]{2,0,1:T(2,128)(2,1)} %get-tuple-element.250), channel_id=1, source_target_pairs={{0,2},{1,3},{2,0},{3,1},{4,6},{5,7},{6,4},{7,5},{8,10},{9,11},{10,... | collective-permute-start | bytes 1772552 | tf_op jit(solution)/shard_map/ppermute | solution.py:195
  23.4 2.4 collective-permute-start.1
  23.5 20.3 %collective-permute-start.2 = (bf16[512,768]{1,0:T(8,128)(2,1)}, bf16[512,768]{1,0:T(8,128)(2,1)}, u32[]{:S(2)}, u32[]{:S(2)}) collective-permute-start(bf16[512,768]{1,0:T(8,128)(2,1)} %constant_dynamic-slice_fusion.11), channel_id=1, source_target_pairs={{0,2},{1,3},{2,0},{3,1},{4,6},{5,7},{6,4},{7,5},{8,10},{9,11},{10,... | collective-permute-start | bytes 2359304 | tf_op jit(solution)/shard_map/ppermute | solution.py:195
  27.3 68.4 %copy-start.4 = (bf16[1,592,1024]{2,1,0:T(8,128)(2,1)}, bf16[1,592,1024]{2,1,0:T(8,128)(2,1)S(1)}, u32[]{:S(2)}) copy-start(bf16[1,592,1024]{2,1,0:T(8,128)(2,1)S(1)} %get-tuple-element.215) | copy-start | bytes 3637252
  35.6 9.9 %copy-start.26 = (bf16[2,577,256]{2,0,1:T(2,128)(2,1)S(1)}, bf16[2,577,256]{2,0,1:T(2,128)(2,1)}, u32[]{:S(2)}) copy-start(bf16[2,577,256]{2,0,1:T(2,128)(2,1)} %get-tuple-element.248) | copy-start | bytes 1772548
  35.6 10.8 %copy-start.79 = (bf16[1024]{0:T(1024)(128)(2,1)S(1)}, bf16[1024]{0:T(1024)(128)(2,1)}, u32[]{:S(2)}) copy-start(bf16[1024]{0:T(1024)(128)(2,1)} %param.24) | copy-start | bytes 6148
  35.6 10.8 %copy-start.80 = (bf16[1024]{0:T(1024)(128)(2,1)S(1)}, bf16[1024]{0:T(1024)(128)(2,1)}, u32[]{:S(2)}) copy-start(bf16[1024]{0:T(1024)(128)(2,1)} %param.21) | copy-start | bytes 6148
  35.6 10.8 %copy-start.81 = (bf16[1024]{0:T(1024)(128)(2,1)S(1)}, bf16[1024]{0:T(1024)(128)(2,1)}, u32[]{:S(2)}) copy-start(bf16[1024]{0:T(1024)(128)(2,1)} %param.25) | copy-start | bytes 6148
  35.7 10.8 %copy-start.82 = (bf16[1024]{0:T(1024)(128)(2,1)S(1)}, bf16[1024]{0:T(1024)(128)(2,1)}, u32[]{:S(2)}) copy-start(bf16[1024]{0:T(1024)(128)(2,1)} %param.29) | copy-start | bytes 6148
  35.7 11.4 %copy-start.84 = (s32[4]{0:T(128)S(1)}, s32[4]{0:T(128)}, u32[]{:S(2)}) copy-start(s32[4]{0:T(128)} %param.17) | copy-start | bytes 52
  43.8 19.4 %collective-permute-start.3 = (bf16[512,768]{1,0:T(8,128)(2,1)}, bf16[512,768]{1,0:T(8,128)(2,1)}, u32[]{:S(2)}, u32[]{:S(2)}) collective-permute-start(bf16[512,768]{1,0:T(8,128)(2,1)} %collective-permute-done.2), channel_id=1, source_target_pairs={{0,4},{4,0},{8,12},{12,8},{16,20},{20,16},{24,28},{28,24},{1,5},{5... | collective-permute-start | bytes 2359304 | tf_op jit(solution)/shard_map/ppermute | solution.py:205
  47.2 14.6 %collective-permute-start.4 = (bf16[144,1024]{1,0:T(8,128)(2,1)}, bf16[144,1024]{1,0:T(8,128)(2,1)}, u32[]{:S(2)}, u32[]{:S(2)}) collective-permute-start(bf16[144,1024]{1,0:T(8,128)(2,1)} %pad_maximum_fusion.7), channel_id=1, source_target_pairs={{0,2},{1,3},{2,0},{3,1},{4,6},{5,7},{6,4},{7,5},{8,10},{9,11},{10,... | collective-permute-start | bytes 884744 | tf_op jit(solution)/shard_map/ppermute | solution.py:195
  48.7 35.5 %collective-permute-start.5 = (bf16[512,1024]{1,0:T(8,128)(2,1)}, bf16[512,1024]{1,0:T(8,128)(2,1)}, u32[]{:S(2)}, u32[]{:S(2)}) collective-permute-start(bf16[512,1024]{1,0:T(8,128)(2,1)} %constant_dynamic-slice_fusion.9), channel_id=1, source_target_pairs={{0,2},{1,3},{2,0},{3,1},{4,6},{5,7},{6,4},{7,5},{8,10},{9,11},{10,... | collective-permute-start | bytes 3145736 | tf_op jit(solution)/shard_map/ppermute | solution.py:195
  61.8 7.9 %copy-start.20 = (bf16[2,592,1024]{2,1,0:T(8,128)(2,1)S(1)}, bf16[2,592,1024]{2,1,0:T(8,128)(2,1)}, u32[]{:S(2)}) copy-start(bf16[2,592,1024]{2,1,0:T(8,128)(2,1)} %copy-done.19) | copy-start | bytes 7274500
  67.9 16.2 %collective-permute-start.6 = (bf16[128,1024]{1,0:T(8,128)(2,1)}, bf16[128,1024]{1,0:T(8,128)(2,1)}, u32[]{:S(2)}, u32[]{:S(2)}) collective-permute-start(bf16[128,1024]{1,0:T(8,128)(2,1)} %slice.222), channel_id=1, source_target_pairs={{0,4},{4,0},{8,12},{12,8},{16,20},{20,16},{24,28},{28,24},{1,5},{5... | collective-permute-start | bytes 786440 | tf_op jit(solution)/shard_map/ppermute | solution.py:205
  73.1 30.7 %collective-permute-start.7 = (bf16[2,577,256]{2,1,0:T(8,128)(2,1)}, bf16[2,577,256]{2,1,0:T(8,128)(2,1)}, u32[]{:S(2)}, u32[]{:S(2)}) collective-permute-start(bf16[2,577,256]{2,1,0:T(8,128)(2,1)} %copy.69), channel_id=1, source_target_pairs={{0,2},{1,3},{2,0},{3,1},{4,6},{5,7},{6,4},{7,5},{8,10},{9,11},{10,... | collective-permute-start | bytes 1772552 | tf_op jit(solution)/shard_map/ppermute | solution.py:195
  74.6 45.2 %collective-permute-start.10 = (bf16[512,1024]{1,0:T(8,128)(2,1)}, bf16[512,1024]{1,0:T(8,128)(2,1)}, u32[]{:S(2)}, u32[]{:S(2)}) collective-permute-start(bf16[512,1024]{1,0:T(8,128)(2,1)} %constant_dynamic-slice_fusion.8), channel_id=1, source_target_pairs={{0,2},{1,3},{2,0},{3,1},{4,6},{5,7},{6,4},{7,5},{8,10},{9,11},{10,... | collective-permute-start | bytes 3145736 | tf_op jit(solution)/shard_map/ppermute | solution.py:195
  75.8 72.4 %copy-start.75 = (f32[1,1024]{1,0:T(1,128)}, f32[1,1024]{1,0:T(1,128)S(1)}, u32[]{:S(2)}) copy-start(f32[1,1024]{1,0:T(1,128)S(1)} %slice_convert_fusion) | copy-start | bytes 12292
  85.6 23.3 %collective-permute-start.8 = (bf16[512,1024]{1,0:T(8,128)(2,1)}, bf16[512,1024]{1,0:T(8,128)(2,1)S(1)}, u32[]{:S(2)}, u32[]{:S(2)}) collective-permute-start(bf16[512,1024]{1,0:T(8,128)(2,1)} %collective-permute-done.5), channel_id=1, source_target_pairs={{0,4},{4,0},{8,12},{12,8},{16,20},{20,16},{24,28},{28,24},{1,5},{5... | collective-permute-start | bytes 3145736 | tf_op jit(solution)/shard_map/ppermute | solution.py:205
  103.8 7.7 %copy-start.18 = (bf16[2,577,512]{2,1,0:T(8,128)(2,1)S(1)}, bf16[2,577,512]{2,1,0:T(8,128)(2,1)}, u32[]{:S(2)}) copy-start(bf16[2,577,512]{2,1,0:T(8,128)(2,1)} %copy_dynamic-update-slice_fusion) | copy-start | bytes 3545092
  112.6 6.2 %collective-permute-start.9 = (bf16[2,577,512]{2,1,0:T(8,128)(2,1)S(1)}, bf16[2,577,512]{2,1,0:T(8,128)(2,1)S(1)}, u32[]{:S(2)}, u32[]{:S(2)}) collective-permute-start(bf16[2,577,512]{2,1,0:T(8,128)(2,1)S(1)} %constant_dynamic-update-slice_fusion), channel_id=1, source_target_pairs={{0,1},{1,0},{2,3},{3,2},{4,5},{5,4},{6,7},{7,6},{8,9},{9,8},{10,11... | collective-permute-start | bytes 3545096 | tf_op jit(solution)/shard_map/ppermute | solution.py:198
  115.4 32.8 %copy-start.86 = (f32[1184,1024]{1,0:T(8,128)}, f32[1184,1024]{1,0:T(8,128)S(1)}, u32[]{:S(2)}) copy-start(f32[1184,1024]{1,0:T(8,128)S(1)} %fusion.72) | copy-start | bytes 14548996
  118.7 19.4 %copy-start.87 = (bf16[1184,1024]{1,0:T(8,128)(2,1)}, bf16[1184,1024]{1,0:T(8,128)(2,1)S(1)}, u32[]{:S(2)}) copy-start(bf16[1184,1024]{1,0:T(8,128)(2,1)S(1)} %get-tuple-element.138) | copy-start | bytes 7274500
  119.8 28.4 %copy-start.11 = (bf16[2,592,1024]{2,1,0:T(8,128)(2,1)}, bf16[2,592,1024]{2,1,0:T(8,128)(2,1)S(1)}, u32[]{:S(2)}) copy-start(bf16[2,592,1024]{2,1,0:T(8,128)(2,1)S(1)} %fusion.28) | copy-start | bytes 7274500
  119.8 25.8 %collective-permute-start.11 = (bf16[512,1024]{1,0:T(8,128)(2,1)}, bf16[512,1024]{1,0:T(8,128)(2,1)S(1)}, u32[]{:S(2)}, u32[]{:S(2)}) collective-permute-start(bf16[512,1024]{1,0:T(8,128)(2,1)} %collective-permute-done.10), channel_id=1, source_target_pairs={{0,4},{4,0},{8,12},{12,8},{16,20},{20,16},{24,28},{28,24},{1,5},{5... | collective-permute-start | bytes 3145736 | tf_op jit(solution)/shard_map/ppermute | solution.py:205
  133.6 51.6 %collective-permute-start.12 = (bf16[1024,1024]{1,0:T(8,128)(2,1)}, bf16[1024,1024]{1,0:T(8,128)(2,1)}, u32[]{:S(2)}, u32[]{:S(2)}) collective-permute-start(bf16[1024,1024]{1,0:T(8,128)(2,1)} %convolution_convert_fusion.5), channel_id=1, source_target_pairs={{0,2},{1,3},{2,0},{3,1},{4,6},{5,7},{6,4},{7,5},{8,10},{9,11},{10,... | collective-permute-start | bytes 6291464 | tf_op jit(solution)/shard_map/ppermute | solution.py:195
  161.7 7.1 %all-to-all-start.3 = ((bf16[2,592,1024]{2,1,0:T(8,128)(2,1)}), bf16[2,592,1024]{2,1,0:T(8,128)(2,1)S(1)}, u32[]{:S(2)}, u32[]{:S(2)}) async-start(bf16[2,592,1024]{2,1,0:T(8,128)(2,1)} %bitcast.150), calls=%async_computation.3 | async-start | bytes 4849664 | tf_op jit(solution)/shard_map/all_to_all | solution.py:202
  165.7 67.6 %collective-permute-start.15 = (bf16[1024,1024]{1,0:T(8,128)(2,1)}, bf16[1024,1024]{1,0:T(8,128)(2,1)}, u32[]{:S(2)}, u32[]{:S(2)}) collective-permute-start(bf16[1024,1024]{1,0:T(8,128)(2,1)} %convolution_convert_fusion.2), channel_id=1, source_target_pairs={{0,2},{1,3},{2,0},{3,1},{4,6},{5,7},{6,4},{7,5},{8,10},{9,11},{10,... | collective-permute-start | bytes 6291464 | tf_op jit(solution)/shard_map/ppermute | solution.py:195
  177.3 13.0 %all-to-all-start.4 = ((bf16[2,592,1024]{2,1,0:T(8,128)(2,1)}), bf16[2,592,1024]{2,1,0:T(8,128)(2,1)}, u32[]{:S(2)}, u32[]{:S(2)}) async-start(bf16[2,592,1024]{2,1,0:T(8,128)(2,1)} %broadcast_in_dim.8), calls=%async_computation.4 | async-start | bytes 4849664 | tf_op jit(solution)/shard_map/all_to_all | solution.py:202
  190.4 25.9 %collective-permute-start.13 = (bf16[512,1024]{1,0:T(8,128)(2,1)}, bf16[512,1024]{1,0:T(8,128)(2,1)}, u32[]{:S(2)}, u32[]{:S(2)}) collective-permute-start(bf16[512,1024]{1,0:T(8,128)(2,1)} %constant_dynamic-slice_fusion.5), channel_id=1, source_target_pairs={{0,4},{4,0},{8,12},{12,8},{16,20},{20,16},{24,28},{28,24},{1,5},{5... | collective-permute-start | bytes 3145736 | tf_op jit(solution)/shard_map/ppermute | solution.py:205
  207.6 12.3 %copy-start.46 = (bf16[1184,768]{1,0:T(8,128)(2,1)S(1)}, bf16[1184,768]{1,0:T(8,128)(2,1)}, u32[]{:S(2)}) copy-start(bf16[1184,768]{1,0:T(8,128)(2,1)} %attn_bwd.2) | copy-start | bytes 5455876
  207.6 13.2 %copy-start.52 = (bf16[1184,256]{1,0:T(8,128)(2,1)S(1)}, bf16[1184,256]{1,0:T(8,128)(2,1)}, u32[]{:S(2)}) copy-start(bf16[1184,256]{1,0:T(8,128)(2,1)} %get-tuple-element.122) | copy-start | bytes 1818628
  218.2 20.1 %collective-permute-start.14 = (bf16[256,1024]{1,0:T(8,128)(2,1)S(1)}, bf16[256,1024]{1,0:T(8,128)(2,1)S(1)}, u32[]{:S(2)}, u32[]{:S(2)}) collective-permute-start(bf16[256,1024]{1,0:T(8,128)(2,1)S(1)} %constant_dynamic-slice_fusion.4), channel_id=1, source_target_pairs={{0,8},{4,12},{8,0},{12,4},{16,24},{20,28},{24,16},{28,20},{1,9},{5... | collective-permute-start | bytes 1572872 | tf_op jit(solution)/shard_map/ppermute | solution.py:205
  231.8 47.4 %collective-permute-start.19 = (bf16[1024,1024]{1,0:T(8,128)(2,1)}, bf16[1024,1024]{1,0:T(8,128)(2,1)}, u32[]{:S(2)}, u32[]{:S(2)}) collective-permute-start(bf16[1024,1024]{1,0:T(8,128)(2,1)} %pad_maximum_fusion), channel_id=1, source_target_pairs={{0,2},{1,3},{2,0},{3,1},{4,6},{5,7},{6,4},{7,5},{8,10},{9,11},{10,... | collective-permute-start | bytes 6291464 | tf_op jit(solution)/shard_map/ppermute | solution.py:195
  238.5 25.1 %collective-permute-start.17 = (bf16[256,1024]{1,0:T(8,128)(2,1)S(1)}, bf16[256,1024]{1,0:T(8,128)(2,1)}, u32[]{:S(2)}, u32[]{:S(2)}) collective-permute-start(bf16[256,1024]{1,0:T(8,128)(2,1)S(1)} %add_convert_fusion.14), channel_id=1, source_target_pairs={{0,16},{4,20},{8,24},{12,28},{16,0},{20,4},{24,8},{28,12},{1,17},{... | collective-permute-start | bytes 1572872 | tf_op jit(solution)/shard_map/ppermute | solution.py:205
  241.2 24.2 %collective-permute-start.16 = (bf16[512,1024]{1,0:T(8,128)(2,1)}, bf16[512,1024]{1,0:T(8,128)(2,1)}, u32[]{:S(2)}, u32[]{:S(2)}) collective-permute-start(bf16[512,1024]{1,0:T(8,128)(2,1)} %constant_dynamic-slice_fusion.3), channel_id=1, source_target_pairs={{0,4},{4,0},{8,12},{12,8},{16,20},{20,16},{24,28},{28,24},{1,5},{5... | collective-permute-start | bytes 3145736 | tf_op jit(solution)/shard_map/ppermute | solution.py:205
  267.3 14.9 %collective-permute-start.18 = (bf16[256,1024]{1,0:T(8,128)(2,1)S(1)}, bf16[256,1024]{1,0:T(8,128)(2,1)S(1)}, u32[]{:S(2)}, u32[]{:S(2)}) collective-permute-start(bf16[256,1024]{1,0:T(8,128)(2,1)S(1)} %constant_dynamic-slice_fusion.2), channel_id=1, source_target_pairs={{0,8},{4,12},{8,0},{12,4},{16,24},{20,28},{24,16},{28,20},{1,9},{5... | collective-permute-start | bytes 1572872 | tf_op jit(solution)/shard_map/ppermute | solution.py:205
  267.9 27.4 %collective-permute-start.20 = (bf16[256,1024]{1,0:T(8,128)(2,1)S(1)}, bf16[256,1024]{1,0:T(8,128)(2,1)}, u32[]{:S(2)}, u32[]{:S(2)}) collective-permute-start(bf16[256,1024]{1,0:T(8,128)(2,1)S(1)} %add_convert_fusion.13), channel_id=1, source_target_pairs={{0,8},{4,12},{8,0},{12,4},{16,24},{20,28},{24,16},{28,20},{1,9},{5... | collective-permute-start | bytes 1572872 | tf_op jit(solution)/shard_map/ppermute | solution.py:205
  283.9 8.3 %all-to-all-start.5 = ((bf16[2,592,1024]{2,1,0:T(8,128)(2,1)}), bf16[2,592,1024]{2,1,0:T(8,128)(2,1)}, u32[]{:S(2)}, u32[]{:S(2)}) async-start(bf16[2,592,1024]{2,1,0:T(8,128)(2,1)} %bitcast.170), calls=%async_computation.5 | async-start | bytes 4849664 | tf_op jit(solution)/shard_map/all_to_all | solution.py:202
  289.1 26.5 %collective-permute-start.21 = (bf16[256,1024]{1,0:T(8,128)(2,1)S(1)}, bf16[256,1024]{1,0:T(8,128)(2,1)}, u32[]{:S(2)}, u32[]{:S(2)}) collective-permute-start(bf16[256,1024]{1,0:T(8,128)(2,1)S(1)} %add_convert_fusion.12), channel_id=1, source_target_pairs={{0,16},{4,20},{8,24},{12,28},{16,0},{20,4},{24,8},{28,12},{1,17},{... | collective-permute-start | bytes 1572872 | tf_op jit(solution)/shard_map/ppermute | solution.py:205
  291.6 25.6 %collective-permute-start.22 = (bf16[512,1024]{1,0:T(8,128)(2,1)}, bf16[512,1024]{1,0:T(8,128)(2,1)}, u32[]{:S(2)}, u32[]{:S(2)}) collective-permute-start(bf16[512,1024]{1,0:T(8,128)(2,1)} %constant_dynamic-slice_fusion.1), channel_id=1, source_target_pairs={{0,4},{4,0},{8,12},{12,8},{16,20},{20,16},{24,28},{28,24},{1,5},{5... | collective-permute-start | bytes 3145736 | tf_op jit(solution)/shard_map/ppermute | solution.py:205
  308.1 7.4 %copy-start.31 = (bf16[256,1024]{1,0:T(8,128)(2,1)S(1)}, bf16[256,1024]{1,0:T(8,128)(2,1)}, u32[]{:S(2)}) copy-start(bf16[256,1024]{1,0:T(8,128)(2,1)} %copy-done.30) | copy-start | bytes 1572868
  320.6 15.1 %collective-permute-start.23 = (bf16[256,1024]{1,0:T(8,128)(2,1)}, bf16[256,1024]{1,0:T(8,128)(2,1)}, u32[]{:S(2)}, u32[]{:S(2)}) collective-permute-start(bf16[256,1024]{1,0:T(8,128)(2,1)} %constant_dynamic-slice_fusion), channel_id=1, source_target_pairs={{0,8},{4,12},{8,0},{12,4},{16,24},{20,28},{24,16},{28,20},{1,9},{5... | collective-permute-start | bytes 1572872 | tf_op jit(solution)/shard_map/ppermute | solution.py:205
  321.6 59.0 %collective-permute-start.35 = (bf16[512,1024]{1,0:T(8,128)(2,1)}, bf16[512,1024]{1,0:T(8,128)(2,1)}, u32[]{:S(2)}, u32[]{:S(2)}) collective-permute-start(bf16[512,1024]{1,0:T(8,128)(2,1)} %maximum_select_fusion.6), channel_id=1, source_target_pairs={{0,4},{4,0},{8,12},{12,8},{16,20},{20,16},{24,28},{28,24},{1,5},{5... | collective-permute-start | bytes 3145736 | tf_op jit(solution)/shard_map/ppermute | solution.py:205
  322.1 8.1 %all-to-all-start.7 = ((bf16[2,592,1024]{2,1,0:T(8,128)(2,1)}), bf16[2,592,1024]{2,1,0:T(8,128)(2,1)}, u32[]{:S(2)}, u32[]{:S(2)}) async-start(bf16[2,592,1024]{2,1,0:T(8,128)(2,1)} %bitcast.165), calls=%async_computation.7 | async-start | bytes 4849664 | tf_op jit(solution)/shard_map/all_to_all | solution.py:202
  327.1 6.5 %collective-permute-start.24 = (f32[6144]{0:T(1024)}, f32[6144]{0:T(1024)}, u32[]{:S(2)}, u32[]{:S(2)}) collective-permute-start(f32[6144]{0:T(1024)} %copy-done.63), channel_id=1, source_target_pairs={{0,1},{1,0},{2,3},{3,2},{4,5},{5,4},{6,7},{7,6},{8,9},{9,8},{10,11... | collective-permute-start | bytes 73736 | tf_op jit(solution)/shard_map/ppermute | solution.py:198
  327.6 23.7 %collective-permute-start.28 = (bf16[256,1024]{1,0:T(8,128)(2,1)S(1)}, bf16[256,1024]{1,0:T(8,128)(2,1)}, u32[]{:S(2)}, u32[]{:S(2)}) collective-permute-start(bf16[256,1024]{1,0:T(8,128)(2,1)S(1)} %add_convert_fusion.11), channel_id=1, source_target_pairs={{0,8},{4,12},{8,0},{12,4},{16,24},{20,28},{24,16},{28,20},{1,9},{5... | collective-permute-start | bytes 1572872 | tf_op jit(solution)/shard_map/ppermute | solution.py:205
  336.9 16.9 %copy-start.32 = (bf16[256,1024]{1,0:T(8,128)(2,1)}, bf16[256,1024]{1,0:T(8,128)(2,1)S(1)}, u32[]{:S(2)}) copy-start(bf16[256,1024]{1,0:T(8,128)(2,1)S(1)} %add_convert_fusion.10) | copy-start | bytes 1572868
  337.0 17.0 %collective-permute-start.27 = (f32[7680]{0:T(1024)S(1)}, f32[7680]{0:T(1024)S(1)}, u32[]{:S(2)}, u32[]{:S(2)}) collective-permute-start(f32[7680]{0:T(1024)S(1)} %fusion.51), channel_id=1, source_target_pairs={{0,2},{1,3},{2,0},{3,1},{4,6},{5,7},{6,4},{7,5},{8,10},{9,11},{10,... | collective-permute-start | bytes 92168 | tf_op jit(solution)/shard_map/ppermute | solution.py:195
  338.5 24.6 %collective-permute-start.26 = (bf16[256,1024]{1,0:T(8,128)(2,1)S(1)}, bf16[256,1024]{1,0:T(8,128)(2,1)}, u32[]{:S(2)}, u32[]{:S(2)}) collective-permute-start(bf16[256,1024]{1,0:T(8,128)(2,1)S(1)} %add_convert_fusion.10), channel_id=1, source_target_pairs={{0,16},{4,20},{8,24},{12,28},{16,0},{20,4},{24,8},{28,12},{1,17},{... | collective-permute-start | bytes 1572872 | tf_op jit(solution)/shard_map/ppermute | solution.py:205
  339.5 14.4 %copy-start.73 = (f32[256]{0:T(256)S(1)}, f32[256]{0:T(256)}, u32[]{:S(2)}) copy-start(f32[256]{0:T(256)} %get-tuple-element.263) | copy-start | bytes 3076
  339.5 14.4 %copy-start.74 = (f32[256]{0:T(256)S(1)}, f32[256]{0:T(256)}, u32[]{:S(2)}) copy-start(f32[256]{0:T(256)} %get-tuple-element.264) | copy-start | bytes 3076
  354.0 9.2 %copy-start.33 = (bf16[256,1024]{1,0:T(8,128)(2,1)S(1)}, bf16[256,1024]{1,0:T(8,128)(2,1)}, u32[]{:S(2)}) copy-start(bf16[256,1024]{1,0:T(8,128)(2,1)} %copy-done.32) | copy-start | bytes 1572868
  354.0 7.1 %collective-permute-start.29 = (f32[7680]{0:T(1024)S(1)}, f32[7680]{0:T(1024)S(1)}, u32[]{:S(2)}, u32[]{:S(2)}) collective-permute-start(f32[7680]{0:T(1024)S(1)} %fusion.54), channel_id=1, source_target_pairs={{0,4},{4,0},{8,12},{12,8},{16,20},{20,16},{24,28},{28,24},{1,5},{5... | collective-permute-start | bytes 92168 | tf_op jit(solution)/shard_map/ppermute | solution.py:205
  355.2 9.3 %all-to-all-start.8 = ((bf16[2,1,577,512]{3,2,1,0:T(8,128)(2,1)}), bf16[2,1,577,512]{3,2,1,0:T(8,128)(2,1)S(1)}, u32[]{:S(2)}, u32[]{:S(2)}) async-start(bf16[2,1,577,512]{3,2,1,0:T(8,128)(2,1)} %pad_maximum_fusion.4), calls=%async_computation.8 | async-start | bytes 2392064 | tf_op jit(solution)/shard_map/all_to_all | solution.py:202
  359.0 7.8 %copy-start.13 = (bf16[2,577,256]{2,1,0:T(8,128)(2,1)S(1)}, bf16[2,577,256]{2,1,0:T(8,128)(2,1)}, u32[]{:S(2)}) copy-start(bf16[2,577,256]{2,1,0:T(8,128)(2,1)} %get-tuple-element.243) | copy-start | bytes 1772548
  359.0 26.8 %collective-permute-start.34 = (bf16[512,1024]{1,0:T(8,128)(2,1)}, bf16[512,1024]{1,0:T(8,128)(2,1)}, u32[]{:S(2)}, u32[]{:S(2)}) collective-permute-start(bf16[512,1024]{1,0:T(8,128)(2,1)} %maximum_select_fusion.7), channel_id=1, source_target_pairs={{0,4},{4,0},{8,12},{12,8},{16,20},{20,16},{24,28},{28,24},{1,5},{5... | collective-permute-start | bytes 3145736 | tf_op jit(solution)/shard_map/ppermute | solution.py:205
  364.4 12.8 %collective-permute-start.30 = (bf16[256,1024]{1,0:T(8,128)(2,1)S(1)}, bf16[256,1024]{1,0:T(8,128)(2,1)S(1)}, u32[]{:S(2)}, u32[]{:S(2)}) collective-permute-start(bf16[256,1024]{1,0:T(8,128)(2,1)S(1)} %add_convert_fusion.9), channel_id=1, source_target_pairs={{0,8},{4,12},{8,0},{12,4},{16,24},{20,28},{24,16},{28,20},{1,9},{5... | collective-permute-start | bytes 1572872 | tf_op jit(solution)/shard_map/ppermute | solution.py:205
  369.1 27.1 %collective-permute-start.25 = (bf16[2,577,512]{2,0,1:T(2,128)(2,1)}, bf16[2,577,512]{2,0,1:T(2,128)(2,1)}, u32[]{:S(2)}, u32[]{:S(2)}) collective-permute-start(bf16[2,577,512]{2,0,1:T(2,128)(2,1)} %copy.58), channel_id=1, source_target_pairs={{0,2},{1,3},{2,0},{3,1},{4,6},{5,7},{6,4},{7,5},{8,10},{9,11},{10,... | collective-permute-start | bytes 3545096 | tf_op jit(solution)/shard_map/ppermute | solution.py:195
  369.6 7.6 %collective-permute-start.31 = (f32[7680]{0:T(1024)S(1)}, f32[7680]{0:T(1024)S(1)}, u32[]{:S(2)}, u32[]{:S(2)}) collective-permute-start(f32[7680]{0:T(1024)S(1)} %add.336), channel_id=1, source_target_pairs={{0,8},{4,12},{8,0},{12,4},{16,24},{20,28},{24,16},{28,20},{1,9},{5... | collective-permute-start | bytes 92168 | tf_op jit(solution)/shard_map/ppermute | solution.py:205
  378.7 7.2 %copy-start.15 = (bf16[512,1024]{1,0:T(8,128)(2,1)S(1)}, bf16[512,1024]{1,0:T(8,128)(2,1)}, u32[]{:S(2)}) copy-start(bf16[512,1024]{1,0:T(8,128)(2,1)} %maximum_select_fusion.7) | copy-start | bytes 3145732
  378.7 29.0 %collective-permute-start.32 = (bf16[512,1024]{1,0:T(8,128)(2,1)}, bf16[512,1024]{1,0:T(8,128)(2,1)}, u32[]{:S(2)}, u32[]{:S(2)}) collective-permute-start(bf16[512,1024]{1,0:T(8,128)(2,1)} %maximum_select_fusion.8), channel_id=1, source_target_pairs={{0,4},{4,0},{8,12},{12,8},{16,20},{20,16},{24,28},{28,24},{1,5},{5... | collective-permute-start | bytes 3145736 | tf_op jit(solution)/shard_map/ppermute | solution.py:205
  385.8 4.9 %collective-permute-start.33 = (f32[7680]{0:T(1024)S(1)}, f32[7680]{0:T(1024)S(1)}, u32[]{:S(2)}, u32[]{:S(2)}) collective-permute-start(f32[7680]{0:T(1024)S(1)} %add.337), channel_id=1, source_target_pairs={{0,16},{4,20},{8,24},{12,28},{16,0},{20,4},{24,8},{28,12},{1,17},{... | collective-permute-start | bytes 92168 | tf_op jit(solution)/shard_map/ppermute | solution.py:205
  (70 other events, 249.9 us)

commit v5 on v4

--- a/solution.py
+++ b/solution.py
@@ -312,6 +312,11 @@
             at = (d_idx >> bit) & 1
             send = yield [total]
             got = dp_swap(send[0], bit)
+            if bit == 0:
+                total = jnp.concatenate(
+                    [jnp.where(at == 0, total, got), jnp.where(at == 0, got, total)], axis=0
+                )
+                continue
             total = jnp.where(
                 at == 0,
                 jnp.concatenate([total, got], 0),

time: 424 us -> 416 us (0.981)
  other arithmetic: 87.7 us -> 80.4 us
  blocking collectives: 22.3 us -> 27.7 us
    all_to_all x4 -> x5, blocking collectives: 22.3 us -> 27.7 us  [core_trade(): return lax.all_to_all(value, 'tensor', 0, 0, axis_index_groups=pairs)]
    select_n x4 -> x3, other arithmetic: 10.2 us -> 5.85 us  [reduce_blocks(): jnp.where(at == 0, jnp.concatenate([total, got], 0), jnp.concatenate([got...]
    all_to_all x5 -> x4, starting transfers between devices: 22.8 us -> 19.3 us  [core_trade(): return lax.all_to_all(value, 'tensor', 0, 0, axis_index_groups=pairs)]
    unnamed x199 -> x191, local copies, waits for them, and re-layouts: 15.1 us -> 14.1 us
  transfers between devices with their start and end apart: 41 -> 40, of which waited for: 22 -> 21; matrix products, arithmetic and copies ran while one was open for 46% -> 45% of each run, Pallas kernels for 10% -> 10%
where the time goes in v5:
time: 416 us; the launch traced here: 409 us
  matrix products  83 us (20%)
  other arithmetic  80.4 us (19%)
  waiting for transfers between devices  66.7 us (16%)
  starting transfers between devices  62.3 us (15%)
  local copies, waits for them, and re-layouts  43.8 us (11%)
  Pallas kernels  42.8 us (10%)
  blocking collectives  27.7 us (7%)
    dot_general x24, matrix products, mm(): return lax.dot_general(left, right, dims, preferred_element_type=F32)  83 us
    ppermute x22, waiting for transfers between devices, dp_swap(): return lax.ppermute(value, 'dp', [(a, a ^ 1 << bit) for a in range(n_dp)])  56.5 us
    all_to_all x5, blocking collectives, core_trade(): return lax.all_to_all(value, 'tensor', 0, 0, axis_index_groups=pairs)  27.7 us
    pallas_call x2, Pallas kernels, attention_backward(): pl.pallas_call(functools.partial(attn_bwd_kernel, seq, width), grid=(imag...  26.1 us
    ppermute x22, starting transfers between devices, dp_swap(): return lax.ppermute(value, 'dp', [(a, a ^ 1 << bit) for a in range(n_dp)])  24.8 us
    all_to_all x4, starting transfers between devices, core_trade(): return lax.all_to_all(value, 'tensor', 0, 0, axis_index_groups=pairs)  19.3 us
    ppermute x11, starting transfers between devices, chip_shift(): return lax.ppermute(value, 'tensor', perm)  17.7 us
    pallas_call x2, Pallas kernels, attention_forward(): pl.pallas_call(functools.partial(attn_fwd_kernel, seq), grid=(images, pai...  16.7 us
  transfers between devices with their start and end apart: 40, of which 21 were waited for; matrix products, arithmetic and copies ran while one was open for 45% of the time, Pallas kernels for 10%

profile of v5, /device:TPU:0, one launch (start us, length us, event | category | flops | bytes accessed | tf_op | source)
XLA Modules:
  0.0 409.3 jit_solution(12228084687876489865)
XLA Ops:
  0.7 4.0 constant_dynamic-slice_fusion.12
  4.7 3.0 collective-permute-start
  7.8 3.8 constant_dynamic-slice_fusion.6
  29.6 6.1 %all_to_all.45 = bf16[2,592,1024]{2,1,0:T(8,128)(2,1)S(1)} all-to-all(bf16[2,592,1024]{2,1,0:T(8,128)(2,1)S(1)} %broadcast_in_dim.6), channel_id=1, replica_groups={{0,1},{2,3},{4,5},{6,7},{8,9},{10,11},{12,13},{14,15},{16,17},{18,19},{..., dimensions={0} | all-to-all | bytes 4849664 | tf_op jit(solution)/shard_map/all_to_all | solution.py:202
  35.8 3.3 fusion.6.q_ref.k_ref.v_ref
  39.1 4.7 %collective-permute-done.2 = bf16[512,768]{1,0:T(8,128)(2,1)} collective-permute-done((bf16[512,768]{1,0:T(8,128)(2,1)}, bf16[512,768]{1,0:T(8,128)(2,1)}, u32[]{:S(2)}, u32[]{:S(2)}) %collective-permute-start.2) | collective-permute-done | bytes 786464 | tf_op jit(solution)/shard_map/ppermute | solution.py:195
  49.2 8.3 %attn_fwd.2 = (bf16[1184,256]{1,0:T(8,128)(2,1)}, f32[2,2,2,592]{3,2,1,0:T(2,128)}) custom-call(bf16[1184,768]{1,0:T(8,128)(2,1)} %fusion.6.q_ref.k_ref.v_ref, bf16[1184,768]{1,0:T(8,128)(2,1)} %fusion.6.q_ref.k_ref.v_ref, bf16[1184,768]{1,0:T(8,128)(2,1)} %fusion.6.q_ref.k_ref.v_ref), custom_call_target="tpu_custom_call" | custom-call | flops 2871001088 | bytes 2424832 | tf_op jit(solution)/shard_map/attn_fwd/pallas_call | solution.py:96
  57.5 4.2 %fusion.69 = f32[1184,1024]{1,0:T(8,128)} fusion(bf16[1184,256]{1,0:T(8,128)(2,1)} %get-tuple-element.133, bf16[256,1024]{1,0:T(8,128)(2,1)} %param.20), kind=kOutput, calls=%fused_computation.220 | convolution fusion | flops 620756992 | bytes 5980160 | tf_op jit(solution)/shard_map/dot_general | solution.py:26
  65.7 2.3 maximum_select_fusion.2
  69.8 3.3 fusion.7.q_ref.k_ref.v_ref
  75.9 8.4 %attn_fwd.3 = (bf16[1184,256]{1,0:T(8,128)(2,1)}, f32[2,2,2,592]{3,2,1,0:T(2,128)}) custom-call(bf16[1184,768]{1,0:T(8,128)(2,1)} %fusion.7.q_ref.k_ref.v_ref, bf16[1184,768]{1,0:T(8,128)(2,1)} %fusion.7.q_ref.k_ref.v_ref, bf16[1184,768]{1,0:T(8,128)(2,1)} %fusion.7.q_ref.k_ref.v_ref), custom_call_target="tpu_custom_call" | custom-call | flops 2871001088 | bytes 2424832 | tf_op jit(solution)/shard_map/attn_fwd/pallas_call | solution.py:96
  86.1 3.4 add_convert_fusion.1
  89.5 5.7 %all_to_all.46 = bf16[2,592,1024]{2,1,0:T(8,128)(2,1)S(1)} all-to-all(bf16[2,592,1024]{2,1,0:T(8,128)(2,1)S(1)} %bitcast.151), channel_id=1, replica_groups={{0,1},{2,3},{4,5},{6,7},{8,9},{10,11},{12,13},{14,15},{16,17},{18,19},{..., dimensions={0} | all-to-all | bytes 4849664 | tf_op jit(solution)/shard_map/all_to_all | solution.py:202
  97.9 6.2 %all_to_all.47 = bf16[2,592,1024]{2,1,0:T(8,128)(2,1)S(1)} all-to-all(bf16[2,592,1024]{2,1,0:T(8,128)(2,1)S(1)} %broadcast_in_dim.7), channel_id=1, replica_groups={{0,1},{2,3},{4,5},{6,7},{8,9},{10,11},{12,13},{14,15},{16,17},{18,19},{..., dimensions={0} | all-to-all | bytes 4849664 | tf_op jit(solution)/shard_map/all_to_all | solution.py:202
  104.1 4.8 %collective-permute-done.8 = bf16[512,1024]{1,0:T(8,128)(2,1)S(1)} collective-permute-done((bf16[512,1024]{1,0:T(8,128)(2,1)}, bf16[512,1024]{1,0:T(8,128)(2,1)S(1)}, u32[]{:S(2)}, u32[]{:S(2)}) %collective-permute-start.8) | collective-permute-done | bytes 1048608 | tf_op jit(solution)/shard_map/ppermute | solution.py:205
  109.0 2.5 maximum_select_fusion
  112.7 2.7 fusion.70
  115.4 3.3 multiply_convert_fusion.3
  120.2 4.4 %convolution_convert_fusion.5 = bf16[1024,1024]{1,0:T(8,128)(2,1)} fusion(bf16[1184,1024]{1,0:T(8,128)(2,1)S(1)} %bitcast.152, f32[1184,1024]{1,0:T(8,128)S(1)} %fusion.70, f32[1024]{0:T(1024)S(1)} %bitcast.174), kind=kOutput, calls=%fused_computation.95 | convolution fusion | flops 2492563456 | bytes 9375744 | tf_op jit(solution)/shard_map/dot_general | solution.py:26
  124.6 4.3 %multiply_convert_fusion.1 = bf16[1184,1024]{1,0:T(8,128)(2,1)S(1)} fusion(bf16[1184,1024]{1,0:T(8,128)(2,1)S(1)} %bitcast.153, bf16[1024,1024]{1,0:T(8,128)(2,1)S(1)} %copy-done.50, f32[1184,1024]{1,0:T(8,128)S(1)} %get-tuple-element.278, f32[1024]{0:T(1024)S(1)} %convert_element_type.292), kind=kOutput, calls=%fused_computation.9 | convolution fusion | flops 2496364544 | bytes 11800576 | tf_op jit(solution)/shard_map/dot_general | solution.py:26
  129.0 4.4 %convolution_convert_fusion.4 = bf16[1024,1024]{1,0:T(8,128)(2,1)} fusion(bf16[1184,1024]{1,0:T(8,128)(2,1)S(1)} %bitcast.168, bf16[1184,1024]{1,0:T(8,128)(2,1)S(1)} %multiply_convert_fusion.1), kind=kOutput, calls=%fused_computation.94 | convolution fusion | flops 2484076544 | bytes 6946816 | tf_op jit(solution)/shard_map/dot_general | solution.py:26
  135.1 2.7 fusion.71
  137.9 4.2 %convolution_convert_fusion.3 = bf16[1024,1024]{1,0:T(8,128)(2,1)} fusion(bf16[1184,1024]{1,0:T(8,128)(2,1)S(1)} %get-tuple-element.138, bf16[1184,1024]{1,0:T(8,128)(2,1)S(1)} %bitcast.154), kind=kOutput, calls=%fused_computation.93 | convolution fusion | flops 2484076544 | bytes 6946816 | tf_op jit(solution)/shard_map/dot_general | solution.py:26
  142.1 3.6 collective-permute-done.11
  145.7 2.5 maximum_select_fusion.1
  148.3 4.3 %multiply_convert_fusion = bf16[1184,1024]{1,0:T(8,128)(2,1)S(1)} fusion(bf16[1184,1024]{1,0:T(8,128)(2,1)S(1)} %bitcast.155, bf16[1024,1024]{1,0:T(8,128)(2,1)S(1)} %maximum_select_fusion.1, f32[1184,1024]{1,0:T(8,128)S(1)} %fusion.70, f32[1024]{0:T(1024)S(1)} %bitcast.175), kind=kOutput, calls=%fused_computation.8 | convolution fusion | flops 2496364544 | bytes 11800576 | tf_op jit(solution)/shard_map/dot_general | solution.py:26
  152.6 4.2 %convolution_convert_fusion.2 = bf16[1024,1024]{1,0:T(8,128)(2,1)} fusion(bf16[1184,1024]{1,0:T(8,128)(2,1)S(1)} %bitcast.169, bf16[1184,1024]{1,0:T(8,128)(2,1)S(1)} %multiply_convert_fusion), kind=kOutput, calls=%fused_computation.92 | convolution fusion | flops 2484076544 | bytes 6946816 | tf_op jit(solution)/shard_map/dot_general | solution.py:26
  156.8 2.7 fusion.72
  161.8 4.2 %all-to-all-start.3 = ((bf16[2,592,1024]{2,1,0:T(8,128)(2,1)}), bf16[2,592,1024]{2,1,0:T(8,128)(2,1)S(1)}, u32[]{:S(2)}, u32[]{:S(2)}) async-start(bf16[2,592,1024]{2,1,0:T(8,128)(2,1)} %bitcast.150), calls=%async_computation.3 | async-start | bytes 4849664 | tf_op jit(solution)/shard_map/all_to_all | solution.py:202
  173.0 2.9 convert_reduce_fusion.6
  177.6 4.9 %all-to-all-start.4 = ((bf16[2,592,1024]{2,1,0:T(8,128)(2,1)}), bf16[2,592,1024]{2,1,0:T(8,128)(2,1)}, u32[]{:S(2)}, u32[]{:S(2)}) async-start(bf16[2,592,1024]{2,1,0:T(8,128)(2,1)} %broadcast_in_dim.8), calls=%async_computation.4 | async-start | bytes 4849664 | tf_op jit(solution)/shard_map/all_to_all | solution.py:202
  185.6 2.5 add_convert_fusion.4
  191.6 3.3 convolution_convert_fusion.1.do_ref
  194.9 12.9 %attn_bwd.2 = bf16[1184,768]{1,0:T(8,128)(2,1)} custom-call(bf16[1184,768]{1,0:T(8,128)(2,1)} %fusion.7.q_ref.k_ref.v_ref, bf16[1184,768]{1,0:T(8,128)(2,1)} %fusion.7.q_ref.k_ref.v_ref, bf16[1184,768]{1,0:T(8,128)(2,1)} %fusion.7.q_ref.k_ref.v_ref, bf16[1184,256]{1,0:T(8,128)(2,1)} %convolution_convert_fusion.1.do_ref, ...), custom_call_target="tpu_custom_call" | custom-call | flops 7177502720 | bytes 4243456 | tf_op jit(solution)/shard_map/attn_bwd/pallas_call | solution.py:119
  207.8 8.7 %collective-permute-done.13 = bf16[512,1024]{1,0:T(8,128)(2,1)} collective-permute-done((bf16[512,1024]{1,0:T(8,128)(2,1)}, bf16[512,1024]{1,0:T(8,128)(2,1)}, u32[]{:S(2)}, u32[]{:S(2)}) %collective-permute-start.13) | collective-permute-done | bytes 1048608 | tf_op jit(solution)/shard_map/ppermute | solution.py:205
  221.1 2.7 convolution_convert_fusion.9
  223.8 4.3 %fusion.73 = f32[1184,1024]{1,0:T(8,128)} fusion(bf16[1184,768]{1,0:T(8,128)(2,1)S(1)} %copy-done.42, bf16[1024,768]{1,0:T(8,128)(2,1)S(1)} %copy-done.45), kind=kOutput, calls=%fused_computation.224 | convolution fusion | flops 1862270976 | bytes 8241152 | tf_op jit(solution)/shard_map/dot_general | solution.py:26
  228.1 2.4 convolution_convert_fusion.7
  233.6 2.5 add_convert_fusion.3
  238.8 2.6 collective-permute-start.17
  242.0 3.3 convolution_convert_fusion.do_ref
  245.3 13.1 %attn_bwd.3 = bf16[1184,768]{1,0:T(8,128)(2,1)} custom-call(bf16[1184,768]{1,0:T(8,128)(2,1)} %fusion.6.q_ref.k_ref.v_ref, bf16[1184,768]{1,0:T(8,128)(2,1)} %fusion.6.q_ref.k_ref.v_ref, bf16[1184,768]{1,0:T(8,128)(2,1)} %fusion.6.q_ref.k_ref.v_ref, bf16[1184,256]{1,0:T(8,128)(2,1)} %convolution_convert_fusion.do_ref, ...), custom_call_target="tpu_custom_call" | custom-call | flops 7177502720 | bytes 4243456 | tf_op jit(solution)/shard_map/attn_bwd/pallas_call | solution.py:119
  258.4 5.4 %collective-permute-done.17 = bf16[256,1024]{1,0:T(8,128)(2,1)} collective-permute-done((bf16[256,1024]{1,0:T(8,128)(2,1)S(1)}, bf16[256,1024]{1,0:T(8,128)(2,1)}, u32[]{:S(2)}, u32[]{:S(2)}) %collective-permute-start.17) | collective-permute-done | bytes 524320 | tf_op jit(solution)/shard_map/ppermute | solution.py:205
  269.7 2.7 convolution_convert_fusion.8
  272.5 2.3 convolution_convert_fusion.6
  274.9 3.6 convolution_add_fusion
  279.4 2.3 add_convert_fusion.2
  284.2 5.2 %all-to-all-start.5 = ((bf16[2,592,1024]{2,1,0:T(8,128)(2,1)}), bf16[2,592,1024]{2,1,0:T(8,128)(2,1)}, u32[]{:S(2)}, u32[]{:S(2)}) async-start(bf16[2,592,1024]{2,1,0:T(8,128)(2,1)} %bitcast.170), calls=%async_computation.5 | async-start | bytes 4849664 | tf_op jit(solution)/shard_map/all_to_all | solution.py:202
  289.3 2.5 collective-permute-start.21
  295.5 2.8 maximum_select_fusion.3
  301.1 2.7 fusion.74
  303.9 4.1 %convolution_add_fusion.1 = bf16[1184,1024]{1,0:T(8,128)(2,1)} fusion(f32[1184,1024]{1,0:T(8,128)S(1)} %fusion.74, bf16[1024,1024]{1,0:T(8,128)(2,1)S(1)} %copy-done.33, f32[1184,1024]{1,0:T(8,128)S(1)} %bitcast.181, f32[1024]{0:T(1024)S(1)} %bitcast.176), kind=kOutput, calls=%fused_computation.16 | convolution fusion | flops 2493939712 | bytes 14225408 | tf_op jit(solution)/shard_map/dot_general | solution.py:26
  308.4 4.8 %all_to_all.48 = bf16[2,1,577,512]{3,2,1,0:T(8,128)(2,1)S(1)} all-to-all(bf16[2,1,577,512]{3,2,1,0:T(8,128)(2,1)S(1)} %pad_maximum_fusion.4), channel_id=1, replica_groups={{0,1},{2,3},{4,5},{6,7},{8,9},{10,11},{12,13},{14,15},{16,17},{18,19},{..., dimensions={0} | all-to-all | bytes 2363392 | tf_op jit(solution)/shard_map/all_to_all | solution.py:202
  322.4 4.9 %all-to-all-start.7 = ((bf16[2,592,1024]{2,1,0:T(8,128)(2,1)}), bf16[2,592,1024]{2,1,0:T(8,128)(2,1)}, u32[]{:S(2)}, u32[]{:S(2)}) async-start(bf16[2,592,1024]{2,1,0:T(8,128)(2,1)} %bitcast.165), calls=%async_computation.7 | async-start | bytes 4849664 | tf_op jit(solution)/shard_map/all_to_all | solution.py:202
  340.0 4.9 %all_to_all.49 = bf16[2,1,577,512]{3,2,1,0:T(8,128)(2,1)S(1)} all-to-all(bf16[2,1,577,512]{3,2,1,0:T(8,128)(2,1)S(1)} %pad_maximum_fusion.5), channel_id=1, replica_groups={{0,1},{2,3},{4,5},{6,7},{8,9},{10,11},{12,13},{14,15},{16,17},{18,19},{..., dimensions={0} | all-to-all | bytes 2363392 | tf_op jit(solution)/shard_map/all_to_all | solution.py:202
  345.0 6.3 %collective-permute-done.28 = bf16[256,1024]{1,0:T(8,128)(2,1)} collective-permute-done((bf16[256,1024]{1,0:T(8,128)(2,1)S(1)}, bf16[256,1024]{1,0:T(8,128)(2,1)}, u32[]{:S(2)}, u32[]{:S(2)}) %collective-permute-start.28) | collective-permute-done | bytes 524320 | tf_op jit(solution)/shard_map/ppermute | solution.py:205
  357.4 2.4 collective-permute-start.25
  359.8 3.6 collective-permute-done.26
  367.5 2.4 maximum_convert_fusion.1
  369.9 6.0 %collective-permute-done.31 = f32[7680]{0:T(1024)S(1)} collective-permute-done((f32[7680]{0:T(1024)S(1)}, f32[7680]{0:T(1024)S(1)}, u32[]{:S(2)}, u32[]{:S(2)}) %collective-permute-start.31) | collective-permute-done | bytes 30752 | tf_op jit(solution)/shard_map/ppermute | solution.py:205
  377.5 2.4 collective-permute-start.32
  380.1 2.4 maximum_convert_fusion
  389.5 11.9 %collective-permute-done.32 = bf16[512,1024]{1,0:T(8,128)(2,1)} collective-permute-done((bf16[512,1024]{1,0:T(8,128)(2,1)}, bf16[512,1024]{1,0:T(8,128)(2,1)}, u32[]{:S(2)}, u32[]{:S(2)}) %collective-permute-start.32) | collective-permute-done | bytes 1048608 | tf_op jit(solution)/shard_map/ppermute | solution.py:205
  405.8 3.3 maximum_convert_fusion.2
  (372 shorter events, 129.5 us)
Async XLA Ops:
  0.6 17.1 %copy-start = (bf16[1024,1024]{1,0:T(8,128)(2,1)S(1)}, bf16[1024,1024]{1,0:T(8,128)(2,1)}, u32[]{:S(2)}) copy-start(bf16[1024,1024]{1,0:T(8,128)(2,1)} %param.26) | copy-start | bytes 6291460
  0.7 7.1 %copy-start.79 = (bf16[2,256]{1,0:T(2,128)(2,1)S(1)}, bf16[2,256]{1,0:T(2,128)(2,1)}, u32[]{:S(2)}) copy-start(bf16[2,256]{1,0:T(2,128)(2,1)} %param.19) | copy-start | bytes 3076
  0.7 7.1 %copy-start.66 = (bf16[1024]{0:T(1024)(128)(2,1)S(1)}, bf16[1024]{0:T(1024)(128)(2,1)}, u32[]{:S(2)}) copy-start(bf16[1024]{0:T(1024)(128)(2,1)} %param.27) | copy-start | bytes 6148
  4.7 16.7 %collective-permute-start = (bf16[2,577,256]{2,0,1:T(2,128)(2,1)}, bf16[2,577,256]{2,0,1:T(2,128)(2,1)}, u32[]{:S(2)}, u32[]{:S(2)}) collective-permute-start(bf16[2,577,256]{2,0,1:T(2,128)(2,1)} %get-tuple-element.256), channel_id=1, source_target_pairs={{0,2},{1,3},{2,0},{3,1},{4,6},{5,7},{6,4},{7,5},{8,10},{9,11},{10,... | collective-permute-start | bytes 1772552 | tf_op jit(solution)/shard_map/ppermute | solution.py:195
  23.4 2.4 collective-permute-start.1
  23.5 20.3 %collective-permute-start.2 = (bf16[512,768]{1,0:T(8,128)(2,1)}, bf16[512,768]{1,0:T(8,128)(2,1)}, u32[]{:S(2)}, u32[]{:S(2)}) collective-permute-start(bf16[512,768]{1,0:T(8,128)(2,1)} %constant_dynamic-slice_fusion.11), channel_id=1, source_target_pairs={{0,2},{1,3},{2,0},{3,1},{4,6},{5,7},{6,4},{7,5},{8,10},{9,11},{10,... | collective-permute-start | bytes 2359304 | tf_op jit(solution)/shard_map/ppermute | solution.py:195
  27.3 68.4 %copy-start.4 = (bf16[1,592,1024]{2,1,0:T(8,128)(2,1)}, bf16[1,592,1024]{2,1,0:T(8,128)(2,1)S(1)}, u32[]{:S(2)}) copy-start(bf16[1,592,1024]{2,1,0:T(8,128)(2,1)S(1)} %get-tuple-element.215) | copy-start | bytes 3637252
  35.7 9.8 %copy-start.24 = (bf16[2,577,256]{2,0,1:T(2,128)(2,1)S(1)}, bf16[2,577,256]{2,0,1:T(2,128)(2,1)}, u32[]{:S(2)}) copy-start(bf16[2,577,256]{2,0,1:T(2,128)(2,1)} %get-tuple-element.254) | copy-start | bytes 1772548
  35.7 10.7 %copy-start.75 = (bf16[1024]{0:T(1024)(128)(2,1)S(1)}, bf16[1024]{0:T(1024)(128)(2,1)}, u32[]{:S(2)}) copy-start(bf16[1024]{0:T(1024)(128)(2,1)} %param.24) | copy-start | bytes 6148
  35.8 10.7 %copy-start.76 = (bf16[1024]{0:T(1024)(128)(2,1)S(1)}, bf16[1024]{0:T(1024)(128)(2,1)}, u32[]{:S(2)}) copy-start(bf16[1024]{0:T(1024)(128)(2,1)} %param.21) | copy-start | bytes 6148
  35.8 10.7 %copy-start.77 = (bf16[1024]{0:T(1024)(128)(2,1)S(1)}, bf16[1024]{0:T(1024)(128)(2,1)}, u32[]{:S(2)}) copy-start(bf16[1024]{0:T(1024)(128)(2,1)} %param.25) | copy-start | bytes 6148
  35.8 10.7 %copy-start.78 = (bf16[1024]{0:T(1024)(128)(2,1)S(1)}, bf16[1024]{0:T(1024)(128)(2,1)}, u32[]{:S(2)}) copy-start(bf16[1024]{0:T(1024)(128)(2,1)} %param.29) | copy-start | bytes 6148
  35.8 11.3 %copy-start.80 = (s32[4]{0:T(128)S(1)}, s32[4]{0:T(128)}, u32[]{:S(2)}) copy-start(s32[4]{0:T(128)} %param.17) | copy-start | bytes 52
  43.8 19.4 %collective-permute-start.3 = (bf16[512,768]{1,0:T(8,128)(2,1)}, bf16[512,768]{1,0:T(8,128)(2,1)}, u32[]{:S(2)}, u32[]{:S(2)}) collective-permute-start(bf16[512,768]{1,0:T(8,128)(2,1)} %collective-permute-done.2), channel_id=1, source_target_pairs={{0,4},{4,0},{8,12},{12,8},{16,20},{20,16},{24,28},{28,24},{1,5},{5... | collective-permute-start | bytes 2359304 | tf_op jit(solution)/shard_map/ppermute | solution.py:205
  47.2 14.6 %collective-permute-start.4 = (bf16[144,1024]{1,0:T(8,128)(2,1)}, bf16[144,1024]{1,0:T(8,128)(2,1)}, u32[]{:S(2)}, u32[]{:S(2)}) collective-permute-start(bf16[144,1024]{1,0:T(8,128)(2,1)} %pad_maximum_fusion.8), channel_id=1, source_target_pairs={{0,2},{1,3},{2,0},{3,1},{4,6},{5,7},{6,4},{7,5},{8,10},{9,11},{10,... | collective-permute-start | bytes 884744 | tf_op jit(solution)/shard_map/ppermute | solution.py:195
  48.7 35.6 %collective-permute-start.5 = (bf16[512,1024]{1,0:T(8,128)(2,1)}, bf16[512,1024]{1,0:T(8,128)(2,1)}, u32[]{:S(2)}, u32[]{:S(2)}) collective-permute-start(bf16[512,1024]{1,0:T(8,128)(2,1)} %constant_dynamic-slice_fusion.9), channel_id=1, source_target_pairs={{0,2},{1,3},{2,0},{3,1},{4,6},{5,7},{6,4},{7,5},{8,10},{9,11},{10,... | collective-permute-start | bytes 3145736 | tf_op jit(solution)/shard_map/ppermute | solution.py:195
  61.8 8.1 %copy-start.18 = (bf16[2,592,1024]{2,1,0:T(8,128)(2,1)S(1)}, bf16[2,592,1024]{2,1,0:T(8,128)(2,1)}, u32[]{:S(2)}) copy-start(bf16[2,592,1024]{2,1,0:T(8,128)(2,1)} %copy-done.17) | copy-start | bytes 7274500
  68.0 16.2 %collective-permute-start.6 = (bf16[128,1024]{1,0:T(8,128)(2,1)}, bf16[128,1024]{1,0:T(8,128)(2,1)}, u32[]{:S(2)}, u32[]{:S(2)}) collective-permute-start(bf16[128,1024]{1,0:T(8,128)(2,1)} %slice.222), channel_id=1, source_target_pairs={{0,4},{4,0},{8,12},{12,8},{16,20},{20,16},{24,28},{28,24},{1,5},{5... | collective-permute-start | bytes 786440 | tf_op jit(solution)/shard_map/ppermute | solution.py:205
  73.1 31.0 %collective-permute-start.7 = (bf16[2,577,256]{2,1,0:T(8,128)(2,1)}, bf16[2,577,256]{2,1,0:T(8,128)(2,1)}, u32[]{:S(2)}, u32[]{:S(2)}) collective-permute-start(bf16[2,577,256]{2,1,0:T(8,128)(2,1)} %copy.69), channel_id=1, source_target_pairs={{0,2},{1,3},{2,0},{3,1},{4,6},{5,7},{6,4},{7,5},{8,10},{9,11},{10,... | collective-permute-start | bytes 1772552 | tf_op jit(solution)/shard_map/ppermute | solution.py:195
  74.7 45.2 %collective-permute-start.10 = (bf16[512,1024]{1,0:T(8,128)(2,1)}, bf16[512,1024]{1,0:T(8,128)(2,1)}, u32[]{:S(2)}, u32[]{:S(2)}) collective-permute-start(bf16[512,1024]{1,0:T(8,128)(2,1)} %constant_dynamic-slice_fusion.8), channel_id=1, source_target_pairs={{0,2},{1,3},{2,0},{3,1},{4,6},{5,7},{6,4},{7,5},{8,10},{9,11},{10,... | collective-permute-start | bytes 3145736 | tf_op jit(solution)/shard_map/ppermute | solution.py:195
  75.9 72.3 %copy-start.71 = (f32[1,1024]{1,0:T(1,128)}, f32[1,1024]{1,0:T(1,128)S(1)}, u32[]{:S(2)}) copy-start(f32[1,1024]{1,0:T(1,128)S(1)} %slice_convert_fusion) | copy-start | bytes 12292
  85.7 23.3 %collective-permute-start.8 = (bf16[512,1024]{1,0:T(8,128)(2,1)}, bf16[512,1024]{1,0:T(8,128)(2,1)S(1)}, u32[]{:S(2)}, u32[]{:S(2)}) collective-permute-start(bf16[512,1024]{1,0:T(8,128)(2,1)} %collective-permute-done.5), channel_id=1, source_target_pairs={{0,4},{4,0},{8,12},{12,8},{16,20},{20,16},{24,28},{28,24},{1,5},{5... | collective-permute-start | bytes 3145736 | tf_op jit(solution)/shard_map/ppermute | solution.py:205
  104.1 7.4 %copy-start.16 = (bf16[2,577,512]{2,1,0:T(8,128)(2,1)S(1)}, bf16[2,577,512]{2,1,0:T(8,128)(2,1)}, u32[]{:S(2)}) copy-start(bf16[2,577,512]{2,1,0:T(8,128)(2,1)} %copy_dynamic-update-slice_fusion) | copy-start | bytes 3545092
  112.6 6.2 %collective-permute-start.9 = (bf16[2,577,512]{2,1,0:T(8,128)(2,1)S(1)}, bf16[2,577,512]{2,1,0:T(8,128)(2,1)S(1)}, u32[]{:S(2)}, u32[]{:S(2)}) collective-permute-start(bf16[2,577,512]{2,1,0:T(8,128)(2,1)S(1)} %constant_dynamic-update-slice_fusion), channel_id=1, source_target_pairs={{0,1},{1,0},{2,3},{3,2},{4,5},{5,4},{6,7},{7,6},{8,9},{9,8},{10,11... | collective-permute-start | bytes 3545096 | tf_op jit(solution)/shard_map/ppermute | solution.py:198
  115.4 32.8 %copy-start.82 = (f32[1184,1024]{1,0:T(8,128)}, f32[1184,1024]{1,0:T(8,128)S(1)}, u32[]{:S(2)}) copy-start(f32[1184,1024]{1,0:T(8,128)S(1)} %fusion.70) | copy-start | bytes 14548996
  118.8 19.1 %copy-start.83 = (bf16[1184,1024]{1,0:T(8,128)(2,1)}, bf16[1184,1024]{1,0:T(8,128)(2,1)S(1)}, u32[]{:S(2)}) copy-start(bf16[1184,1024]{1,0:T(8,128)(2,1)S(1)} %get-tuple-element.138) | copy-start | bytes 7274500
  119.8 28.4 %copy-start.11 = (bf16[2,592,1024]{2,1,0:T(8,128)(2,1)}, bf16[2,592,1024]{2,1,0:T(8,128)(2,1)S(1)}, u32[]{:S(2)}) copy-start(bf16[2,592,1024]{2,1,0:T(8,128)(2,1)S(1)} %fusion.28) | copy-start | bytes 7274500
  119.9 25.8 %collective-permute-start.11 = (bf16[512,1024]{1,0:T(8,128)(2,1)}, bf16[512,1024]{1,0:T(8,128)(2,1)S(1)}, u32[]{:S(2)}, u32[]{:S(2)}) collective-permute-start(bf16[512,1024]{1,0:T(8,128)(2,1)} %collective-permute-done.10), channel_id=1, source_target_pairs={{0,4},{4,0},{8,12},{12,8},{16,20},{20,16},{24,28},{28,24},{1,5},{5... | collective-permute-start | bytes 3145736 | tf_op jit(solution)/shard_map/ppermute | solution.py:205
  133.3 52.1 %collective-permute-start.12 = (bf16[1024,1024]{1,0:T(8,128)(2,1)}, bf16[1024,1024]{1,0:T(8,128)(2,1)}, u32[]{:S(2)}, u32[]{:S(2)}) collective-permute-start(bf16[1024,1024]{1,0:T(8,128)(2,1)} %convolution_convert_fusion.5), channel_id=1, source_target_pairs={{0,2},{1,3},{2,0},{3,1},{4,6},{5,7},{6,4},{7,5},{8,10},{9,11},{10,... | collective-permute-start | bytes 6291464 | tf_op jit(solution)/shard_map/ppermute | solution.py:195
  161.8 7.3 %all-to-all-start.3 = ((bf16[2,592,1024]{2,1,0:T(8,128)(2,1)}), bf16[2,592,1024]{2,1,0:T(8,128)(2,1)S(1)}, u32[]{:S(2)}, u32[]{:S(2)}) async-start(bf16[2,592,1024]{2,1,0:T(8,128)(2,1)} %bitcast.150), calls=%async_computation.3 | async-start | bytes 4849664 | tf_op jit(solution)/shard_map/all_to_all | solution.py:202
  166.0 67.6 %collective-permute-start.15 = (bf16[1024,1024]{1,0:T(8,128)(2,1)}, bf16[1024,1024]{1,0:T(8,128)(2,1)}, u32[]{:S(2)}, u32[]{:S(2)}) collective-permute-start(bf16[1024,1024]{1,0:T(8,128)(2,1)} %convolution_convert_fusion.2), channel_id=1, source_target_pairs={{0,2},{1,3},{2,0},{3,1},{4,6},{5,7},{6,4},{7,5},{8,10},{9,11},{10,... | collective-permute-start | bytes 6291464 | tf_op jit(solution)/shard_map/ppermute | solution.py:195
  177.6 13.1 %all-to-all-start.4 = ((bf16[2,592,1024]{2,1,0:T(8,128)(2,1)}), bf16[2,592,1024]{2,1,0:T(8,128)(2,1)}, u32[]{:S(2)}, u32[]{:S(2)}) async-start(bf16[2,592,1024]{2,1,0:T(8,128)(2,1)} %broadcast_in_dim.8), calls=%async_computation.4 | async-start | bytes 4849664 | tf_op jit(solution)/shard_map/all_to_all | solution.py:202
  185.4 6.2 %copy-start.31 = (bf16[256,1024]{1,0:T(8,128)(2,1)S(1)}, bf16[256,1024]{1,0:T(8,128)(2,1)}, u32[]{:S(2)}) copy-start(bf16[256,1024]{1,0:T(8,128)(2,1)} %copy-done.30) | copy-start | bytes 1572868
  190.7 25.9 %collective-permute-start.13 = (bf16[512,1024]{1,0:T(8,128)(2,1)}, bf16[512,1024]{1,0:T(8,128)(2,1)}, u32[]{:S(2)}, u32[]{:S(2)}) collective-permute-start(bf16[512,1024]{1,0:T(8,128)(2,1)} %constant_dynamic-slice_fusion.5), channel_id=1, source_target_pairs={{0,4},{4,0},{8,12},{12,8},{16,20},{20,16},{24,28},{28,24},{1,5},{5... | collective-permute-start | bytes 3145736 | tf_op jit(solution)/shard_map/ppermute | solution.py:205
  207.8 12.3 %copy-start.42 = (bf16[1184,768]{1,0:T(8,128)(2,1)S(1)}, bf16[1184,768]{1,0:T(8,128)(2,1)}, u32[]{:S(2)}) copy-start(bf16[1184,768]{1,0:T(8,128)(2,1)} %attn_bwd.2) | copy-start | bytes 5455876
  207.8 13.2 %copy-start.48 = (bf16[1184,256]{1,0:T(8,128)(2,1)S(1)}, bf16[1184,256]{1,0:T(8,128)(2,1)}, u32[]{:S(2)}) copy-start(bf16[1184,256]{1,0:T(8,128)(2,1)} %get-tuple-element.122) | copy-start | bytes 1818628
  218.5 20.0 %collective-permute-start.14 = (bf16[256,1024]{1,0:T(8,128)(2,1)S(1)}, bf16[256,1024]{1,0:T(8,128)(2,1)S(1)}, u32[]{:S(2)}, u32[]{:S(2)}) collective-permute-start(bf16[256,1024]{1,0:T(8,128)(2,1)S(1)} %constant_dynamic-slice_fusion.4), channel_id=1, source_target_pairs={{0,8},{4,12},{8,0},{12,4},{16,24},{20,28},{24,16},{28,20},{1,9},{5... | collective-permute-start | bytes 1572872 | tf_op jit(solution)/shard_map/ppermute | solution.py:205
  232.1 47.3 %collective-permute-start.19 = (bf16[1024,1024]{1,0:T(8,128)(2,1)}, bf16[1024,1024]{1,0:T(8,128)(2,1)}, u32[]{:S(2)}, u32[]{:S(2)}) collective-permute-start(bf16[1024,1024]{1,0:T(8,128)(2,1)} %pad_maximum_fusion), channel_id=1, source_target_pairs={{0,2},{1,3},{2,0},{3,1},{4,6},{5,7},{6,4},{7,5},{8,10},{9,11},{10,... | collective-permute-start | bytes 6291464 | tf_op jit(solution)/shard_map/ppermute | solution.py:195
  238.8 25.1 %collective-permute-start.17 = (bf16[256,1024]{1,0:T(8,128)(2,1)S(1)}, bf16[256,1024]{1,0:T(8,128)(2,1)}, u32[]{:S(2)}, u32[]{:S(2)}) collective-permute-start(bf16[256,1024]{1,0:T(8,128)(2,1)S(1)} %add_convert_fusion.14), channel_id=1, source_target_pairs={{0,16},{4,20},{8,24},{12,28},{16,0},{20,4},{24,8},{28,12},{1,17},{... | collective-permute-start | bytes 1572872 | tf_op jit(solution)/shard_map/ppermute | solution.py:205
  241.4 24.2 %collective-permute-start.16 = (bf16[512,1024]{1,0:T(8,128)(2,1)}, bf16[512,1024]{1,0:T(8,128)(2,1)}, u32[]{:S(2)}, u32[]{:S(2)}) collective-permute-start(bf16[512,1024]{1,0:T(8,128)(2,1)} %constant_dynamic-slice_fusion.3), channel_id=1, source_target_pairs={{0,4},{4,0},{8,12},{12,8},{16,20},{20,16},{24,28},{28,24},{1,5},{5... | collective-permute-start | bytes 3145736 | tf_op jit(solution)/shard_map/ppermute | solution.py:205
  267.6 14.9 %collective-permute-start.18 = (bf16[256,1024]{1,0:T(8,128)(2,1)S(1)}, bf16[256,1024]{1,0:T(8,128)(2,1)S(1)}, u32[]{:S(2)}, u32[]{:S(2)}) collective-permute-start(bf16[256,1024]{1,0:T(8,128)(2,1)S(1)} %constant_dynamic-slice_fusion.2), channel_id=1, source_target_pairs={{0,8},{4,12},{8,0},{12,4},{16,24},{20,28},{24,16},{28,20},{1,9},{5... | collective-permute-start | bytes 1572872 | tf_op jit(solution)/shard_map/ppermute | solution.py:205
  268.1 27.4 %collective-permute-start.20 = (bf16[256,1024]{1,0:T(8,128)(2,1)S(1)}, bf16[256,1024]{1,0:T(8,128)(2,1)}, u32[]{:S(2)}, u32[]{:S(2)}) collective-permute-start(bf16[256,1024]{1,0:T(8,128)(2,1)S(1)} %add_convert_fusion.13), channel_id=1, source_target_pairs={{0,8},{4,12},{8,0},{12,4},{16,24},{20,28},{24,16},{28,20},{1,9},{5... | collective-permute-start | bytes 1572872 | tf_op jit(solution)/shard_map/ppermute | solution.py:205
  283.0 6.3 %copy-start.28 = (bf16[256,1024]{1,0:T(8,128)(2,1)}, bf16[256,1024]{1,0:T(8,128)(2,1)S(1)}, u32[]{:S(2)}) copy-start(bf16[256,1024]{1,0:T(8,128)(2,1)S(1)} %add_convert_fusion.12) | copy-start | bytes 1572868
  284.2 8.4 %all-to-all-start.5 = ((bf16[2,592,1024]{2,1,0:T(8,128)(2,1)}), bf16[2,592,1024]{2,1,0:T(8,128)(2,1)}, u32[]{:S(2)}, u32[]{:S(2)}) async-start(bf16[2,592,1024]{2,1,0:T(8,128)(2,1)} %bitcast.170), calls=%async_computation.5 | async-start | bytes 4849664 | tf_op jit(solution)/shard_map/all_to_all | solution.py:202
  289.3 26.5 %collective-permute-start.21 = (bf16[256,1024]{1,0:T(8,128)(2,1)S(1)}, bf16[256,1024]{1,0:T(8,128)(2,1)}, u32[]{:S(2)}, u32[]{:S(2)}) collective-permute-start(bf16[256,1024]{1,0:T(8,128)(2,1)S(1)} %add_convert_fusion.12), channel_id=1, source_target_pairs={{0,16},{4,20},{8,24},{12,28},{16,0},{20,4},{24,8},{28,12},{1,17},{... | collective-permute-start | bytes 1572872 | tf_op jit(solution)/shard_map/ppermute | solution.py:205
  291.9 25.6 %collective-permute-start.22 = (bf16[512,1024]{1,0:T(8,128)(2,1)}, bf16[512,1024]{1,0:T(8,128)(2,1)}, u32[]{:S(2)}, u32[]{:S(2)}) collective-permute-start(bf16[512,1024]{1,0:T(8,128)(2,1)} %constant_dynamic-slice_fusion.1), channel_id=1, source_target_pairs={{0,4},{4,0},{8,12},{12,8},{16,20},{20,16},{24,28},{28,24},{1,5},{5... | collective-permute-start | bytes 3145736 | tf_op jit(solution)/shard_map/ppermute | solution.py:205
  308.4 7.5 %copy-start.29 = (bf16[256,1024]{1,0:T(8,128)(2,1)S(1)}, bf16[256,1024]{1,0:T(8,128)(2,1)}, u32[]{:S(2)}) copy-start(bf16[256,1024]{1,0:T(8,128)(2,1)} %copy-done.28) | copy-start | bytes 1572868
  320.9 15.1 %collective-permute-start.23 = (bf16[256,1024]{1,0:T(8,128)(2,1)}, bf16[256,1024]{1,0:T(8,128)(2,1)}, u32[]{:S(2)}, u32[]{:S(2)}) collective-permute-start(bf16[256,1024]{1,0:T(8,128)(2,1)} %constant_dynamic-slice_fusion), channel_id=1, source_target_pairs={{0,8},{4,12},{8,0},{12,4},{16,24},{20,28},{24,16},{28,20},{1,9},{5... | collective-permute-start | bytes 1572872 | tf_op jit(solution)/shard_map/ppermute | solution.py:205
  321.9 41.8 %collective-permute-start.35 = (bf16[512,1024]{1,0:T(8,128)(2,1)}, bf16[512,1024]{1,0:T(8,128)(2,1)}, u32[]{:S(2)}, u32[]{:S(2)}) collective-permute-start(bf16[512,1024]{1,0:T(8,128)(2,1)} %maximum_select_fusion.3), channel_id=1, source_target_pairs={{0,4},{4,0},{8,12},{12,8},{16,20},{20,16},{24,28},{28,24},{1,5},{5... | collective-permute-start | bytes 3145736 | tf_op jit(solution)/shard_map/ppermute | solution.py:205
  322.4 8.2 %all-to-all-start.7 = ((bf16[2,592,1024]{2,1,0:T(8,128)(2,1)}), bf16[2,592,1024]{2,1,0:T(8,128)(2,1)}, u32[]{:S(2)}, u32[]{:S(2)}) async-start(bf16[2,592,1024]{2,1,0:T(8,128)(2,1)} %bitcast.165), calls=%async_computation.7 | async-start | bytes 4849664 | tf_op jit(solution)/shard_map/all_to_all | solution.py:202
  327.4 6.5 %collective-permute-start.24 = (f32[6144]{0:T(1024)}, f32[6144]{0:T(1024)}, u32[]{:S(2)}, u32[]{:S(2)}) collective-permute-start(f32[6144]{0:T(1024)} %copy-done.59), channel_id=1, source_target_pairs={{0,1},{1,0},{2,3},{3,2},{4,5},{5,4},{6,7},{7,6},{8,9},{9,8},{10,11... | collective-permute-start | bytes 73736 | tf_op jit(solution)/shard_map/ppermute | solution.py:198
  327.9 23.5 %collective-permute-start.28 = (bf16[256,1024]{1,0:T(8,128)(2,1)S(1)}, bf16[256,1024]{1,0:T(8,128)(2,1)}, u32[]{:S(2)}, u32[]{:S(2)}) collective-permute-start(bf16[256,1024]{1,0:T(8,128)(2,1)S(1)} %add_convert_fusion.11), channel_id=1, source_target_pairs={{0,8},{4,12},{8,0},{12,4},{16,24},{20,28},{24,16},{28,20},{1,9},{5... | collective-permute-start | bytes 1572872 | tf_op jit(solution)/shard_map/ppermute | solution.py:205
  337.3 15.7 %collective-permute-start.27 = (f32[7680]{0:T(1024)S(1)}, f32[7680]{0:T(1024)S(1)}, u32[]{:S(2)}, u32[]{:S(2)}) collective-permute-start(f32[7680]{0:T(1024)S(1)} %fusion.49), channel_id=1, source_target_pairs={{0,2},{1,3},{2,0},{3,1},{4,6},{5,7},{6,4},{7,5},{8,10},{9,11},{10,... | collective-permute-start | bytes 92168 | tf_op jit(solution)/shard_map/ppermute | solution.py:195
  338.9 24.5 %collective-permute-start.26 = (bf16[256,1024]{1,0:T(8,128)(2,1)S(1)}, bf16[256,1024]{1,0:T(8,128)(2,1)S(1)}, u32[]{:S(2)}, u32[]{:S(2)}) collective-permute-start(bf16[256,1024]{1,0:T(8,128)(2,1)S(1)} %add_convert_fusion.10), channel_id=1, source_target_pairs={{0,16},{4,20},{8,24},{12,28},{16,0},{20,4},{24,8},{28,12},{1,17},{... | collective-permute-start | bytes 1572872 | tf_op jit(solution)/shard_map/ppermute | solution.py:205
  344.9 8.1 %copy-start.69 = (f32[256]{0:T(256)S(1)}, f32[256]{0:T(256)}, u32[]{:S(2)}) copy-start(f32[256]{0:T(256)} %get-tuple-element.269) | copy-start | bytes 3076
  344.9 8.1 %copy-start.70 = (f32[256]{0:T(256)S(1)}, f32[256]{0:T(256)}, u32[]{:S(2)}) copy-start(f32[256]{0:T(256)} %get-tuple-element.270) | copy-start | bytes 3076
  344.9 10.2 %copy-start.13 = (bf16[2,577,256]{2,1,0:T(8,128)(2,1)S(1)}, bf16[2,577,256]{2,1,0:T(8,128)(2,1)}, u32[]{:S(2)}) copy-start(bf16[2,577,256]{2,1,0:T(8,128)(2,1)} %get-tuple-element.249) | copy-start | bytes 1772548
  353.0 6.8 %collective-permute-start.29 = (f32[7680]{0:T(1024)S(1)}, f32[7680]{0:T(1024)S(1)}, u32[]{:S(2)}, u32[]{:S(2)}) collective-permute-start(f32[7680]{0:T(1024)S(1)} %fusion.52), channel_id=1, source_target_pairs={{0,4},{4,0},{8,12},{12,8},{16,20},{20,16},{24,28},{28,24},{1,5},{5... | collective-permute-start | bytes 92168 | tf_op jit(solution)/shard_map/ppermute | solution.py:205
  353.1 26.8 %collective-permute-start.34 = (bf16[512,1024]{1,0:T(8,128)(2,1)S(1)}, bf16[512,1024]{1,0:T(8,128)(2,1)S(1)}, u32[]{:S(2)}, u32[]{:S(2)}) collective-permute-start(bf16[512,1024]{1,0:T(8,128)(2,1)S(1)} %maximum_select_fusion.4), channel_id=1, source_target_pairs={{0,4},{4,0},{8,12},{12,8},{16,20},{20,16},{24,28},{28,24},{1,5},{5... | collective-permute-start | bytes 3145736 | tf_op jit(solution)/shard_map/ppermute | solution.py:205
  357.4 27.1 %collective-permute-start.25 = (bf16[2,577,512]{2,0,1:T(2,128)(2,1)}, bf16[2,577,512]{2,0,1:T(2,128)(2,1)}, u32[]{:S(2)}, u32[]{:S(2)}) collective-permute-start(bf16[2,577,512]{2,0,1:T(2,128)(2,1)} %copy.58), channel_id=1, source_target_pairs={{0,2},{1,3},{2,0},{3,1},{4,6},{5,7},{6,4},{7,5},{8,10},{9,11},{10,... | collective-permute-start | bytes 3545096 | tf_op jit(solution)/shard_map/ppermute | solution.py:195
  363.6 12.3 %collective-permute-start.30 = (bf16[256,1024]{1,0:T(8,128)(2,1)S(1)}, bf16[256,1024]{1,0:T(8,128)(2,1)S(1)}, u32[]{:S(2)}, u32[]{:S(2)}) collective-permute-start(bf16[256,1024]{1,0:T(8,128)(2,1)S(1)} %add_convert_fusion.9), channel_id=1, source_target_pairs={{0,8},{4,12},{8,0},{12,4},{16,24},{20,28},{24,16},{28,20},{1,9},{5... | collective-permute-start | bytes 1572872 | tf_op jit(solution)/shard_map/ppermute | solution.py:205
  365.4 10.5 %collective-permute-start.31 = (f32[7680]{0:T(1024)S(1)}, f32[7680]{0:T(1024)S(1)}, u32[]{:S(2)}, u32[]{:S(2)}) collective-permute-start(f32[7680]{0:T(1024)S(1)} %add.336), channel_id=1, source_target_pairs={{0,8},{4,12},{8,0},{12,4},{16,24},{20,28},{24,16},{28,20},{1,9},{5... | collective-permute-start | bytes 92168 | tf_op jit(solution)/shard_map/ppermute | solution.py:205
  377.4 5.1 %collective-permute-start.33 = (f32[7680]{0:T(1024)S(1)}, f32[7680]{0:T(1024)S(1)}, u32[]{:S(2)}, u32[]{:S(2)}) collective-permute-start(f32[7680]{0:T(1024)S(1)} %add.337), channel_id=1, source_target_pairs={{0,16},{4,20},{8,24},{12,28},{16,0},{20,4},{24,8},{28,12},{1,17},{... | collective-permute-start | bytes 92168 | tf_op jit(solution)/shard_map/ppermute | solution.py:205
  377.5 23.9 %collective-permute-start.32 = (bf16[512,1024]{1,0:T(8,128)(2,1)}, bf16[512,1024]{1,0:T(8,128)(2,1)}, u32[]{:S(2)}, u32[]{:S(2)}) collective-permute-start(bf16[512,1024]{1,0:T(8,128)(2,1)} %maximum_select_fusion.5), channel_id=1, source_target_pairs={{0,4},{4,0},{8,12},{12,8},{16,20},{20,16},{24,28},{28,24},{1,5},{5... | collective-permute-start | bytes 3145736 | tf_op jit(solution)/shard_map/ppermute | solution.py:205
  (65 other events, 222.5 us)

commit v6 on v5

--- a/solution.py
+++ b/solution.py
@@ -288,30 +288,28 @@
     def add(left, right):
         return (left.astype(F32) + right.astype(F32)).astype(BF16)
 
-    def reduce_blocks(blocks, dp_first):
-        first = 0
-        if dp_first:
-            cut = [halves(block, 0) for block in blocks]
-            send = yield [jnp.concatenate([c[1] for c in cut], 0)]
-            got = dp_swap(send[0], 0)
-            size = cut[0][0].shape[0]
-            blocks = [add(c[0], got[n * size : (n + 1) * size]) for n, c in enumerate(cut)]
-            first = 1
+    def reduce_blocks(blocks):
         send = yield blocks[1:]
-        total = blocks[0].astype(F32)
-        for step in steps:
-            total = total + chip_shift(send[step - 1], chips - step).astype(F32)
+        got = [chip_shift(send[step - 1], chips - step) for step in steps]
+        total = (yield blocks[0]).astype(F32)
+        for piece in got:
+            total = total + piece.astype(F32)
         total = total.astype(BF16)
-        for bit in range(first, bits - 1):
+        for bit in range(bits - 1):
             keep, send = halves(total, bit)
-            send = yield [send]
-            total = add(keep, dp_swap(send[0], bit))
-        send = yield [total]
-        total = add(total, dp_swap(send[0], bits - 1))
+            send = yield send
+            got = dp_swap(send, bit)
+            keep = yield keep
+            total = add(keep, got)
+        send = yield total
+        got = dp_swap(send, bits - 1)
+        keep = yield total
+        total = add(keep, got)
         for bit in reversed(range(bits - 1)):
             at = (d_idx >> bit) & 1
-            send = yield [total]
-            got = dp_swap(send[0], bit)
+            send = yield total
+            got = dp_swap(send, bit)
+            total = yield total
             if bit == 0:
                 total = jnp.concatenate(
                     [jnp.where(at == 0, total, got), jnp.where(at == 0, got, total)], axis=0
@@ -324,26 +322,27 @@
             )
         return total
 
-    def begin(blocks, dp_first=False):
-        flow = reduce_blocks(blocks, dp_first)
-        return [flow, next(flow), None]
-
-    def tie(value, *flows):
-        flows = [flow for flow in flows if flow[2] is None]
-        value, sends = lax.optimization_barrier((value, [flow[1] for flow in flows]))
-        for flow, send in zip(flows, sends):
-            advance(flow, send)
-        return value
-
-    def advance(flow, send):
+    def begin(flow):
+        return [flow, flow.send(next(flow)), None]
+
+    def advance(flow):
         try:
-            flow[1] = flow[0].send(send)
+            flow[1] = flow[0].send(flow[1])
         except StopIteration as end:
             flow[1:] = [], end.value
 
+    def tie(value, *flows):
+        for phase in range(2):
+            going = [flow for flow in flows if flow[2] is None]
+            value, held = lax.optimization_barrier((value, [flow[1] for flow in going]))
+            for flow, item in zip(going, held):
+                flow[1] = item
+                advance(flow)
+        return value
+
     def finish(flow):
         while flow[2] is None:
-            advance(flow, flow[1])
+            advance(flow)
         return flow[2]
 
     def hold(*values):
@@ -445,10 +444,8 @@
         d_hidden.append((mm(dy, wd[r], NT) * slopes[r]).astype(BF16))
         up_blocks.append(mm(normed_two, d_hidden[r], TN).astype(BF16))
     d_hidden, up_blocks = lax.optimization_barrier((d_hidden, up_blocks))
-    flow_down = begin(down_blocks)
-    flow_up = begin(up_blocks)
-    flow_down[1] = flow_down[0].send(flow_down[1])
-    flow_up[1] = flow_up[0].send(flow_up[1])
+    flow_down = begin(reduce_blocks(down_blocks))
+    flow_up = begin(reduce_blocks(up_blocks))
     for r in steps:
         part_two = part_two + mm(d_hidden[r], wu[r], NT)
     back_two, g_gain_two, g_shift_two = norm_back(exchange(part_two), unit_two, inv_two, gain_two)
@@ -475,8 +472,7 @@
             last, attn_blocks[r] = hold(last, attn_blocks[r])
             if r == chips - 1:
                 last = tie(last, flow_down, flow_up)
-    flow_attn = begin(attn_blocks)
-    flow_attn[1] = flow_attn[0].send(flow_attn[1])
+    flow_attn = begin(reduce_blocks(attn_blocks))
     part_one = tie(part_one, flow_up, flow_attn)
     back_one, g_gain_one, g_shift_one = norm_back(
         tie(exchange(part_one), flow_down), unit_one, inv_one, gain_one
@@ -496,7 +492,8 @@
         )
         if split:
             send = yield shared
-            shared = shared + core_swap(send)
+            got = core_swap(send)
+            shared = (yield shared) + got
         own = []
         for r in range(chips):
             rows_sum = jnp.sum(grads[r], axis=0, dtype=F32)
@@ -505,16 +502,17 @@
                 jnp.concatenate([shared, hidden_sum, rows_sum[:width], rows_sum[2 * width :]])
             )
         send = yield own[1:]
-        vector = own[0]
-        for step in steps:
-            vector = vector + chip_shift(send[step - 1], chips - step)
-        for bit in range(bits):
+        got = [chip_shift(send[step - 1], chips - step) for step in steps]
+        vector = yield own[0]
+        for piece in got:
+            vector = vector + piece
+        for bit in list(range(1, bits)) + [0]:
             send = yield vector
-            vector = vector + dp_swap(send, bit)
+            got = dp_swap(send, bit)
+            vector = (yield vector) + got
         return vector
 
-    flow_small = reduce_small()
-    flow_small = [flow_small, next(flow_small), None]
+    flow_small = begin(reduce_small())
 
     mlp_part = mm(after(acts[0], input_rows), w_down, NN)
     for r in steps:
@@ -523,15 +521,18 @@
     mlp_part = tie(after(mlp_part, keep), flow_up, flow_attn, flow_small)
     out = (resid + (exchange(mlp_part) + bias_down.astype(F32))).astype(BF16)
     out = tie(out, flow_attn, flow_small)
+    token = tie(after(slot_mask, out), flow_up)
+    token, out = hold(token, out)
     keep = [jnp.concatenate(pair, axis=2) for pair in zip(own_columns(out), keep)]
     both = scatter_rows(keep)
     layer_out, input_grad = both[:, :, :width], both[:, :, width:]
 
-    token = tie(after(slot_mask, keep), flow_up, flow_small)
+    token = tie(after(token, keep), flow_small)
     token = tie(token, flow_attn, flow_small)
     grad_up = finish(flow_up).astype(F32)
     token, grad_up = hold(token, grad_up)
-    token = tie(token, flow_attn, flow_small)
+    token = tie(token, flow_small)
+    token = tie(token, flow_attn)
     vector = finish(flow_small)
     vecs = [vector[n * full : (n + 1) * full] for n in range(6)]
     mine = vector[6 * full :]

time: 416 us -> 421 us (1.012)
  waiting for transfers between devices: 66.7 us -> 81.4 us
  starting transfers between devices: 62.3 us -> 55.2 us
  matrix products: 83 us -> 76.1 us
  blocking collectives: 27.7 us -> 33.4 us
    ppermute x22, waiting for transfers between devices: 56.5 us -> 70.3 us  [dp_swap(): return lax.ppermute(value, 'dp', [(a, a ^ 1 << bit) for a in range(n_dp)])]
    dot_general x24, matrix products: 83 us -> 76.1 us  [mm(): return lax.dot_general(left, right, dims, preferred_element_type=F32)]
    all_to_all x5 -> x6, blocking collectives: 27.7 us -> 33.4 us  [core_trade(): return lax.all_to_all(value, 'tensor', 0, 0, axis_index_groups=pairs)]
    all_to_all x4 -> x3, starting transfers between devices: 19.3 us -> 14.3 us  [core_trade(): return lax.all_to_all(value, 'tensor', 0, 0, axis_index_groups=pairs)]
    unnamed x191 -> x181, local copies, waits for them, and re-layouts: 14.1 us -> 13.2 us
  transfers between devices with their start and end apart: 40 -> 39, of which waited for: 21 -> 18; matrix products, arithmetic and copies ran while one was open for 45% -> 43% of each run, Pallas kernels for 10% -> 10%
where the time goes in v6:
time: 421 us; the launch traced here: 415 us
  waiting for transfers between devices  81.4 us (19%)
  other arithmetic  81.1 us (19%)
  matrix products  76.1 us (18%)
  starting transfers between devices  55.2 us (13%)
  Pallas kernels  43 us (10%)
  local copies, waits for them, and re-layouts  42.4 us (10%)
  blocking collectives  33.4 us (8%)
    dot_general x24, matrix products, mm(): return lax.dot_general(left, right, dims, preferred_element_type=F32)  76.1 us
    ppermute x22, waiting for transfers between devices, dp_swap(): return lax.ppermute(value, 'dp', [(a, a ^ 1 << bit) for a in range(n_dp)])  70.3 us
    all_to_all x6, blocking collectives, core_trade(): return lax.all_to_all(value, 'tensor', 0, 0, axis_index_groups=pairs)  33.4 us
    pallas_call x2, Pallas kernels, attention_backward(): pl.pallas_call(functools.partial(attn_bwd_kernel, seq, width), grid=(imag...  26.3 us
    ppermute x22, starting transfers between devices, dp_swap(): return lax.ppermute(value, 'dp', [(a, a ^ 1 << bit) for a in range(n_dp)])  25.8 us
    pallas_call x2, Pallas kernels, attention_forward(): pl.pallas_call(functools.partial(attn_fwd_kernel, seq), grid=(images, pai...  16.7 us
    ppermute x11, starting transfers between devices, chip_shift(): return lax.ppermute(value, 'tensor', perm)  14.8 us
    all_to_all x3, starting transfers between devices, core_trade(): return lax.all_to_all(value, 'tensor', 0, 0, axis_index_groups=pairs)  14.3 us
  transfers between devices with their start and end apart: 39, of which 18 were waited for; matrix products, arithmetic and copies ran while one was open for 43% of the time, Pallas kernels for 10%

profile of v6, /device:TPU:0, one launch (start us, length us, event | category | flops | bytes accessed | tf_op | source)
XLA Modules:
  0.0 415.4 jit_solution(6337199081466037870)
XLA Ops:
  0.7 4.0 constant_dynamic-slice_fusion.18
  4.7 3.0 collective-permute-start
  7.8 3.8 constant_dynamic-slice_fusion.12
  29.6 6.3 %all_to_all.45 = bf16[2,592,1024]{2,1,0:T(8,128)(2,1)S(1)} all-to-all(bf16[2,592,1024]{2,1,0:T(8,128)(2,1)S(1)} %broadcast_in_dim.6), channel_id=1, replica_groups={{0,1},{2,3},{4,5},{6,7},{8,9},{10,11},{12,13},{14,15},{16,17},{18,19},{..., dimensions={0} | all-to-all | bytes 4849664 | tf_op jit(solution)/shard_map/all_to_all | solution.py:202
  36.0 3.3 fusion.6.q_ref.k_ref.v_ref
  39.4 4.5 %collective-permute-done.2 = bf16[512,768]{1,0:T(8,128)(2,1)} collective-permute-done((bf16[512,768]{1,0:T(8,128)(2,1)}, bf16[512,768]{1,0:T(8,128)(2,1)}, u32[]{:S(2)}, u32[]{:S(2)}) %collective-permute-start.2) | collective-permute-done | bytes 786464 | tf_op jit(solution)/shard_map/ppermute | solution.py:195
  48.6 8.3 %attn_fwd.2 = (bf16[1184,256]{1,0:T(8,128)(2,1)}, f32[2,2,2,592]{3,2,1,0:T(2,128)}) custom-call(bf16[1184,768]{1,0:T(8,128)(2,1)} %fusion.6.q_ref.k_ref.v_ref, bf16[1184,768]{1,0:T(8,128)(2,1)} %fusion.6.q_ref.k_ref.v_ref, bf16[1184,768]{1,0:T(8,128)(2,1)} %fusion.6.q_ref.k_ref.v_ref), custom_call_target="tpu_custom_call" | custom-call | flops 2871001088 | bytes 2424832 | tf_op jit(solution)/shard_map/attn_fwd/pallas_call | solution.py:96
  57.0 4.2 %fusion.68 = f32[1184,1024]{1,0:T(8,128)} fusion(bf16[1184,256]{1,0:T(8,128)(2,1)} %get-tuple-element.162, bf16[256,1024]{1,0:T(8,128)(2,1)} %param.20), kind=kOutput, calls=%fused_computation.226 | convolution fusion | flops 620756992 | bytes 5980160 | tf_op jit(solution)/shard_map/dot_general | solution.py:26
  65.7 2.2 maximum_select_fusion.2
  69.7 3.3 fusion.7.q_ref.k_ref.v_ref
  75.7 8.4 %attn_fwd.3 = (bf16[1184,256]{1,0:T(8,128)(2,1)}, f32[2,2,2,592]{3,2,1,0:T(2,128)}) custom-call(bf16[1184,768]{1,0:T(8,128)(2,1)} %fusion.7.q_ref.k_ref.v_ref, bf16[1184,768]{1,0:T(8,128)(2,1)} %fusion.7.q_ref.k_ref.v_ref, bf16[1184,768]{1,0:T(8,128)(2,1)} %fusion.7.q_ref.k_ref.v_ref), custom_call_target="tpu_custom_call" | custom-call | flops 2871001088 | bytes 2424832 | tf_op jit(solution)/shard_map/attn_fwd/pallas_call | solution.py:96
  85.9 3.4 add_convert_fusion.1
  89.3 5.7 %all_to_all.46 = bf16[2,592,1024]{2,1,0:T(8,128)(2,1)S(1)} all-to-all(bf16[2,592,1024]{2,1,0:T(8,128)(2,1)S(1)} %bitcast.151), channel_id=1, replica_groups={{0,1},{2,3},{4,5},{6,7},{8,9},{10,11},{12,13},{14,15},{16,17},{18,19},{..., dimensions={0} | all-to-all | bytes 4849664 | tf_op jit(solution)/shard_map/all_to_all | solution.py:202
  97.8 5.8 %all_to_all.47 = bf16[2,592,1024]{2,1,0:T(8,128)(2,1)S(1)} all-to-all(bf16[2,592,1024]{2,1,0:T(8,128)(2,1)S(1)} %broadcast_in_dim.7), channel_id=1, replica_groups={{0,1},{2,3},{4,5},{6,7},{8,9},{10,11},{12,13},{14,15},{16,17},{18,19},{..., dimensions={0} | all-to-all | bytes 4849664 | tf_op jit(solution)/shard_map/all_to_all | solution.py:202
  103.6 5.2 %collective-permute-done.8 = bf16[512,1024]{1,0:T(8,128)(2,1)S(1)} collective-permute-done((bf16[512,1024]{1,0:T(8,128)(2,1)}, bf16[512,1024]{1,0:T(8,128)(2,1)S(1)}, u32[]{:S(2)}, u32[]{:S(2)}) %collective-permute-start.8) | collective-permute-done | bytes 1048608 | tf_op jit(solution)/shard_map/ppermute | solution.py:205
  108.8 2.6 maximum_select_fusion
  112.7 2.7 fusion.69
  115.4 3.3 multiply_convert_fusion.3
  120.2 4.3 %convolution_convert_fusion.5 = bf16[1024,1024]{1,0:T(8,128)(2,1)} fusion(bf16[1184,1024]{1,0:T(8,128)(2,1)S(1)} %bitcast.152, f32[1184,1024]{1,0:T(8,128)S(1)} %fusion.69, f32[1024]{0:T(1024)S(1)} %bitcast.178), kind=kOutput, calls=%fused_computation.96 | convolution fusion | flops 2492563456 | bytes 9375744 | tf_op jit(solution)/shard_map/dot_general | solution.py:26
  124.5 4.3 %multiply_convert_fusion.1 = bf16[1184,1024]{1,0:T(8,128)(2,1)S(1)} fusion(bf16[1184,1024]{1,0:T(8,128)(2,1)S(1)} %bitcast.153, bf16[1024,1024]{1,0:T(8,128)(2,1)S(1)} %copy-done.48, f32[1184,1024]{1,0:T(8,128)S(1)} %get-tuple-element.332, f32[1024]{0:T(1024)S(1)} %convert_element_type.292), kind=kOutput, calls=%fused_computation.9 | convolution fusion | flops 2496364544 | bytes 11800576 | tf_op jit(solution)/shard_map/dot_general | solution.py:26
  128.9 4.4 %convolution_convert_fusion.4 = bf16[1024,1024]{1,0:T(8,128)(2,1)} fusion(bf16[1184,1024]{1,0:T(8,128)(2,1)S(1)} %bitcast.172, bf16[1184,1024]{1,0:T(8,128)(2,1)S(1)} %multiply_convert_fusion.1), kind=kOutput, calls=%fused_computation.95 | convolution fusion | flops 2484076544 | bytes 6946816 | tf_op jit(solution)/shard_map/dot_general | solution.py:26
  135.1 2.7 fusion.70
  137.8 4.2 %convolution_convert_fusion.3 = bf16[1024,1024]{1,0:T(8,128)(2,1)} fusion(bf16[1184,1024]{1,0:T(8,128)(2,1)S(1)} %get-tuple-element.173, bf16[1184,1024]{1,0:T(8,128)(2,1)S(1)} %bitcast.154), kind=kOutput, calls=%fused_computation.94 | convolution fusion | flops 2484076544 | bytes 6946816 | tf_op jit(solution)/shard_map/dot_general | solution.py:26
  142.0 3.6 collective-permute-done.11
  145.6 2.5 maximum_select_fusion.1
  148.2 4.3 %multiply_convert_fusion = bf16[1184,1024]{1,0:T(8,128)(2,1)S(1)} fusion(bf16[1184,1024]{1,0:T(8,128)(2,1)S(1)} %bitcast.155, bf16[1024,1024]{1,0:T(8,128)(2,1)S(1)} %maximum_select_fusion.1, f32[1184,1024]{1,0:T(8,128)S(1)} %fusion.69, f32[1024]{0:T(1024)S(1)} %bitcast.179), kind=kOutput, calls=%fused_computation.8 | convolution fusion | flops 2496364544 | bytes 11800576 | tf_op jit(solution)/shard_map/dot_general | solution.py:26
  152.6 4.2 %convolution_convert_fusion.2 = bf16[1024,1024]{1,0:T(8,128)(2,1)} fusion(bf16[1184,1024]{1,0:T(8,128)(2,1)S(1)} %bitcast.173, bf16[1184,1024]{1,0:T(8,128)(2,1)S(1)} %multiply_convert_fusion), kind=kOutput, calls=%fused_computation.93 | convolution fusion | flops 2484076544 | bytes 6946816 | tf_op jit(solution)/shard_map/dot_general | solution.py:26
  156.7 2.7 fusion.71
  159.5 2.3 add_convert_fusion
  161.8 4.2 %all-to-all-start.3 = ((bf16[2,592,1024]{2,1,0:T(8,128)(2,1)}), bf16[2,592,1024]{2,1,0:T(8,128)(2,1)S(1)}, u32[]{:S(2)}, u32[]{:S(2)}) async-start(bf16[2,592,1024]{2,1,0:T(8,128)(2,1)} %bitcast.150), calls=%async_computation.3 | async-start | bytes 4849664 | tf_op jit(solution)/shard_map/all_to_all | solution.py:202
  173.0 2.9 convert_reduce_fusion.6
  176.2 5.8 %all_to_all.48 = bf16[2,592,1024]{2,1,0:T(8,128)(2,1)S(1)} all-to-all(bf16[2,592,1024]{2,1,0:T(8,128)(2,1)S(1)} %broadcast_in_dim.8), channel_id=1, replica_groups={{0,1},{2,3},{4,5},{6,7},{8,9},{10,11},{12,13},{14,15},{16,17},{18,19},{..., dimensions={0} | all-to-all | bytes 4849664 | tf_op jit(solution)/shard_map/all_to_all | solution.py:202
  185.2 2.5 add_convert_fusion.4
  191.5 13.1 %attn_bwd.2 = bf16[1184,768]{1,0:T(8,128)(2,1)} custom-call(bf16[1184,768]{1,0:T(8,128)(2,1)} %fusion.7.q_ref.k_ref.v_ref, bf16[1184,768]{1,0:T(8,128)(2,1)} %fusion.7.q_ref.k_ref.v_ref, bf16[1184,768]{1,0:T(8,128)(2,1)} %fusion.7.q_ref.k_ref.v_ref, bf16[1184,256]{1,0:T(8,128)(2,1)} %convolution_convert_fusion.1.do_ref, ...), custom_call_target="tpu_custom_call" | custom-call | flops 7177502720 | bytes 4243456 | tf_op jit(solution)/shard_map/attn_bwd/pallas_call | solution.py:119
  204.6 9.8 %collective-permute-done.13 = bf16[512,1024]{1,0:T(8,128)(2,1)} collective-permute-done((bf16[512,1024]{1,0:T(8,128)(2,1)}, bf16[512,1024]{1,0:T(8,128)(2,1)}, u32[]{:S(2)}, u32[]{:S(2)}) %collective-permute-start.13) | collective-permute-done | bytes 1048608 | tf_op jit(solution)/shard_map/ppermute | solution.py:205
  218.7 2.4 convolution_convert_fusion.7
  225.2 4.4 %fusion.72 = f32[1184,1024]{1,0:T(8,128)} fusion(bf16[1184,768]{1,0:T(8,128)(2,1)S(1)} %copy-done.40, bf16[1024,768]{1,0:T(8,128)(2,1)S(1)} %copy-done.43), kind=kOutput, calls=%fused_computation.230 | convolution fusion | flops 1862270976 | bytes 8241152 | tf_op jit(solution)/shard_map/dot_general | solution.py:26
  229.6 2.5 add_convert_fusion.3
  234.3 2.6 collective-permute-start.17
  239.1 13.1 %attn_bwd.3 = bf16[1184,768]{1,0:T(8,128)(2,1)} custom-call(bf16[1184,768]{1,0:T(8,128)(2,1)} %fusion.6.q_ref.k_ref.v_ref, bf16[1184,768]{1,0:T(8,128)(2,1)} %fusion.6.q_ref.k_ref.v_ref, bf16[1184,768]{1,0:T(8,128)(2,1)} %fusion.6.q_ref.k_ref.v_ref, bf16[1184,256]{1,0:T(8,128)(2,1)} %convolution_convert_fusion.do_ref, ...), custom_call_target="tpu_custom_call" | custom-call | flops 7177502720 | bytes 4243456 | tf_op jit(solution)/shard_map/attn_bwd/pallas_call | solution.py:119
  252.2 7.1 %collective-permute-done.17 = bf16[256,1024]{1,0:T(8,128)(2,1)} collective-permute-done((bf16[256,1024]{1,0:T(8,128)(2,1)}, bf16[256,1024]{1,0:T(8,128)(2,1)}, u32[]{:S(2)}, u32[]{:S(2)}) %collective-permute-start.17) | collective-permute-done | bytes 524320 | tf_op jit(solution)/shard_map/ppermute | solution.py:205
  259.3 2.2 add_convert_fusion.13
  266.4 2.3 convolution_convert_fusion.6
  270.1 3.6 convolution_add_fusion
  274.6 2.6 add_convert_fusion.2
  279.9 5.2 %all-to-all-start.5 = ((bf16[2,592,1024]{2,1,0:T(8,128)(2,1)}), bf16[2,592,1024]{2,1,0:T(8,128)(2,1)}, u32[]{:S(2)}, u32[]{:S(2)}) async-start(bf16[2,592,1024]{2,1,0:T(8,128)(2,1)} %bitcast.174), calls=%async_computation.5 | async-start | bytes 4849664 | tf_op jit(solution)/shard_map/all_to_all | solution.py:202
  288.3 2.2 convert_element_type.339
  291.3 3.1 maximum_select_fusion.3
  297.9 2.7 fusion.73
  300.6 4.2 convolution_add_fusion.1
  305.1 4.7 %all_to_all.49 = bf16[2,1,577,512]{3,2,1,0:T(8,128)(2,1)S(1)} all-to-all(bf16[2,1,577,512]{3,2,1,0:T(8,128)(2,1)S(1)} %pad_maximum_fusion.5), channel_id=1, replica_groups={{0,1},{2,3},{4,5},{6,7},{8,9},{10,11},{12,13},{14,15},{16,17},{18,19},{..., dimensions={0} | all-to-all | bytes 2363392 | tf_op jit(solution)/shard_map/all_to_all | solution.py:202
  318.9 4.9 %all-to-all-start.7 = ((bf16[2,592,1024]{2,1,0:T(8,128)(2,1)}), bf16[2,592,1024]{2,1,0:T(8,128)(2,1)}, u32[]{:S(2)}, u32[]{:S(2)}) async-start(bf16[2,592,1024]{2,1,0:T(8,128)(2,1)} %bitcast.169), calls=%async_computation.7 | async-start | bytes 4849664 | tf_op jit(solution)/shard_map/all_to_all | solution.py:202
  324.5 2.6 all-to-all-done.7
  327.1 2.2 convert_element_type.351
  331.4 3.1 maximum_select_fusion.5
  335.5 5.9 %collective-permute-done.24 = bf16[256,1024]{1,0:T(8,128)(2,1)} collective-permute-done((bf16[256,1024]{1,0:T(8,128)(2,1)}, bf16[256,1024]{1,0:T(8,128)(2,1)}, u32[]{:S(2)}, u32[]{:S(2)}) %collective-permute-start.24) | collective-permute-done | bytes 524320 | tf_op jit(solution)/shard_map/ppermute | solution.py:205
  344.3 2.6 collective-permute-start.28
  347.1 5.1 %all_to_all.50 = bf16[2,1,577,512]{3,2,1,0:T(8,128)(2,1)S(1)} all-to-all(bf16[2,1,577,512]{3,2,1,0:T(8,128)(2,1)S(1)} %pad_maximum_fusion.6), channel_id=1, replica_groups={{0,1},{2,3},{4,5},{6,7},{8,9},{10,11},{12,13},{14,15},{16,17},{18,19},{..., dimensions={0} | all-to-all | bytes 2363392 | tf_op jit(solution)/shard_map/all_to_all | solution.py:202
  355.4 15.2 %collective-permute-done.29 = f32[7680]{0:T(1024)S(1)} collective-permute-done((f32[7680]{0:T(1024)S(1)}, f32[7680]{0:T(1024)S(1)}, u32[]{:S(2)}, u32[]{:S(2)}) %collective-permute-start.29) | collective-permute-done | bytes 30752 | tf_op jit(solution)/shard_map/ppermute | solution.py:205
  373.9 2.4 maximum_convert_fusion.1
  377.6 6.7 %collective-permute-done.30 = bf16[256,1024]{1,0:T(8,128)(2,1)S(1)} collective-permute-done((bf16[256,1024]{1,0:T(8,128)(2,1)S(1)}, bf16[256,1024]{1,0:T(8,128)(2,1)S(1)}, u32[]{:S(2)}, u32[]{:S(2)}) %collective-permute-start.30) | collective-permute-done | bytes 524320 | tf_op jit(solution)/shard_map/ppermute | solution.py:205
  388.2 2.4 maximum_convert_fusion
  395.7 13.1 %collective-permute-done.31 = bf16[512,1024]{1,0:T(8,128)(2,1)S(1)} collective-permute-done((bf16[512,1024]{1,0:T(8,128)(2,1)S(1)}, bf16[512,1024]{1,0:T(8,128)(2,1)S(1)}, u32[]{:S(2)}, u32[]{:S(2)}) %collective-permute-start.31) | collective-permute-done | bytes 1048608 | tf_op jit(solution)/shard_map/ppermute | solution.py:205
  411.7 3.3 maximum_convert_fusion.2
  (362 shorter events, 120.1 us)
Async XLA Ops:
  0.6 17.2 %copy-start = (bf16[1024,1024]{1,0:T(8,128)(2,1)S(1)}, bf16[1024,1024]{1,0:T(8,128)(2,1)}, u32[]{:S(2)}) copy-start(bf16[1024,1024]{1,0:T(8,128)(2,1)} %param.26) | copy-start | bytes 6291460
  0.7 7.1 %copy-start.74 = (bf16[2,256]{1,0:T(2,128)(2,1)S(1)}, bf16[2,256]{1,0:T(2,128)(2,1)}, u32[]{:S(2)}) copy-start(bf16[2,256]{1,0:T(2,128)(2,1)} %param.19) | copy-start | bytes 3076
  0.7 7.1 %copy-start.61 = (bf16[1024]{0:T(1024)(128)(2,1)S(1)}, bf16[1024]{0:T(1024)(128)(2,1)}, u32[]{:S(2)}) copy-start(bf16[1024]{0:T(1024)(128)(2,1)} %param.27) | copy-start | bytes 6148
  4.7 16.7 %collective-permute-start = (bf16[2,577,256]{2,0,1:T(2,128)(2,1)}, bf16[2,577,256]{2,0,1:T(2,128)(2,1)}, u32[]{:S(2)}, u32[]{:S(2)}) collective-permute-start(bf16[2,577,256]{2,0,1:T(2,128)(2,1)} %get-tuple-element.302), channel_id=1, source_target_pairs={{0,2},{1,3},{2,0},{3,1},{4,6},{5,7},{6,4},{7,5},{8,10},{9,11},{10,... | collective-permute-start | bytes 1772552 | tf_op jit(solution)/shard_map/ppermute | solution.py:195
  23.4 2.4 collective-permute-start.1
  23.5 20.3 %collective-permute-start.2 = (bf16[512,768]{1,0:T(8,128)(2,1)}, bf16[512,768]{1,0:T(8,128)(2,1)}, u32[]{:S(2)}, u32[]{:S(2)}) collective-permute-start(bf16[512,768]{1,0:T(8,128)(2,1)} %constant_dynamic-slice_fusion.17), channel_id=1, source_target_pairs={{0,2},{1,3},{2,0},{3,1},{4,6},{5,7},{6,4},{7,5},{8,10},{9,11},{10,... | collective-permute-start | bytes 2359304 | tf_op jit(solution)/shard_map/ppermute | solution.py:195
  27.3 68.2 %copy-start.4 = (bf16[1,592,1024]{2,1,0:T(8,128)(2,1)}, bf16[1,592,1024]{2,1,0:T(8,128)(2,1)S(1)}, u32[]{:S(2)}) copy-start(bf16[1,592,1024]{2,1,0:T(8,128)(2,1)S(1)} %get-tuple-element.255) | copy-start | bytes 3637252
  29.6 6.4 %copy-start.33 = (bf16[1024,256]{1,0:T(8,128)(2,1)S(1)}, bf16[1024,256]{1,0:T(8,128)(2,1)}, u32[]{:S(2)}) copy-start(bf16[1024,256]{1,0:T(8,128)(2,1)} %copy-done.32) | copy-start | bytes 1572868
  29.6 6.4 %copy-start.35 = (bf16[1024,256]{1,0:T(8,128)(2,1)S(1)}, bf16[1024,256]{1,0:T(8,128)(2,1)}, u32[]{:S(2)}) copy-start(bf16[1024,256]{1,0:T(8,128)(2,1)} %get-tuple-element.282) | copy-start | bytes 1572868
  29.6 6.4 %copy-start.37 = (bf16[1024,256]{1,0:T(8,128)(2,1)S(1)}, bf16[1024,256]{1,0:T(8,128)(2,1)}, u32[]{:S(2)}) copy-start(bf16[1024,256]{1,0:T(8,128)(2,1)} %get-tuple-element.283) | copy-start | bytes 1572868
  29.6 6.4 %copy-start.76 = (f32[768]{0:T(1024)S(1)}, f32[768]{0:T(1024)}, u32[]{:S(2)}) copy-start(f32[768]{0:T(1024)} %constant.107.clone.1) | copy-start | bytes 9220
  36.0 9.6 %copy-start.24 = (bf16[2,577,256]{2,0,1:T(2,128)(2,1)S(1)}, bf16[2,577,256]{2,0,1:T(2,128)(2,1)}, u32[]{:S(2)}) copy-start(bf16[2,577,256]{2,0,1:T(2,128)(2,1)} %get-tuple-element.300) | copy-start | bytes 1772548
  36.0 10.5 %copy-start.70 = (bf16[1024]{0:T(1024)(128)(2,1)S(1)}, bf16[1024]{0:T(1024)(128)(2,1)}, u32[]{:S(2)}) copy-start(bf16[1024]{0:T(1024)(128)(2,1)} %param.24) | copy-start | bytes 6148
  36.0 10.5 %copy-start.71 = (bf16[1024]{0:T(1024)(128)(2,1)S(1)}, bf16[1024]{0:T(1024)(128)(2,1)}, u32[]{:S(2)}) copy-start(bf16[1024]{0:T(1024)(128)(2,1)} %param.21) | copy-start | bytes 6148
  36.0 10.5 %copy-start.72 = (bf16[1024]{0:T(1024)(128)(2,1)S(1)}, bf16[1024]{0:T(1024)(128)(2,1)}, u32[]{:S(2)}) copy-start(bf16[1024]{0:T(1024)(128)(2,1)} %param.25) | copy-start | bytes 6148
  36.0 10.5 %copy-start.75 = (s32[4]{0:T(128)S(1)}, s32[4]{0:T(128)}, u32[]{:S(2)}) copy-start(s32[4]{0:T(128)} %param.17) | copy-start | bytes 52
  43.8 19.4 %collective-permute-start.3 = (bf16[512,768]{1,0:T(8,128)(2,1)}, bf16[512,768]{1,0:T(8,128)(2,1)}, u32[]{:S(2)}, u32[]{:S(2)}) collective-permute-start(bf16[512,768]{1,0:T(8,128)(2,1)} %collective-permute-done.2), channel_id=1, source_target_pairs={{0,4},{4,0},{8,12},{12,8},{16,20},{20,16},{24,28},{28,24},{1,5},{5... | collective-permute-start | bytes 2359304 | tf_op jit(solution)/shard_map/ppermute | solution.py:205
  46.6 14.6 %collective-permute-start.4 = (bf16[144,1024]{1,0:T(8,128)(2,1)}, bf16[144,1024]{1,0:T(8,128)(2,1)}, u32[]{:S(2)}, u32[]{:S(2)}) collective-permute-start(bf16[144,1024]{1,0:T(8,128)(2,1)} %pad_maximum_fusion.9), channel_id=1, source_target_pairs={{0,2},{1,3},{2,0},{3,1},{4,6},{5,7},{6,4},{7,5},{8,10},{9,11},{10,... | collective-permute-start | bytes 884744 | tf_op jit(solution)/shard_map/ppermute | solution.py:195
  48.1 36.0 %collective-permute-start.5 = (bf16[512,1024]{1,0:T(8,128)(2,1)}, bf16[512,1024]{1,0:T(8,128)(2,1)}, u32[]{:S(2)}, u32[]{:S(2)}) collective-permute-start(bf16[512,1024]{1,0:T(8,128)(2,1)} %constant_dynamic-slice_fusion.15), channel_id=1, source_target_pairs={{0,2},{1,3},{2,0},{3,1},{4,6},{5,7},{6,4},{7,5},{8,10},{9,11},{10,... | collective-permute-start | bytes 3145736 | tf_op jit(solution)/shard_map/ppermute | solution.py:195
  61.2 8.5 %copy-start.14 = (bf16[2,592,1024]{2,1,0:T(8,128)(2,1)S(1)}, bf16[2,592,1024]{2,1,0:T(8,128)(2,1)}, u32[]{:S(2)}) copy-start(bf16[2,592,1024]{2,1,0:T(8,128)(2,1)} %copy-done.13) | copy-start | bytes 7274500
  67.9 16.2 %collective-permute-start.6 = (bf16[128,1024]{1,0:T(8,128)(2,1)}, bf16[128,1024]{1,0:T(8,128)(2,1)}, u32[]{:S(2)}, u32[]{:S(2)}) collective-permute-start(bf16[128,1024]{1,0:T(8,128)(2,1)} %slice.222), channel_id=1, source_target_pairs={{0,4},{4,0},{8,12},{12,8},{16,20},{20,16},{24,28},{28,24},{1,5},{5... | collective-permute-start | bytes 786440 | tf_op jit(solution)/shard_map/ppermute | solution.py:205
  73.0 30.6 %collective-permute-start.7 = (bf16[2,577,256]{2,1,0:T(8,128)(2,1)}, bf16[2,577,256]{2,1,0:T(8,128)(2,1)}, u32[]{:S(2)}, u32[]{:S(2)}) collective-permute-start(bf16[2,577,256]{2,1,0:T(8,128)(2,1)} %copy.69), channel_id=1, source_target_pairs={{0,2},{1,3},{2,0},{3,1},{4,6},{5,7},{6,4},{7,5},{8,10},{9,11},{10,... | collective-permute-start | bytes 1772552 | tf_op jit(solution)/shard_map/ppermute | solution.py:195
  74.5 45.3 %collective-permute-start.10 = (bf16[512,1024]{1,0:T(8,128)(2,1)}, bf16[512,1024]{1,0:T(8,128)(2,1)}, u32[]{:S(2)}, u32[]{:S(2)}) collective-permute-start(bf16[512,1024]{1,0:T(8,128)(2,1)} %constant_dynamic-slice_fusion.14), channel_id=1, source_target_pairs={{0,2},{1,3},{2,0},{3,1},{4,6},{5,7},{6,4},{7,5},{8,10},{9,11},{10,... | collective-permute-start | bytes 3145736 | tf_op jit(solution)/shard_map/ppermute | solution.py:195
  75.7 72.4 %copy-start.66 = (f32[1,1024]{1,0:T(1,128)}, f32[1,1024]{1,0:T(1,128)S(1)}, u32[]{:S(2)}) copy-start(f32[1,1024]{1,0:T(1,128)S(1)} %slice_convert_fusion) | copy-start | bytes 12292
  85.5 23.3 %collective-permute-start.8 = (bf16[512,1024]{1,0:T(8,128)(2,1)}, bf16[512,1024]{1,0:T(8,128)(2,1)S(1)}, u32[]{:S(2)}, u32[]{:S(2)}) collective-permute-start(bf16[512,1024]{1,0:T(8,128)(2,1)} %collective-permute-done.5), channel_id=1, source_target_pairs={{0,4},{4,0},{8,12},{12,8},{16,20},{20,16},{24,28},{28,24},{1,5},{5... | collective-permute-start | bytes 3145736 | tf_op jit(solution)/shard_map/ppermute | solution.py:205
  103.6 7.8 %copy-start.12 = (bf16[2,577,512]{2,1,0:T(8,128)(2,1)S(1)}, bf16[2,577,512]{2,1,0:T(8,128)(2,1)}, u32[]{:S(2)}) copy-start(bf16[2,577,512]{2,1,0:T(8,128)(2,1)} %copy_dynamic-update-slice_fusion) | copy-start | bytes 3545092
  112.6 6.2 %collective-permute-start.9 = (bf16[2,577,512]{2,1,0:T(8,128)(2,1)S(1)}, bf16[2,577,512]{2,1,0:T(8,128)(2,1)S(1)}, u32[]{:S(2)}, u32[]{:S(2)}) collective-permute-start(bf16[2,577,512]{2,1,0:T(8,128)(2,1)S(1)} %constant_dynamic-update-slice_fusion), channel_id=1, source_target_pairs={{0,1},{1,0},{2,3},{3,2},{4,5},{5,4},{6,7},{7,6},{8,9},{9,8},{10,11... | collective-permute-start | bytes 3545096 | tf_op jit(solution)/shard_map/ppermute | solution.py:198
  115.4 32.8 %copy-start.77 = (f32[1184,1024]{1,0:T(8,128)}, f32[1184,1024]{1,0:T(8,128)S(1)}, u32[]{:S(2)}) copy-start(f32[1184,1024]{1,0:T(8,128)S(1)} %fusion.69) | copy-start | bytes 14548996
  118.7 19.1 %copy-start.78 = (bf16[1184,1024]{1,0:T(8,128)(2,1)}, bf16[1184,1024]{1,0:T(8,128)(2,1)S(1)}, u32[]{:S(2)}) copy-start(bf16[1184,1024]{1,0:T(8,128)(2,1)S(1)} %get-tuple-element.173) | copy-start | bytes 7274500
  119.8 28.4 %copy-start.7 = (bf16[2,592,1024]{2,1,0:T(8,128)(2,1)}, bf16[2,592,1024]{2,1,0:T(8,128)(2,1)S(1)}, u32[]{:S(2)}) copy-start(bf16[2,592,1024]{2,1,0:T(8,128)(2,1)S(1)} %fusion.28) | copy-start | bytes 7274500
  119.8 25.8 %collective-permute-start.11 = (bf16[512,1024]{1,0:T(8,128)(2,1)}, bf16[512,1024]{1,0:T(8,128)(2,1)S(1)}, u32[]{:S(2)}, u32[]{:S(2)}) collective-permute-start(bf16[512,1024]{1,0:T(8,128)(2,1)} %collective-permute-done.10), channel_id=1, source_target_pairs={{0,4},{4,0},{8,12},{12,8},{16,20},{20,16},{24,28},{28,24},{1,5},{5... | collective-permute-start | bytes 3145736 | tf_op jit(solution)/shard_map/ppermute | solution.py:205
  128.9 6.2 %copy-start.20 = (bf16[1184,1024]{1,0:T(8,128)(2,1)}, bf16[1184,1024]{1,0:T(8,128)(2,1)S(1)}, u32[]{:S(2)}) copy-start(bf16[1184,1024]{1,0:T(8,128)(2,1)S(1)} %multiply_convert_fusion.1) | copy-start | bytes 7274500
  133.3 51.7 %collective-permute-start.12 = (bf16[1024,1024]{1,0:T(8,128)(2,1)}, bf16[1024,1024]{1,0:T(8,128)(2,1)}, u32[]{:S(2)}, u32[]{:S(2)}) collective-permute-start(bf16[1024,1024]{1,0:T(8,128)(2,1)} %convolution_convert_fusion.5), channel_id=1, source_target_pairs={{0,2},{1,3},{2,0},{3,1},{4,6},{5,7},{6,4},{7,5},{8,10},{9,11},{10,... | collective-permute-start | bytes 6291464 | tf_op jit(solution)/shard_map/ppermute | solution.py:195
  161.8 7.3 %all-to-all-start.3 = ((bf16[2,592,1024]{2,1,0:T(8,128)(2,1)}), bf16[2,592,1024]{2,1,0:T(8,128)(2,1)S(1)}, u32[]{:S(2)}, u32[]{:S(2)}) async-start(bf16[2,592,1024]{2,1,0:T(8,128)(2,1)} %bitcast.150), calls=%async_computation.3 | async-start | bytes 4849664 | tf_op jit(solution)/shard_map/all_to_all | solution.py:202
  166.0 63.6 %collective-permute-start.15 = (bf16[1024,1024]{1,0:T(8,128)(2,1)}, bf16[1024,1024]{1,0:T(8,128)(2,1)}, u32[]{:S(2)}, u32[]{:S(2)}) collective-permute-start(bf16[1024,1024]{1,0:T(8,128)(2,1)} %convolution_convert_fusion.2), channel_id=1, source_target_pairs={{0,2},{1,3},{2,0},{3,1},{4,6},{5,7},{6,4},{7,5},{8,10},{9,11},{10,... | collective-permute-start | bytes 6291464 | tf_op jit(solution)/shard_map/ppermute | solution.py:195
  176.2 5.8 %copy-start.23 = (bf16[1184,1024]{1,0:T(8,128)(2,1)S(1)}, bf16[1184,1024]{1,0:T(8,128)(2,1)}, u32[]{:S(2)}) copy-start(bf16[1184,1024]{1,0:T(8,128)(2,1)} %copy-done.22) | copy-start | bytes 7274500
  182.0 7.8 %copy-start.17 = (bf16[2,592,1024]{2,1,0:T(8,128)(2,1)}, bf16[2,592,1024]{2,1,0:T(8,128)(2,1)S(1)}, u32[]{:S(2)}) copy-start(bf16[2,592,1024]{2,1,0:T(8,128)(2,1)S(1)} %all_to_all.48) | copy-start | bytes 7274500
  188.9 25.5 %collective-permute-start.13 = (bf16[512,1024]{1,0:T(8,128)(2,1)}, bf16[512,1024]{1,0:T(8,128)(2,1)}, u32[]{:S(2)}, u32[]{:S(2)}) collective-permute-start(bf16[512,1024]{1,0:T(8,128)(2,1)} %get-tuple-element.144), channel_id=1, source_target_pairs={{0,4},{4,0},{8,12},{12,8},{16,20},{20,16},{24,28},{28,24},{1,5},{5... | collective-permute-start | bytes 3145736 | tf_op jit(solution)/shard_map/ppermute | solution.py:205
  204.6 13.2 %copy-start.18 = (bf16[2,592,1024]{2,1,0:T(8,128)(2,1)S(1)}, bf16[2,592,1024]{2,1,0:T(8,128)(2,1)}, u32[]{:S(2)}) copy-start(bf16[2,592,1024]{2,1,0:T(8,128)(2,1)} %copy-done.17) | copy-start | bytes 7274500
  204.6 13.2 %copy-start.46 = (bf16[1184,256]{1,0:T(8,128)(2,1)S(1)}, bf16[1184,256]{1,0:T(8,128)(2,1)}, u32[]{:S(2)}) copy-start(bf16[1184,256]{1,0:T(8,128)(2,1)} %get-tuple-element.146) | copy-start | bytes 1818628
  216.2 17.1 %collective-permute-start.14 = (bf16[256,1024]{1,0:T(8,128)(2,1)S(1)}, bf16[256,1024]{1,0:T(8,128)(2,1)S(1)}, u32[]{:S(2)}, u32[]{:S(2)}) collective-permute-start(bf16[256,1024]{1,0:T(8,128)(2,1)S(1)} %get-tuple-element.151), channel_id=1, source_target_pairs={{0,8},{4,12},{8,0},{12,4},{16,24},{20,28},{24,16},{28,20},{1,9},{5... | collective-permute-start | bytes 1572872 | tf_op jit(solution)/shard_map/ppermute | solution.py:205
  222.7 51.9 %collective-permute-start.19 = (bf16[1024,1024]{1,0:T(8,128)(2,1)}, bf16[1024,1024]{1,0:T(8,128)(2,1)}, u32[]{:S(2)}, u32[]{:S(2)}) collective-permute-start(bf16[1024,1024]{1,0:T(8,128)(2,1)} %pad_maximum_fusion), channel_id=1, source_target_pairs={{0,2},{1,3},{2,0},{3,1},{4,6},{5,7},{6,4},{7,5},{8,10},{9,11},{10,... | collective-permute-start | bytes 6291464 | tf_op jit(solution)/shard_map/ppermute | solution.py:195
  234.3 25.0 %collective-permute-start.17 = (bf16[256,1024]{1,0:T(8,128)(2,1)}, bf16[256,1024]{1,0:T(8,128)(2,1)}, u32[]{:S(2)}, u32[]{:S(2)}) collective-permute-start(bf16[256,1024]{1,0:T(8,128)(2,1)} %add_convert_fusion.14), channel_id=1, source_target_pairs={{0,16},{4,20},{8,24},{12,28},{16,0},{20,4},{24,8},{28,12},{1,17},{... | collective-permute-start | bytes 1572872 | tf_op jit(solution)/shard_map/ppermute | solution.py:205
  236.9 24.6 %collective-permute-start.16 = (bf16[512,1024]{1,0:T(8,128)(2,1)}, bf16[512,1024]{1,0:T(8,128)(2,1)}, u32[]{:S(2)}, u32[]{:S(2)}) collective-permute-start(bf16[512,1024]{1,0:T(8,128)(2,1)} %get-tuple-element.158), channel_id=1, source_target_pairs={{0,4},{4,0},{8,12},{12,8},{16,20},{20,16},{24,28},{28,24},{1,5},{5... | collective-permute-start | bytes 3145736 | tf_op jit(solution)/shard_map/ppermute | solution.py:205
  263.4 14.9 %collective-permute-start.18 = (bf16[256,1024]{1,0:T(8,128)(2,1)S(1)}, bf16[256,1024]{1,0:T(8,128)(2,1)S(1)}, u32[]{:S(2)}, u32[]{:S(2)}) collective-permute-start(bf16[256,1024]{1,0:T(8,128)(2,1)S(1)} %get-tuple-element.165), channel_id=1, source_target_pairs={{0,8},{4,12},{8,0},{12,4},{16,24},{20,28},{24,16},{28,20},{1,9},{5... | collective-permute-start | bytes 1572872 | tf_op jit(solution)/shard_map/ppermute | solution.py:205
  264.1 27.2 %collective-permute-start.20 = (bf16[256,1024]{1,0:T(8,128)(2,1)}, bf16[256,1024]{1,0:T(8,128)(2,1)}, u32[]{:S(2)}, u32[]{:S(2)}) collective-permute-start(bf16[256,1024]{1,0:T(8,128)(2,1)} %add_convert_fusion.13), channel_id=1, source_target_pairs={{0,8},{4,12},{8,0},{12,4},{16,24},{20,28},{24,16},{28,20},{1,9},{5... | collective-permute-start | bytes 1572872 | tf_op jit(solution)/shard_map/ppermute | solution.py:205
  279.9 8.4 %all-to-all-start.5 = ((bf16[2,592,1024]{2,1,0:T(8,128)(2,1)}), bf16[2,592,1024]{2,1,0:T(8,128)(2,1)}, u32[]{:S(2)}, u32[]{:S(2)}) async-start(bf16[2,592,1024]{2,1,0:T(8,128)(2,1)} %bitcast.174), calls=%async_computation.5 | async-start | bytes 4849664 | tf_op jit(solution)/shard_map/all_to_all | solution.py:202
  285.1 26.6 %collective-permute-start.21 = (bf16[256,1024]{1,0:T(8,128)(2,1)S(1)}, bf16[256,1024]{1,0:T(8,128)(2,1)}, u32[]{:S(2)}, u32[]{:S(2)}) collective-permute-start(bf16[256,1024]{1,0:T(8,128)(2,1)S(1)} %add_convert_fusion.12), channel_id=1, source_target_pairs={{0,16},{4,20},{8,24},{12,28},{16,0},{20,4},{24,8},{28,12},{1,17},{... | collective-permute-start | bytes 1572872 | tf_op jit(solution)/shard_map/ppermute | solution.py:205
  287.2 26.6 %collective-permute-start.22 = (bf16[512,1024]{1,0:T(8,128)(2,1)}, bf16[512,1024]{1,0:T(8,128)(2,1)}, u32[]{:S(2)}, u32[]{:S(2)}) collective-permute-start(bf16[512,1024]{1,0:T(8,128)(2,1)} %get-tuple-element.180), channel_id=1, source_target_pairs={{0,4},{4,0},{8,12},{12,8},{16,20},{20,16},{24,28},{28,24},{1,5},{5... | collective-permute-start | bytes 3145736 | tf_op jit(solution)/shard_map/ppermute | solution.py:205
  296.6 14.1 %collective-permute-start.23 = (f32[6144]{0:T(1024)S(1)}, f32[6144]{0:T(1024)S(1)}, u32[]{:S(2)}, u32[]{:S(2)}) collective-permute-start(f32[6144]{0:T(1024)S(1)} %constant_dynamic-update-slice_fusion.2), channel_id=1, source_target_pairs={{0,1},{1,0},{2,3},{3,2},{4,5},{5,4},{6,7},{7,6},{8,9},{9,8},{10,11... | collective-permute-start | bytes 73736 | tf_op jit(solution)/shard_map/ppermute | solution.py:198
  316.3 15.1 %collective-permute-start.33 = (bf16[256,1024]{1,0:T(8,128)(2,1)}, bf16[256,1024]{1,0:T(8,128)(2,1)}, u32[]{:S(2)}, u32[]{:S(2)}) collective-permute-start(bf16[256,1024]{1,0:T(8,128)(2,1)} %add_convert_fusion.11), channel_id=1, source_target_pairs={{0,8},{4,12},{8,0},{12,4},{16,24},{20,28},{24,16},{28,20},{1,9},{5... | collective-permute-start | bytes 1572872 | tf_op jit(solution)/shard_map/ppermute | solution.py:205
  317.4 24.1 %collective-permute-start.24 = (bf16[256,1024]{1,0:T(8,128)(2,1)}, bf16[256,1024]{1,0:T(8,128)(2,1)}, u32[]{:S(2)}, u32[]{:S(2)}) collective-permute-start(bf16[256,1024]{1,0:T(8,128)(2,1)} %get-tuple-element.186), channel_id=1, source_target_pairs={{0,8},{4,12},{8,0},{12,4},{16,24},{20,28},{24,16},{28,20},{1,9},{5... | collective-permute-start | bytes 1572872 | tf_op jit(solution)/shard_map/ppermute | solution.py:205
  318.3 52.7 %collective-permute-start.35 = (bf16[512,1024]{1,0:T(8,128)(2,1)}, bf16[512,1024]{1,0:T(8,128)(2,1)}, u32[]{:S(2)}, u32[]{:S(2)}) collective-permute-start(bf16[512,1024]{1,0:T(8,128)(2,1)} %maximum_select_fusion.3), channel_id=1, source_target_pairs={{0,4},{4,0},{8,12},{12,8},{16,20},{20,16},{24,28},{28,24},{1,5},{5... | collective-permute-start | bytes 3145736 | tf_op jit(solution)/shard_map/ppermute | solution.py:205
  318.9 8.2 %all-to-all-start.7 = ((bf16[2,592,1024]{2,1,0:T(8,128)(2,1)}), bf16[2,592,1024]{2,1,0:T(8,128)(2,1)}, u32[]{:S(2)}, u32[]{:S(2)}) async-start(bf16[2,592,1024]{2,1,0:T(8,128)(2,1)} %bitcast.169), calls=%async_computation.7 | async-start | bytes 4849664 | tf_op jit(solution)/shard_map/all_to_all | solution.py:202
  323.9 6.4 %collective-permute-start.25 = (f32[7680]{0:T(1024)}, f32[7680]{0:T(1024)}, u32[]{:S(2)}, u32[]{:S(2)}) collective-permute-start(f32[7680]{0:T(1024)} %get-tuple-element.188), channel_id=1, source_target_pairs={{0,2},{1,3},{2,0},{3,1},{4,6},{5,7},{6,4},{7,5},{8,10},{9,11},{10,... | collective-permute-start | bytes 92168 | tf_op jit(solution)/shard_map/ppermute | solution.py:195
  334.4 52.1 %collective-permute-start.34 = (bf16[512,1024]{1,0:T(8,128)(2,1)}, bf16[512,1024]{1,0:T(8,128)(2,1)}, u32[]{:S(2)}, u32[]{:S(2)}) collective-permute-start(bf16[512,1024]{1,0:T(8,128)(2,1)} %maximum_select_fusion.5), channel_id=1, source_target_pairs={{0,4},{4,0},{8,12},{12,8},{16,20},{20,16},{24,28},{28,24},{1,5},{5... | collective-permute-start | bytes 3145736 | tf_op jit(solution)/shard_map/ppermute | solution.py:205
  342.8 9.5 %collective-permute-start.27 = (f32[7680]{0:T(1024)S(1)}, f32[7680]{0:T(1024)S(1)}, u32[]{:S(2)}, u32[]{:S(2)}) collective-permute-start(f32[7680]{0:T(1024)S(1)} %add.334), channel_id=1, source_target_pairs={{0,8},{4,12},{8,0},{12,4},{16,24},{20,28},{24,16},{28,20},{1,9},{5... | collective-permute-start | bytes 92168 | tf_op jit(solution)/shard_map/ppermute | solution.py:205
  344.3 26.4 %collective-permute-start.28 = (bf16[256,1024]{1,0:T(8,128)(2,1)S(1)}, bf16[256,1024]{1,0:T(8,128)(2,1)S(1)}, u32[]{:S(2)}, u32[]{:S(2)}) collective-permute-start(bf16[256,1024]{1,0:T(8,128)(2,1)S(1)} %add_convert_fusion.10), channel_id=1, source_target_pairs={{0,16},{4,20},{8,24},{12,28},{16,0},{20,4},{24,8},{28,12},{1,17},{... | collective-permute-start | bytes 1572872 | tf_op jit(solution)/shard_map/ppermute | solution.py:205
  352.3 18.4 %collective-permute-start.29 = (f32[7680]{0:T(1024)S(1)}, f32[7680]{0:T(1024)S(1)}, u32[]{:S(2)}, u32[]{:S(2)}) collective-permute-start(f32[7680]{0:T(1024)S(1)} %add.335), channel_id=1, source_target_pairs={{0,16},{4,20},{8,24},{12,28},{16,0},{20,4},{24,8},{28,12},{1,17},{... | collective-permute-start | bytes 92168 | tf_op jit(solution)/shard_map/ppermute | solution.py:205
  353.0 18.0 %copy-start.11 = (bf16[512,1024]{1,0:T(8,128)(2,1)S(1)}, bf16[512,1024]{1,0:T(8,128)(2,1)}, u32[]{:S(2)}) copy-start(bf16[512,1024]{1,0:T(8,128)(2,1)} %maximum_select_fusion.3) | copy-start | bytes 3145732
  354.9 35.8 %collective-permute-start.26 = (bf16[2,577,512]{2,0,1:T(2,128)(2,1)}, bf16[2,577,512]{2,0,1:T(2,128)(2,1)}, u32[]{:S(2)}, u32[]{:S(2)}) collective-permute-start(bf16[2,577,512]{2,0,1:T(2,128)(2,1)} %copy.58), channel_id=1, source_target_pairs={{0,2},{1,3},{2,0},{3,1},{4,6},{5,7},{6,4},{7,5},{8,10},{9,11},{10,... | collective-permute-start | bytes 3545096 | tf_op jit(solution)/shard_map/ppermute | solution.py:195
  370.9 13.4 %collective-permute-start.30 = (bf16[256,1024]{1,0:T(8,128)(2,1)S(1)}, bf16[256,1024]{1,0:T(8,128)(2,1)S(1)}, u32[]{:S(2)}, u32[]{:S(2)}) collective-permute-start(bf16[256,1024]{1,0:T(8,128)(2,1)S(1)} %add_convert_fusion.9), channel_id=1, source_target_pairs={{0,8},{4,12},{8,0},{12,4},{16,24},{20,28},{24,16},{28,20},{1,9},{5... | collective-permute-start | bytes 1572872 | tf_op jit(solution)/shard_map/ppermute | solution.py:205
  372.3 4.0 collective-permute-start.32
  384.7 24.1 %collective-permute-start.31 = (bf16[512,1024]{1,0:T(8,128)(2,1)S(1)}, bf16[512,1024]{1,0:T(8,128)(2,1)S(1)}, u32[]{:S(2)}, u32[]{:S(2)}) collective-permute-start(bf16[512,1024]{1,0:T(8,128)(2,1)S(1)} %maximum_select_fusion.4), channel_id=1, source_target_pairs={{0,4},{4,0},{8,12},{12,8},{16,20},{20,16},{24,28},{28,24},{1,5},{5... | collective-permute-start | bytes 3145736 | tf_op jit(solution)/shard_map/ppermute | solution.py:205
  (59 other events, 190.8 us)
